TPU v7x, 32 devices: a whole 2x2x4 slice. The times are simulated.
32 devices in a mesh: orbit: 4 (over x, core), group: 8 (over z, y).
Axes of the slice: x: 2, y: 2, z: 4, core: 2. Of those that a mesh axis runs over, the one named last changes fastest.
Arguments:
- along_jac: bfloat16 [8, 64, 2, 128, 256], P('group', 'orbit'), may hold values from -0.375 to 0.375
- along_res: float32 [8, 64, 2, 128], P('group', 'orbit'), may hold values from -6 to 6
- along_e: float32 [8, 64, 2, 128], P('group', 'orbit'), may hold values from -6 to 6
- along_count: int32 [8, 64], P('group', 'orbit'), may hold values from 32 to 128, as said below
- damping: float32 [8, 64], P('group', 'orbit'), may hold values from 0.05 to 1
- cross_jac: bfloat16 [8, 256, 2, 128, 256], P('group', 'orbit'), may hold values from -0.375 to 0.375
- cross_res: float32 [8, 256, 2, 128], P('group', 'orbit'), may hold values from -6 to 6
- cross_e: float32 [8, 256, 2, 128], P('group', 'orbit'), may hold values from -6 to 6
- cross_own: int32 [8, 256], P('group', 'orbit'), may hold values from 0 to 15
- cross_group: int32 [8, 256, 1], P('group', 'orbit'), may hold values from 0 to 7; in each aligned block of 64 rows (0 to 63, 64 to 127, ..., all dimensions but the last counted through in order) at most 16 rows name the same one
- cross_other: int32 [8, 256], P('group', 'orbit'), may hold values from 0 to 15
Outputs:
- solution: float32 [8, 64, 256], P('group', 'orbit')
- residual: float32 [8, 64, 256], P('group', 'orbit')
Inputs may be any that keep to these rules, and one draw needn't show every extreme that they name: along_count of some scene equals 128 in every draw, and every count is at least 32. `cross_group`: among the 64 crossover blocks of one device no partner group is named more than 16 times, a bound that some block reaches.
All inputs are finite; a program needn't handle non-finite values.
Results may differ from a plain program's by a relative error of at most 0.015.
Values may be sent and summed in bfloat16 or wider, within the bound.
No kernel may reach another device: no remote copies, remote signals or barrier semaphores. Data moves between devices by JAX's collectives and lax.ppermute only.
A program may use at most 64 MiB of HBM per device.

v0:
```python
import jax
import jax.numpy as jnp
from jax import lax
from jax.sharding import PartitionSpec as P

ITERS = 4


def passed_along(block, axis, distance):
    devices = range(lax.axis_size(axis))
    route = [((i - distance) % len(devices), i) for i in devices]
    return lax.ppermute(block, axis, route)


def project(jac, va, vb):
    r1 = jnp.einsum("btp,bp->bt", jac[:, 0], va, preferred_element_type=jnp.float32)
    r2 = jnp.einsum("btp,bp->bt", jac[:, 1], vb, preferred_element_type=jnp.float32)
    return (r1, r2)


def settle(jac, heights, r1, r2):
    e1 = heights[:, 0]
    e2 = heights[:, 1]
    z = (e1 * r1 + e2 * r2) / (1.0 + e1 * e1 + e2 * e2)
    q1 = (r1 - e1 * z).astype(jnp.bfloat16)
    q2 = (r2 - e2 * z).astype(jnp.bfloat16)
    t1 = jnp.einsum("btp,bt->bp", jac[:, 0], q1, preferred_element_type=jnp.float32)
    t2 = jnp.einsum("btp,bt->bp", jac[:, 1], q2, preferred_element_type=jnp.float32)
    return (t1, t2)


def on_device(
    along_jac,
    along_res,
    along_e,
    along_count,
    damping,
    cross_jac,
    cross_res,
    cross_e,
    cross_own,
    cross_group,
    cross_other,
):
    ajac = along_jac[0]
    ares = along_res[0]
    aheights = along_e[0]
    counts = along_count[0]
    scene_damp = damping[0]
    cjac = cross_jac[0]
    cres = cross_res[0]
    cheights = cross_e[0]
    own = cross_own[0]
    partner = cross_group[0, :, 0]
    other = cross_other[0]
    scenes = ajac.shape[0]
    ties = ajac.shape[2]
    width = ajac.shape[3]
    links = cjac.shape[0]
    groups = lax.axis_size("group")
    slots = max(2, 2 * links // groups)
    highest = lax.Precision.HIGHEST
    live = (jnp.arange(ties)[None, :] < counts[:, None]).astype(jnp.float32)
    own_table = (own[:, None] == jnp.arange(scenes)[None, :]).astype(jnp.float32)
    member = (partner[:, None] == jnp.arange(groups)[None, :]).astype(jnp.int32)
    before = jnp.cumsum(member, axis=0) - member
    rank = jnp.sum(before * member, axis=1)
    slot = partner * slots + rank
    slot_ints = (slot[:, None] == jnp.arange(groups * slots)[None, :]).astype(jnp.int32)
    asked = jnp.sum(slot_ints * other[:, None], axis=0).reshape(groups, slots)
    filled = jnp.sum(slot_ints, axis=0).reshape(groups, slots)
    got_index, got_live = (
        lax.all_to_all(asked, "group", split_axis=0, concat_axis=0, tiled=True),
        lax.all_to_all(filled, "group", split_axis=0, concat_axis=0, tiled=True),
    )
    got_index = got_index.reshape(-1)
    got_live = got_live.reshape(-1)
    recv_table = (
        (got_index[:, None] == jnp.arange(scenes)[None, :]) & (got_live[:, None] > 0)
    ).astype(jnp.float32)
    slot_table = slot_ints.astype(jnp.float32)
    live_rows = got_live[:, None].astype(jnp.bfloat16)

    def deliver(terms):
        placed = jnp.dot(slot_table.T, terms, precision=highest)
        back = lax.all_to_all(
            placed.reshape(groups, slots, width), "group", split_axis=0, concat_axis=0, tiled=True
        )
        return jnp.dot(recv_table.T, back.reshape(groups * slots, width), precision=highest)

    def backward(a1, a2, c1, c2):
        t1, t2 = settle(ajac, aheights, a1, a2)
        tail = passed_along(t2[-1:], "orbit", 1)
        out = t1 + jnp.concatenate([tail, t2[:-1]], axis=0)
        u1, u2 = settle(cjac, cheights, c1, c2)
        out = out + jnp.dot(own_table.T, u1, precision=highest)
        return out + deliver(u2)

    def squares(vector):
        return lax.psum(jnp.sum(vector * vector), ("orbit", "group"))

    rhs = -backward(ares[:, 0] * live, ares[:, 1] * live, cres[:, 0], cres[:, 1])
    solution = jnp.zeros_like(rhs)
    residual = rhs
    direction = rhs
    norm_now = squares(residual)
    for step in range(ITERS):
        operate_rounded = direction.astype(jnp.bfloat16)
        following = passed_along(operate_rounded[:1], "orbit", -1)
        shifted = jnp.concatenate([operate_rounded[1:], following], axis=0)
        operate_a1, operate_a2 = project(ajac, operate_rounded, shifted)
        sent = operate_rounded[got_index] * live_rows
        fetch_back = lax.all_to_all(
            sent.reshape(groups, slots, width), "group", split_axis=0, concat_axis=0, tiled=True
        )
        operate_c1, operate_c2 = project(
            cjac, operate_rounded[own], fetch_back.reshape(groups * slots, width)[slot]
        )
        image = scene_damp[:, None] * direction + backward(
            operate_a1 * live, operate_a2 * live, operate_c1, operate_c2
        )
        alpha = norm_now / lax.psum(jnp.sum(direction * image), ("orbit", "group"))
        solution = solution + alpha * direction
        residual = residual - alpha * image
        norm_next = squares(residual)
        direction = residual + norm_next / norm_now * direction
        norm_now = norm_next
    return (solution[None], residual[None])


def solution(mesh):
    placed = (
        P("group", "orbit", None, None, None),
        P("group", "orbit", None, None),
        P("group", "orbit", None, None),
        P("group", "orbit"),
        P("group", "orbit"),
        P("group", "orbit", None, None, None),
        P("group", "orbit", None, None),
        P("group", "orbit", None, None),
        P("group", "orbit"),
        P("group", "orbit", None),
        P("group", "orbit"),
    )
    return jax.shard_map(
        on_device,
        mesh=mesh,
        in_specs=placed,
        out_specs=(P("group", "orbit", None), P("group", "orbit", None)),
        check_vma=False,
    )
```

profile of v0, /device:TPU:0, one launch (start us, length us, event | category | flops | bytes accessed | tf_op | source)
XLA Modules:
  0.0 484.8 jit_solution(4477345328644448425)
XLA Ops:
  4.4 7.3 %all-to-all-start = ((s32[8,1,16]{2,1,0:T(1,128)}), s32[8,1,16]{2,1,0:T(1,128)S(1)}, u32[]{:S(2)}, u32[]{:S(2)}) async-start(s32[8,1,16]{2,1,0:T(1,128)} %bitcast.27), calls=%async_computation | async-start | bytes 8192 | tf_op jit(solution)/shard_map/all_to_all | solution.py:73
  14.0 1.5 fusion.84
  16.2 1.0 fusion.196
  18.0 3.0 fusion.17
  21.0 1.0 fusion.34
  22.1 2.8 fusion.8
  25.9 6.0 %all-to-all-start.1 = ((s32[8,1,16]{2,1,0:T(1,128)}), s32[8,1,16]{2,1,0:T(1,128)S(1)}, u32[]{:S(2)}, u32[]{:S(2)}) async-start(s32[8,1,16]{2,1,0:T(1,128)} %bitcast.28), calls=%async_computation.1 | async-start | bytes 8192 | tf_op jit(solution)/shard_map/all_to_all | solution.py:74
  32.0 6.3 %all-to-all-done.1 = s32[8,1,16]{2,1,0:T(1,128)S(1)} async-done(((s32[8,1,16]{2,1,0:T(1,128)}), s32[8,1,16]{2,1,0:T(1,128)S(1)}, u32[]{:S(2)}, u32[]{:S(2)}) %all-to-all-start.1) | async-done | bytes 544 | tf_op jit(solution)/shard_map/all_to_all | solution.py:74
  38.3 3.5 all-to-all-start.2
  43.2 6.1 %all-to-all-done.2 = f32[8,16,256]{2,1,0:T(8,128)S(1)} async-done(((f32[8,16,256]{2,1,0:T(8,128)}), f32[8,16,256]{2,1,0:T(8,128)S(1)}, u32[]{:S(2)}, u32[]{:S(2)}) %all-to-all-start.2) | async-done | bytes 131104 | tf_op jit(solution)/shard_map/all_to_all | solution.py:86
  50.6 3.4 fusion.7
  55.6 3.3 all-to-all-start.3
  59.4 0.9 collective-permute-done.1
  61.0 1.4 collective-permute-start.2
  62.6 3.1 all-to-all-done.3
  66.5 3.4 fusion.16
  69.9 2.8 fusion.15
  72.8 1.0 fusion.30
  73.8 3.4 all-to-all-start.4
  77.2 2.8 fusion.6
  80.0 4.4 all-to-all-done.4
  85.6 38.4 %all-reduce = (f32[]{:T(128)}, f32[]{:T(128)}) all-reduce(f32[]{:T(128)} %get-tuple-element.3, f32[]{:T(128)} %get-tuple-element.2), channel_id=1, replica_groups=mesh['orbit'=4,'group'=8] {'orbit','group'}, use_global_device_ids=true, to_apply=%region_5.6 | all-reduce | flops 2 | bytes 16 | tf_op jit(solution)/shard_map/psum | solution.py:100
  126.0 41.0 %psum.58 = f32[]{:T(128)} all-reduce(f32[]{:T(128)} %multiply_reduce_fusion.5), channel_id=1, replica_groups=mesh['orbit'=4,'group'=8] {'orbit','group'}, use_global_device_ids=true, to_apply=%region_9.10 | all-reduce | flops 1 | bytes 8 | tf_op jit(solution)/shard_map/psum | solution.py:100
  170.0 3.4 fusion.5
  174.1 4.7 all-to-all-start.5
  179.2 0.9 collective-permute-done.3
  180.8 1.2 collective-permute-start.4
  182.3 3.4 all-to-all-done.5
  186.4 3.4 fusion.14
  189.8 2.8 fusion.13
  192.7 1.0 fusion.26
  193.7 3.4 all-to-all-start.6
  197.1 2.8 fusion.4
  199.9 4.4 all-to-all-done.6
  204.6 0.9 multiply_reduce_fusion.4
  205.5 38.0 %psum.59 = f32[]{:T(128)} all-reduce(f32[]{:T(128)} %get-tuple-element.45), channel_id=1, replica_groups=mesh['orbit'=4,'group'=8] {'orbit','group'}, use_global_device_ids=true, to_apply=%region_11.12 | all-reduce | flops 1 | bytes 8 | tf_op jit(solution)/shard_map/psum | solution.py:122
  245.5 41.1 %psum.60 = f32[]{:T(128)} all-reduce(f32[]{:T(128)} %get-tuple-element.14), channel_id=1, replica_groups=mesh['orbit'=4,'group'=8] {'orbit','group'}, use_global_device_ids=true, to_apply=%region_13.14 | all-reduce | flops 1 | bytes 8 | tf_op jit(solution)/shard_map/psum | solution.py:100
  289.5 3.4 fusion.3
  293.6 4.7 all-to-all-start.7
  298.7 0.9 collective-permute-done.5
  300.3 1.2 collective-permute-start.6
  301.8 3.4 all-to-all-done.7
  305.9 3.4 fusion.12
  309.3 2.8 fusion.11
  312.2 1.0 fusion.22
  313.2 3.4 all-to-all-start.8
  316.6 2.8 fusion.2
  319.4 4.4 all-to-all-done.8
  324.2 0.9 multiply_reduce_fusion.2
  325.0 38.2 %psum.61 = f32[]{:T(128)} all-reduce(f32[]{:T(128)} %get-tuple-element.47), channel_id=1, replica_groups=mesh['orbit'=4,'group'=8] {'orbit','group'}, use_global_device_ids=true, to_apply=%region_15.16 | all-reduce | flops 1 | bytes 8 | tf_op jit(solution)/shard_map/psum | solution.py:122
  365.2 41.1 %psum.62 = f32[]{:T(128)} all-reduce(f32[]{:T(128)} %get-tuple-element.10), channel_id=1, replica_groups=mesh['orbit'=4,'group'=8] {'orbit','group'}, use_global_device_ids=true, to_apply=%region_17.18 | all-reduce | flops 1 | bytes 8 | tf_op jit(solution)/shard_map/psum | solution.py:100
  409.2 3.4 fusion.1
  413.3 4.7 all-to-all-start.9
  418.4 0.9 collective-permute-done.7
  420.1 1.3 collective-permute-start.8
  421.6 3.3 all-to-all-done.9
  425.6 3.4 fusion.10
  429.1 2.8 fusion.9
  431.9 1.0 fusion.18
  432.9 3.4 all-to-all-start.10
  436.3 2.8 fusion
  439.2 4.4 all-to-all-done.10
  443.9 0.9 multiply_reduce_fusion
  444.8 38.0 %psum.63 = f32[]{:T(128)} all-reduce(f32[]{:T(128)} %get-tuple-element.49), channel_id=1, replica_groups=mesh['orbit'=4,'group'=8] {'orbit','group'}, use_global_device_ids=true, to_apply=%region_19.20 | all-reduce | flops 1 | bytes 8 | tf_op jit(solution)/shard_map/psum | solution.py:122
  (121 shorter events, 32.6 us)
Async XLA Ops:
  4.4 21.5 %all-to-all-start = ((s32[8,1,16]{2,1,0:T(1,128)}), s32[8,1,16]{2,1,0:T(1,128)S(1)}, u32[]{:S(2)}, u32[]{:S(2)}) async-start(s32[8,1,16]{2,1,0:T(1,128)} %bitcast.27), calls=%async_computation | async-start | bytes 8192 | tf_op jit(solution)/shard_map/all_to_all | solution.py:73
  15.4 34.2 %collective-permute-start = (f32[1,256]{1,0:T(1,128)S(1)}, f32[1,256]{1,0:T(1,128)S(1)}, u32[]{:S(2)}, u32[]{:S(2)}) collective-permute-start(f32[1,256]{1,0:T(1,128)S(1)} %slice.198), channel_id=1, source_target_pairs={{24,0},{0,8},{8,16},{16,24},{25,1},{1,9},{9,17},{17,25},{26,2},{2,... | collective-permute-start | bytes 3080 | tf_op jit(solution)/shard_map/ppermute | solution.py:12
  18.0 6.9 %copy-start = (bf16[1,16,2,128,256]{4,3,2,1,0:T(8,128)(2,1)S(1)}, bf16[1,16,2,128,256]{4,3,2,1,0:T(8,128)(2,1)}, u32[]{:S(2)}) copy-start(bf16[1,16,2,128,256]{4,3,2,1,0:T(8,128)(2,1)} %param.11) | copy-start | bytes 6291460
  18.0 7.1 %copy-start.1 = (s32[1,64]{1,0:T(1,128)S(1)}, s32[1,64]{1,0:T(1,128)}, u32[]{:S(2)}) copy-start(s32[1,64]{1,0:T(1,128)} %param.19) | copy-start | bytes 772
  25.9 12.4 %all-to-all-start.1 = ((s32[8,1,16]{2,1,0:T(1,128)}), s32[8,1,16]{2,1,0:T(1,128)S(1)}, u32[]{:S(2)}, u32[]{:S(2)}) async-start(s32[8,1,16]{2,1,0:T(1,128)} %bitcast.28), calls=%async_computation.1 | async-start | bytes 8192 | tf_op jit(solution)/shard_map/all_to_all | solution.py:74
  38.3 22.4 %copy-start.2 = (s32[1,16]{1,0:T(1,128)S(1)}, s32[1,16]{1,0:T(1,128)}, u32[]{:S(2)}) copy-start(s32[1,16]{1,0:T(1,128)} %param.14) | copy-start | bytes 196
  38.3 11.0 %all-to-all-start.2 = ((f32[8,16,256]{2,1,0:T(8,128)}), f32[8,16,256]{2,1,0:T(8,128)S(1)}, u32[]{:S(2)}, u32[]{:S(2)}) async-start(f32[8,16,256]{2,1,0:T(8,128)} %bitcast.32), calls=%async_computation.2 | async-start | bytes 262144 | tf_op jit(solution)/shard_map/all_to_all | solution.py:86
  55.6 10.2 %all-to-all-start.3 = ((bf16[8,16,256]{2,1,0:T(8,128)(2,1)}), bf16[8,16,256]{2,1,0:T(8,128)(2,1)S(1)}, u32[]{:S(2)}, u32[]{:S(2)}) async-start(bf16[8,16,256]{2,1,0:T(8,128)(2,1)} %broadcast_multiply_fusion.3), calls=%async_computation.3 | async-start | bytes 131072 | tf_op jit(solution)/shard_map/all_to_all | solution.py:113
  58.9 1.4 collective-permute-start.1
  61.0 23.7 %collective-permute-start.2 = (f32[1,256]{1,0:T(1,128)S(1)}, f32[1,256]{1,0:T(1,128)S(1)}, u32[]{:S(2)}, u32[]{:S(2)}) collective-permute-start(f32[1,256]{1,0:T(1,128)S(1)} %slice.208), channel_id=1, source_target_pairs={{24,0},{0,8},{8,16},{16,24},{25,1},{1,9},{9,17},{17,25},{26,2},{2,... | collective-permute-start | bytes 3080 | tf_op jit(solution)/shard_map/ppermute | solution.py:12
  69.9 14.8 %copy-start.3 = (f32[1,16]{1,0:T(1,128)S(1)}, f32[1,16]{1,0:T(1,128)}, u32[]{:S(2)}) copy-start(f32[1,16]{1,0:T(1,128)} %param.15) | copy-start | bytes 196
  73.8 10.7 %all-to-all-start.4 = ((f32[8,16,256]{2,1,0:T(8,128)}), f32[8,16,256]{2,1,0:T(8,128)S(1)}, u32[]{:S(2)}, u32[]{:S(2)}) async-start(f32[8,16,256]{2,1,0:T(8,128)} %bitcast.65), calls=%async_computation.4 | async-start | bytes 262144 | tf_op jit(solution)/shard_map/all_to_all | solution.py:86
  174.1 11.6 %all-to-all-start.5 = ((bf16[8,16,256]{2,1,0:T(8,128)(2,1)}), bf16[8,16,256]{2,1,0:T(8,128)(2,1)S(1)}, u32[]{:S(2)}, u32[]{:S(2)}) async-start(bf16[8,16,256]{2,1,0:T(8,128)(2,1)} %broadcast_multiply_fusion.2), calls=%async_computation.5 | async-start | bytes 131072 | tf_op jit(solution)/shard_map/all_to_all | solution.py:113
  178.8 1.3 collective-permute-start.3
  180.8 23.8 %collective-permute-start.4 = (f32[1,256]{1,0:T(1,128)S(1)}, f32[1,256]{1,0:T(1,128)S(1)}, u32[]{:S(2)}, u32[]{:S(2)}) collective-permute-start(f32[1,256]{1,0:T(1,128)S(1)} %slice.212), channel_id=1, source_target_pairs={{24,0},{0,8},{8,16},{16,24},{25,1},{1,9},{9,17},{17,25},{26,2},{2,... | collective-permute-start | bytes 3080 | tf_op jit(solution)/shard_map/ppermute | solution.py:12
  193.7 10.7 %all-to-all-start.6 = ((f32[8,16,256]{2,1,0:T(8,128)}), f32[8,16,256]{2,1,0:T(8,128)S(1)}, u32[]{:S(2)}, u32[]{:S(2)}) async-start(f32[8,16,256]{2,1,0:T(8,128)} %bitcast.89), calls=%async_computation.6 | async-start | bytes 262144 | tf_op jit(solution)/shard_map/all_to_all | solution.py:86
  293.6 11.6 %all-to-all-start.7 = ((bf16[8,16,256]{2,1,0:T(8,128)(2,1)}), bf16[8,16,256]{2,1,0:T(8,128)(2,1)S(1)}, u32[]{:S(2)}, u32[]{:S(2)}) async-start(bf16[8,16,256]{2,1,0:T(8,128)(2,1)} %broadcast_multiply_fusion.1), calls=%async_computation.7 | async-start | bytes 131072 | tf_op jit(solution)/shard_map/all_to_all | solution.py:113
  298.3 1.3 collective-permute-start.5
  300.3 23.8 %collective-permute-start.6 = (f32[1,256]{1,0:T(1,128)S(1)}, f32[1,256]{1,0:T(1,128)S(1)}, u32[]{:S(2)}, u32[]{:S(2)}) collective-permute-start(f32[1,256]{1,0:T(1,128)S(1)} %slice.216), channel_id=1, source_target_pairs={{24,0},{0,8},{8,16},{16,24},{25,1},{1,9},{9,17},{17,25},{26,2},{2,... | collective-permute-start | bytes 3080 | tf_op jit(solution)/shard_map/ppermute | solution.py:12
  313.2 10.7 %all-to-all-start.8 = ((f32[8,16,256]{2,1,0:T(8,128)}), f32[8,16,256]{2,1,0:T(8,128)S(1)}, u32[]{:S(2)}, u32[]{:S(2)}) async-start(f32[8,16,256]{2,1,0:T(8,128)} %bitcast.113), calls=%async_computation.8 | async-start | bytes 262144 | tf_op jit(solution)/shard_map/all_to_all | solution.py:86
  413.3 11.6 %all-to-all-start.9 = ((bf16[8,16,256]{2,1,0:T(8,128)(2,1)}), bf16[8,16,256]{2,1,0:T(8,128)(2,1)S(1)}, u32[]{:S(2)}, u32[]{:S(2)}) async-start(bf16[8,16,256]{2,1,0:T(8,128)(2,1)} %broadcast_multiply_fusion), calls=%async_computation.9 | async-start | bytes 131072 | tf_op jit(solution)/shard_map/all_to_all | solution.py:113
  418.0 1.3 collective-permute-start.7
  420.1 23.8 %collective-permute-start.8 = (f32[1,256]{1,0:T(1,128)S(1)}, f32[1,256]{1,0:T(1,128)S(1)}, u32[]{:S(2)}, u32[]{:S(2)}) collective-permute-start(f32[1,256]{1,0:T(1,128)S(1)} %slice.220), channel_id=1, source_target_pairs={{24,0},{0,8},{8,16},{16,24},{25,1},{1,9},{9,17},{17,25},{26,2},{2,... | collective-permute-start | bytes 3080 | tf_op jit(solution)/shard_map/ppermute | solution.py:12
  432.9 10.7 %all-to-all-start.10 = ((f32[8,16,256]{2,1,0:T(8,128)}), f32[8,16,256]{2,1,0:T(8,128)S(1)}, u32[]{:S(2)}, u32[]{:S(2)}) async-start(f32[8,16,256]{2,1,0:T(8,128)} %bitcast.137), calls=%async_computation.10 | async-start | bytes 262144 | tf_op jit(solution)/shard_map/all_to_all | solution.py:86
where the time goes:
time: 488 us; the launch traced here: 485 us
  blocking collectives  276 us (57%)
  matrix products  72.7 us (15%)
  starting transfers between devices  53.1 us (11%)
  waiting for transfers between devices  47.1 us (10%)
  local copies, waits for them, and re-layouts  14.6 us (3%)
  other arithmetic  11.1 us (2%)
  between operations  10.4 us (2%)
    psum x4, blocking collectives, squares(): return lax.psum(jnp.sum(vector * vector), ('orbit', 'group'))  162 us
    psum x3, blocking collectives, on_device(): alpha = norm_now / lax.psum(jnp.sum(direction * image), ('orbit', 'group'))  114 us
    all_to_all x5, waiting for transfers between devices, deliver(): lax.all_to_all(placed.reshape(groups, slots, width), 'group', split_axis=...  23.9 us
    all_to_all x4, starting transfers between devices, on_device(): lax.all_to_all(sent.reshape(groups, slots, width), 'group', split_axis=0,...  17.5 us
    all_to_all x5, starting transfers between devices, deliver(): lax.all_to_all(placed.reshape(groups, slots, width), 'group', split_axis=...  17 us
    dot_general x10, matrix products, settle(): jnp.einsum('btp,bt->bp', jac[:, 1], q2, preferred_element_type=jnp.float32)  16.9 us
    dot_general x10, matrix products, settle(): jnp.einsum('btp,bt->bp', jac[:, 0], q1, preferred_element_type=jnp.float32)  15.5 us
    dot_general x8, matrix products, project(): jnp.einsum('btp,bp->bt', jac[:, 1], vb, preferred_element_type=jnp.float32)  15 us
  transfers between devices with their start and end apart: 20, of which 14 were waited for; matrix products, arithmetic and copies ran while one was open for 13% of the time, Pallas kernels for 0%

commit v1 on v0

v1 whole, which is shorter than its diff:
```python
import functools

import jax
import jax.numpy as jnp
from jax import lax
from jax.experimental import pallas as pl
from jax.experimental.pallas import tpu as pltpu
from jax.sharding import PartitionSpec as P

ITERS = 4
F32, BF16 = jnp.float32, jnp.bfloat16
OCTET = 8


def dot(a, b):
    return lax.dot_general(a, b, (((1,), (0,)), ((), ())), preferred_element_type=F32)


def dot_t(a, b):
    return lax.dot_general(a, b, (((1,), (1,)), ((), ())), preferred_element_type=F32)


def halves(x):
    high = x.astype(BF16)
    return high, (x - high.astype(F32)).astype(BF16)


def row_of(shape):
    return lax.broadcasted_iota(jnp.int32, shape, 0)


def octets(refs, body):
    slot = 0
    for ref in refs:
        blocks = ref.shape[0]
        if blocks <= OCTET:
            body(ref, 0, slot, blocks)
        else:

            @pl.loop(0, blocks // OCTET)
            def _(i, ref=ref, slot=slot):
                at = pl.multiple_of(i * OCTET, OCTET)
                body(ref, at, pl.multiple_of(slot + at, OCTET), OCTET)

        slot += -(-blocks // OCTET) * OCTET


def project_kernel(field_ref, pick1_ref, pick2_ref, cjac_ref, ajac_ref, ejac_ref, out_ref, l1_ref, l2_ref):
    ties = out_ref.shape[1] // 2
    high, low = halves(field_ref[...])
    for pick_ref, left_ref in ((pick1_ref, l1_ref), (pick2_ref, l2_ref)):
        left_ref[0] = dot(pick_ref[...], high)
        left_ref[1] = dot(pick_ref[...], low)

    def body(ref, at, slot, count):
        rows = pl.ds(slot, OCTET)
        left = jnp.concatenate([l1_ref[0, rows], l2_ref[0, rows], l1_ref[1, rows], l2_ref[1, rows]])
        left = left.astype(BF16)
        total = jnp.zeros((OCTET, 2 * ties), F32)
        for j in range(count):
            got = dot_t(left, ref[at + j])
            one = got[0:8, :ties] + got[16:24, :ties]
            two = got[8:16, ties:] + got[24:32, ties:]
            got = jnp.concatenate([one, two], axis=1)
            total = jnp.where(row_of(total.shape) == j, got, total)
        out_ref[rows] = total

    octets((cjac_ref, ajac_ref, ejac_ref), body)


def backward(q1_ref, q2_ref, put1_ref, put2_ref, cjac_ref, ajac_ref, ejac_ref, t1_ref, t2_ref):
    ties = q1_ref.shape[1]
    width = t1_ref.shape[1]

    def body(ref, at, slot, count):
        rows = pl.ds(slot, OCTET)
        zero = jnp.zeros((OCTET, ties), F32)
        q1, q2 = q1_ref[rows], q2_ref[rows]
        total = jnp.zeros((2 * OCTET, width), F32)
        for j in range(count):
            chosen = row_of(q1.shape) == j
            top = jnp.concatenate([jnp.where(chosen, q1, 0.0), zero], axis=1)
            low = jnp.concatenate([zero, jnp.where(chosen, q2, 0.0)], axis=1)
            total = total + dot(jnp.concatenate([top, low]).astype(BF16), ref[at + j])
        t1_ref[rows] = total[:OCTET]
        t2_ref[rows] = total[OCTET:]

    octets((cjac_ref, ajac_ref, ejac_ref), body)
    out = None
    for t_ref, put_ref in ((t1_ref, put1_ref), (t2_ref, put2_ref)):
        for part in halves(t_ref[...]):
            term = dot(put_ref[...], part)
            out = term if out is None else out + term
    return out


def rhs_kernel(res_ref, coef_ref, put1_ref, put2_ref, cjac_ref, ajac_ref, ejac_ref, out_ref, q1_ref, q2_ref, t1_ref, t2_ref):
    ties = q1_ref.shape[1]
    r1, r2 = res_ref[:, :ties], res_ref[:, ties:]
    q1_ref[...] = coef_ref[0] * r1 - coef_ref[1] * r2
    q2_ref[...] = coef_ref[2] * r2 - coef_ref[1] * r1
    out = backward(q1_ref, q2_ref, put1_ref, put2_ref, cjac_ref, ajac_ref, ejac_ref, t1_ref, t2_ref)
    out_ref[...] = out.astype(BF16)


def gather_kernel(scenes, start, mine_ref, got_ref, *refs):
    first = pl.multiple_of(lax.axis_index("group") * scenes, scenes)
    field = mine_ref[...].astype(F32) + got_ref[...].astype(F32)
    if start:
        out_ref, packet_ref = refs
        field = -field
    else:
        res_ref, out_ref, packet_ref = refs
    out_ref[...] = field
    packet_ref[...] = jnp.zeros_like(packet_ref)
    if not start:
        res = res_ref[...]
        half = packet_ref.shape[1] // 2
        packet_ref[0:1, :half] = jnp.full((1, half), jnp.sum(res * res), F32)
        packet_ref[0:1, half:] = jnp.full((1, half), jnp.sum(res * field), F32)
    packet_ref[1:2, :] = out_ref[pl.ds(first, OCTET), :][0:1]
    packet_ref[2:3, :] = out_ref[pl.ds(pl.multiple_of(first + scenes - OCTET, OCTET), OCTET), :][OCTET - 1 :]


def outside(packet_refs, ajac_ref, ejac_ref, part_ref, slot):
    _, one, _, three = packet_refs
    ties = part_ref.shape[1] // 2
    last = ajac_ref.shape[0] - 1
    even = lax.axis_index("orbit") % 2 == 0
    after = jnp.where(even, one[1:2, :], three[1:2, :])
    ahead = jnp.where(even, three[2:3, :], one[2:3, :])
    sub = row_of((OCTET, after.shape[1]))
    both = jnp.where(sub == last % OCTET, after, jnp.where(sub == 0, ahead, 0.0))
    high = both.astype(BF16).astype(F32)
    left = jnp.concatenate([high, both - high]).astype(BF16)
    got = dot_t(left, ajac_ref[last])
    got = got[:OCTET] + got[OCTET:]
    tail = pl.ds(slot + last - last % OCTET, OCTET)
    keep = row_of((OCTET, ties)) == last % OCTET
    part_ref[tail, ties:] = part_ref[tail, ties:] + jnp.where(keep, got[:, ties:], 0.0)
    got = dot_t(left, ejac_ref[0])
    got = got[:OCTET] + got[OCTET:]
    tail = pl.ds(slot + last + 1, OCTET)
    keep = row_of((OCTET, ties)) == 0
    part_ref[tail, :ties] = part_ref[tail, :ties] + jnp.where(keep, got[:, :ties], 0.0)


def scalars(packet_refs, scal_ref, step):
    mine, one, two, three = (ref[0:1, :] for ref in packet_refs)
    sums = (mine + one) + (two + three)
    half = sums.shape[1] // 2
    now, along = sums[:, :half], sums[:, half:]
    if step == 0:
        beta = jnp.zeros_like(now)
        alpha = now / along
    else:
        before, last = scal_ref[0:1, :], scal_ref[1:2, :]
        beta = now / before
        alpha = now / (along - beta * now / last)
    return now, alpha, beta


def wide(x):
    return jnp.concatenate([x, x], axis=1)


def step_kernel(step, scenes, *refs):
    refs = list(refs)
    take = lambda n: [refs.pop(0) for _ in range(n)]
    (part_ref,) = take(1)
    packet_refs = take(4)
    coef_ref, put1_ref, put2_ref, damp_ref, cjac_ref, ajac_ref, ejac_ref = take(7)
    (res_ref,) = take(1)
    if step >= 1:
        field_ref, obs_ref, x_ref = take(3)
    if step >= 2:
        image_ref, shadow_ref, dir_ref, scal_ref = take(4)
    (sent_ref, out_obs_ref) = take(2)
    if step >= 1:
        out_res_ref, out_image_ref, out_shadow_ref, out_dir_ref, out_x_ref, out_scal_ref = take(6)
    part_scr, q1_ref, q2_ref, t1_ref, t2_ref, c_ref = take(6)
    ties = q1_ref.shape[1]
    first = pl.multiple_of(lax.axis_index("group") * scenes, scenes)
    own = pl.ds(first, scenes)

    part_scr[...] = part_ref[...]
    outside(packet_refs, ajac_ref, ejac_ref, part_scr, cjac_ref.shape[0])
    if step == 0:
        out_obs_ref[...] = part_scr[...]
        now_res_ref = res_ref
    else:
        now, alpha, beta = scalars(packet_refs, None if step == 1 else scal_ref, step - 1)
        out_scal_ref[...] = jnp.zeros_like(out_scal_ref)
        out_scal_ref[0:1, :] = now
        out_scal_ref[1:2, :] = alpha
        alpha, beta = wide(alpha), wide(beta)
        image, shadow, direction = field_ref[...], part_scr[...], res_ref[own]
        if step >= 2:
            image = image + beta * image_ref[...]
            shadow = shadow + beta * shadow_ref[...]
            direction = direction + beta * dir_ref[...]
            out_x_ref[...] = x_ref[...] + alpha * direction
        else:
            out_x_ref[...] = alpha * direction
        out_image_ref[...] = image
        out_shadow_ref[...] = shadow
        out_dir_ref[...] = direction
        out_res_ref[...] = res_ref[...] - alpha * image
        out_obs_ref[...] = obs_ref[...] - alpha * shadow
        now_res_ref = out_res_ref
    r1, r2 = out_obs_ref[:, :ties], out_obs_ref[:, ties:]
    q1_ref[...] = coef_ref[0] * r1 - coef_ref[1] * r2
    q2_ref[...] = coef_ref[2] * r2 - coef_ref[1] * r1
    c_ref[...] = backward(q1_ref, q2_ref, put1_ref, put2_ref, cjac_ref, ajac_ref, ejac_ref, t1_ref, t2_ref)
    c_ref[own] = c_ref[own] + damp_ref[...] * now_res_ref[own]
    sent_ref[...] = c_ref[...].astype(BF16)


def final_kernel(step, scenes, *refs):
    field_ref, m, a, b, c, res_ref, image_ref, dir_ref, x_ref, scal_ref, out_x_ref, out_res_ref = refs
    own = pl.ds(pl.multiple_of(lax.axis_index("group") * scenes, scenes), scenes)
    now, alpha, beta = scalars((m, a, b, c), scal_ref, step)
    alpha, beta = wide(alpha), wide(beta)
    res = res_ref[own]
    out_x_ref[...] = x_ref[...] + alpha * (res + beta * dir_ref[...])
    out_res_ref[...] = res - alpha * (field_ref[own] + beta * image_ref[own])


def call(kernel, outs, scratch, name, args, flops=0):
    whole = pl.BlockSpec(memory_space=pltpu.VMEM)
    moved = sum(a.size * a.dtype.itemsize for a in args)
    return pl.pallas_call(
        kernel,
        out_shape=[jax.ShapeDtypeStruct(*o) for o in outs],
        in_specs=[whole] * len(args),
        out_specs=[whole] * len(outs),
        scratch_shapes=[pltpu.VMEM(*s) for s in scratch],
        cost_estimate=pl.CostEstimate(flops=flops, bytes_accessed=moved, transcendentals=0),
        compiler_params=pltpu.CompilerParams(vmem_limit_bytes=VMEM_LIMIT),
        name=name,
    )(*args)


VMEM_LIMIT = 16 << 20


def group_sum_but_last(sent):
    n, g = lax.axis_size("orbit"), lax.axis_size("group")
    stages = g.bit_length() - 1
    for stage in range(stages):
        route = []
        for o in range(n):
            mask = 1 << ((stage + o % 2) % stages)
            route += [(o * g + i, o * g + (i ^ mask)) for i in range(g)]
        got = lax.ppermute(sent, ("orbit", "group"), route)
        if stage == stages - 1:
            return sent, got
        sent = lax.optimization_barrier((sent.astype(F32) + got.astype(F32)).astype(BF16))


def orbit_packets(packet):
    n = lax.axis_size("orbit")
    return [packet] + [lax.ppermute(packet, "orbit", [(i, i ^ mask) for i in range(n)]) for mask in range(1, n)]


def on_device(
    along_jac,
    along_res,
    along_e,
    along_count,
    damping,
    cross_jac,
    cross_res,
    cross_e,
    cross_own,
    cross_group,
    cross_other,
):
    scenes, _, ties, width = along_jac.shape[1:]
    links = cross_jac.shape[1]
    groups = lax.axis_size("group")
    rows = groups * scenes
    first = lax.axis_index("group") * scenes
    ajac = along_jac[0].reshape(scenes, 2 * ties, width)
    cjac = cross_jac[0].reshape(links, 2 * ties, width)
    slots = links + scenes + OCTET

    def pass_on(block):
        n = lax.axis_size("orbit")
        return lax.ppermute(block, "orbit", [(i, (i + 1) % n) for i in range(n)])

    live = (jnp.arange(ties)[None, :] < along_count[0][:, None]).astype(F32)
    ejac = pass_on(ajac[-1:])
    small = pass_on(jnp.concatenate([along_e[0, -1], along_res[0, -1], live[-1:], live[-1:] * 0, live[-1:] * 0, live[-1:] * 0], axis=0))

    fill = lambda a: jnp.pad(a, ((0, OCTET - 1), (0, 0)))
    stacked = lambda c, a, e: jnp.concatenate([c, a, fill(e)], axis=0)
    e1 = stacked(cross_e[0, :, 0], along_e[0, :, 0], small[0:1])
    e2 = stacked(cross_e[0, :, 1], along_e[0, :, 1], small[1:2])
    res1 = stacked(cross_res[0, :, 0], along_res[0, :, 0], small[2:3])
    res2 = stacked(cross_res[0, :, 1], along_res[0, :, 1], small[3:4])
    keep = stacked(jnp.ones((links, ties), F32), live, small[4:5])
    over = keep / (1.0 + e1 * e1 + e2 * e2)
    coef = jnp.stack([(1.0 + e2 * e2) * over, e1 * e2 * over, (1.0 + e1 * e1) * over])
    observed = jnp.concatenate([res1, res2], axis=1)
    here = first + jnp.arange(scenes)
    none = jnp.full((OCTET,), -1)
    one = jnp.concatenate([first + cross_own[0], here, none])
    two = jnp.concatenate([cross_group[0, :, 0] * scenes + cross_other[0], here[1:], none[:1], first[None], none[1:]])
    numbers = jnp.arange(rows)
    pick1, pick2 = ((v[:, None] == numbers[None, :]).astype(BF16) for v in (one, two))
    put1, put2 = ((v[None, :] == numbers[:, None]).astype(BF16) for v in (one, two))
    damp = jnp.broadcast_to(damping[0][:, None], (scenes, width))

    jacs = (cjac, ajac, ejac)
    work = 2 * (links + scenes + 1) * 32 * 2 * ties * width
    tie = (slots, ties)
    pair = (slots, 2 * ties)
    full = (rows, width)
    own = (scenes, width)
    terms = [(tie, F32), (tie, F32), ((slots, width), F32), ((slots, width), F32)]

    def project(field):
        scratch = [((2, slots, width), F32)] * 2
        return call(project_kernel, [(pair, F32)], scratch, "project", (field, pick1, pick2) + jacs, work)[0]

    def finish(sums, res=None):
        args = sums if res is None else sums + (res,)
        kernel = functools.partial(gather_kernel, scenes, res is None)
        field, packet = call(kernel, [(full, F32), ((OCTET, width), F32)], [], "finish", args)
        return field, orbit_packets(packet)

    (sent,) = call(rhs_kernel, [(full, BF16)], terms, "rhs", (observed, coef, put1, put2) + jacs, work)
    res, packets = finish(group_sum_but_last(sent))
    part = project(res)
    fixed = (coef, put1, put2, damp) + jacs
    scratch = [(pair, F32)] + terms + [(full, F32)]
    sent, obs = call(
        functools.partial(step_kernel, 0, scenes),
        [(full, BF16), (pair, F32)],
        scratch,
        "step",
        (part, *packets) + fixed + (res,),
        work,
    )
    state = ()
    x = jnp.zeros(own, F32)
    for step in range(1, ITERS):
        field, packets = finish(group_sum_but_last(sent), res)
        part = project(field)
        sent, obs, res, image, shadow, direction, x, scal = call(
            functools.partial(step_kernel, step, scenes),
            [(full, BF16), (pair, F32), (full, F32), (full, F32), (pair, F32), (own, F32), (own, F32), ((OCTET, width // 2), F32)],
            scratch,
            "step",
            (part, *packets) + fixed + (res, field, obs, x) + state,
            work,
        )
        state = (image, shadow, direction, scal)
    field, packets = finish(group_sum_but_last(sent), res)
    x, res = call(
        functools.partial(final_kernel, ITERS - 1, scenes),
        [(own, F32), (own, F32)],
        [],
        "final",
        (field, *packets, res, image, direction, x, scal),
    )
    return x[None], res[None]


def solution(mesh):
    placed = (
        P("group", "orbit", None, None, None),
        P("group", "orbit", None, None),
        P("group", "orbit", None, None),
        P("group", "orbit"),
        P("group", "orbit"),
        P("group", "orbit", None, None, None),
        P("group", "orbit", None, None),
        P("group", "orbit", None, None),
        P("group", "orbit"),
        P("group", "orbit", None),
        P("group", "orbit"),
    )
    return jax.shard_map(
        on_device,
        mesh=mesh,
        in_specs=placed,
        out_specs=(P("group", "orbit", None), P("group", "orbit", None)),
        check_vma=False,
    )
```

time: 488 us -> 135 us (0.28)
  blocking collectives: 276 us -> 0 us
  matrix products: 72.7 us -> 0 us
  Pallas kernels: 0 us -> 34.5 us
  starting transfers between devices: 53.1 us -> 43 us
  between operations: 10.4 us -> 1.01 us
  other arithmetic: 11.1 us -> 3.37 us
  waiting for transfers between devices: 47.1 us -> 41.8 us
    psum x7 -> x0, blocking collectives: 276 us -> none  [the longest x4 162 us: squares(): return lax.psum(jnp.sum(vector * vector), ('orbit', 'group'))]
    dot_general x51 -> x0, matrix products: 72.7 us -> none  [the longest x10 16.9 us: settle(): jnp.einsum('btp,bt->bp', jac[:, 1], q2, preferred_element_type=jnp.float32)]
    all_to_all x11 -> x0, starting transfers between devices: 47.8 us -> none  [the longest x4 17.5 us: on_device(): lax.all_to_all(sent.reshape(groups, slots, width), 'group', split_axis=0,...]
    all_to_all x11 -> x0, waiting for transfers between devices: 43.5 us -> none  [the longest x5 23.9 us: deliver(): lax.all_to_all(placed.reshape(groups, slots, width), 'group', split_axis=...]
    ppermute x9 -> x32, waiting for transfers between devices: 3.69 us -> 41.8 us  [the longest x15 39.8 us: group_sum_but_last(): got = lax.ppermute(sent, ('orbit', 'group'), route)]
    ppermute x9 -> x32, starting transfers between devices: 5.24 us -> 43 us  [the longest x15 30.2 us: group_sum_but_last(): got = lax.ppermute(sent, ('orbit', 'group'), route)]
    pallas_call x0 -> x15, Pallas kernels: none -> 34.5 us  [call(): pl.pallas_call(kernel, out_shape=[jax.ShapeDtypeStruct(*o) for o in outs]...]
    gather x12 -> x0, local copies, waits for them, and re-layouts: 9 us -> none  [the longest x4 3.41 us: on_device(): sent = operate_rounded[got_index] * live_rows]
  transfers between devices with their start and end apart: 20 -> 32, of which waited for: 14 -> 17; matrix products, arithmetic and copies ran while one was open for 13% -> 5% of each run, Pallas kernels for 0% -> 13%
where the time goes in v1:
time: 135 us; the launch traced here: 134 us
  starting transfers between devices  43 us (32%)
  waiting for transfers between devices  41.8 us (31%)
  Pallas kernels  34.5 us (26%)
  local copies, waits for them, and re-layouts  10.4 us (8%)
  other arithmetic  3.37 us (2%)
    ppermute x15, waiting for transfers between devices, group_sum_but_last(): got = lax.ppermute(sent, ('orbit', 'group'), route)  39.8 us
    pallas_call x15, Pallas kernels, call(): pl.pallas_call(kernel, out_shape=[jax.ShapeDtypeStruct(*o) for o in outs]...  34.5 us
    ppermute x15, starting transfers between devices, group_sum_but_last(): got = lax.ppermute(sent, ('orbit', 'group'), route)  30.2 us
    ppermute x15, starting transfers between devices, orbit_packets(): lax.ppermute(packet, 'orbit', [(i, i ^ mask) for i in range(n)])  9.59 us
    unnamed x10, local copies, waits for them, and re-layouts  4.98 us
    ppermute x2, starting transfers between devices, pass_on(): return lax.ppermute(block, 'orbit', [(i, (i + 1) % n) for i in range(n)])  3.18 us
  transfers between devices with their start and end apart: 32, of which 17 were waited for; matrix products, arithmetic and copies ran while one was open for 5% of the time, Pallas kernels for 13%

profile of v1, /device:TPU:0, one launch (start us, length us, event | category | flops | bytes accessed | tf_op | source)
XLA Modules:
  0.0 134.1 jit_solution(1807827739711523076)
XLA Ops:
  0.6 0.7 fusion.9
  1.4 0.7 slice_bitcast_fusion
  2.6 0.9 slice.75
  3.5 2.6 %collective-permute-start.1 = (bf16[1,256,256]{2,1,0:T(8,128)(2,1)S(1)}, bf16[1,256,256]{2,1,0:T(8,128)(2,1)S(1)}, u32[]{:S(2)}, u32[]{:S(2)}) collective-permute-start(bf16[1,256,256]{2,1,0:T(8,128)(2,1)S(1)} %bitcast.72), channel_id=1, source_target_pairs={{0,8},{8,16},{16,24},{24,0},{1,9},{9,17},{17,25},{25,1},{2,10},{10... | collective-permute-start | bytes 393224 | tf_op jit(solution)/shard_map/ppermute | solution.py:290
  6.2 0.8 fusion.13
  7.1 0.7 add_bitcast_fusion
  7.7 1.0 fusion.11
  8.7 1.0 fusion.10
  9.7 0.7 bitcast_add_fusion
  10.6 0.8 fusion.12
  11.4 0.7 select_bitcast_fusion
  12.4 3.4 %copy-done = bf16[1,64,2,128,256]{4,3,2,1,0:T(8,128)(2,1)S(1)} copy-done((bf16[1,64,2,128,256]{4,3,2,1,0:T(8,128)(2,1)S(1)}, bf16[1,64,2,128,256]{4,3,2,1,0:T(8,128)(2,1)}, u32[]{:S(2)}) %copy-start) | copy-done | bytes 8388632
  15.8 1.6 %copy-done.2 = bf16[1,16,2,128,256]{4,3,2,1,0:T(8,128)(2,1)S(1)} copy-done((bf16[1,16,2,128,256]{4,3,2,1,0:T(8,128)(2,1)S(1)}, bf16[1,16,2,128,256]{4,3,2,1,0:T(8,128)(2,1)}, u32[]{:S(2)}) %copy-start.2) | copy-done | bytes 2097176
  17.4 2.9 %rhs.1 = bf16[128,256]{1,0:T(8,128)(2,1)S(1)} custom-call(f32[88,256]{1,0:T(8,128)S(1)} %fusion.res_ref, f32[3,88,128]{2,1,0:T(8,128)S(1)} %pad_maximum_fusion.coef_ref.refs_5_, bf16[128,88]{1,0:T(8,128)(2,1)S(1)} %get-tuple-element.94.put1_ref.refs_6_, bf16[128,88]{1,0:T(8,128)(2,1)S(1)} %get-tuple-element.95.put2_ref.refs_7_, ...), custom_call_target="tpu_custom_call" | custom-call | flops 339738624 | bytes 10887168 | tf_op jit(solution)/shard_map/rhs/pallas_call | solution.py:232
  20.3 1.6 %collective-permute-start.2 = (bf16[128,256]{1,0:T(8,128)(2,1)S(1)}, bf16[128,256]{1,0:T(8,128)(2,1)S(1)}, u32[]{:S(2)}, u32[]{:S(2)}) collective-permute-start(bf16[128,256]{1,0:T(8,128)(2,1)S(1)} %rhs.1), channel_id=1, source_target_pairs={{0,1},{1,0},{2,3},{3,2},{4,5},{5,4},{6,7},{7,6},{8,10},{9,11},{10,... | collective-permute-start | bytes 196616 | tf_op jit(solution)/shard_map/ppermute | solution.py:255
  21.9 2.7 %collective-permute-done.2 = bf16[128,256]{1,0:T(8,128)(2,1)S(1)} collective-permute-done((bf16[128,256]{1,0:T(8,128)(2,1)S(1)}, bf16[128,256]{1,0:T(8,128)(2,1)S(1)}, u32[]{:S(2)}, u32[]{:S(2)}) %collective-permute-start.2) | collective-permute-done | bytes 65568 | tf_op jit(solution)/shard_map/ppermute | solution.py:255
  24.6 1.6 %collective-permute-start.3 = (bf16[128,256]{1,0:T(8,128)(2,1)S(1)}, bf16[128,256]{1,0:T(8,128)(2,1)S(1)}, u32[]{:S(2)}, u32[]{:S(2)}) collective-permute-start(bf16[128,256]{1,0:T(8,128)(2,1)S(1)} %add_convert_fusion.9), channel_id=1, source_target_pairs={{0,2},{1,3},{2,0},{3,1},{4,6},{5,7},{6,4},{7,5},{8,12},{9,13},{10,... | collective-permute-start | bytes 196616 | tf_op jit(solution)/shard_map/ppermute | solution.py:255
  26.3 2.7 %collective-permute-done.3 = bf16[128,256]{1,0:T(8,128)(2,1)S(1)} collective-permute-done((bf16[128,256]{1,0:T(8,128)(2,1)S(1)}, bf16[128,256]{1,0:T(8,128)(2,1)S(1)}, u32[]{:S(2)}, u32[]{:S(2)}) %collective-permute-start.3) | collective-permute-done | bytes 65568 | tf_op jit(solution)/shard_map/ppermute | solution.py:255
  29.0 2.7 %collective-permute-start.4 = (bf16[128,256]{1,0:T(8,128)(2,1)S(1)}, bf16[128,256]{1,0:T(8,128)(2,1)S(1)}, u32[]{:S(2)}, u32[]{:S(2)}) collective-permute-start(bf16[128,256]{1,0:T(8,128)(2,1)S(1)} %add_convert_fusion.8.mine_ref), channel_id=1, source_target_pairs={{0,4},{1,5},{2,6},{3,7},{4,0},{5,1},{6,2},{7,3},{8,9},{9,8},{10,11... | collective-permute-start | bytes 196616 | tf_op jit(solution)/shard_map/ppermute | solution.py:255
  31.7 2.5 %collective-permute-done.4.got_ref = bf16[128,256]{1,0:T(8,128)(2,1)S(1)} collective-permute-done((bf16[128,256]{1,0:T(8,128)(2,1)S(1)}, bf16[128,256]{1,0:T(8,128)(2,1)S(1)}, u32[]{:S(2)}, u32[]{:S(2)}) %collective-permute-start.4) | collective-permute-done | bytes 65568 | tf_op jit(solution)/shard_map/ppermute | solution.py:255
  34.6 1.6 %collective-permute-start.5 = (f32[8,256]{1,0:T(8,128)S(1)}, f32[8,256]{1,0:T(8,128)S(1)}, u32[]{:S(2)}, u32[]{:S(2)}) collective-permute-start(f32[8,256]{1,0:T(8,128)S(1)} %get-tuple-element.39.refs_1_), channel_id=1, source_target_pairs={{0,8},{8,0},{16,24},{24,16},{1,9},{9,1},{17,25},{25,17},{2,10},{10... | collective-permute-start | bytes 24584 | tf_op jit(solution)/shard_map/ppermute | solution.py:263
  36.2 4.4 %project.4.refs_0_ = f32[88,256]{1,0:T(8,128)S(1)} custom-call(f32[128,256]{1,0:T(8,128)S(1)} %get-tuple-element.38.field_ref.refs_12_.refs_0_, bf16[88,128]{1,0:T(8,128)(2,1)S(1)} %get-tuple-element.96.pick1_ref, bf16[88,128]{1,0:T(8,128)(2,1)S(1)} %get-tuple-element.97.pick2_ref, bf16[64,256,256]{2,1,0:T(8,128)(2,1)S(1)} %bitcast.51, ...), custom_call_target="tpu_custom_call" | custom-call | flops 339738624 | bytes 10792960 | tf_op jit(solution)/shard_map/project/pallas_call | solution.py:232
  40.7 3.1 %step.4 = (bf16[128,256]{1,0:T(8,128)(2,1)S(1)}, f32[88,256]{1,0:T(8,128)S(1)}) custom-call(f32[88,256]{1,0:T(8,128)S(1)} %project.4.refs_0_, f32[8,256]{1,0:T(8,128)S(1)} %get-tuple-element.39.refs_1_, f32[8,256]{1,0:T(8,128)S(1)} %collective-permute-done.5.refs_2_, f32[8,256]{1,0:T(8,128)S(1)} %collective-permute-done.6.refs_3_, ...), custom_call_target="tpu_custom_call" | custom-call | flops 339738624 | bytes 11067392 | tf_op jit(solution)/shard_map/step/pallas_call | solution.py:232
  43.8 1.6 %collective-permute-start.8 = (bf16[128,256]{1,0:T(8,128)(2,1)S(1)}, bf16[128,256]{1,0:T(8,128)(2,1)S(1)}, u32[]{:S(2)}, u32[]{:S(2)}) collective-permute-start(bf16[128,256]{1,0:T(8,128)(2,1)S(1)} %get-tuple-element.40), channel_id=1, source_target_pairs={{0,1},{1,0},{2,3},{3,2},{4,5},{5,4},{6,7},{7,6},{8,10},{9,11},{10,... | collective-permute-start | bytes 196616 | tf_op jit(solution)/shard_map/ppermute | solution.py:255
  45.4 2.7 %collective-permute-done.8 = bf16[128,256]{1,0:T(8,128)(2,1)S(1)} collective-permute-done((bf16[128,256]{1,0:T(8,128)(2,1)S(1)}, bf16[128,256]{1,0:T(8,128)(2,1)S(1)}, u32[]{:S(2)}, u32[]{:S(2)}) %collective-permute-start.8) | collective-permute-done | bytes 65568 | tf_op jit(solution)/shard_map/ppermute | solution.py:255
  48.1 1.6 %collective-permute-start.9 = (bf16[128,256]{1,0:T(8,128)(2,1)S(1)}, bf16[128,256]{1,0:T(8,128)(2,1)S(1)}, u32[]{:S(2)}, u32[]{:S(2)}) collective-permute-start(bf16[128,256]{1,0:T(8,128)(2,1)S(1)} %add_convert_fusion.7), channel_id=1, source_target_pairs={{0,2},{1,3},{2,0},{3,1},{4,6},{5,7},{6,4},{7,5},{8,12},{9,13},{10,... | collective-permute-start | bytes 196616 | tf_op jit(solution)/shard_map/ppermute | solution.py:255
  49.8 2.8 %collective-permute-done.9 = bf16[128,256]{1,0:T(8,128)(2,1)S(1)} collective-permute-done((bf16[128,256]{1,0:T(8,128)(2,1)S(1)}, bf16[128,256]{1,0:T(8,128)(2,1)S(1)}, u32[]{:S(2)}, u32[]{:S(2)}) %collective-permute-start.9) | collective-permute-done | bytes 65568 | tf_op jit(solution)/shard_map/ppermute | solution.py:255
  52.6 2.6 %collective-permute-start.10 = (bf16[128,256]{1,0:T(8,128)(2,1)S(1)}, bf16[128,256]{1,0:T(8,128)(2,1)S(1)}, u32[]{:S(2)}, u32[]{:S(2)}) collective-permute-start(bf16[128,256]{1,0:T(8,128)(2,1)S(1)} %add_convert_fusion.6.mine_ref), channel_id=1, source_target_pairs={{0,4},{1,5},{2,6},{3,7},{4,0},{5,1},{6,2},{7,3},{8,9},{9,8},{10,11... | collective-permute-start | bytes 196616 | tf_op jit(solution)/shard_map/ppermute | solution.py:255
  55.3 2.6 %collective-permute-done.10.got_ref = bf16[128,256]{1,0:T(8,128)(2,1)S(1)} collective-permute-done((bf16[128,256]{1,0:T(8,128)(2,1)S(1)}, bf16[128,256]{1,0:T(8,128)(2,1)S(1)}, u32[]{:S(2)}, u32[]{:S(2)}) %collective-permute-start.10) | collective-permute-done | bytes 65568 | tf_op jit(solution)/shard_map/ppermute | solution.py:255
  58.1 0.8 collective-permute-start.12
  59.0 1.0 collective-permute-start.11
  60.0 4.4 %project.5.refs_0_ = f32[88,256]{1,0:T(8,128)S(1)} custom-call(f32[128,256]{1,0:T(8,128)S(1)} %get-tuple-element.41.field_ref.refs_13_, bf16[88,128]{1,0:T(8,128)(2,1)S(1)} %get-tuple-element.96.pick1_ref, bf16[88,128]{1,0:T(8,128)(2,1)S(1)} %get-tuple-element.97.pick2_ref, bf16[64,256,256]{2,1,0:T(8,128)(2,1)S(1)} %bitcast.53, ...), custom_call_target="tpu_custom_call" | custom-call | flops 339738624 | bytes 10792960 | tf_op jit(solution)/shard_map/project/pallas_call | solution.py:232
  64.4 3.1 %step.5 = (bf16[128,256]{1,0:T(8,128)(2,1)S(1)}, f32[88,256]{1,0:T(8,128)S(1)}, f32[128,256]{1,0:T(8,128)S(1)}, f32[128,256]{1,0:T(8,128)S(1)}, f32[88,256]{1,0:...) custom-call(f32[88,256]{1,0:T(8,128)S(1)} %project.5.refs_0_, ...), custom_call_target="tpu_custom_call" | custom-call | flops 339738624 | bytes 11304960 | tf_op jit(solution)/shard_map/step/pallas_call | solution.py:232
  67.6 1.6 %collective-permute-start.14 = (bf16[128,256]{1,0:T(8,128)(2,1)S(1)}, bf16[128,256]{1,0:T(8,128)(2,1)S(1)}, u32[]{:S(2)}, u32[]{:S(2)}) collective-permute-start(bf16[128,256]{1,0:T(8,128)(2,1)S(1)} %get-tuple-element.44), channel_id=1, source_target_pairs={{0,1},{1,0},{2,3},{3,2},{4,5},{5,4},{6,7},{7,6},{8,10},{9,11},{10,... | collective-permute-start | bytes 196616 | tf_op jit(solution)/shard_map/ppermute | solution.py:255
  69.1 2.7 %collective-permute-done.14 = bf16[128,256]{1,0:T(8,128)(2,1)S(1)} collective-permute-done((bf16[128,256]{1,0:T(8,128)(2,1)S(1)}, bf16[128,256]{1,0:T(8,128)(2,1)S(1)}, u32[]{:S(2)}, u32[]{:S(2)}) %collective-permute-start.14) | collective-permute-done | bytes 65568 | tf_op jit(solution)/shard_map/ppermute | solution.py:255
  71.9 1.9 %collective-permute-start.15 = (bf16[128,256]{1,0:T(8,128)(2,1)S(1)}, bf16[128,256]{1,0:T(8,128)(2,1)S(1)}, u32[]{:S(2)}, u32[]{:S(2)}) collective-permute-start(bf16[128,256]{1,0:T(8,128)(2,1)S(1)} %add_convert_fusion.5), channel_id=1, source_target_pairs={{0,2},{1,3},{2,0},{3,1},{4,6},{5,7},{6,4},{7,5},{8,12},{9,13},{10,... | collective-permute-start | bytes 196616 | tf_op jit(solution)/shard_map/ppermute | solution.py:255
  73.8 2.6 %collective-permute-done.15 = bf16[128,256]{1,0:T(8,128)(2,1)S(1)} collective-permute-done((bf16[128,256]{1,0:T(8,128)(2,1)S(1)}, bf16[128,256]{1,0:T(8,128)(2,1)S(1)}, u32[]{:S(2)}, u32[]{:S(2)}) %collective-permute-start.15) | collective-permute-done | bytes 65568 | tf_op jit(solution)/shard_map/ppermute | solution.py:255
  76.4 2.6 %collective-permute-start.16 = (bf16[128,256]{1,0:T(8,128)(2,1)S(1)}, bf16[128,256]{1,0:T(8,128)(2,1)S(1)}, u32[]{:S(2)}, u32[]{:S(2)}) collective-permute-start(bf16[128,256]{1,0:T(8,128)(2,1)S(1)} %add_convert_fusion.4.mine_ref), channel_id=1, source_target_pairs={{0,4},{1,5},{2,6},{3,7},{4,0},{5,1},{6,2},{7,3},{8,9},{9,8},{10,11... | collective-permute-start | bytes 196616 | tf_op jit(solution)/shard_map/ppermute | solution.py:255
  79.1 2.6 %collective-permute-done.16.got_ref = bf16[128,256]{1,0:T(8,128)(2,1)S(1)} collective-permute-done((bf16[128,256]{1,0:T(8,128)(2,1)S(1)}, bf16[128,256]{1,0:T(8,128)(2,1)S(1)}, u32[]{:S(2)}, u32[]{:S(2)}) %collective-permute-start.16) | collective-permute-done | bytes 65568 | tf_op jit(solution)/shard_map/ppermute | solution.py:255
  81.9 0.8 collective-permute-start.18
  82.8 1.0 collective-permute-start.17
  83.8 4.4 %project.6.refs_0_ = f32[88,256]{1,0:T(8,128)S(1)} custom-call(f32[128,256]{1,0:T(8,128)S(1)} %get-tuple-element.46.field_ref.refs_13_, bf16[88,128]{1,0:T(8,128)(2,1)S(1)} %get-tuple-element.96.pick1_ref, bf16[88,128]{1,0:T(8,128)(2,1)S(1)} %get-tuple-element.97.pick2_ref, bf16[64,256,256]{2,1,0:T(8,128)(2,1)S(1)} %bitcast.55, ...), custom_call_target="tpu_custom_call" | custom-call | flops 339738624 | bytes 10792960 | tf_op jit(solution)/shard_map/project/pallas_call | solution.py:232
  88.2 3.1 %step.6 = (bf16[128,256]{1,0:T(8,128)(2,1)S(1)}, f32[88,256]{1,0:T(8,128)S(1)}, f32[128,256]{1,0:T(8,128)S(1)}, f32[128,256]{1,0:T(8,128)S(1)}, f32[88,256]{1,0:...) custom-call(f32[88,256]{1,0:T(8,128)S(1)} %project.6.refs_0_, ...), custom_call_target="tpu_custom_call" | custom-call | flops 339738624 | bytes 11546624 | tf_op jit(solution)/shard_map/step/pallas_call | solution.py:232
  91.3 1.6 %collective-permute-start.20 = (bf16[128,256]{1,0:T(8,128)(2,1)S(1)}, bf16[128,256]{1,0:T(8,128)(2,1)S(1)}, u32[]{:S(2)}, u32[]{:S(2)}) collective-permute-start(bf16[128,256]{1,0:T(8,128)(2,1)S(1)} %get-tuple-element.54), channel_id=1, source_target_pairs={{0,1},{1,0},{2,3},{3,2},{4,5},{5,4},{6,7},{7,6},{8,10},{9,11},{10,... | collective-permute-start | bytes 196616 | tf_op jit(solution)/shard_map/ppermute | solution.py:255
  92.9 2.7 %collective-permute-done.20 = bf16[128,256]{1,0:T(8,128)(2,1)S(1)} collective-permute-done((bf16[128,256]{1,0:T(8,128)(2,1)S(1)}, bf16[128,256]{1,0:T(8,128)(2,1)S(1)}, u32[]{:S(2)}, u32[]{:S(2)}) %collective-permute-start.20) | collective-permute-done | bytes 65568 | tf_op jit(solution)/shard_map/ppermute | solution.py:255
  95.7 1.9 %collective-permute-start.21 = (bf16[128,256]{1,0:T(8,128)(2,1)S(1)}, bf16[128,256]{1,0:T(8,128)(2,1)S(1)}, u32[]{:S(2)}, u32[]{:S(2)}) collective-permute-start(bf16[128,256]{1,0:T(8,128)(2,1)S(1)} %add_convert_fusion.3), channel_id=1, source_target_pairs={{0,2},{1,3},{2,0},{3,1},{4,6},{5,7},{6,4},{7,5},{8,12},{9,13},{10,... | collective-permute-start | bytes 196616 | tf_op jit(solution)/shard_map/ppermute | solution.py:255
  97.6 2.6 %collective-permute-done.21 = bf16[128,256]{1,0:T(8,128)(2,1)S(1)} collective-permute-done((bf16[128,256]{1,0:T(8,128)(2,1)S(1)}, bf16[128,256]{1,0:T(8,128)(2,1)S(1)}, u32[]{:S(2)}, u32[]{:S(2)}) %collective-permute-start.21) | collective-permute-done | bytes 65568 | tf_op jit(solution)/shard_map/ppermute | solution.py:255
  100.2 2.6 %collective-permute-start.22 = (bf16[128,256]{1,0:T(8,128)(2,1)S(1)}, bf16[128,256]{1,0:T(8,128)(2,1)S(1)}, u32[]{:S(2)}, u32[]{:S(2)}) collective-permute-start(bf16[128,256]{1,0:T(8,128)(2,1)S(1)} %add_convert_fusion.2.mine_ref), channel_id=1, source_target_pairs={{0,4},{1,5},{2,6},{3,7},{4,0},{5,1},{6,2},{7,3},{8,9},{9,8},{10,11... | collective-permute-start | bytes 196616 | tf_op jit(solution)/shard_map/ppermute | solution.py:255
  102.9 2.6 %collective-permute-done.22.got_ref = bf16[128,256]{1,0:T(8,128)(2,1)S(1)} collective-permute-done((bf16[128,256]{1,0:T(8,128)(2,1)S(1)}, bf16[128,256]{1,0:T(8,128)(2,1)S(1)}, u32[]{:S(2)}, u32[]{:S(2)}) %collective-permute-start.22) | collective-permute-done | bytes 65568 | tf_op jit(solution)/shard_map/ppermute | solution.py:255
  105.7 0.8 collective-permute-start.24
  106.6 1.0 collective-permute-start.23
  107.6 4.4 %project.7.refs_0_ = f32[88,256]{1,0:T(8,128)S(1)} custom-call(f32[128,256]{1,0:T(8,128)S(1)} %get-tuple-element.56.field_ref.refs_13_, bf16[88,128]{1,0:T(8,128)(2,1)S(1)} %get-tuple-element.96.pick1_ref, bf16[88,128]{1,0:T(8,128)(2,1)S(1)} %get-tuple-element.97.pick2_ref, bf16[64,256,256]{2,1,0:T(8,128)(2,1)S(1)} %bitcast.57, ...), custom_call_target="tpu_custom_call" | custom-call | flops 339738624 | bytes 10792960 | tf_op jit(solution)/shard_map/project/pallas_call | solution.py:232
  112.0 3.4 %step.7 = (bf16[128,256]{1,0:T(8,128)(2,1)S(1)}, f32[88,256]{1,0:T(8,128)}, f32[128,256]{1,0:T(8,128)S(1)}, f32[128,256]{1,0:T(8,128)S(1)}, f32[88,256]{1,0:T(8,...) custom-call(f32[88,256]{1,0:T(8,128)S(1)} %project.7.refs_0_, ...), custom_call_target="tpu_custom_call" | custom-call | flops 339738624 | bytes 11546624 | tf_op jit(solution)/shard_map/step/pallas_call | solution.py:232
  115.5 1.5 %collective-permute-start.26 = (bf16[128,256]{1,0:T(8,128)(2,1)S(1)}, bf16[128,256]{1,0:T(8,128)(2,1)S(1)}, u32[]{:S(2)}, u32[]{:S(2)}) collective-permute-start(bf16[128,256]{1,0:T(8,128)(2,1)S(1)} %get-tuple-element.64), channel_id=1, source_target_pairs={{0,1},{1,0},{2,3},{3,2},{4,5},{5,4},{6,7},{7,6},{8,10},{9,11},{10,... | collective-permute-start | bytes 196616 | tf_op jit(solution)/shard_map/ppermute | solution.py:255
  117.0 2.7 %collective-permute-done.26 = bf16[128,256]{1,0:T(8,128)(2,1)S(1)} collective-permute-done((bf16[128,256]{1,0:T(8,128)(2,1)S(1)}, bf16[128,256]{1,0:T(8,128)(2,1)S(1)}, u32[]{:S(2)}, u32[]{:S(2)}) %collective-permute-start.26) | collective-permute-done | bytes 65568 | tf_op jit(solution)/shard_map/ppermute | solution.py:255
  119.7 1.9 %collective-permute-start.27 = (bf16[128,256]{1,0:T(8,128)(2,1)S(1)}, bf16[128,256]{1,0:T(8,128)(2,1)S(1)}, u32[]{:S(2)}, u32[]{:S(2)}) collective-permute-start(bf16[128,256]{1,0:T(8,128)(2,1)S(1)} %add_convert_fusion.1), channel_id=1, source_target_pairs={{0,2},{1,3},{2,0},{3,1},{4,6},{5,7},{6,4},{7,5},{8,12},{9,13},{10,... | collective-permute-start | bytes 196616 | tf_op jit(solution)/shard_map/ppermute | solution.py:255
  121.7 2.6 %collective-permute-done.27 = bf16[128,256]{1,0:T(8,128)(2,1)S(1)} collective-permute-done((bf16[128,256]{1,0:T(8,128)(2,1)S(1)}, bf16[128,256]{1,0:T(8,128)(2,1)S(1)}, u32[]{:S(2)}, u32[]{:S(2)}) %collective-permute-start.27) | collective-permute-done | bytes 65568 | tf_op jit(solution)/shard_map/ppermute | solution.py:255
  124.3 2.6 %collective-permute-start.28 = (bf16[128,256]{1,0:T(8,128)(2,1)S(1)}, bf16[128,256]{1,0:T(8,128)(2,1)S(1)}, u32[]{:S(2)}, u32[]{:S(2)}) collective-permute-start(bf16[128,256]{1,0:T(8,128)(2,1)S(1)} %add_convert_fusion.mine_ref), channel_id=1, source_target_pairs={{0,4},{1,5},{2,6},{3,7},{4,0},{5,1},{6,2},{7,3},{8,9},{9,8},{10,11... | collective-permute-start | bytes 196616 | tf_op jit(solution)/shard_map/ppermute | solution.py:255
  126.9 2.6 %collective-permute-done.28.got_ref = bf16[128,256]{1,0:T(8,128)(2,1)S(1)} collective-permute-done((bf16[128,256]{1,0:T(8,128)(2,1)S(1)}, bf16[128,256]{1,0:T(8,128)(2,1)S(1)}, u32[]{:S(2)}, u32[]{:S(2)}) %collective-permute-start.28) | collective-permute-done | bytes 65568 | tf_op jit(solution)/shard_map/ppermute | solution.py:255
  129.8 0.8 collective-permute-start.30
  130.6 1.0 collective-permute-start.29
  131.6 1.2 collective-permute-done.31.refs_4_
  132.8 0.7 collective-permute-done.30.refs_3_
  133.5 0.6 final.1
  (66 shorter events, 2.9 us)
Async XLA Ops:
  2.1 9.3 %collective-permute-start = (f32[8,128]{1,0:T(8,128)S(1)}, f32[8,128]{1,0:T(8,128)S(1)}, u32[]{:S(2)}, u32[]{:S(2)}) collective-permute-start(f32[8,128]{1,0:T(8,128)S(1)} %concatenate.100), channel_id=1, source_target_pairs={{0,8},{8,16},{16,24},{24,0},{1,9},{9,17},{17,25},{25,1},{2,10},{10... | collective-permute-start | bytes 12296 | tf_op jit(solution)/shard_map/ppermute | solution.py:290
  3.5 8.8 %collective-permute-start.1 = (bf16[1,256,256]{2,1,0:T(8,128)(2,1)S(1)}, bf16[1,256,256]{2,1,0:T(8,128)(2,1)S(1)}, u32[]{:S(2)}, u32[]{:S(2)}) collective-permute-start(bf16[1,256,256]{2,1,0:T(8,128)(2,1)S(1)} %bitcast.72), channel_id=1, source_target_pairs={{0,8},{8,16},{16,24},{24,0},{1,9},{9,17},{17,25},{25,1},{2,10},{10... | collective-permute-start | bytes 393224 | tf_op jit(solution)/shard_map/ppermute | solution.py:290
  12.4 3.4 %copy-start = (bf16[1,64,2,128,256]{4,3,2,1,0:T(8,128)(2,1)S(1)}, bf16[1,64,2,128,256]{4,3,2,1,0:T(8,128)(2,1)}, u32[]{:S(2)}) copy-start(bf16[1,64,2,128,256]{4,3,2,1,0:T(8,128)(2,1)} %param.16) | copy-start | bytes 25165828
  15.8 1.6 %copy-start.2 = (bf16[1,16,2,128,256]{4,3,2,1,0:T(8,128)(2,1)S(1)}, bf16[1,16,2,128,256]{4,3,2,1,0:T(8,128)(2,1)}, u32[]{:S(2)}) copy-start(bf16[1,16,2,128,256]{4,3,2,1,0:T(8,128)(2,1)} %param.11) | copy-start | bytes 6291460
  17.4 18.8 %copy-start.1 = (bf16[1,64,2,128,256]{4,3,2,1,0:T(8,128)(2,1)S(1)}, bf16[1,64,2,128,256]{4,3,2,1,0:T(8,128)(2,1)}, u32[]{:S(2)}) copy-start(bf16[1,64,2,128,256]{4,3,2,1,0:T(8,128)(2,1)} %param.16) | copy-start | bytes 25165828
  17.4 18.8 %copy-start.3 = (bf16[1,16,2,128,256]{4,3,2,1,0:T(8,128)(2,1)S(1)}, bf16[1,16,2,128,256]{4,3,2,1,0:T(8,128)(2,1)}, u32[]{:S(2)}) copy-start(bf16[1,16,2,128,256]{4,3,2,1,0:T(8,128)(2,1)} %param.11) | copy-start | bytes 6291460
  20.3 20.4 %copy-start.4 = (f32[1,16]{1,0:T(1,128)S(1)}, f32[1,16]{1,0:T(1,128)}, u32[]{:S(2)}) copy-start(f32[1,16]{1,0:T(1,128)} %param.15) | copy-start | bytes 196
  20.3 4.3 %collective-permute-start.2 = (bf16[128,256]{1,0:T(8,128)(2,1)S(1)}, bf16[128,256]{1,0:T(8,128)(2,1)S(1)}, u32[]{:S(2)}, u32[]{:S(2)}) collective-permute-start(bf16[128,256]{1,0:T(8,128)(2,1)S(1)} %rhs.1), channel_id=1, source_target_pairs={{0,1},{1,0},{2,3},{3,2},{4,5},{5,4},{6,7},{7,6},{8,10},{9,11},{10,... | collective-permute-start | bytes 196616 | tf_op jit(solution)/shard_map/ppermute | solution.py:255
  24.6 4.3 %collective-permute-start.3 = (bf16[128,256]{1,0:T(8,128)(2,1)S(1)}, bf16[128,256]{1,0:T(8,128)(2,1)S(1)}, u32[]{:S(2)}, u32[]{:S(2)}) collective-permute-start(bf16[128,256]{1,0:T(8,128)(2,1)S(1)} %add_convert_fusion.9), channel_id=1, source_target_pairs={{0,2},{1,3},{2,0},{3,1},{4,6},{5,7},{6,4},{7,5},{8,12},{9,13},{10,... | collective-permute-start | bytes 196616 | tf_op jit(solution)/shard_map/ppermute | solution.py:255
  29.0 5.2 %collective-permute-start.4 = (bf16[128,256]{1,0:T(8,128)(2,1)S(1)}, bf16[128,256]{1,0:T(8,128)(2,1)S(1)}, u32[]{:S(2)}, u32[]{:S(2)}) collective-permute-start(bf16[128,256]{1,0:T(8,128)(2,1)S(1)} %add_convert_fusion.8.mine_ref), channel_id=1, source_target_pairs={{0,4},{1,5},{2,6},{3,7},{4,0},{5,1},{6,2},{7,3},{8,9},{9,8},{10,11... | collective-permute-start | bytes 196616 | tf_op jit(solution)/shard_map/ppermute | solution.py:255
  34.2 6.3 %collective-permute-start.7 = (f32[8,256]{1,0:T(8,128)S(1)}, f32[8,256]{1,0:T(8,128)S(1)}, u32[]{:S(2)}, u32[]{:S(2)}) collective-permute-start(f32[8,256]{1,0:T(8,128)S(1)} %get-tuple-element.39.refs_1_), channel_id=1, source_target_pairs={{0,24},{8,16},{16,8},{24,0},{1,25},{9,17},{17,9},{25,1},{2,26},{10... | collective-permute-start | bytes 24584 | tf_op jit(solution)/shard_map/ppermute | solution.py:263
  34.3 6.3 %collective-permute-start.6 = (f32[8,256]{1,0:T(8,128)S(1)}, f32[8,256]{1,0:T(8,128)S(1)}, u32[]{:S(2)}, u32[]{:S(2)}) collective-permute-start(f32[8,256]{1,0:T(8,128)S(1)} %get-tuple-element.39.refs_1_), channel_id=1, source_target_pairs={{0,16},{8,24},{16,0},{24,8},{1,17},{9,25},{17,1},{25,9},{2,18},{10... | collective-permute-start | bytes 24584 | tf_op jit(solution)/shard_map/ppermute | solution.py:263
  34.6 6.0 %collective-permute-start.5 = (f32[8,256]{1,0:T(8,128)S(1)}, f32[8,256]{1,0:T(8,128)S(1)}, u32[]{:S(2)}, u32[]{:S(2)}) collective-permute-start(f32[8,256]{1,0:T(8,128)S(1)} %get-tuple-element.39.refs_1_), channel_id=1, source_target_pairs={{0,8},{8,0},{16,24},{24,16},{1,9},{9,1},{17,25},{25,17},{2,10},{10... | collective-permute-start | bytes 24584 | tf_op jit(solution)/shard_map/ppermute | solution.py:263
  43.8 4.3 %collective-permute-start.8 = (bf16[128,256]{1,0:T(8,128)(2,1)S(1)}, bf16[128,256]{1,0:T(8,128)(2,1)S(1)}, u32[]{:S(2)}, u32[]{:S(2)}) collective-permute-start(bf16[128,256]{1,0:T(8,128)(2,1)S(1)} %get-tuple-element.40), channel_id=1, source_target_pairs={{0,1},{1,0},{2,3},{3,2},{4,5},{5,4},{6,7},{7,6},{8,10},{9,11},{10,... | collective-permute-start | bytes 196616 | tf_op jit(solution)/shard_map/ppermute | solution.py:255
  48.1 4.5 %collective-permute-start.9 = (bf16[128,256]{1,0:T(8,128)(2,1)S(1)}, bf16[128,256]{1,0:T(8,128)(2,1)S(1)}, u32[]{:S(2)}, u32[]{:S(2)}) collective-permute-start(bf16[128,256]{1,0:T(8,128)(2,1)S(1)} %add_convert_fusion.7), channel_id=1, source_target_pairs={{0,2},{1,3},{2,0},{3,1},{4,6},{5,7},{6,4},{7,5},{8,12},{9,13},{10,... | collective-permute-start | bytes 196616 | tf_op jit(solution)/shard_map/ppermute | solution.py:255
  52.6 5.2 %collective-permute-start.10 = (bf16[128,256]{1,0:T(8,128)(2,1)S(1)}, bf16[128,256]{1,0:T(8,128)(2,1)S(1)}, u32[]{:S(2)}, u32[]{:S(2)}) collective-permute-start(bf16[128,256]{1,0:T(8,128)(2,1)S(1)} %add_convert_fusion.6.mine_ref), channel_id=1, source_target_pairs={{0,4},{1,5},{2,6},{3,7},{4,0},{5,1},{6,2},{7,3},{8,9},{9,8},{10,11... | collective-permute-start | bytes 196616 | tf_op jit(solution)/shard_map/ppermute | solution.py:255
  58.1 6.3 %collective-permute-start.13 = (f32[8,256]{1,0:T(8,128)S(1)}, f32[8,256]{1,0:T(8,128)S(1)}, u32[]{:S(2)}, u32[]{:S(2)}) collective-permute-start(f32[8,256]{1,0:T(8,128)S(1)} %get-tuple-element.42.refs_1_), channel_id=1, source_target_pairs={{0,24},{8,16},{16,8},{24,0},{1,25},{9,17},{17,9},{25,1},{2,26},{10... | collective-permute-start | bytes 24584 | tf_op jit(solution)/shard_map/ppermute | solution.py:263
  58.1 6.3 %collective-permute-start.12 = (f32[8,256]{1,0:T(8,128)S(1)}, f32[8,256]{1,0:T(8,128)S(1)}, u32[]{:S(2)}, u32[]{:S(2)}) collective-permute-start(f32[8,256]{1,0:T(8,128)S(1)} %get-tuple-element.42.refs_1_), channel_id=1, source_target_pairs={{0,16},{8,24},{16,0},{24,8},{1,17},{9,25},{17,1},{25,9},{2,18},{10... | collective-permute-start | bytes 24584 | tf_op jit(solution)/shard_map/ppermute | solution.py:263
  59.0 5.5 %collective-permute-start.11 = (f32[8,256]{1,0:T(8,128)S(1)}, f32[8,256]{1,0:T(8,128)S(1)}, u32[]{:S(2)}, u32[]{:S(2)}) collective-permute-start(f32[8,256]{1,0:T(8,128)S(1)} %get-tuple-element.42.refs_1_), channel_id=1, source_target_pairs={{0,8},{8,0},{16,24},{24,16},{1,9},{9,1},{17,25},{25,17},{2,10},{10... | collective-permute-start | bytes 24584 | tf_op jit(solution)/shard_map/ppermute | solution.py:263
  67.6 4.3 %collective-permute-start.14 = (bf16[128,256]{1,0:T(8,128)(2,1)S(1)}, bf16[128,256]{1,0:T(8,128)(2,1)S(1)}, u32[]{:S(2)}, u32[]{:S(2)}) collective-permute-start(bf16[128,256]{1,0:T(8,128)(2,1)S(1)} %get-tuple-element.44), channel_id=1, source_target_pairs={{0,1},{1,0},{2,3},{3,2},{4,5},{5,4},{6,7},{7,6},{8,10},{9,11},{10,... | collective-permute-start | bytes 196616 | tf_op jit(solution)/shard_map/ppermute | solution.py:255
  71.9 4.5 %collective-permute-start.15 = (bf16[128,256]{1,0:T(8,128)(2,1)S(1)}, bf16[128,256]{1,0:T(8,128)(2,1)S(1)}, u32[]{:S(2)}, u32[]{:S(2)}) collective-permute-start(bf16[128,256]{1,0:T(8,128)(2,1)S(1)} %add_convert_fusion.5), channel_id=1, source_target_pairs={{0,2},{1,3},{2,0},{3,1},{4,6},{5,7},{6,4},{7,5},{8,12},{9,13},{10,... | collective-permute-start | bytes 196616 | tf_op jit(solution)/shard_map/ppermute | solution.py:255
  76.4 5.2 %collective-permute-start.16 = (bf16[128,256]{1,0:T(8,128)(2,1)S(1)}, bf16[128,256]{1,0:T(8,128)(2,1)S(1)}, u32[]{:S(2)}, u32[]{:S(2)}) collective-permute-start(bf16[128,256]{1,0:T(8,128)(2,1)S(1)} %add_convert_fusion.4.mine_ref), channel_id=1, source_target_pairs={{0,4},{1,5},{2,6},{3,7},{4,0},{5,1},{6,2},{7,3},{8,9},{9,8},{10,11... | collective-permute-start | bytes 196616 | tf_op jit(solution)/shard_map/ppermute | solution.py:255
  81.9 6.3 %collective-permute-start.19 = (f32[8,256]{1,0:T(8,128)S(1)}, f32[8,256]{1,0:T(8,128)S(1)}, u32[]{:S(2)}, u32[]{:S(2)}) collective-permute-start(f32[8,256]{1,0:T(8,128)S(1)} %get-tuple-element.47.refs_1_), channel_id=1, source_target_pairs={{0,24},{8,16},{16,8},{24,0},{1,25},{9,17},{17,9},{25,1},{2,26},{10... | collective-permute-start | bytes 24584 | tf_op jit(solution)/shard_map/ppermute | solution.py:263
  81.9 6.3 %collective-permute-start.18 = (f32[8,256]{1,0:T(8,128)S(1)}, f32[8,256]{1,0:T(8,128)S(1)}, u32[]{:S(2)}, u32[]{:S(2)}) collective-permute-start(f32[8,256]{1,0:T(8,128)S(1)} %get-tuple-element.47.refs_1_), channel_id=1, source_target_pairs={{0,16},{8,24},{16,0},{24,8},{1,17},{9,25},{17,1},{25,9},{2,18},{10... | collective-permute-start | bytes 24584 | tf_op jit(solution)/shard_map/ppermute | solution.py:263
  82.8 5.5 %collective-permute-start.17 = (f32[8,256]{1,0:T(8,128)S(1)}, f32[8,256]{1,0:T(8,128)S(1)}, u32[]{:S(2)}, u32[]{:S(2)}) collective-permute-start(f32[8,256]{1,0:T(8,128)S(1)} %get-tuple-element.47.refs_1_), channel_id=1, source_target_pairs={{0,8},{8,0},{16,24},{24,16},{1,9},{9,1},{17,25},{25,17},{2,10},{10... | collective-permute-start | bytes 24584 | tf_op jit(solution)/shard_map/ppermute | solution.py:263
  91.3 4.3 %collective-permute-start.20 = (bf16[128,256]{1,0:T(8,128)(2,1)S(1)}, bf16[128,256]{1,0:T(8,128)(2,1)S(1)}, u32[]{:S(2)}, u32[]{:S(2)}) collective-permute-start(bf16[128,256]{1,0:T(8,128)(2,1)S(1)} %get-tuple-element.54), channel_id=1, source_target_pairs={{0,1},{1,0},{2,3},{3,2},{4,5},{5,4},{6,7},{7,6},{8,10},{9,11},{10,... | collective-permute-start | bytes 196616 | tf_op jit(solution)/shard_map/ppermute | solution.py:255
  95.7 4.5 %collective-permute-start.21 = (bf16[128,256]{1,0:T(8,128)(2,1)S(1)}, bf16[128,256]{1,0:T(8,128)(2,1)S(1)}, u32[]{:S(2)}, u32[]{:S(2)}) collective-permute-start(bf16[128,256]{1,0:T(8,128)(2,1)S(1)} %add_convert_fusion.3), channel_id=1, source_target_pairs={{0,2},{1,3},{2,0},{3,1},{4,6},{5,7},{6,4},{7,5},{8,12},{9,13},{10,... | collective-permute-start | bytes 196616 | tf_op jit(solution)/shard_map/ppermute | solution.py:255
  100.2 5.2 %collective-permute-start.22 = (bf16[128,256]{1,0:T(8,128)(2,1)S(1)}, bf16[128,256]{1,0:T(8,128)(2,1)S(1)}, u32[]{:S(2)}, u32[]{:S(2)}) collective-permute-start(bf16[128,256]{1,0:T(8,128)(2,1)S(1)} %add_convert_fusion.2.mine_ref), channel_id=1, source_target_pairs={{0,4},{1,5},{2,6},{3,7},{4,0},{5,1},{6,2},{7,3},{8,9},{9,8},{10,11... | collective-permute-start | bytes 196616 | tf_op jit(solution)/shard_map/ppermute | solution.py:255
  105.7 6.3 %collective-permute-start.25 = (f32[8,256]{1,0:T(8,128)S(1)}, f32[8,256]{1,0:T(8,128)S(1)}, u32[]{:S(2)}, u32[]{:S(2)}) collective-permute-start(f32[8,256]{1,0:T(8,128)S(1)} %get-tuple-element.57.refs_1_), channel_id=1, source_target_pairs={{0,24},{8,16},{16,8},{24,0},{1,25},{9,17},{17,9},{25,1},{2,26},{10... | collective-permute-start | bytes 24584 | tf_op jit(solution)/shard_map/ppermute | solution.py:263
  105.7 6.3 %collective-permute-start.24 = (f32[8,256]{1,0:T(8,128)S(1)}, f32[8,256]{1,0:T(8,128)S(1)}, u32[]{:S(2)}, u32[]{:S(2)}) collective-permute-start(f32[8,256]{1,0:T(8,128)S(1)} %get-tuple-element.57.refs_1_), channel_id=1, source_target_pairs={{0,16},{8,24},{16,0},{24,8},{1,17},{9,25},{17,1},{25,9},{2,18},{10... | collective-permute-start | bytes 24584 | tf_op jit(solution)/shard_map/ppermute | solution.py:263
  106.6 5.5 %collective-permute-start.23 = (f32[8,256]{1,0:T(8,128)S(1)}, f32[8,256]{1,0:T(8,128)S(1)}, u32[]{:S(2)}, u32[]{:S(2)}) collective-permute-start(f32[8,256]{1,0:T(8,128)S(1)} %get-tuple-element.57.refs_1_), channel_id=1, source_target_pairs={{0,8},{8,0},{16,24},{24,16},{1,9},{9,1},{17,25},{25,17},{2,10},{10... | collective-permute-start | bytes 24584 | tf_op jit(solution)/shard_map/ppermute | solution.py:263
  115.5 4.3 %collective-permute-start.26 = (bf16[128,256]{1,0:T(8,128)(2,1)S(1)}, bf16[128,256]{1,0:T(8,128)(2,1)S(1)}, u32[]{:S(2)}, u32[]{:S(2)}) collective-permute-start(bf16[128,256]{1,0:T(8,128)(2,1)S(1)} %get-tuple-element.64), channel_id=1, source_target_pairs={{0,1},{1,0},{2,3},{3,2},{4,5},{5,4},{6,7},{7,6},{8,10},{9,11},{10,... | collective-permute-start | bytes 196616 | tf_op jit(solution)/shard_map/ppermute | solution.py:255
  119.7 4.5 %collective-permute-start.27 = (bf16[128,256]{1,0:T(8,128)(2,1)S(1)}, bf16[128,256]{1,0:T(8,128)(2,1)S(1)}, u32[]{:S(2)}, u32[]{:S(2)}) collective-permute-start(bf16[128,256]{1,0:T(8,128)(2,1)S(1)} %add_convert_fusion.1), channel_id=1, source_target_pairs={{0,2},{1,3},{2,0},{3,1},{4,6},{5,7},{6,4},{7,5},{8,12},{9,13},{10,... | collective-permute-start | bytes 196616 | tf_op jit(solution)/shard_map/ppermute | solution.py:255
  124.3 5.2 %collective-permute-start.28 = (bf16[128,256]{1,0:T(8,128)(2,1)S(1)}, bf16[128,256]{1,0:T(8,128)(2,1)S(1)}, u32[]{:S(2)}, u32[]{:S(2)}) collective-permute-start(bf16[128,256]{1,0:T(8,128)(2,1)S(1)} %add_convert_fusion.mine_ref), channel_id=1, source_target_pairs={{0,4},{1,5},{2,6},{3,7},{4,0},{5,1},{6,2},{7,3},{8,9},{9,8},{10,11... | collective-permute-start | bytes 196616 | tf_op jit(solution)/shard_map/ppermute | solution.py:255
  129.7 3.1 %collective-permute-start.31 = (f32[8,256]{1,0:T(8,128)S(1)}, f32[8,256]{1,0:T(8,128)S(1)}, u32[]{:S(2)}, u32[]{:S(2)}) collective-permute-start(f32[8,256]{1,0:T(8,128)S(1)} %get-tuple-element.67.refs_1_), channel_id=1, source_target_pairs={{0,24},{8,16},{16,8},{24,0},{1,25},{9,17},{17,9},{25,1},{2,26},{10... | collective-permute-start | bytes 24584 | tf_op jit(solution)/shard_map/ppermute | solution.py:263
  129.8 3.7 %collective-permute-start.30 = (f32[8,256]{1,0:T(8,128)S(1)}, f32[8,256]{1,0:T(8,128)S(1)}, u32[]{:S(2)}, u32[]{:S(2)}) collective-permute-start(f32[8,256]{1,0:T(8,128)S(1)} %get-tuple-element.67.refs_1_), channel_id=1, source_target_pairs={{0,16},{8,24},{16,0},{24,8},{1,17},{9,25},{17,1},{25,9},{2,18},{10... | collective-permute-start | bytes 24584 | tf_op jit(solution)/shard_map/ppermute | solution.py:263
  130.6 2.9 %collective-permute-start.29 = (f32[8,256]{1,0:T(8,128)S(1)}, f32[8,256]{1,0:T(8,128)S(1)}, u32[]{:S(2)}, u32[]{:S(2)}) collective-permute-start(f32[8,256]{1,0:T(8,128)S(1)} %get-tuple-element.67.refs_1_), channel_id=1, source_target_pairs={{0,8},{8,0},{16,24},{24,16},{1,9},{9,1},{17,25},{25,17},{2,10},{10... | collective-permute-start | bytes 24584 | tf_op jit(solution)/shard_map/ppermute | solution.py:263

commit v2 on v1

--- a/solution.py
+++ b/solution.py
@@ -58,7 +58,7 @@
         left = left.astype(BF16)
         total = jnp.zeros((OCTET, 2 * ties), F32)
         for j in range(count):
-            got = dot_t(left, ref[at + j])
+            got = dot(left, ref[at + j])
             one = got[0:8, :ties] + got[16:24, :ties]
             two = got[8:16, ties:] + got[24:32, ties:]
             got = jnp.concatenate([one, two], axis=1)
@@ -66,6 +66,15 @@
         out_ref[rows] = total
 
     octets((cjac_ref, ajac_ref, ejac_ref), body)
+
+
+def turn_kernel(*refs):
+    half = len(refs) // 2
+    for ref, out_ref in zip(refs[:half], refs[half:]):
+
+        @pl.loop(0, ref.shape[0])
+        def _(i, ref=ref, out_ref=out_ref):
+            out_ref[i] = ref[i].T
 
 
 def backward(q1_ref, q2_ref, put1_ref, put2_ref, cjac_ref, ajac_ref, ejac_ref, t1_ref, t2_ref):
@@ -103,9 +112,12 @@
     out_ref[...] = out.astype(BF16)
 
 
-def gather_kernel(scenes, start, mine_ref, got_ref, *refs):
+def gather_kernel(scenes, start, parts, *refs):
     first = pl.multiple_of(lax.axis_index("group") * scenes, scenes)
-    field = mine_ref[...].astype(F32) + got_ref[...].astype(F32)
+    field = refs[0][...].astype(F32)
+    for ref in refs[1:parts]:
+        field = field + ref[...].astype(F32)
+    refs = refs[parts:]
     if start:
         out_ref, packet_ref = refs
         field = -field
@@ -245,17 +257,27 @@
 
 
 def group_sum_but_last(sent):
-    n, g = lax.axis_size("orbit"), lax.axis_size("group")
-    stages = g.bit_length() - 1
-    for stage in range(stages):
-        route = []
-        for o in range(n):
-            mask = 1 << ((stage + o % 2) % stages)
-            route += [(o * g + i, o * g + (i ^ mask)) for i in range(g)]
-        got = lax.ppermute(sent, ("orbit", "group"), route)
-        if stage == stages - 1:
-            return sent, got
-        sent = lax.optimization_barrier((sent.astype(F32) + got.astype(F32)).astype(BF16))
+    size = lax.axis_size("group")
+    stride, pairs = 1, None
+    while stride < size:
+        masks = (1, 2, 3) if 4 * stride <= size else (1,)
+        got = [swap(sent, "group", mask * stride) for mask in masks]
+        stride *= len(masks) + 1
+        pairs = [sent] + got
+        if stride < size or len(pairs) > 2:
+            low = [p.astype(F32) for p in pairs]
+            total = low[0] + low[1]
+            if len(low) > 2:
+                total = total + (low[2] + low[3])
+            if stride < size:
+                sent = lax.optimization_barrier(total.astype(BF16))
+            else:
+                pairs = [total]
+    return pairs
+
+
+def swap(block, axis, mask):
+    return lax.ppermute(block, axis, [(i, i ^ mask) for i in range(lax.axis_size(axis))])
 
 
 def orbit_packets(packet):
@@ -322,15 +344,16 @@
 
     def project(field):
         scratch = [((2, slots, width), F32)] * 2
-        return call(project_kernel, [(pair, F32)], scratch, "project", (field, pick1, pick2) + jacs, work)[0]
+        return call(project_kernel, [(pair, F32)], scratch, "project", (field, pick1, pick2) + turned, work)[0]
 
     def finish(sums, res=None):
-        args = sums if res is None else sums + (res,)
-        kernel = functools.partial(gather_kernel, scenes, res is None)
+        args = sums if res is None else sums + [res]
+        kernel = functools.partial(gather_kernel, scenes, res is None, len(sums))
         field, packet = call(kernel, [(full, F32), ((OCTET, width), F32)], [], "finish", args)
         return field, orbit_packets(packet)
 
     (sent,) = call(rhs_kernel, [(full, BF16)], terms, "rhs", (observed, coef, put1, put2) + jacs, work)
+    turned = tuple(call(turn_kernel, [(j.shape, BF16) for j in jacs], [], "turn", jacs, work))
     res, packets = finish(group_sum_but_last(sent))
     part = project(res)
     fixed = (coef, put1, put2, damp) + jacs

time: 135 us -> 125 us (0.926)
  starting transfers between devices: 43 us -> 35.8 us
  waiting for transfers between devices: 41.8 us -> 37 us
  Pallas kernels: 34.5 us -> 36.8 us
    ppermute x15 -> x20, starting transfers between devices: 30.2 us -> 23 us  [swap(): lax.ppermute(block, axis, [(i, i ^ mask) for i in range(lax.axis_size(axi...]
    ppermute x15 -> x20, waiting for transfers between devices: 39.8 us -> 35.1 us  [swap(): lax.ppermute(block, axis, [(i, i ^ mask) for i in range(lax.axis_size(axi...]
    pallas_call x15 -> x16, Pallas kernels: 34.5 us -> 36.8 us  [call(): pl.pallas_call(kernel, out_shape=[jax.ShapeDtypeStruct(*o) for o in outs]...]
  transfers between devices with their start and end apart: 32 -> 37, of which waited for: 17 -> 21; matrix products, arithmetic and copies ran while one was open for 5% -> 6% of each run, Pallas kernels for 13% -> 16%
where the time goes in v2:
time: 125 us; the launch traced here: 124 us
  waiting for transfers between devices  37 us (30%)
  Pallas kernels  36.8 us (29%)
  starting transfers between devices  35.8 us (29%)
  local copies, waits for them, and re-layouts  10.4 us (8%)
  other arithmetic  3.36 us (3%)
    pallas_call x16, Pallas kernels, call(): pl.pallas_call(kernel, out_shape=[jax.ShapeDtypeStruct(*o) for o in outs]...  36.8 us
    ppermute x20, waiting for transfers between devices, swap(): lax.ppermute(block, axis, [(i, i ^ mask) for i in range(lax.axis_size(axi...  35.1 us
    ppermute x20, starting transfers between devices, swap(): lax.ppermute(block, axis, [(i, i ^ mask) for i in range(lax.axis_size(axi...  23 us
    ppermute x15, starting transfers between devices, orbit_packets(): lax.ppermute(packet, 'orbit', [(i, i ^ mask) for i in range(n)])  9.59 us
    unnamed x10, local copies, waits for them, and re-layouts  4.98 us
    ppermute x2, starting transfers between devices, pass_on(): return lax.ppermute(block, 'orbit', [(i, (i + 1) % n) for i in range(n)])  3.18 us
  transfers between devices with their start and end apart: 37, of which 21 were waited for; matrix products, arithmetic and copies ran while one was open for 6% of the time, Pallas kernels for 16%

profile of v2, /device:TPU:0, one launch (start us, length us, event | category | flops | bytes accessed | tf_op | source)
XLA Modules:
  0.0 124.4 jit_solution(1068162981197898509)
XLA Ops:
  0.6 0.7 fusion.9
  1.4 0.7 slice_bitcast_fusion
  2.1 0.5 collective-permute-start
  2.6 0.9 slice.75
  3.5 2.6 %collective-permute-start.1 = (bf16[1,256,256]{2,1,0:T(8,128)(2,1)S(1)}, bf16[1,256,256]{2,1,0:T(8,128)(2,1)S(1)}, u32[]{:S(2)}, u32[]{:S(2)}) collective-permute-start(bf16[1,256,256]{2,1,0:T(8,128)(2,1)S(1)} %bitcast.66), channel_id=1, source_target_pairs={{0,8},{8,16},{16,24},{24,0},{1,9},{9,17},{17,25},{25,1},{2,10},{10... | collective-permute-start | bytes 393224 | tf_op jit(solution)/shard_map/ppermute | solution.py:312
  6.2 0.8 fusion.13
  7.1 0.7 add_bitcast_fusion
  7.7 1.0 fusion.11
  8.7 1.0 fusion.10
  9.7 0.7 bitcast_add_fusion
  10.6 0.8 fusion.12
  11.4 0.7 select_bitcast_fusion
  12.4 3.4 %copy-done = bf16[1,64,2,128,256]{4,3,2,1,0:T(8,128)(2,1)S(1)} copy-done((bf16[1,64,2,128,256]{4,3,2,1,0:T(8,128)(2,1)S(1)}, bf16[1,64,2,128,256]{4,3,2,1,0:T(8,128)(2,1)}, u32[]{:S(2)}) %copy-start) | copy-done | bytes 8388632
  15.8 1.6 %copy-done.2 = bf16[1,16,2,128,256]{4,3,2,1,0:T(8,128)(2,1)S(1)} copy-done((bf16[1,16,2,128,256]{4,3,2,1,0:T(8,128)(2,1)S(1)}, bf16[1,16,2,128,256]{4,3,2,1,0:T(8,128)(2,1)}, u32[]{:S(2)}) %copy-start.2) | copy-done | bytes 2097176
  17.4 2.9 %rhs.1 = bf16[128,256]{1,0:T(8,128)(2,1)S(1)} custom-call(f32[88,256]{1,0:T(8,128)S(1)} %fusion.res_ref, f32[3,88,128]{2,1,0:T(8,128)S(1)} %pad_maximum_fusion.coef_ref.refs_5_, bf16[128,88]{1,0:T(8,128)(2,1)S(1)} %get-tuple-element.100.put1_ref.refs_6_, bf16[128,88]{1,0:T(8,128)(2,1)S(1)} %get-tuple-element.101.put2_ref.refs_7_, ...), custom_call_target="tpu_custom_call" | custom-call | flops 339738624 | bytes 10887168 | tf_op jit(solution)/shard_map/rhs/pallas_call | solution.py:244
  20.3 2.6 %collective-permute-start.4 = (bf16[128,256]{1,0:T(8,128)(2,1)S(1)}, bf16[128,256]{1,0:T(8,128)(2,1)S(1)}, u32[]{:S(2)}, u32[]{:S(2)}) collective-permute-start(bf16[128,256]{1,0:T(8,128)(2,1)S(1)} %rhs.1), channel_id=1, source_target_pairs={{0,3},{1,2},{2,1},{3,0},{4,7},{5,6},{6,5},{7,4},{8,11},{9,10},{10,... | collective-permute-start | bytes 196616 | tf_op jit(solution)/shard_map/ppermute | solution.py:280
  22.9 0.5 collective-permute-start.3
  23.3 0.5 collective-permute-start.2
  23.8 2.0 %collective-permute-done.4 = bf16[128,256]{1,0:T(8,128)(2,1)S(1)} collective-permute-done((bf16[128,256]{1,0:T(8,128)(2,1)S(1)}, bf16[128,256]{1,0:T(8,128)(2,1)S(1)}, u32[]{:S(2)}, u32[]{:S(2)}) %collective-permute-start.4) | collective-permute-done | bytes 65568 | tf_op jit(solution)/shard_map/ppermute | solution.py:280
  25.9 1.3 %collective-permute-done.3 = bf16[128,256]{1,0:T(8,128)(2,1)S(1)} collective-permute-done((bf16[128,256]{1,0:T(8,128)(2,1)S(1)}, bf16[128,256]{1,0:T(8,128)(2,1)S(1)}, u32[]{:S(2)}, u32[]{:S(2)}) %collective-permute-start.3) | collective-permute-done | bytes 65568 | tf_op jit(solution)/shard_map/ppermute | solution.py:280
  27.6 2.7 %collective-permute-start.5 = (bf16[128,256]{1,0:T(8,128)(2,1)S(1)}, bf16[128,256]{1,0:T(8,128)(2,1)S(1)}, u32[]{:S(2)}, u32[]{:S(2)}) collective-permute-start(bf16[128,256]{1,0:T(8,128)(2,1)S(1)} %add_convert_fusion.4.refs_0_), channel_id=1, source_target_pairs={{0,4},{1,5},{2,6},{3,7},{4,0},{5,1},{6,2},{7,3},{8,12},{9,13},{10,... | collective-permute-start | bytes 196616 | tf_op jit(solution)/shard_map/ppermute | solution.py:280
  30.4 7.1 %turn.1 = (bf16[64,256,256]{2,1,0:T(8,128)(2,1)S(1)}, bf16[16,256,256]{2,1,0:T(8,128)(2,1)S(1)}, bf16[1,256,256]{2,1,0:T(8,128)(2,1)S(1)}) custom-call(bf16[64,256,256]{2,1,0:T(8,128)(2,1)S(1)} %bitcast.51, bf16[16,256,256]{2,1,0:T(8,128)(2,1)S(1)} %bitcast.57, bf16[1,256,256]{2,1,0:T(8,128)(2,1)S(1)} %collective-permute-done.1.ejac_ref.refs_2_.refs_11_), custom_call_target="tpu_custom_call" | custom-call | flops 339738624 | bytes 10616832 | tf_op jit(solution)/shard_map/turn/pallas_call | solution.py:244
  37.6 0.6 collective-permute-start.7
  38.2 1.2 %collective-permute-start.6 = (f32[8,256]{1,0:T(8,128)S(1)}, f32[8,256]{1,0:T(8,128)S(1)}, u32[]{:S(2)}, u32[]{:S(2)}) collective-permute-start(f32[8,256]{1,0:T(8,128)S(1)} %get-tuple-element.45.refs_1_), channel_id=1, source_target_pairs={{0,8},{8,0},{16,24},{24,16},{1,9},{9,1},{17,25},{25,17},{2,10},{10... | collective-permute-start | bytes 24584 | tf_op jit(solution)/shard_map/ppermute | solution.py:285
  39.5 3.2 %project.4.refs_0_ = f32[88,256]{1,0:T(8,128)S(1)} custom-call(f32[128,256]{1,0:T(8,128)S(1)} %get-tuple-element.41.field_ref.refs_12_.refs_2_, bf16[88,128]{1,0:T(8,128)(2,1)S(1)} %get-tuple-element.102.pick1_ref, bf16[88,128]{1,0:T(8,128)(2,1)S(1)} %get-tuple-element.103.pick2_ref, bf16[64,256,256]{2,1,0:T(8,128)(2,1)S(1)} %get-tuple-element.42.cjac_ref, ...), custom_call_target="tpu_custom_call" | custom-call | flops 339738624 | bytes 10792960 | tf_op jit(solution)/shard_map/project/pallas_call | solution.py:244
  42.8 3.1 %step.4 = (bf16[128,256]{1,0:T(8,128)(2,1)S(1)}, f32[88,256]{1,0:T(8,128)S(1)}) custom-call(f32[88,256]{1,0:T(8,128)S(1)} %project.4.refs_0_, f32[8,256]{1,0:T(8,128)S(1)} %get-tuple-element.45.refs_1_, f32[8,256]{1,0:T(8,128)S(1)} %collective-permute-done.6.refs_2_, f32[8,256]{1,0:T(8,128)S(1)} %collective-permute-done.7.refs_3_, ...), custom_call_target="tpu_custom_call" | custom-call | flops 339738624 | bytes 11067392 | tf_op jit(solution)/shard_map/step/pallas_call | solution.py:244
  45.9 1.7 %collective-permute-start.11 = (bf16[128,256]{1,0:T(8,128)(2,1)S(1)}, bf16[128,256]{1,0:T(8,128)(2,1)S(1)}, u32[]{:S(2)}, u32[]{:S(2)}) collective-permute-start(bf16[128,256]{1,0:T(8,128)(2,1)S(1)} %get-tuple-element.46), channel_id=1, source_target_pairs={{0,3},{1,2},{2,1},{3,0},{4,7},{5,6},{6,5},{7,4},{8,11},{9,10},{10,... | collective-permute-start | bytes 196616 | tf_op jit(solution)/shard_map/ppermute | solution.py:280
  48.0 1.4 %collective-permute-start.9 = (bf16[128,256]{1,0:T(8,128)(2,1)S(1)}, bf16[128,256]{1,0:T(8,128)(2,1)S(1)}, u32[]{:S(2)}, u32[]{:S(2)}) collective-permute-start(bf16[128,256]{1,0:T(8,128)(2,1)S(1)} %get-tuple-element.46), channel_id=1, source_target_pairs={{0,1},{1,0},{2,3},{3,2},{4,5},{5,4},{6,7},{7,6},{8,9},{9,8},{10,11... | collective-permute-start | bytes 196616 | tf_op jit(solution)/shard_map/ppermute | solution.py:280
  49.4 2.0 %collective-permute-done.11 = bf16[128,256]{1,0:T(8,128)(2,1)S(1)} collective-permute-done((bf16[128,256]{1,0:T(8,128)(2,1)S(1)}, bf16[128,256]{1,0:T(8,128)(2,1)S(1)}, u32[]{:S(2)}, u32[]{:S(2)}) %collective-permute-start.11) | collective-permute-done | bytes 65568 | tf_op jit(solution)/shard_map/ppermute | solution.py:280
  52.7 4.8 %collective-permute-done.12.refs_1_ = bf16[128,256]{1,0:T(8,128)(2,1)S(1)} collective-permute-done((bf16[128,256]{1,0:T(8,128)(2,1)S(1)}, bf16[128,256]{1,0:T(8,128)(2,1)S(1)}, u32[]{:S(2)}, u32[]{:S(2)}) %collective-permute-start.12) | collective-permute-done | bytes 65568 | tf_op jit(solution)/shard_map/ppermute | solution.py:280
  57.8 1.0 collective-permute-start.14
  58.8 0.8 collective-permute-start.13
  59.6 3.2 %project.5.refs_0_ = f32[88,256]{1,0:T(8,128)S(1)} custom-call(f32[128,256]{1,0:T(8,128)S(1)} %get-tuple-element.47.field_ref.refs_13_, bf16[88,128]{1,0:T(8,128)(2,1)S(1)} %get-tuple-element.102.pick1_ref, bf16[88,128]{1,0:T(8,128)(2,1)S(1)} %get-tuple-element.103.pick2_ref, bf16[64,256,256]{2,1,0:T(8,128)(2,1)S(1)} %get-tuple-element.42.cjac_ref, ...), custom_call_target="tpu_custom_call" | custom-call | flops 339738624 | bytes 10792960 | tf_op jit(solution)/shard_map/project/pallas_call | solution.py:244
  62.9 3.1 %step.5 = (bf16[128,256]{1,0:T(8,128)(2,1)S(1)}, f32[88,256]{1,0:T(8,128)S(1)}, f32[128,256]{1,0:T(8,128)S(1)}, f32[128,256]{1,0:T(8,128)S(1)}, f32[88,256]{1,0:...) custom-call(f32[88,256]{1,0:T(8,128)S(1)} %project.5.refs_0_, ...), custom_call_target="tpu_custom_call" | custom-call | flops 339738624 | bytes 11304960 | tf_op jit(solution)/shard_map/step/pallas_call | solution.py:244
  66.0 2.5 %collective-permute-start.18 = (bf16[128,256]{1,0:T(8,128)(2,1)S(1)}, bf16[128,256]{1,0:T(8,128)(2,1)S(1)}, u32[]{:S(2)}, u32[]{:S(2)}) collective-permute-start(bf16[128,256]{1,0:T(8,128)(2,1)S(1)} %get-tuple-element.50), channel_id=1, source_target_pairs={{0,3},{1,2},{2,1},{3,0},{4,7},{5,6},{6,5},{7,4},{8,11},{9,10},{10,... | collective-permute-start | bytes 196616 | tf_op jit(solution)/shard_map/ppermute | solution.py:280
  69.0 0.6 collective-permute-start.16
  69.5 2.0 %collective-permute-done.18 = bf16[128,256]{1,0:T(8,128)(2,1)S(1)} collective-permute-done((bf16[128,256]{1,0:T(8,128)(2,1)S(1)}, bf16[128,256]{1,0:T(8,128)(2,1)S(1)}, u32[]{:S(2)}, u32[]{:S(2)}) %collective-permute-start.18) | collective-permute-done | bytes 65568 | tf_op jit(solution)/shard_map/ppermute | solution.py:280
  71.6 1.2 collective-permute-done.17
  73.3 0.5 collective-permute-start.19
  73.8 4.7 %collective-permute-done.19.refs_1_ = bf16[128,256]{1,0:T(8,128)(2,1)S(1)} collective-permute-done((bf16[128,256]{1,0:T(8,128)(2,1)S(1)}, bf16[128,256]{1,0:T(8,128)(2,1)S(1)}, u32[]{:S(2)}, u32[]{:S(2)}) %collective-permute-start.19) | collective-permute-done | bytes 65568 | tf_op jit(solution)/shard_map/ppermute | solution.py:280
  78.8 0.6 collective-permute-start.21
  79.4 1.2 collective-permute-start.20
  80.6 3.2 %project.6.refs_0_ = f32[88,256]{1,0:T(8,128)S(1)} custom-call(f32[128,256]{1,0:T(8,128)S(1)} %get-tuple-element.52.field_ref.refs_13_, bf16[88,128]{1,0:T(8,128)(2,1)S(1)} %get-tuple-element.102.pick1_ref, bf16[88,128]{1,0:T(8,128)(2,1)S(1)} %get-tuple-element.103.pick2_ref, bf16[64,256,256]{2,1,0:T(8,128)(2,1)S(1)} %get-tuple-element.42.cjac_ref, ...), custom_call_target="tpu_custom_call" | custom-call | flops 339738624 | bytes 10792960 | tf_op jit(solution)/shard_map/project/pallas_call | solution.py:244
  83.8 3.1 %step.6 = (bf16[128,256]{1,0:T(8,128)(2,1)S(1)}, f32[88,256]{1,0:T(8,128)S(1)}, f32[128,256]{1,0:T(8,128)S(1)}, f32[128,256]{1,0:T(8,128)S(1)}, f32[88,256]{1,0:...) custom-call(f32[88,256]{1,0:T(8,128)S(1)} %project.6.refs_0_, ...), custom_call_target="tpu_custom_call" | custom-call | flops 339738624 | bytes 11546624 | tf_op jit(solution)/shard_map/step/pallas_call | solution.py:244
  86.9 1.7 %collective-permute-start.25 = (bf16[128,256]{1,0:T(8,128)(2,1)S(1)}, bf16[128,256]{1,0:T(8,128)(2,1)S(1)}, u32[]{:S(2)}, u32[]{:S(2)}) collective-permute-start(bf16[128,256]{1,0:T(8,128)(2,1)S(1)} %get-tuple-element.60), channel_id=1, source_target_pairs={{0,3},{1,2},{2,1},{3,0},{4,7},{5,6},{6,5},{7,4},{8,11},{9,10},{10,... | collective-permute-start | bytes 196616 | tf_op jit(solution)/shard_map/ppermute | solution.py:280
  89.1 1.4 %collective-permute-start.23 = (bf16[128,256]{1,0:T(8,128)(2,1)S(1)}, bf16[128,256]{1,0:T(8,128)(2,1)S(1)}, u32[]{:S(2)}, u32[]{:S(2)}) collective-permute-start(bf16[128,256]{1,0:T(8,128)(2,1)S(1)} %get-tuple-element.60), channel_id=1, source_target_pairs={{0,1},{1,0},{2,3},{3,2},{4,5},{5,4},{6,7},{7,6},{8,9},{9,8},{10,11... | collective-permute-start | bytes 196616 | tf_op jit(solution)/shard_map/ppermute | solution.py:280
  90.5 2.0 %collective-permute-done.25 = bf16[128,256]{1,0:T(8,128)(2,1)S(1)} collective-permute-done((bf16[128,256]{1,0:T(8,128)(2,1)S(1)}, bf16[128,256]{1,0:T(8,128)(2,1)S(1)}, u32[]{:S(2)}, u32[]{:S(2)}) %collective-permute-start.25) | collective-permute-done | bytes 65568 | tf_op jit(solution)/shard_map/ppermute | solution.py:280
  93.4 0.9 collective-permute-start.26
  94.2 4.4 %collective-permute-done.26.refs_1_ = bf16[128,256]{1,0:T(8,128)(2,1)S(1)} collective-permute-done((bf16[128,256]{1,0:T(8,128)(2,1)S(1)}, bf16[128,256]{1,0:T(8,128)(2,1)S(1)}, u32[]{:S(2)}, u32[]{:S(2)}) %collective-permute-start.26) | collective-permute-done | bytes 65568 | tf_op jit(solution)/shard_map/ppermute | solution.py:280
  98.9 1.0 collective-permute-start.28
  99.9 0.8 collective-permute-start.27
  100.7 3.2 %project.7.refs_0_ = f32[88,256]{1,0:T(8,128)S(1)} custom-call(f32[128,256]{1,0:T(8,128)S(1)} %get-tuple-element.62.field_ref.refs_13_, bf16[88,128]{1,0:T(8,128)(2,1)S(1)} %get-tuple-element.102.pick1_ref, bf16[88,128]{1,0:T(8,128)(2,1)S(1)} %get-tuple-element.103.pick2_ref, bf16[64,256,256]{2,1,0:T(8,128)(2,1)S(1)} %get-tuple-element.42.cjac_ref, ...), custom_call_target="tpu_custom_call" | custom-call | flops 339738624 | bytes 10792960 | tf_op jit(solution)/shard_map/project/pallas_call | solution.py:244
  103.9 3.4 %step.7 = (bf16[128,256]{1,0:T(8,128)(2,1)S(1)}, f32[88,256]{1,0:T(8,128)}, f32[128,256]{1,0:T(8,128)S(1)}, f32[128,256]{1,0:T(8,128)S(1)}, f32[88,256]{1,0:T(8,...) custom-call(f32[88,256]{1,0:T(8,128)S(1)} %project.7.refs_0_, ...), custom_call_target="tpu_custom_call" | custom-call | flops 339738624 | bytes 11546624 | tf_op jit(solution)/shard_map/step/pallas_call | solution.py:244
  107.4 2.4 %collective-permute-start.32 = (bf16[128,256]{1,0:T(8,128)(2,1)S(1)}, bf16[128,256]{1,0:T(8,128)(2,1)S(1)}, u32[]{:S(2)}, u32[]{:S(2)}) collective-permute-start(bf16[128,256]{1,0:T(8,128)(2,1)S(1)} %get-tuple-element.70), channel_id=1, source_target_pairs={{0,3},{1,2},{2,1},{3,0},{4,7},{5,6},{6,5},{7,4},{8,11},{9,10},{10,... | collective-permute-start | bytes 196616 | tf_op jit(solution)/shard_map/ppermute | solution.py:280
  110.3 0.6 collective-permute-start.30
  110.8 2.0 %collective-permute-done.32 = bf16[128,256]{1,0:T(8,128)(2,1)S(1)} collective-permute-done((bf16[128,256]{1,0:T(8,128)(2,1)S(1)}, bf16[128,256]{1,0:T(8,128)(2,1)S(1)}, u32[]{:S(2)}, u32[]{:S(2)}) %collective-permute-start.32) | collective-permute-done | bytes 65568 | tf_op jit(solution)/shard_map/ppermute | solution.py:280
  112.9 1.2 collective-permute-done.31
  114.6 0.8 collective-permute-start.33
  115.4 4.4 %collective-permute-done.33.refs_1_ = bf16[128,256]{1,0:T(8,128)(2,1)S(1)} collective-permute-done((bf16[128,256]{1,0:T(8,128)(2,1)S(1)}, bf16[128,256]{1,0:T(8,128)(2,1)S(1)}, u32[]{:S(2)}, u32[]{:S(2)}) %collective-permute-start.33) | collective-permute-done | bytes 65568 | tf_op jit(solution)/shard_map/ppermute | solution.py:280
  120.1 0.6 collective-permute-start.35
  120.7 1.2 collective-permute-start.34
  121.9 1.2 collective-permute-done.36.refs_4_
  123.1 0.7 collective-permute-done.35.refs_3_
  123.8 0.6 final.1
  (72 shorter events, 7.1 us)
Async XLA Ops:
  2.1 9.3 %collective-permute-start = (f32[8,128]{1,0:T(8,128)S(1)}, f32[8,128]{1,0:T(8,128)S(1)}, u32[]{:S(2)}, u32[]{:S(2)}) collective-permute-start(f32[8,128]{1,0:T(8,128)S(1)} %concatenate.100), channel_id=1, source_target_pairs={{0,8},{8,16},{16,24},{24,0},{1,9},{9,17},{17,25},{25,1},{2,10},{10... | collective-permute-start | bytes 12296 | tf_op jit(solution)/shard_map/ppermute | solution.py:312
  3.5 8.8 %collective-permute-start.1 = (bf16[1,256,256]{2,1,0:T(8,128)(2,1)S(1)}, bf16[1,256,256]{2,1,0:T(8,128)(2,1)S(1)}, u32[]{:S(2)}, u32[]{:S(2)}) collective-permute-start(bf16[1,256,256]{2,1,0:T(8,128)(2,1)S(1)} %bitcast.66), channel_id=1, source_target_pairs={{0,8},{8,16},{16,24},{24,0},{1,9},{9,17},{17,25},{25,1},{2,10},{10... | collective-permute-start | bytes 393224 | tf_op jit(solution)/shard_map/ppermute | solution.py:312
  12.4 3.4 %copy-start = (bf16[1,64,2,128,256]{4,3,2,1,0:T(8,128)(2,1)S(1)}, bf16[1,64,2,128,256]{4,3,2,1,0:T(8,128)(2,1)}, u32[]{:S(2)}) copy-start(bf16[1,64,2,128,256]{4,3,2,1,0:T(8,128)(2,1)} %param.16) | copy-start | bytes 25165828
  15.8 1.6 %copy-start.2 = (bf16[1,16,2,128,256]{4,3,2,1,0:T(8,128)(2,1)S(1)}, bf16[1,16,2,128,256]{4,3,2,1,0:T(8,128)(2,1)}, u32[]{:S(2)}) copy-start(bf16[1,16,2,128,256]{4,3,2,1,0:T(8,128)(2,1)} %param.11) | copy-start | bytes 6291460
  17.4 13.0 %copy-start.1 = (bf16[1,64,2,128,256]{4,3,2,1,0:T(8,128)(2,1)S(1)}, bf16[1,64,2,128,256]{4,3,2,1,0:T(8,128)(2,1)}, u32[]{:S(2)}) copy-start(bf16[1,64,2,128,256]{4,3,2,1,0:T(8,128)(2,1)} %param.16) | copy-start | bytes 25165828
  17.4 13.0 %copy-start.3 = (bf16[1,16,2,128,256]{4,3,2,1,0:T(8,128)(2,1)S(1)}, bf16[1,16,2,128,256]{4,3,2,1,0:T(8,128)(2,1)}, u32[]{:S(2)}) copy-start(bf16[1,16,2,128,256]{4,3,2,1,0:T(8,128)(2,1)} %param.11) | copy-start | bytes 6291460
  20.3 5.6 %collective-permute-start.4 = (bf16[128,256]{1,0:T(8,128)(2,1)S(1)}, bf16[128,256]{1,0:T(8,128)(2,1)S(1)}, u32[]{:S(2)}, u32[]{:S(2)}) collective-permute-start(bf16[128,256]{1,0:T(8,128)(2,1)S(1)} %rhs.1), channel_id=1, source_target_pairs={{0,3},{1,2},{2,1},{3,0},{4,7},{5,6},{6,5},{7,4},{8,11},{9,10},{10,... | collective-permute-start | bytes 196616 | tf_op jit(solution)/shard_map/ppermute | solution.py:280
  22.9 4.3 %collective-permute-start.3 = (bf16[128,256]{1,0:T(8,128)(2,1)S(1)}, bf16[128,256]{1,0:T(8,128)(2,1)S(1)}, u32[]{:S(2)}, u32[]{:S(2)}) collective-permute-start(bf16[128,256]{1,0:T(8,128)(2,1)S(1)} %rhs.1), channel_id=1, source_target_pairs={{0,2},{1,3},{2,0},{3,1},{4,6},{5,7},{6,4},{7,5},{8,10},{9,11},{10,... | collective-permute-start | bytes 196616 | tf_op jit(solution)/shard_map/ppermute | solution.py:280
  23.3 4.3 %collective-permute-start.2 = (bf16[128,256]{1,0:T(8,128)(2,1)S(1)}, bf16[128,256]{1,0:T(8,128)(2,1)S(1)}, u32[]{:S(2)}, u32[]{:S(2)}) collective-permute-start(bf16[128,256]{1,0:T(8,128)(2,1)S(1)} %rhs.1), channel_id=1, source_target_pairs={{0,1},{1,0},{2,3},{3,2},{4,5},{5,4},{6,7},{7,6},{8,9},{9,8},{10,11... | collective-permute-start | bytes 196616 | tf_op jit(solution)/shard_map/ppermute | solution.py:280
  27.6 9.9 %collective-permute-start.5 = (bf16[128,256]{1,0:T(8,128)(2,1)S(1)}, bf16[128,256]{1,0:T(8,128)(2,1)S(1)}, u32[]{:S(2)}, u32[]{:S(2)}) collective-permute-start(bf16[128,256]{1,0:T(8,128)(2,1)S(1)} %add_convert_fusion.4.refs_0_), channel_id=1, source_target_pairs={{0,4},{1,5},{2,6},{3,7},{4,0},{5,1},{6,2},{7,3},{8,12},{9,13},{10,... | collective-permute-start | bytes 196616 | tf_op jit(solution)/shard_map/ppermute | solution.py:280
  30.4 12.3 %copy-start.4 = (f32[1,16]{1,0:T(1,128)S(1)}, f32[1,16]{1,0:T(1,128)}, u32[]{:S(2)}) copy-start(f32[1,16]{1,0:T(1,128)} %param.15) | copy-start | bytes 196
  37.6 5.1 %collective-permute-start.8 = (f32[8,256]{1,0:T(8,128)S(1)}, f32[8,256]{1,0:T(8,128)S(1)}, u32[]{:S(2)}, u32[]{:S(2)}) collective-permute-start(f32[8,256]{1,0:T(8,128)S(1)} %get-tuple-element.45.refs_1_), channel_id=1, source_target_pairs={{0,24},{8,16},{16,8},{24,0},{1,25},{9,17},{17,9},{25,1},{2,26},{10... | collective-permute-start | bytes 24584 | tf_op jit(solution)/shard_map/ppermute | solution.py:285
  37.6 5.1 %collective-permute-start.7 = (f32[8,256]{1,0:T(8,128)S(1)}, f32[8,256]{1,0:T(8,128)S(1)}, u32[]{:S(2)}, u32[]{:S(2)}) collective-permute-start(f32[8,256]{1,0:T(8,128)S(1)} %get-tuple-element.45.refs_1_), channel_id=1, source_target_pairs={{0,16},{8,24},{16,0},{24,8},{1,17},{9,25},{17,1},{25,9},{2,18},{10... | collective-permute-start | bytes 24584 | tf_op jit(solution)/shard_map/ppermute | solution.py:285
  38.2 4.5 %collective-permute-start.6 = (f32[8,256]{1,0:T(8,128)S(1)}, f32[8,256]{1,0:T(8,128)S(1)}, u32[]{:S(2)}, u32[]{:S(2)}) collective-permute-start(f32[8,256]{1,0:T(8,128)S(1)} %get-tuple-element.45.refs_1_), channel_id=1, source_target_pairs={{0,8},{8,0},{16,24},{24,16},{1,9},{9,1},{17,25},{25,17},{2,10},{10... | collective-permute-start | bytes 24584 | tf_op jit(solution)/shard_map/ppermute | solution.py:285
  45.9 5.6 %collective-permute-start.11 = (bf16[128,256]{1,0:T(8,128)(2,1)S(1)}, bf16[128,256]{1,0:T(8,128)(2,1)S(1)}, u32[]{:S(2)}, u32[]{:S(2)}) collective-permute-start(bf16[128,256]{1,0:T(8,128)(2,1)S(1)} %get-tuple-element.46), channel_id=1, source_target_pairs={{0,3},{1,2},{2,1},{3,0},{4,7},{5,6},{6,5},{7,4},{8,11},{9,10},{10,... | collective-permute-start | bytes 196616 | tf_op jit(solution)/shard_map/ppermute | solution.py:280
  47.5 4.3 %collective-permute-start.10 = (bf16[128,256]{1,0:T(8,128)(2,1)S(1)}, bf16[128,256]{1,0:T(8,128)(2,1)S(1)}, u32[]{:S(2)}, u32[]{:S(2)}) collective-permute-start(bf16[128,256]{1,0:T(8,128)(2,1)S(1)} %get-tuple-element.46), channel_id=1, source_target_pairs={{0,2},{1,3},{2,0},{3,1},{4,6},{5,7},{6,4},{7,5},{8,10},{9,11},{10,... | collective-permute-start | bytes 196616 | tf_op jit(solution)/shard_map/ppermute | solution.py:280
  48.0 4.3 %collective-permute-start.9 = (bf16[128,256]{1,0:T(8,128)(2,1)S(1)}, bf16[128,256]{1,0:T(8,128)(2,1)S(1)}, u32[]{:S(2)}, u32[]{:S(2)}) collective-permute-start(bf16[128,256]{1,0:T(8,128)(2,1)S(1)} %get-tuple-element.46), channel_id=1, source_target_pairs={{0,1},{1,0},{2,3},{3,2},{4,5},{5,4},{6,7},{7,6},{8,9},{9,8},{10,11... | collective-permute-start | bytes 196616 | tf_op jit(solution)/shard_map/ppermute | solution.py:280
  52.3 5.2 %collective-permute-start.12 = (bf16[128,256]{1,0:T(8,128)(2,1)S(1)}, bf16[128,256]{1,0:T(8,128)(2,1)S(1)}, u32[]{:S(2)}, u32[]{:S(2)}) collective-permute-start(bf16[128,256]{1,0:T(8,128)(2,1)S(1)} %add_convert_fusion.3.refs_0_), channel_id=1, source_target_pairs={{0,4},{1,5},{2,6},{3,7},{4,0},{5,1},{6,2},{7,3},{8,12},{9,13},{10,... | collective-permute-start | bytes 196616 | tf_op jit(solution)/shard_map/ppermute | solution.py:280
  57.7 5.1 %collective-permute-start.15 = (f32[8,256]{1,0:T(8,128)S(1)}, f32[8,256]{1,0:T(8,128)S(1)}, u32[]{:S(2)}, u32[]{:S(2)}) collective-permute-start(f32[8,256]{1,0:T(8,128)S(1)} %get-tuple-element.48.refs_1_), channel_id=1, source_target_pairs={{0,24},{8,16},{16,8},{24,0},{1,25},{9,17},{17,9},{25,1},{2,26},{10... | collective-permute-start | bytes 24584 | tf_op jit(solution)/shard_map/ppermute | solution.py:285
  57.8 5.1 %collective-permute-start.14 = (f32[8,256]{1,0:T(8,128)S(1)}, f32[8,256]{1,0:T(8,128)S(1)}, u32[]{:S(2)}, u32[]{:S(2)}) collective-permute-start(f32[8,256]{1,0:T(8,128)S(1)} %get-tuple-element.48.refs_1_), channel_id=1, source_target_pairs={{0,16},{8,24},{16,0},{24,8},{1,17},{9,25},{17,1},{25,9},{2,18},{10... | collective-permute-start | bytes 24584 | tf_op jit(solution)/shard_map/ppermute | solution.py:285
  58.8 4.0 %collective-permute-start.13 = (f32[8,256]{1,0:T(8,128)S(1)}, f32[8,256]{1,0:T(8,128)S(1)}, u32[]{:S(2)}, u32[]{:S(2)}) collective-permute-start(f32[8,256]{1,0:T(8,128)S(1)} %get-tuple-element.48.refs_1_), channel_id=1, source_target_pairs={{0,8},{8,0},{16,24},{24,16},{1,9},{9,1},{17,25},{25,17},{2,10},{10... | collective-permute-start | bytes 24584 | tf_op jit(solution)/shard_map/ppermute | solution.py:285
  66.0 5.6 %collective-permute-start.18 = (bf16[128,256]{1,0:T(8,128)(2,1)S(1)}, bf16[128,256]{1,0:T(8,128)(2,1)S(1)}, u32[]{:S(2)}, u32[]{:S(2)}) collective-permute-start(bf16[128,256]{1,0:T(8,128)(2,1)S(1)} %get-tuple-element.50), channel_id=1, source_target_pairs={{0,3},{1,2},{2,1},{3,0},{4,7},{5,6},{6,5},{7,4},{8,11},{9,10},{10,... | collective-permute-start | bytes 196616 | tf_op jit(solution)/shard_map/ppermute | solution.py:280
  68.5 4.3 %collective-permute-start.17 = (bf16[128,256]{1,0:T(8,128)(2,1)S(1)}, bf16[128,256]{1,0:T(8,128)(2,1)S(1)}, u32[]{:S(2)}, u32[]{:S(2)}) collective-permute-start(bf16[128,256]{1,0:T(8,128)(2,1)S(1)} %get-tuple-element.50), channel_id=1, source_target_pairs={{0,2},{1,3},{2,0},{3,1},{4,6},{5,7},{6,4},{7,5},{8,10},{9,11},{10,... | collective-permute-start | bytes 196616 | tf_op jit(solution)/shard_map/ppermute | solution.py:280
  69.0 4.3 %collective-permute-start.16 = (bf16[128,256]{1,0:T(8,128)(2,1)S(1)}, bf16[128,256]{1,0:T(8,128)(2,1)S(1)}, u32[]{:S(2)}, u32[]{:S(2)}) collective-permute-start(bf16[128,256]{1,0:T(8,128)(2,1)S(1)} %get-tuple-element.50), channel_id=1, source_target_pairs={{0,1},{1,0},{2,3},{3,2},{4,5},{5,4},{6,7},{7,6},{8,9},{9,8},{10,11... | collective-permute-start | bytes 196616 | tf_op jit(solution)/shard_map/ppermute | solution.py:280
  73.3 5.2 %collective-permute-start.19 = (bf16[128,256]{1,0:T(8,128)(2,1)S(1)}, bf16[128,256]{1,0:T(8,128)(2,1)S(1)}, u32[]{:S(2)}, u32[]{:S(2)}) collective-permute-start(bf16[128,256]{1,0:T(8,128)(2,1)S(1)} %add_convert_fusion.2.refs_0_), channel_id=1, source_target_pairs={{0,4},{1,5},{2,6},{3,7},{4,0},{5,1},{6,2},{7,3},{8,12},{9,13},{10,... | collective-permute-start | bytes 196616 | tf_op jit(solution)/shard_map/ppermute | solution.py:280
  78.7 5.1 %collective-permute-start.22 = (f32[8,256]{1,0:T(8,128)S(1)}, f32[8,256]{1,0:T(8,128)S(1)}, u32[]{:S(2)}, u32[]{:S(2)}) collective-permute-start(f32[8,256]{1,0:T(8,128)S(1)} %get-tuple-element.53.refs_1_), channel_id=1, source_target_pairs={{0,24},{8,16},{16,8},{24,0},{1,25},{9,17},{17,9},{25,1},{2,26},{10... | collective-permute-start | bytes 24584 | tf_op jit(solution)/shard_map/ppermute | solution.py:285
  78.8 5.1 %collective-permute-start.21 = (f32[8,256]{1,0:T(8,128)S(1)}, f32[8,256]{1,0:T(8,128)S(1)}, u32[]{:S(2)}, u32[]{:S(2)}) collective-permute-start(f32[8,256]{1,0:T(8,128)S(1)} %get-tuple-element.53.refs_1_), channel_id=1, source_target_pairs={{0,16},{8,24},{16,0},{24,8},{1,17},{9,25},{17,1},{25,9},{2,18},{10... | collective-permute-start | bytes 24584 | tf_op jit(solution)/shard_map/ppermute | solution.py:285
  79.4 4.5 %collective-permute-start.20 = (f32[8,256]{1,0:T(8,128)S(1)}, f32[8,256]{1,0:T(8,128)S(1)}, u32[]{:S(2)}, u32[]{:S(2)}) collective-permute-start(f32[8,256]{1,0:T(8,128)S(1)} %get-tuple-element.53.refs_1_), channel_id=1, source_target_pairs={{0,8},{8,0},{16,24},{24,16},{1,9},{9,1},{17,25},{25,17},{2,10},{10... | collective-permute-start | bytes 24584 | tf_op jit(solution)/shard_map/ppermute | solution.py:285
  86.9 5.6 %collective-permute-start.25 = (bf16[128,256]{1,0:T(8,128)(2,1)S(1)}, bf16[128,256]{1,0:T(8,128)(2,1)S(1)}, u32[]{:S(2)}, u32[]{:S(2)}) collective-permute-start(bf16[128,256]{1,0:T(8,128)(2,1)S(1)} %get-tuple-element.60), channel_id=1, source_target_pairs={{0,3},{1,2},{2,1},{3,0},{4,7},{5,6},{6,5},{7,4},{8,11},{9,10},{10,... | collective-permute-start | bytes 196616 | tf_op jit(solution)/shard_map/ppermute | solution.py:280
  88.6 4.3 %collective-permute-start.24 = (bf16[128,256]{1,0:T(8,128)(2,1)S(1)}, bf16[128,256]{1,0:T(8,128)(2,1)S(1)}, u32[]{:S(2)}, u32[]{:S(2)}) collective-permute-start(bf16[128,256]{1,0:T(8,128)(2,1)S(1)} %get-tuple-element.60), channel_id=1, source_target_pairs={{0,2},{1,3},{2,0},{3,1},{4,6},{5,7},{6,4},{7,5},{8,10},{9,11},{10,... | collective-permute-start | bytes 196616 | tf_op jit(solution)/shard_map/ppermute | solution.py:280
  89.1 4.3 %collective-permute-start.23 = (bf16[128,256]{1,0:T(8,128)(2,1)S(1)}, bf16[128,256]{1,0:T(8,128)(2,1)S(1)}, u32[]{:S(2)}, u32[]{:S(2)}) collective-permute-start(bf16[128,256]{1,0:T(8,128)(2,1)S(1)} %get-tuple-element.60), channel_id=1, source_target_pairs={{0,1},{1,0},{2,3},{3,2},{4,5},{5,4},{6,7},{7,6},{8,9},{9,8},{10,11... | collective-permute-start | bytes 196616 | tf_op jit(solution)/shard_map/ppermute | solution.py:280
  93.4 5.2 %collective-permute-start.26 = (bf16[128,256]{1,0:T(8,128)(2,1)S(1)}, bf16[128,256]{1,0:T(8,128)(2,1)S(1)}, u32[]{:S(2)}, u32[]{:S(2)}) collective-permute-start(bf16[128,256]{1,0:T(8,128)(2,1)S(1)} %add_convert_fusion.1.refs_0_), channel_id=1, source_target_pairs={{0,4},{1,5},{2,6},{3,7},{4,0},{5,1},{6,2},{7,3},{8,12},{9,13},{10,... | collective-permute-start | bytes 196616 | tf_op jit(solution)/shard_map/ppermute | solution.py:280
  98.8 5.1 %collective-permute-start.29 = (f32[8,256]{1,0:T(8,128)S(1)}, f32[8,256]{1,0:T(8,128)S(1)}, u32[]{:S(2)}, u32[]{:S(2)}) collective-permute-start(f32[8,256]{1,0:T(8,128)S(1)} %get-tuple-element.63.refs_1_), channel_id=1, source_target_pairs={{0,24},{8,16},{16,8},{24,0},{1,25},{9,17},{17,9},{25,1},{2,26},{10... | collective-permute-start | bytes 24584 | tf_op jit(solution)/shard_map/ppermute | solution.py:285
  98.9 5.1 %collective-permute-start.28 = (f32[8,256]{1,0:T(8,128)S(1)}, f32[8,256]{1,0:T(8,128)S(1)}, u32[]{:S(2)}, u32[]{:S(2)}) collective-permute-start(f32[8,256]{1,0:T(8,128)S(1)} %get-tuple-element.63.refs_1_), channel_id=1, source_target_pairs={{0,16},{8,24},{16,0},{24,8},{1,17},{9,25},{17,1},{25,9},{2,18},{10... | collective-permute-start | bytes 24584 | tf_op jit(solution)/shard_map/ppermute | solution.py:285
  99.9 4.0 %collective-permute-start.27 = (f32[8,256]{1,0:T(8,128)S(1)}, f32[8,256]{1,0:T(8,128)S(1)}, u32[]{:S(2)}, u32[]{:S(2)}) collective-permute-start(f32[8,256]{1,0:T(8,128)S(1)} %get-tuple-element.63.refs_1_), channel_id=1, source_target_pairs={{0,8},{8,0},{16,24},{24,16},{1,9},{9,1},{17,25},{25,17},{2,10},{10... | collective-permute-start | bytes 24584 | tf_op jit(solution)/shard_map/ppermute | solution.py:285
  107.4 5.5 %collective-permute-start.32 = (bf16[128,256]{1,0:T(8,128)(2,1)S(1)}, bf16[128,256]{1,0:T(8,128)(2,1)S(1)}, u32[]{:S(2)}, u32[]{:S(2)}) collective-permute-start(bf16[128,256]{1,0:T(8,128)(2,1)S(1)} %get-tuple-element.70), channel_id=1, source_target_pairs={{0,3},{1,2},{2,1},{3,0},{4,7},{5,6},{6,5},{7,4},{8,11},{9,10},{10,... | collective-permute-start | bytes 196616 | tf_op jit(solution)/shard_map/ppermute | solution.py:280
  109.8 4.3 %collective-permute-start.31 = (bf16[128,256]{1,0:T(8,128)(2,1)S(1)}, bf16[128,256]{1,0:T(8,128)(2,1)S(1)}, u32[]{:S(2)}, u32[]{:S(2)}) collective-permute-start(bf16[128,256]{1,0:T(8,128)(2,1)S(1)} %get-tuple-element.70), channel_id=1, source_target_pairs={{0,2},{1,3},{2,0},{3,1},{4,6},{5,7},{6,4},{7,5},{8,10},{9,11},{10,... | collective-permute-start | bytes 196616 | tf_op jit(solution)/shard_map/ppermute | solution.py:280
  110.3 4.3 %collective-permute-start.30 = (bf16[128,256]{1,0:T(8,128)(2,1)S(1)}, bf16[128,256]{1,0:T(8,128)(2,1)S(1)}, u32[]{:S(2)}, u32[]{:S(2)}) collective-permute-start(bf16[128,256]{1,0:T(8,128)(2,1)S(1)} %get-tuple-element.70), channel_id=1, source_target_pairs={{0,1},{1,0},{2,3},{3,2},{4,5},{5,4},{6,7},{7,6},{8,9},{9,8},{10,11... | collective-permute-start | bytes 196616 | tf_op jit(solution)/shard_map/ppermute | solution.py:280
  114.6 5.2 %collective-permute-start.33 = (bf16[128,256]{1,0:T(8,128)(2,1)S(1)}, bf16[128,256]{1,0:T(8,128)(2,1)S(1)}, u32[]{:S(2)}, u32[]{:S(2)}) collective-permute-start(bf16[128,256]{1,0:T(8,128)(2,1)S(1)} %add_convert_fusion.refs_0_), channel_id=1, source_target_pairs={{0,4},{1,5},{2,6},{3,7},{4,0},{5,1},{6,2},{7,3},{8,12},{9,13},{10,... | collective-permute-start | bytes 196616 | tf_op jit(solution)/shard_map/ppermute | solution.py:280
  120.0 3.1 %collective-permute-start.36 = (f32[8,256]{1,0:T(8,128)S(1)}, f32[8,256]{1,0:T(8,128)S(1)}, u32[]{:S(2)}, u32[]{:S(2)}) collective-permute-start(f32[8,256]{1,0:T(8,128)S(1)} %get-tuple-element.73.refs_1_), channel_id=1, source_target_pairs={{0,24},{8,16},{16,8},{24,0},{1,25},{9,17},{17,9},{25,1},{2,26},{10... | collective-permute-start | bytes 24584 | tf_op jit(solution)/shard_map/ppermute | solution.py:285
  120.1 3.7 %collective-permute-start.35 = (f32[8,256]{1,0:T(8,128)S(1)}, f32[8,256]{1,0:T(8,128)S(1)}, u32[]{:S(2)}, u32[]{:S(2)}) collective-permute-start(f32[8,256]{1,0:T(8,128)S(1)} %get-tuple-element.73.refs_1_), channel_id=1, source_target_pairs={{0,16},{8,24},{16,0},{24,8},{1,17},{9,25},{17,1},{25,9},{2,18},{10... | collective-permute-start | bytes 24584 | tf_op jit(solution)/shard_map/ppermute | solution.py:285
  120.7 3.1 %collective-permute-start.34 = (f32[8,256]{1,0:T(8,128)S(1)}, f32[8,256]{1,0:T(8,128)S(1)}, u32[]{:S(2)}, u32[]{:S(2)}) collective-permute-start(f32[8,256]{1,0:T(8,128)S(1)} %get-tuple-element.73.refs_1_), channel_id=1, source_target_pairs={{0,8},{8,0},{16,24},{24,16},{1,9},{9,1},{17,25},{25,17},{2,10},{10... | collective-permute-start | bytes 24584 | tf_op jit(solution)/shard_map/ppermute | solution.py:285

commit v3 on v2

--- a/solution.py
+++ b/solution.py
@@ -31,70 +31,66 @@
 
 def octets(refs, body):
     slot = 0
-    for ref in refs:
+    for number, ref in enumerate(refs):
         blocks = ref.shape[0]
         if blocks <= OCTET:
-            body(ref, 0, slot, blocks)
+            body(number, ref, 0, slot, blocks)
         else:
 
             @pl.loop(0, blocks // OCTET)
-            def _(i, ref=ref, slot=slot):
+            def _(i, number=number, ref=ref, slot=slot):
                 at = pl.multiple_of(i * OCTET, OCTET)
-                body(ref, at, pl.multiple_of(slot + at, OCTET), OCTET)
+                body(number, ref, at, pl.multiple_of(slot + at, OCTET), OCTET)
 
         slot += -(-blocks // OCTET) * OCTET
 
 
-def project_kernel(field_ref, pick1_ref, pick2_ref, cjac_ref, ajac_ref, ejac_ref, out_ref, l1_ref, l2_ref):
+def project_kernel(turned, field_ref, pick1_ref, pick2_ref, *refs):
+    *jac_refs, out_ref, l1_ref, l2_ref = refs
+    product = [dot if is_turned else dot_t for is_turned in turned]
     ties = out_ref.shape[1] // 2
     high, low = halves(field_ref[...])
     for pick_ref, left_ref in ((pick1_ref, l1_ref), (pick2_ref, l2_ref)):
         left_ref[0] = dot(pick_ref[...], high)
         left_ref[1] = dot(pick_ref[...], low)
 
-    def body(ref, at, slot, count):
+    def body(number, ref, at, slot, count):
         rows = pl.ds(slot, OCTET)
         left = jnp.concatenate([l1_ref[0, rows], l2_ref[0, rows], l1_ref[1, rows], l2_ref[1, rows]])
         left = left.astype(BF16)
         total = jnp.zeros((OCTET, 2 * ties), F32)
         for j in range(count):
-            got = dot(left, ref[at + j])
+            got = product[number](left, ref[at + j])
             one = got[0:8, :ties] + got[16:24, :ties]
             two = got[8:16, ties:] + got[24:32, ties:]
             got = jnp.concatenate([one, two], axis=1)
             total = jnp.where(row_of(total.shape) == j, got, total)
         out_ref[rows] = total
 
-    octets((cjac_ref, ajac_ref, ejac_ref), body)
-
-
-def turn_kernel(*refs):
+    octets(jac_refs, body)
+
+
+def turn_kernel(start, after_ref, *refs):
     half = len(refs) // 2
     for ref, out_ref in zip(refs[:half], refs[half:]):
 
-        @pl.loop(0, ref.shape[0])
+        @pl.loop(0, out_ref.shape[0])
         def _(i, ref=ref, out_ref=out_ref):
-            out_ref[i] = ref[i].T
-
-
-def backward(q1_ref, q2_ref, put1_ref, put2_ref, cjac_ref, ajac_ref, ejac_ref, t1_ref, t2_ref):
-    ties = q1_ref.shape[1]
-    width = t1_ref.shape[1]
-
-    def body(ref, at, slot, count):
-        rows = pl.ds(slot, OCTET)
-        zero = jnp.zeros((OCTET, ties), F32)
-        q1, q2 = q1_ref[rows], q2_ref[rows]
-        total = jnp.zeros((2 * OCTET, width), F32)
-        for j in range(count):
-            chosen = row_of(q1.shape) == j
-            top = jnp.concatenate([jnp.where(chosen, q1, 0.0), zero], axis=1)
-            low = jnp.concatenate([zero, jnp.where(chosen, q2, 0.0)], axis=1)
-            total = total + dot(jnp.concatenate([top, low]).astype(BF16), ref[at + j])
-        t1_ref[rows] = total[:OCTET]
-        t2_ref[rows] = total[OCTET:]
-
-    octets((cjac_ref, ajac_ref, ejac_ref), body)
+            out_ref[i] = ref[start + i].T
+
+
+def terms(q1, q2, ref, at, count):
+    zero = jnp.zeros_like(q1)
+    total = jnp.zeros((2 * OCTET, ref.shape[2]), F32)
+    for j in range(count):
+        chosen = row_of(q1.shape) == j
+        top = jnp.concatenate([jnp.where(chosen, q1, 0.0), zero], axis=1)
+        low = jnp.concatenate([zero, jnp.where(chosen, q2, 0.0)], axis=1)
+        total = total + dot(jnp.concatenate([top, low]).astype(BF16), ref[at + j])
+    return total[:OCTET], total[OCTET:]
+
+
+def scatter(t1_ref, t2_ref, put1_ref, put2_ref):
     out = None
     for t_ref, put_ref in ((t1_ref, put1_ref), (t2_ref, put2_ref)):
         for part in halves(t_ref[...]):
@@ -103,13 +99,122 @@
     return out
 
 
-def rhs_kernel(res_ref, coef_ref, put1_ref, put2_ref, cjac_ref, ajac_ref, ejac_ref, out_ref, q1_ref, q2_ref, t1_ref, t2_ref):
-    ties = q1_ref.shape[1]
-    r1, r2 = res_ref[:, :ties], res_ref[:, ties:]
-    q1_ref[...] = coef_ref[0] * r1 - coef_ref[1] * r2
-    q2_ref[...] = coef_ref[2] * r2 - coef_ref[1] * r1
-    out = backward(q1_ref, q2_ref, put1_ref, put2_ref, cjac_ref, ajac_ref, ejac_ref, t1_ref, t2_ref)
-    out_ref[...] = out.astype(BF16)
+def backward(q1_ref, q2_ref, put1_ref, put2_ref, cjac_ref, ajac_ref, ejac_ref, t1_ref, t2_ref):
+    def body(number, ref, at, slot, count):
+        rows = pl.ds(slot, OCTET)
+        t1_ref[rows], t2_ref[rows] = terms(q1_ref[rows], q2_ref[rows], ref, at, count)
+
+    octets((cjac_ref, ajac_ref, ejac_ref), body)
+    return scatter(t1_ref, t2_ref, put1_ref, put2_ref)
+
+
+def elimination(e1, e2, live):
+    over = live / (1.0 + e1 * e1 + e2 * e2)
+    return (1.0 + e2 * e2) * over, e1 * e2 * over, (1.0 + e1 * e1) * over
+
+
+def settled(c11, c12, c22, r1, r2):
+    return c11 * r1 - c12 * r2, c22 * r2 - c12 * r1
+
+
+def live_rows(count_ref, out_ref):
+    lane = lax.broadcasted_iota(jnp.int32, (1, out_ref.shape[1]), 1)
+    for i in range(out_ref.shape[0]):
+        out_ref[i : i + 1, :] = jnp.where(lane < count_ref[0, i], 1.0, 0.0)
+
+
+def fetch(pairs, sems):
+    copies = [pltpu.make_async_copy(a, b, sems.at[i]) for i, (a, b) in enumerate(pairs)]
+    for copy in copies:
+        copy.start()
+    return copies
+
+
+def pack_kernel(jac_ref, e_ref, res_ref, count_ref, out_jac_ref, out_ref, pair_ref, tally_ref, sems):
+    last = jac_ref.shape[0] - 1
+    block = pl.ds(last, 1)
+    copies = fetch(
+        [
+            (jac_ref.at[block], out_jac_ref),
+            (e_ref.at[block], pair_ref.at[0:1]),
+            (res_ref.at[block], pair_ref.at[1:2]),
+            (count_ref, tally_ref),
+        ],
+        sems,
+    )
+    for copy in copies[1:]:
+        copy.wait()
+    lane = lax.broadcasted_iota(jnp.int32, (1, out_ref.shape[1]), 1)
+    out_ref[...] = jnp.zeros_like(out_ref)
+    out_ref[0:2, :] = pair_ref[0]
+    out_ref[2:4, :] = pair_ref[1]
+    out_ref[4:5, :] = jnp.where(lane < tally_ref[0, last], 1.0, 0.0)
+    copies[0].wait()
+
+
+def setup_kernel(cjac_ref, ajac_ref, *refs):
+    far_refs, refs = refs[:8], refs[8:]
+    (out_cjac_ref, out_ajac_ref, coef_ref, put1_ref, put2_ref, pick1_ref, pick2_ref, t1_ref, t2_ref) = refs[:9]
+    live_ref, q1_ref, q2_ref, index_ref, sems = refs[9:14]
+    near_refs, near_sems = refs[14:22], refs[22]
+    near = fetch(list(zip(far_refs, near_refs)), near_sems)
+    ce_ref, cres_ref, ae_ref, ares_ref, count_ref, own_ref, group_ref, other_ref = near_refs
+    copies = []
+    for ref, out_ref in ((cjac_ref, out_cjac_ref), (ajac_ref, out_ajac_ref)):
+        for at in range(0, ref.shape[0], OCTET):
+            part = pl.ds(at, OCTET)
+            copies.append(pltpu.make_async_copy(ref.at[part], out_ref.at[part], sems.at[len(copies)]))
+            copies[-1].start()
+    links, scenes = cjac_ref.shape[0], ajac_ref.shape[0]
+    blocks = links + scenes
+    for copy in near:
+        copy.wait()
+    live_ref[0:links] = jnp.ones((links, live_ref.shape[1]), F32)
+    live_rows(count_ref, live_ref.at[links:blocks])
+    for rows, e_ref, res_ref in ((slice(0, links), ce_ref, cres_ref), (slice(links, blocks), ae_ref, ares_ref)):
+        c = elimination(e_ref[:, 0, :], e_ref[:, 1, :], live_ref[rows])
+        for i in range(3):
+            coef_ref[i, rows] = c[i]
+        q1_ref[rows], q2_ref[rows] = settled(*c, res_ref[:, 0, :], res_ref[:, 1, :])
+
+    first = lax.axis_index("group") * scenes
+    slots = put1_ref.shape[1]
+    index_ref[...] = jnp.zeros_like(index_ref)
+    index_ref[0:1, :links] = own_ref[...] + first
+    index_ref[1:2, :links] = group_ref[...] * scenes + other_ref[...]
+    lane = lax.broadcasted_iota(jnp.int32, (1, index_ref.shape[1]), 1)
+    one = jnp.where(lane < links, index_ref[0:1, :], jnp.where(lane < blocks, first + lane - links, -1))
+    two = jnp.where(lane < blocks - 1, first + lane - links + 1, jnp.where(lane == blocks, first, -1))
+    two = jnp.where(lane < links, index_ref[1:2, :], two)
+    for index, put_ref, pick_ref in ((one, put1_ref, pick1_ref), (two, put2_ref, pick2_ref)):
+        shape = (put_ref.shape[0], index.shape[1])
+        table = jnp.where(row_of(shape) == index, 1.0, 0.0)
+        put_ref[...] = table[:, :slots].astype(BF16)
+        pick_ref[...] = table.T[:slots].astype(BF16)
+
+    octet = 0
+    for ref in (out_cjac_ref, out_ajac_ref):
+        for at in range(0, ref.shape[0], OCTET):
+            copies[octet].wait()
+            rows = pl.ds(octet * OCTET, OCTET)
+            t1_ref[rows], t2_ref[rows] = terms(q1_ref[rows], q2_ref[rows], ref, at, OCTET)
+            octet += 1
+
+
+def rhs_kernel(coef_ref, t1_ref, t2_ref, small_ref, ejac_ref, put1_ref, put2_ref, out_ref, out_coef_ref, all1_ref, all2_ref):
+    blocks = t1_ref.shape[0]
+    rows = pl.ds(blocks, OCTET)
+    e1, e2, r1, r2, live = (small_ref[i : i + 1, :] for i in range(5))
+    c = elimination(e1, e2, live)
+    fill = lambda x: jnp.where(row_of((OCTET, x.shape[1])) == 0, x, 0.0)
+    for i in range(3):
+        out_coef_ref[i, :blocks] = coef_ref[i]
+        out_coef_ref[i, rows] = fill(c[i])
+    q1, q2 = settled(*c, r1, r2)
+    all1_ref[:blocks] = t1_ref[...]
+    all2_ref[:blocks] = t2_ref[...]
+    all1_ref[rows], all2_ref[rows] = terms(fill(q1), fill(q2), ejac_ref, 0, 1)
+    out_ref[...] = scatter(all1_ref, all2_ref, put1_ref, put2_ref).astype(BF16)
 
 
 def gather_kernel(scenes, start, parts, *refs):
@@ -221,10 +326,13 @@
         out_obs_ref[...] = obs_ref[...] - alpha * shadow
         now_res_ref = out_res_ref
     r1, r2 = out_obs_ref[:, :ties], out_obs_ref[:, ties:]
-    q1_ref[...] = coef_ref[0] * r1 - coef_ref[1] * r2
-    q2_ref[...] = coef_ref[2] * r2 - coef_ref[1] * r1
+    q1_ref[...], q2_ref[...] = settled(coef_ref[0], coef_ref[1], coef_ref[2], r1, r2)
     c_ref[...] = backward(q1_ref, q2_ref, put1_ref, put2_ref, cjac_ref, ajac_ref, ejac_ref, t1_ref, t2_ref)
-    c_ref[own] = c_ref[own] + damp_ref[...] * now_res_ref[own]
+    inside = now_res_ref[own]
+    damped = jnp.zeros_like(inside)
+    for i in range(scenes):
+        damped = jnp.where(row_of(inside.shape) == i, damp_ref[0, i] * inside, damped)
+    c_ref[own] = c_ref[own] + damped
     sent_ref[...] = c_ref[...].astype(BF16)
 
 
@@ -238,17 +346,21 @@
     out_res_ref[...] = res - alpha * (field_ref[own] + beta * image_ref[own])
 
 
-def call(kernel, outs, scratch, name, args, flops=0):
-    whole = pl.BlockSpec(memory_space=pltpu.VMEM)
+def call(kernel, outs, scratch, name, args, flops=0, spaces={}, limit=None):
+    args = [
+        pltpu.with_memory_space_constraint(a, pltpu.HBM) if spaces.get(i) == pltpu.HBM else a
+        for i, a in enumerate(args)
+    ]
+    at = lambda i: pl.BlockSpec(memory_space=spaces.get(i, pltpu.VMEM))
     moved = sum(a.size * a.dtype.itemsize for a in args)
     return pl.pallas_call(
         kernel,
         out_shape=[jax.ShapeDtypeStruct(*o) for o in outs],
-        in_specs=[whole] * len(args),
-        out_specs=[whole] * len(outs),
-        scratch_shapes=[pltpu.VMEM(*s) for s in scratch],
+        in_specs=[at(i) for i in range(len(args))],
+        out_specs=[pl.BlockSpec(memory_space=pltpu.VMEM)] * len(outs),
+        scratch_shapes=[pltpu.VMEM(*s) if isinstance(s, tuple) else s for s in scratch],
         cost_estimate=pl.CostEstimate(flops=flops, bytes_accessed=moved, transcendentals=0),
-        compiler_params=pltpu.CompilerParams(vmem_limit_bytes=VMEM_LIMIT),
+        compiler_params=pltpu.CompilerParams(vmem_limit_bytes=limit or VMEM_LIMIT),
         name=name,
     )(*args)
 
@@ -256,7 +368,7 @@
 VMEM_LIMIT = 16 << 20
 
 
-def group_sum_but_last(sent):
+def group_sum_but_last(sent, first=(), between=None):
     size = lax.axis_size("group")
     stride, pairs = 1, None
     while stride < size:
@@ -270,7 +382,10 @@
             if len(low) > 2:
                 total = total + (low[2] + low[3])
             if stride < size:
-                sent = lax.optimization_barrier(total.astype(BF16))
+                sent, first = lax.optimization_barrier((total.astype(BF16), first))
+                if between is not None:
+                    between(sent, first)
+                    first, between = (), None
             else:
                 pairs = [total]
     return pairs
@@ -302,7 +417,6 @@
     links = cross_jac.shape[1]
     groups = lax.axis_size("group")
     rows = groups * scenes
-    first = lax.axis_index("group") * scenes
     ajac = along_jac[0].reshape(scenes, 2 * ties, width)
     cjac = cross_jac[0].reshape(links, 2 * ties, width)
     slots = links + scenes + OCTET
@@ -311,40 +425,65 @@
         n = lax.axis_size("orbit")
         return lax.ppermute(block, "orbit", [(i, (i + 1) % n) for i in range(n)])
 
-    live = (jnp.arange(ties)[None, :] < along_count[0][:, None]).astype(F32)
-    ejac = pass_on(ajac[-1:])
-    small = pass_on(jnp.concatenate([along_e[0, -1], along_res[0, -1], live[-1:], live[-1:] * 0, live[-1:] * 0, live[-1:] * 0], axis=0))
-
-    fill = lambda a: jnp.pad(a, ((0, OCTET - 1), (0, 0)))
-    stacked = lambda c, a, e: jnp.concatenate([c, a, fill(e)], axis=0)
-    e1 = stacked(cross_e[0, :, 0], along_e[0, :, 0], small[0:1])
-    e2 = stacked(cross_e[0, :, 1], along_e[0, :, 1], small[1:2])
-    res1 = stacked(cross_res[0, :, 0], along_res[0, :, 0], small[2:3])
-    res2 = stacked(cross_res[0, :, 1], along_res[0, :, 1], small[3:4])
-    keep = stacked(jnp.ones((links, ties), F32), live, small[4:5])
-    over = keep / (1.0 + e1 * e1 + e2 * e2)
-    coef = jnp.stack([(1.0 + e2 * e2) * over, e1 * e2 * over, (1.0 + e1 * e1) * over])
-    observed = jnp.concatenate([res1, res2], axis=1)
-    here = first + jnp.arange(scenes)
-    none = jnp.full((OCTET,), -1)
-    one = jnp.concatenate([first + cross_own[0], here, none])
-    two = jnp.concatenate([cross_group[0, :, 0] * scenes + cross_other[0], here[1:], none[:1], first[None], none[1:]])
-    numbers = jnp.arange(rows)
-    pick1, pick2 = ((v[:, None] == numbers[None, :]).astype(BF16) for v in (one, two))
-    put1, put2 = ((v[None, :] == numbers[:, None]).astype(BF16) for v in (one, two))
-    damp = jnp.broadcast_to(damping[0][:, None], (scenes, width))
-
-    jacs = (cjac, ajac, ejac)
     work = 2 * (links + scenes + 1) * 32 * 2 * ties * width
     tie = (slots, ties)
     pair = (slots, 2 * ties)
     full = (rows, width)
     own = (scenes, width)
-    terms = [(tie, F32), (tie, F32), ((slots, width), F32), ((slots, width), F32)]
-
-    def project(field):
+    lanes = -(-slots // 128) * 128
+    term_space = [((slots, width), F32)] * 2
+    sems = pltpu.SemaphoreType.DMA
+    pack_args = (ajac, along_e[0], along_res[0], along_count)
+    packed = call(
+        pack_kernel,
+        [((1, 2 * ties, width), BF16), ((OCTET, ties), F32)],
+        [((2, 2, ties), F32), pltpu.SMEM((1, scenes), jnp.int32), sems((4,))],
+        "pack",
+        pack_args,
+        spaces={i: pltpu.HBM for i in range(4)},
+    )
+    ejac, small = pass_on(packed[0]), pass_on(packed[1])
+    blocks = links + scenes
+    part_tie = (blocks, ties)
+    put = ((rows, slots), BF16)
+    pick = ((slots, rows), BF16)
+    cjac, ajac, coef, put1, put2, pick1, pick2, t1, t2 = call(
+        setup_kernel,
+        [
+            (cjac.shape, BF16),
+            (ajac.shape, BF16),
+            ((3,) + part_tie, F32),
+            put,
+            put,
+            pick,
+            pick,
+            ((blocks, width), F32),
+            ((blocks, width), F32),
+        ],
+        [(part_tie, F32)] * 3
+        + [((OCTET, lanes), jnp.int32), sems((blocks // OCTET,))]
+        + [((links, 2, ties), F32)] * 2
+        + [((scenes, 2, ties), F32)] * 2
+        + [pltpu.SMEM((1, scenes), jnp.int32)]
+        + [((1, links), jnp.int32)] * 3
+        + [sems((8,))],
+        "setup",
+        (cjac, ajac, cross_e[0], cross_res[0], along_e[0], along_res[0], along_count)
+        + (cross_own, cross_group[:, :, 0], cross_other),
+        work,
+        {i: pltpu.HBM for i in range(10)},
+    )
+    jacs = (cjac, ajac, ejac)
+
+    def turn(start, count, refs, after):
+        outs = [((min(count, j.shape[0]),) + j.shape[1:], BF16) for j in refs]
+        share = work * sum(o[0][0] for o in outs) // blocks
+        return call(functools.partial(turn_kernel, start), outs, [], "turn", (after,) + refs, share)
+
+    def project(field, turned, refs):
         scratch = [((2, slots, width), F32)] * 2
-        return call(project_kernel, [(pair, F32)], scratch, "project", (field, pick1, pick2) + turned, work)[0]
+        kernel = functools.partial(project_kernel, turned)
+        return call(kernel, [(pair, F32)], scratch, "project", (field, pick1, pick2) + tuple(refs), work)[0]
 
     def finish(sums, res=None):
         args = sums if res is None else sums + [res]
@@ -352,12 +491,26 @@
         field, packet = call(kernel, [(full, F32), ((OCTET, width), F32)], [], "finish", args)
         return field, orbit_packets(packet)
 
-    (sent,) = call(rhs_kernel, [(full, BF16)], terms, "rhs", (observed, coef, put1, put2) + jacs, work)
-    turned = tuple(call(turn_kernel, [(j.shape, BF16) for j in jacs], [], "turn", jacs, work))
-    res, packets = finish(group_sum_but_last(sent))
-    part = project(res)
-    fixed = (coef, put1, put2, damp) + jacs
-    scratch = [(pair, F32)] + terms + [(full, F32)]
+    sent, coef = call(
+        rhs_kernel,
+        [(full, BF16), ((3,) + tie, F32)],
+        term_space,
+        "rhs",
+        (coef, t1, t2, small, ejac, put1, put2),
+        work // blocks,
+    )
+    half = links // 2
+    turned = []
+
+    def more(after, done):
+        turned.extend([*done, *turn(half, links - half, (cjac,), after)])
+
+    sums = group_sum_but_last(sent, turn(0, half, (cjac,), sent), more)
+    res, packets = finish(sums)
+    part = project(res, (True, True, False, False), turned + [ajac, ejac])
+    fixed = (coef, put1, put2, damping) + jacs
+    damp_at = {8: pltpu.SMEM}
+    scratch = [(pair, F32), (tie, F32), (tie, F32)] + term_space + [(full, F32)]
     sent, obs = call(
         functools.partial(step_kernel, 0, scenes),
         [(full, BF16), (pair, F32)],
@@ -365,12 +518,14 @@
         "step",
         (part, *packets) + fixed + (res,),
         work,
-    )
+        damp_at,
+    )
+    turned += turn(0, scenes, (ajac, ejac), sent)
     state = ()
     x = jnp.zeros(own, F32)
     for step in range(1, ITERS):
         field, packets = finish(group_sum_but_last(sent), res)
-        part = project(field)
+        part = project(field, (True,) * 4, turned)
         sent, obs, res, image, shadow, direction, x, scal = call(
             functools.partial(step_kernel, step, scenes),
             [(full, BF16), (pair, F32), (full, F32), (full, F32), (pair, F32), (own, F32), (own, F32), ((OCTET, width // 2), F32)],
@@ -378,6 +533,7 @@
             "step",
             (part, *packets) + fixed + (res, field, obs, x) + state,
             work,
+            damp_at,
         )
         state = (image, shadow, direction, scal)
     field, packets = finish(group_sum_but_last(sent), res)

time: 125 us -> 117 us (0.936)
  local copies, waits for them, and re-layouts: 10.4 us -> 0.01 us
  waiting for transfers between devices: 37 us -> 27.9 us
  Pallas kernels: 36.8 us -> 45.5 us
  starting transfers between devices: 35.8 us -> 42.4 us
  other arithmetic: 3.36 us -> 0.19 us
    ppermute x20, waiting for transfers between devices: 35.1 us -> 25.9 us  [swap(): lax.ppermute(block, axis, [(i, i ^ mask) for i in range(lax.axis_size(axi...]
    pallas_call x16 -> x20, Pallas kernels: 36.8 us -> 45.5 us  [call(): pl.pallas_call(kernel, out_shape=[jax.ShapeDtypeStruct(*o) for o in outs]...]
    ppermute x20, starting transfers between devices: 23 us -> 29.6 us  [swap(): lax.ppermute(block, axis, [(i, i ^ mask) for i in range(lax.axis_size(axi...]
    unnamed x10 -> x2, local copies, waits for them, and re-layouts: 4.98 us -> 0.01 us
    slice x7 -> x0, local copies, waits for them, and re-layouts: 4.56 us -> none  [the longest x2 1.79 us: on_device(): e2 = stacked(cross_e[0, :, 1], along_e[0, :, 1], small[1:2])]
    concatenate x4 -> x0, other arithmetic: 1.54 us -> none  [the longest x2 1.46 us: on_device(): stacked = lambda c, a, e: jnp.concatenate([c, a, fill(e)], axis=0)]
    add x3 -> x0, other arithmetic: 1.34 us -> none  [the longest x1 0.68 us: on_device(): cross_group[0, :, 0] * scenes + cross_other[0]]
  transfers between devices with their start and end apart: 37 -> 37, of which waited for: 21 -> 20; matrix products, arithmetic and copies ran while one was open for 6% -> 0% of each run, Pallas kernels for 16% -> 24%
where the time goes in v3:
time: 117 us
  Pallas kernels  45.5 us (39%)
  starting transfers between devices  42.4 us (36%)
  waiting for transfers between devices  27.9 us (24%)
    pallas_call x20, Pallas kernels, call(): pl.pallas_call(kernel, out_shape=[jax.ShapeDtypeStruct(*o) for o in outs]...  45.5 us
    ppermute x20, starting transfers between devices, swap(): lax.ppermute(block, axis, [(i, i ^ mask) for i in range(lax.axis_size(axi...  29.6 us
    ppermute x20, waiting for transfers between devices, swap(): lax.ppermute(block, axis, [(i, i ^ mask) for i in range(lax.axis_size(axi...  25.9 us
    ppermute x15, starting transfers between devices, orbit_packets(): lax.ppermute(packet, 'orbit', [(i, i ^ mask) for i in range(n)])  9.62 us
    ppermute x2, starting transfers between devices, pass_on(): return lax.ppermute(block, 'orbit', [(i, (i + 1) % n) for i in range(n)])  3.13 us
  transfers between devices with their start and end apart: 37, of which 20 were waited for; matrix products, arithmetic and copies ran while one was open for 0% of the time, Pallas kernels for 24%

profile of v3, /device:TPU:0, one launch (start us, length us, event | category | flops | bytes accessed | tf_op | source)
XLA Modules:
  0.0 116.9 jit_solution(4373674104347877867)
XLA Ops:
  0.6 0.9 pack.1
  1.6 0.5 collective-permute-start.1
  2.1 2.6 %collective-permute-start = (f32[8,128]{1,0:T(8,128)S(1)}, f32[8,128]{1,0:T(8,128)S(1)}, u32[]{:S(2)}, u32[]{:S(2)}) collective-permute-start(f32[8,128]{1,0:T(8,128)S(1)} %get-tuple-element.58), channel_id=1, source_target_pairs={{0,8},{8,16},{16,24},{24,0},{1,9},{9,17},{17,25},{25,1},{2,10},{10... | collective-permute-start | bytes 12296 | tf_op jit(solution)/shard_map/ppermute | solution.py:426
  4.7 7.8 %setup.1 = (bf16[64,256,256]{2,1,0:T(8,128)(2,1)S(1)}, bf16[16,256,256]{2,1,0:T(8,128)(2,1)S(1)}, f32[3,80,128]{2,1,0:T(8,128)S(1)}, bf16[128,88]{1,0:T(8,128)(2...) custom-call(bf16[64,256,256]{2,1,0:T(8,128)(2,1)} %bitcast.9, ...), custom_call_target="tpu_custom_call" | custom-call | flops 339738624 | bytes 10650432 | tf_op jit(solution)/shard_map/setup/pallas_call | solution.py:356
  12.9 2.6 %collective-permute-start.4 = (bf16[128,256]{1,0:T(8,128)(2,1)S(1)}, bf16[128,256]{1,0:T(8,128)(2,1)S(1)}, u32[]{:S(2)}, u32[]{:S(2)}) collective-permute-start(bf16[128,256]{1,0:T(8,128)(2,1)S(1)} %get-tuple-element.62.after_ref), channel_id=1, source_target_pairs={{0,3},{1,2},{2,1},{3,0},{4,7},{5,6},{6,5},{7,4},{8,11},{9,10},{10,... | collective-permute-start | bytes 196616 | tf_op jit(solution)/shard_map/ppermute | solution.py:395
  15.5 0.4 collective-permute-start.3
  16.0 0.5 collective-permute-start.2
  16.5 2.8 %turn.3.refs_0_ = bf16[32,256,256]{2,1,0:T(8,128)(2,1)S(1)} custom-call(bf16[128,256]{1,0:T(8,128)(2,1)S(1)} %get-tuple-element.62.after_ref, bf16[64,256,256]{2,1,0:T(8,128)(2,1)S(1)} %get-tuple-element.63.refs_0_.refs_9_), custom_call_target="tpu_custom_call" | custom-call | flops 135895456 | bytes 8454144 | tf_op jit(solution)/shard_map/turn/pallas_call | solution.py:356
  19.3 0.5 collective-permute-done.3
  19.8 0.4 collective-permute-done.2
  20.3 2.7 %collective-permute-start.5 = (bf16[128,256]{1,0:T(8,128)(2,1)S(1)}, bf16[128,256]{1,0:T(8,128)(2,1)S(1)}, u32[]{:S(2)}, u32[]{:S(2)}) collective-permute-start(bf16[128,256]{1,0:T(8,128)(2,1)S(1)} %add_convert_fusion.4.refs_0_.after_ref), channel_id=1, source_target_pairs={{0,4},{1,5},{2,6},{3,7},{4,0},{5,1},{6,2},{7,3},{8,12},{9,13},{10,... | collective-permute-start | bytes 196616 | tf_op jit(solution)/shard_map/ppermute | solution.py:395
  22.9 2.8 %turn.4.refs_1_ = bf16[32,256,256]{2,1,0:T(8,128)(2,1)S(1)} custom-call(bf16[128,256]{1,0:T(8,128)(2,1)S(1)} %add_convert_fusion.4.refs_0_.after_ref, bf16[64,256,256]{2,1,0:T(8,128)(2,1)S(1)} %get-tuple-element.63.refs_0_.refs_9_), custom_call_target="tpu_custom_call" | custom-call | flops 135895456 | bytes 8454144 | tf_op jit(solution)/shard_map/turn/pallas_call | solution.py:356
  25.9 0.6 collective-permute-start.7
  26.5 1.2 %collective-permute-start.6 = (f32[8,256]{1,0:T(8,128)S(1)}, f32[8,256]{1,0:T(8,128)S(1)}, u32[]{:S(2)}, u32[]{:S(2)}) collective-permute-start(f32[8,256]{1,0:T(8,128)S(1)} %get-tuple-element.70.refs_1_), channel_id=1, source_target_pairs={{0,8},{8,0},{16,24},{24,16},{1,9},{9,1},{17,25},{25,17},{2,10},{10... | collective-permute-start | bytes 24584 | tf_op jit(solution)/shard_map/ppermute | solution.py:400
  27.7 3.4 %project.4.refs_0_ = f32[88,256]{1,0:T(8,128)S(1)} custom-call(f32[128,256]{1,0:T(8,128)S(1)} %get-tuple-element.65.field_ref.refs_12_.refs_2_, bf16[88,128]{1,0:T(8,128)(2,1)S(1)} %get-tuple-element.66.pick1_ref, bf16[88,128]{1,0:T(8,128)(2,1)S(1)} %get-tuple-element.67.pick2_ref, bf16[32,256,256]{2,1,0:T(8,128)(2,1)S(1)} %turn.3.refs_0_, ...), custom_call_target="tpu_custom_call" | custom-call | flops 339738624 | bytes 10792960 | tf_op jit(solution)/shard_map/project/pallas_call | solution.py:356
  31.2 3.6 %step.4 = (bf16[128,256]{1,0:T(8,128)(2,1)S(1)}, f32[88,256]{1,0:T(8,128)S(1)}) custom-call(f32[88,256]{1,0:T(8,128)S(1)} %project.4.refs_0_, f32[8,256]{1,0:T(8,128)S(1)} %get-tuple-element.70.refs_1_, f32[8,256]{1,0:T(8,128)S(1)} %collective-permute-done.6.refs_2_, f32[8,256]{1,0:T(8,128)S(1)} %collective-permute-done.7.refs_3_, ...), custom_call_target="tpu_custom_call" | custom-call | flops 339738624 | bytes 11051072 | tf_op jit(solution)/shard_map/step/pallas_call | solution.py:356
  34.8 1.7 %collective-permute-start.11 = (bf16[128,256]{1,0:T(8,128)(2,1)S(1)}, bf16[128,256]{1,0:T(8,128)(2,1)S(1)}, u32[]{:S(2)}, u32[]{:S(2)}) collective-permute-start(bf16[128,256]{1,0:T(8,128)(2,1)S(1)} %get-tuple-element.72.after_ref), channel_id=1, source_target_pairs={{0,3},{1,2},{2,1},{3,0},{4,7},{5,6},{6,5},{7,4},{8,11},{9,10},{10,... | collective-permute-start | bytes 196616 | tf_op jit(solution)/shard_map/ppermute | solution.py:395
  36.5 0.4 collective-permute-start.10
  37.0 1.4 %collective-permute-start.9 = (bf16[128,256]{1,0:T(8,128)(2,1)S(1)}, bf16[128,256]{1,0:T(8,128)(2,1)S(1)}, u32[]{:S(2)}, u32[]{:S(2)}) collective-permute-start(bf16[128,256]{1,0:T(8,128)(2,1)S(1)} %get-tuple-element.72.after_ref), channel_id=1, source_target_pairs={{0,1},{1,0},{2,3},{3,2},{4,5},{5,4},{6,7},{7,6},{8,9},{9,8},{10,11... | collective-permute-start | bytes 196616 | tf_op jit(solution)/shard_map/ppermute | solution.py:395
  38.4 2.0 %collective-permute-done.11 = bf16[128,256]{1,0:T(8,128)(2,1)S(1)} collective-permute-done((bf16[128,256]{1,0:T(8,128)(2,1)S(1)}, bf16[128,256]{1,0:T(8,128)(2,1)S(1)}, u32[]{:S(2)}, u32[]{:S(2)}) %collective-permute-start.11) | collective-permute-done | bytes 65568 | tf_op jit(solution)/shard_map/ppermute | solution.py:395
  40.4 0.4 collective-permute-done.10
  40.8 0.4 collective-permute-done.9
  41.3 2.7 %collective-permute-start.12 = (bf16[128,256]{1,0:T(8,128)(2,1)S(1)}, bf16[128,256]{1,0:T(8,128)(2,1)S(1)}, u32[]{:S(2)}, u32[]{:S(2)}) collective-permute-start(bf16[128,256]{1,0:T(8,128)(2,1)S(1)} %add_convert_fusion.3.refs_0_), channel_id=1, source_target_pairs={{0,4},{1,5},{2,6},{3,7},{4,0},{5,1},{6,2},{7,3},{8,12},{9,13},{10,... | collective-permute-start | bytes 196616 | tf_op jit(solution)/shard_map/ppermute | solution.py:395
  44.0 1.5 %turn.5 = (bf16[16,256,256]{2,1,0:T(8,128)(2,1)S(1)}, bf16[1,256,256]{2,1,0:T(8,128)(2,1)S(1)}) custom-call(bf16[128,256]{1,0:T(8,128)(2,1)S(1)} %get-tuple-element.72.after_ref, bf16[16,256,256]{2,1,0:T(8,128)(2,1)S(1)} %get-tuple-element.69.refs_2_.refs_10_.refs_0_, bf16[1,256,256]{2,1,0:T(8,128)(2,1)S(1)} %collective-permute-done.1.ejac_ref.refs_3_.refs_11_.refs_1_), custom_call_target="tpu_custom_call" | custom-call | flops 72194456 | bytes 2293760 | tf_op jit(solution)/shard_map/turn/pallas_call | solution.py:356
  45.4 1.2 %collective-permute-done.12.refs_1_ = bf16[128,256]{1,0:T(8,128)(2,1)S(1)} collective-permute-done((bf16[128,256]{1,0:T(8,128)(2,1)S(1)}, bf16[128,256]{1,0:T(8,128)(2,1)S(1)}, u32[]{:S(2)}, u32[]{:S(2)}) %collective-permute-start.12) | collective-permute-done | bytes 65568 | tf_op jit(solution)/shard_map/ppermute | solution.py:395
  46.9 1.8 %collective-permute-start.14 = (f32[8,256]{1,0:T(8,128)S(1)}, f32[8,256]{1,0:T(8,128)S(1)}, u32[]{:S(2)}, u32[]{:S(2)}) collective-permute-start(f32[8,256]{1,0:T(8,128)S(1)} %get-tuple-element.76.refs_1_), channel_id=1, source_target_pairs={{0,16},{8,24},{16,0},{24,8},{1,17},{9,25},{17,1},{25,9},{2,18},{10... | collective-permute-start | bytes 24584 | tf_op jit(solution)/shard_map/ppermute | solution.py:400
  48.8 3.2 %project.5.refs_0_ = f32[88,256]{1,0:T(8,128)S(1)} custom-call(f32[128,256]{1,0:T(8,128)S(1)} %get-tuple-element.73.field_ref.refs_13_, bf16[88,128]{1,0:T(8,128)(2,1)S(1)} %get-tuple-element.66.pick1_ref, bf16[88,128]{1,0:T(8,128)(2,1)S(1)} %get-tuple-element.67.pick2_ref, bf16[32,256,256]{2,1,0:T(8,128)(2,1)S(1)} %turn.3.refs_0_, ...), custom_call_target="tpu_custom_call" | custom-call | flops 339738624 | bytes 10792960 | tf_op jit(solution)/shard_map/project/pallas_call | solution.py:356
  52.0 3.6 %step.5 = (bf16[128,256]{1,0:T(8,128)(2,1)S(1)}, f32[88,256]{1,0:T(8,128)S(1)}, f32[128,256]{1,0:T(8,128)S(1)}, f32[128,256]{1,0:T(8,128)S(1)}, f32[88,256]{1,0:...) custom-call(f32[88,256]{1,0:T(8,128)S(1)} %project.5.refs_0_, ...), custom_call_target="tpu_custom_call" | custom-call | flops 339738624 | bytes 11288640 | tf_op jit(solution)/shard_map/step/pallas_call | solution.py:356
  55.7 2.3 %collective-permute-start.18 = (bf16[128,256]{1,0:T(8,128)(2,1)S(1)}, bf16[128,256]{1,0:T(8,128)(2,1)S(1)}, u32[]{:S(2)}, u32[]{:S(2)}) collective-permute-start(bf16[128,256]{1,0:T(8,128)(2,1)S(1)} %get-tuple-element.78), channel_id=1, source_target_pairs={{0,3},{1,2},{2,1},{3,0},{4,7},{5,6},{6,5},{7,4},{8,11},{9,10},{10,... | collective-permute-start | bytes 196616 | tf_op jit(solution)/shard_map/ppermute | solution.py:395
  58.0 0.6 collective-permute-start.17
  58.5 0.7 collective-permute-start.16
  59.2 2.4 %collective-permute-done.18 = bf16[128,256]{1,0:T(8,128)(2,1)S(1)} collective-permute-done((bf16[128,256]{1,0:T(8,128)(2,1)S(1)}, bf16[128,256]{1,0:T(8,128)(2,1)S(1)}, u32[]{:S(2)}, u32[]{:S(2)}) %collective-permute-start.18) | collective-permute-done | bytes 65568 | tf_op jit(solution)/shard_map/ppermute | solution.py:395
  61.6 0.7 collective-permute-done.17
  62.3 0.6 collective-permute-done.16
  62.9 2.6 %collective-permute-start.19 = (bf16[128,256]{1,0:T(8,128)(2,1)S(1)}, bf16[128,256]{1,0:T(8,128)(2,1)S(1)}, u32[]{:S(2)}, u32[]{:S(2)}) collective-permute-start(bf16[128,256]{1,0:T(8,128)(2,1)S(1)} %add_convert_fusion.2.refs_0_), channel_id=1, source_target_pairs={{0,4},{1,5},{2,6},{3,7},{4,0},{5,1},{6,2},{7,3},{8,12},{9,13},{10,... | collective-permute-start | bytes 196616 | tf_op jit(solution)/shard_map/ppermute | solution.py:395
  65.4 2.8 %collective-permute-done.19.refs_1_ = bf16[128,256]{1,0:T(8,128)(2,1)S(1)} collective-permute-done((bf16[128,256]{1,0:T(8,128)(2,1)S(1)}, bf16[128,256]{1,0:T(8,128)(2,1)S(1)}, u32[]{:S(2)}, u32[]{:S(2)}) %collective-permute-start.19) | collective-permute-done | bytes 65568 | tf_op jit(solution)/shard_map/ppermute | solution.py:395
  68.5 0.8 collective-permute-start.21
  69.4 1.0 collective-permute-start.20
  70.4 3.2 %project.6.refs_0_ = f32[88,256]{1,0:T(8,128)S(1)} custom-call(f32[128,256]{1,0:T(8,128)S(1)} %get-tuple-element.80.field_ref.refs_13_, bf16[88,128]{1,0:T(8,128)(2,1)S(1)} %get-tuple-element.66.pick1_ref, bf16[88,128]{1,0:T(8,128)(2,1)S(1)} %get-tuple-element.67.pick2_ref, bf16[32,256,256]{2,1,0:T(8,128)(2,1)S(1)} %turn.3.refs_0_, ...), custom_call_target="tpu_custom_call" | custom-call | flops 339738624 | bytes 10792960 | tf_op jit(solution)/shard_map/project/pallas_call | solution.py:356
  73.6 3.7 %step.6 = (bf16[128,256]{1,0:T(8,128)(2,1)S(1)}, f32[88,256]{1,0:T(8,128)S(1)}, f32[128,256]{1,0:T(8,128)S(1)}, f32[128,256]{1,0:T(8,128)S(1)}, f32[88,256]{1,0:...) custom-call(f32[88,256]{1,0:T(8,128)S(1)} %project.6.refs_0_, ...), custom_call_target="tpu_custom_call" | custom-call | flops 339738624 | bytes 11530304 | tf_op jit(solution)/shard_map/step/pallas_call | solution.py:356
  77.3 1.7 %collective-permute-start.25 = (bf16[128,256]{1,0:T(8,128)(2,1)S(1)}, bf16[128,256]{1,0:T(8,128)(2,1)S(1)}, u32[]{:S(2)}, u32[]{:S(2)}) collective-permute-start(bf16[128,256]{1,0:T(8,128)(2,1)S(1)} %get-tuple-element.88), channel_id=1, source_target_pairs={{0,3},{1,2},{2,1},{3,0},{4,7},{5,6},{6,5},{7,4},{8,11},{9,10},{10,... | collective-permute-start | bytes 196616 | tf_op jit(solution)/shard_map/ppermute | solution.py:395
  79.0 1.0 collective-permute-start.24
  80.0 0.9 collective-permute-start.23
  80.9 2.2 %collective-permute-done.25 = bf16[128,256]{1,0:T(8,128)(2,1)S(1)} collective-permute-done((bf16[128,256]{1,0:T(8,128)(2,1)S(1)}, bf16[128,256]{1,0:T(8,128)(2,1)S(1)}, u32[]{:S(2)}, u32[]{:S(2)}) %collective-permute-start.25) | collective-permute-done | bytes 65568 | tf_op jit(solution)/shard_map/ppermute | solution.py:395
  83.1 0.8 collective-permute-done.24
  83.8 0.4 collective-permute-done.23
  84.3 2.1 %collective-permute-start.26 = (bf16[128,256]{1,0:T(8,128)(2,1)S(1)}, bf16[128,256]{1,0:T(8,128)(2,1)S(1)}, u32[]{:S(2)}, u32[]{:S(2)}) collective-permute-start(bf16[128,256]{1,0:T(8,128)(2,1)S(1)} %add_convert_fusion.1.refs_0_), channel_id=1, source_target_pairs={{0,4},{1,5},{2,6},{3,7},{4,0},{5,1},{6,2},{7,3},{8,12},{9,13},{10,... | collective-permute-start | bytes 196616 | tf_op jit(solution)/shard_map/ppermute | solution.py:395
  86.4 3.8 %collective-permute-done.26.refs_1_ = bf16[128,256]{1,0:T(8,128)(2,1)S(1)} collective-permute-done((bf16[128,256]{1,0:T(8,128)(2,1)S(1)}, bf16[128,256]{1,0:T(8,128)(2,1)S(1)}, u32[]{:S(2)}, u32[]{:S(2)}) %collective-permute-start.26) | collective-permute-done | bytes 65568 | tf_op jit(solution)/shard_map/ppermute | solution.py:395
  90.5 1.3 %collective-permute-start.28 = (f32[8,256]{1,0:T(8,128)S(1)}, f32[8,256]{1,0:T(8,128)S(1)}, u32[]{:S(2)}, u32[]{:S(2)}) collective-permute-start(f32[8,256]{1,0:T(8,128)S(1)} %get-tuple-element.91.refs_1_), channel_id=1, source_target_pairs={{0,16},{8,24},{16,0},{24,8},{1,17},{9,25},{17,1},{25,9},{2,18},{10... | collective-permute-start | bytes 24584 | tf_op jit(solution)/shard_map/ppermute | solution.py:400
  91.8 0.5 collective-permute-start.27
  92.3 3.2 %project.7.refs_0_ = f32[88,256]{1,0:T(8,128)S(1)} custom-call(f32[128,256]{1,0:T(8,128)S(1)} %get-tuple-element.90.field_ref.refs_13_, bf16[88,128]{1,0:T(8,128)(2,1)S(1)} %get-tuple-element.66.pick1_ref, bf16[88,128]{1,0:T(8,128)(2,1)S(1)} %get-tuple-element.67.pick2_ref, bf16[32,256,256]{2,1,0:T(8,128)(2,1)S(1)} %turn.3.refs_0_, ...), custom_call_target="tpu_custom_call" | custom-call | flops 339738624 | bytes 10792960 | tf_op jit(solution)/shard_map/project/pallas_call | solution.py:356
  95.6 4.0 %step.7 = (bf16[128,256]{1,0:T(8,128)(2,1)S(1)}, f32[88,256]{1,0:T(8,128)}, f32[128,256]{1,0:T(8,128)S(1)}, f32[128,256]{1,0:T(8,128)S(1)}, f32[88,256]{1,0:T(8,...) custom-call(f32[88,256]{1,0:T(8,128)S(1)} %project.7.refs_0_, ...), custom_call_target="tpu_custom_call" | custom-call | flops 339738624 | bytes 11530304 | tf_op jit(solution)/shard_map/step/pallas_call | solution.py:356
  99.6 1.2 collective-permute-start.32
  100.7 0.9 collective-permute-start.31
  101.6 1.5 %collective-permute-start.30 = (bf16[128,256]{1,0:T(8,128)(2,1)S(1)}, bf16[128,256]{1,0:T(8,128)(2,1)S(1)}, u32[]{:S(2)}, u32[]{:S(2)}) collective-permute-start(bf16[128,256]{1,0:T(8,128)(2,1)S(1)} %get-tuple-element.98), channel_id=1, source_target_pairs={{0,1},{1,0},{2,3},{3,2},{4,5},{5,4},{6,7},{7,6},{8,9},{9,8},{10,11... | collective-permute-start | bytes 196616 | tf_op jit(solution)/shard_map/ppermute | solution.py:395
  103.1 2.2 %collective-permute-done.32 = bf16[128,256]{1,0:T(8,128)(2,1)S(1)} collective-permute-done((bf16[128,256]{1,0:T(8,128)(2,1)S(1)}, bf16[128,256]{1,0:T(8,128)(2,1)S(1)}, u32[]{:S(2)}, u32[]{:S(2)}) %collective-permute-start.32) | collective-permute-done | bytes 65568 | tf_op jit(solution)/shard_map/ppermute | solution.py:395
  105.4 0.7 collective-permute-done.30
  106.2 1.9 %collective-permute-start.33 = (bf16[128,256]{1,0:T(8,128)(2,1)S(1)}, bf16[128,256]{1,0:T(8,128)(2,1)S(1)}, u32[]{:S(2)}, u32[]{:S(2)}) collective-permute-start(bf16[128,256]{1,0:T(8,128)(2,1)S(1)} %add_convert_fusion.refs_0_), channel_id=1, source_target_pairs={{0,4},{1,5},{2,6},{3,7},{4,0},{5,1},{6,2},{7,3},{8,12},{9,13},{10,... | collective-permute-start | bytes 196616 | tf_op jit(solution)/shard_map/ppermute | solution.py:395
  108.1 4.0 %collective-permute-done.33.refs_1_ = bf16[128,256]{1,0:T(8,128)(2,1)S(1)} collective-permute-done((bf16[128,256]{1,0:T(8,128)(2,1)S(1)}, bf16[128,256]{1,0:T(8,128)(2,1)S(1)}, u32[]{:S(2)}, u32[]{:S(2)}) %collective-permute-start.33) | collective-permute-done | bytes 65568 | tf_op jit(solution)/shard_map/ppermute | solution.py:395
  112.5 1.0 collective-permute-start.35
  113.4 0.9 collective-permute-start.34
  114.3 1.2 %collective-permute-done.36.refs_4_ = f32[8,256]{1,0:T(8,128)S(1)} collective-permute-done((f32[8,256]{1,0:T(8,128)S(1)}, f32[8,256]{1,0:T(8,128)S(1)}, u32[]{:S(2)}, u32[]{:S(2)}) %collective-permute-start.36) | collective-permute-done | bytes 8224 | tf_op jit(solution)/shard_map/ppermute | solution.py:400
  115.5 0.7 collective-permute-done.35.refs_3_
  116.2 0.6 final.1
  (38 shorter events, 2.0 us)
Async XLA Ops:
  1.6 11.0 %collective-permute-start.1 = (bf16[1,256,256]{2,1,0:T(8,128)(2,1)S(1)}, bf16[1,256,256]{2,1,0:T(8,128)(2,1)S(1)}, u32[]{:S(2)}, u32[]{:S(2)}) collective-permute-start(bf16[1,256,256]{2,1,0:T(8,128)(2,1)S(1)} %get-tuple-element.59), channel_id=1, source_target_pairs={{0,8},{8,16},{16,24},{24,0},{1,9},{9,17},{17,25},{25,1},{2,10},{10... | collective-permute-start | bytes 393224 | tf_op jit(solution)/shard_map/ppermute | solution.py:426
  2.1 10.4 %collective-permute-start = (f32[8,128]{1,0:T(8,128)S(1)}, f32[8,128]{1,0:T(8,128)S(1)}, u32[]{:S(2)}, u32[]{:S(2)}) collective-permute-start(f32[8,128]{1,0:T(8,128)S(1)} %get-tuple-element.58), channel_id=1, source_target_pairs={{0,8},{8,16},{16,24},{24,0},{1,9},{9,17},{17,25},{25,1},{2,10},{10... | collective-permute-start | bytes 12296 | tf_op jit(solution)/shard_map/ppermute | solution.py:426
  12.9 6.4 %collective-permute-start.4 = (bf16[128,256]{1,0:T(8,128)(2,1)S(1)}, bf16[128,256]{1,0:T(8,128)(2,1)S(1)}, u32[]{:S(2)}, u32[]{:S(2)}) collective-permute-start(bf16[128,256]{1,0:T(8,128)(2,1)S(1)} %get-tuple-element.62.after_ref), channel_id=1, source_target_pairs={{0,3},{1,2},{2,1},{3,0},{4,7},{5,6},{6,5},{7,4},{8,11},{9,10},{10,... | collective-permute-start | bytes 196616 | tf_op jit(solution)/shard_map/ppermute | solution.py:395
  15.5 4.3 %collective-permute-start.3 = (bf16[128,256]{1,0:T(8,128)(2,1)S(1)}, bf16[128,256]{1,0:T(8,128)(2,1)S(1)}, u32[]{:S(2)}, u32[]{:S(2)}) collective-permute-start(bf16[128,256]{1,0:T(8,128)(2,1)S(1)} %get-tuple-element.62.after_ref), channel_id=1, source_target_pairs={{0,2},{1,3},{2,0},{3,1},{4,6},{5,7},{6,4},{7,5},{8,10},{9,11},{10,... | collective-permute-start | bytes 196616 | tf_op jit(solution)/shard_map/ppermute | solution.py:395
  16.0 4.3 %collective-permute-start.2 = (bf16[128,256]{1,0:T(8,128)(2,1)S(1)}, bf16[128,256]{1,0:T(8,128)(2,1)S(1)}, u32[]{:S(2)}, u32[]{:S(2)}) collective-permute-start(bf16[128,256]{1,0:T(8,128)(2,1)S(1)} %get-tuple-element.62.after_ref), channel_id=1, source_target_pairs={{0,1},{1,0},{2,3},{3,2},{4,5},{5,4},{6,7},{7,6},{8,9},{9,8},{10,11... | collective-permute-start | bytes 196616 | tf_op jit(solution)/shard_map/ppermute | solution.py:395
  20.3 5.5 %collective-permute-start.5 = (bf16[128,256]{1,0:T(8,128)(2,1)S(1)}, bf16[128,256]{1,0:T(8,128)(2,1)S(1)}, u32[]{:S(2)}, u32[]{:S(2)}) collective-permute-start(bf16[128,256]{1,0:T(8,128)(2,1)S(1)} %add_convert_fusion.4.refs_0_.after_ref), channel_id=1, source_target_pairs={{0,4},{1,5},{2,6},{3,7},{4,0},{5,1},{6,2},{7,3},{8,12},{9,13},{10,... | collective-permute-start | bytes 196616 | tf_op jit(solution)/shard_map/ppermute | solution.py:395
  25.8 5.3 %collective-permute-start.8 = (f32[8,256]{1,0:T(8,128)S(1)}, f32[8,256]{1,0:T(8,128)S(1)}, u32[]{:S(2)}, u32[]{:S(2)}) collective-permute-start(f32[8,256]{1,0:T(8,128)S(1)} %get-tuple-element.70.refs_1_), channel_id=1, source_target_pairs={{0,24},{8,16},{16,8},{24,0},{1,25},{9,17},{17,9},{25,1},{2,26},{10... | collective-permute-start | bytes 24584 | tf_op jit(solution)/shard_map/ppermute | solution.py:400
  25.9 5.3 %collective-permute-start.7 = (f32[8,256]{1,0:T(8,128)S(1)}, f32[8,256]{1,0:T(8,128)S(1)}, u32[]{:S(2)}, u32[]{:S(2)}) collective-permute-start(f32[8,256]{1,0:T(8,128)S(1)} %get-tuple-element.70.refs_1_), channel_id=1, source_target_pairs={{0,16},{8,24},{16,0},{24,8},{1,17},{9,25},{17,1},{25,9},{2,18},{10... | collective-permute-start | bytes 24584 | tf_op jit(solution)/shard_map/ppermute | solution.py:400
  26.5 4.7 %collective-permute-start.6 = (f32[8,256]{1,0:T(8,128)S(1)}, f32[8,256]{1,0:T(8,128)S(1)}, u32[]{:S(2)}, u32[]{:S(2)}) collective-permute-start(f32[8,256]{1,0:T(8,128)S(1)} %get-tuple-element.70.refs_1_), channel_id=1, source_target_pairs={{0,8},{8,0},{16,24},{24,16},{1,9},{9,1},{17,25},{25,17},{2,10},{10... | collective-permute-start | bytes 24584 | tf_op jit(solution)/shard_map/ppermute | solution.py:400
  27.7 3.5 %copy-start = (f32[1,16]{1,0:T(1,128)S(1)}, f32[1,16]{1,0:T(1,128)}, u32[]{:S(2)}) copy-start(f32[1,16]{1,0:T(1,128)} %refs_8_.7) | copy-start | bytes 196
  34.8 5.6 %collective-permute-start.11 = (bf16[128,256]{1,0:T(8,128)(2,1)S(1)}, bf16[128,256]{1,0:T(8,128)(2,1)S(1)}, u32[]{:S(2)}, u32[]{:S(2)}) collective-permute-start(bf16[128,256]{1,0:T(8,128)(2,1)S(1)} %get-tuple-element.72.after_ref), channel_id=1, source_target_pairs={{0,3},{1,2},{2,1},{3,0},{4,7},{5,6},{6,5},{7,4},{8,11},{9,10},{10,... | collective-permute-start | bytes 196616 | tf_op jit(solution)/shard_map/ppermute | solution.py:395
  36.5 4.3 %collective-permute-start.10 = (bf16[128,256]{1,0:T(8,128)(2,1)S(1)}, bf16[128,256]{1,0:T(8,128)(2,1)S(1)}, u32[]{:S(2)}, u32[]{:S(2)}) collective-permute-start(bf16[128,256]{1,0:T(8,128)(2,1)S(1)} %get-tuple-element.72.after_ref), channel_id=1, source_target_pairs={{0,2},{1,3},{2,0},{3,1},{4,6},{5,7},{6,4},{7,5},{8,10},{9,11},{10,... | collective-permute-start | bytes 196616 | tf_op jit(solution)/shard_map/ppermute | solution.py:395
  37.0 4.3 %collective-permute-start.9 = (bf16[128,256]{1,0:T(8,128)(2,1)S(1)}, bf16[128,256]{1,0:T(8,128)(2,1)S(1)}, u32[]{:S(2)}, u32[]{:S(2)}) collective-permute-start(bf16[128,256]{1,0:T(8,128)(2,1)S(1)} %get-tuple-element.72.after_ref), channel_id=1, source_target_pairs={{0,1},{1,0},{2,3},{3,2},{4,5},{5,4},{6,7},{7,6},{8,9},{9,8},{10,11... | collective-permute-start | bytes 196616 | tf_op jit(solution)/shard_map/ppermute | solution.py:395
  41.3 5.3 %collective-permute-start.12 = (bf16[128,256]{1,0:T(8,128)(2,1)S(1)}, bf16[128,256]{1,0:T(8,128)(2,1)S(1)}, u32[]{:S(2)}, u32[]{:S(2)}) collective-permute-start(bf16[128,256]{1,0:T(8,128)(2,1)S(1)} %add_convert_fusion.3.refs_0_), channel_id=1, source_target_pairs={{0,4},{1,5},{2,6},{3,7},{4,0},{5,1},{6,2},{7,3},{8,12},{9,13},{10,... | collective-permute-start | bytes 196616 | tf_op jit(solution)/shard_map/ppermute | solution.py:395
  46.8 5.2 %collective-permute-start.15 = (f32[8,256]{1,0:T(8,128)S(1)}, f32[8,256]{1,0:T(8,128)S(1)}, u32[]{:S(2)}, u32[]{:S(2)}) collective-permute-start(f32[8,256]{1,0:T(8,128)S(1)} %get-tuple-element.76.refs_1_), channel_id=1, source_target_pairs={{0,24},{8,16},{16,8},{24,0},{1,25},{9,17},{17,9},{25,1},{2,26},{10... | collective-permute-start | bytes 24584 | tf_op jit(solution)/shard_map/ppermute | solution.py:400
  46.9 5.1 %collective-permute-start.14 = (f32[8,256]{1,0:T(8,128)S(1)}, f32[8,256]{1,0:T(8,128)S(1)}, u32[]{:S(2)}, u32[]{:S(2)}) collective-permute-start(f32[8,256]{1,0:T(8,128)S(1)} %get-tuple-element.76.refs_1_), channel_id=1, source_target_pairs={{0,16},{8,24},{16,0},{24,8},{1,17},{9,25},{17,1},{25,9},{2,18},{10... | collective-permute-start | bytes 24584 | tf_op jit(solution)/shard_map/ppermute | solution.py:400
  48.7 3.3 %collective-permute-start.13 = (f32[8,256]{1,0:T(8,128)S(1)}, f32[8,256]{1,0:T(8,128)S(1)}, u32[]{:S(2)}, u32[]{:S(2)}) collective-permute-start(f32[8,256]{1,0:T(8,128)S(1)} %get-tuple-element.76.refs_1_), channel_id=1, source_target_pairs={{0,8},{8,0},{16,24},{24,16},{1,9},{9,1},{17,25},{25,17},{2,10},{10... | collective-permute-start | bytes 24584 | tf_op jit(solution)/shard_map/ppermute | solution.py:400
  55.7 5.9 %collective-permute-start.18 = (bf16[128,256]{1,0:T(8,128)(2,1)S(1)}, bf16[128,256]{1,0:T(8,128)(2,1)S(1)}, u32[]{:S(2)}, u32[]{:S(2)}) collective-permute-start(bf16[128,256]{1,0:T(8,128)(2,1)S(1)} %get-tuple-element.78), channel_id=1, source_target_pairs={{0,3},{1,2},{2,1},{3,0},{4,7},{5,6},{6,5},{7,4},{8,11},{9,10},{10,... | collective-permute-start | bytes 196616 | tf_op jit(solution)/shard_map/ppermute | solution.py:395
  58.0 4.3 %collective-permute-start.17 = (bf16[128,256]{1,0:T(8,128)(2,1)S(1)}, bf16[128,256]{1,0:T(8,128)(2,1)S(1)}, u32[]{:S(2)}, u32[]{:S(2)}) collective-permute-start(bf16[128,256]{1,0:T(8,128)(2,1)S(1)} %get-tuple-element.78), channel_id=1, source_target_pairs={{0,2},{1,3},{2,0},{3,1},{4,6},{5,7},{6,4},{7,5},{8,10},{9,11},{10,... | collective-permute-start | bytes 196616 | tf_op jit(solution)/shard_map/ppermute | solution.py:395
  58.5 4.3 %collective-permute-start.16 = (bf16[128,256]{1,0:T(8,128)(2,1)S(1)}, bf16[128,256]{1,0:T(8,128)(2,1)S(1)}, u32[]{:S(2)}, u32[]{:S(2)}) collective-permute-start(bf16[128,256]{1,0:T(8,128)(2,1)S(1)} %get-tuple-element.78), channel_id=1, source_target_pairs={{0,1},{1,0},{2,3},{3,2},{4,5},{5,4},{6,7},{7,6},{8,9},{9,8},{10,11... | collective-permute-start | bytes 196616 | tf_op jit(solution)/shard_map/ppermute | solution.py:395
  62.9 5.4 %collective-permute-start.19 = (bf16[128,256]{1,0:T(8,128)(2,1)S(1)}, bf16[128,256]{1,0:T(8,128)(2,1)S(1)}, u32[]{:S(2)}, u32[]{:S(2)}) collective-permute-start(bf16[128,256]{1,0:T(8,128)(2,1)S(1)} %add_convert_fusion.2.refs_0_), channel_id=1, source_target_pairs={{0,4},{1,5},{2,6},{3,7},{4,0},{5,1},{6,2},{7,3},{8,12},{9,13},{10,... | collective-permute-start | bytes 196616 | tf_op jit(solution)/shard_map/ppermute | solution.py:395
  68.5 5.1 %collective-permute-start.22 = (f32[8,256]{1,0:T(8,128)S(1)}, f32[8,256]{1,0:T(8,128)S(1)}, u32[]{:S(2)}, u32[]{:S(2)}) collective-permute-start(f32[8,256]{1,0:T(8,128)S(1)} %get-tuple-element.81.refs_1_), channel_id=1, source_target_pairs={{0,24},{8,16},{16,8},{24,0},{1,25},{9,17},{17,9},{25,1},{2,26},{10... | collective-permute-start | bytes 24584 | tf_op jit(solution)/shard_map/ppermute | solution.py:400
  68.5 5.1 %collective-permute-start.21 = (f32[8,256]{1,0:T(8,128)S(1)}, f32[8,256]{1,0:T(8,128)S(1)}, u32[]{:S(2)}, u32[]{:S(2)}) collective-permute-start(f32[8,256]{1,0:T(8,128)S(1)} %get-tuple-element.81.refs_1_), channel_id=1, source_target_pairs={{0,16},{8,24},{16,0},{24,8},{1,17},{9,25},{17,1},{25,9},{2,18},{10... | collective-permute-start | bytes 24584 | tf_op jit(solution)/shard_map/ppermute | solution.py:400
  69.4 4.2 %collective-permute-start.20 = (f32[8,256]{1,0:T(8,128)S(1)}, f32[8,256]{1,0:T(8,128)S(1)}, u32[]{:S(2)}, u32[]{:S(2)}) collective-permute-start(f32[8,256]{1,0:T(8,128)S(1)} %get-tuple-element.81.refs_1_), channel_id=1, source_target_pairs={{0,8},{8,0},{16,24},{24,16},{1,9},{9,1},{17,25},{25,17},{2,10},{10... | collective-permute-start | bytes 24584 | tf_op jit(solution)/shard_map/ppermute | solution.py:400
  77.3 5.8 %collective-permute-start.25 = (bf16[128,256]{1,0:T(8,128)(2,1)S(1)}, bf16[128,256]{1,0:T(8,128)(2,1)S(1)}, u32[]{:S(2)}, u32[]{:S(2)}) collective-permute-start(bf16[128,256]{1,0:T(8,128)(2,1)S(1)} %get-tuple-element.88), channel_id=1, source_target_pairs={{0,3},{1,2},{2,1},{3,0},{4,7},{5,6},{6,5},{7,4},{8,11},{9,10},{10,... | collective-permute-start | bytes 196616 | tf_op jit(solution)/shard_map/ppermute | solution.py:395
  79.0 4.9 %collective-permute-start.24 = (bf16[128,256]{1,0:T(8,128)(2,1)S(1)}, bf16[128,256]{1,0:T(8,128)(2,1)S(1)}, u32[]{:S(2)}, u32[]{:S(2)}) collective-permute-start(bf16[128,256]{1,0:T(8,128)(2,1)S(1)} %get-tuple-element.88), channel_id=1, source_target_pairs={{0,2},{1,3},{2,0},{3,1},{4,6},{5,7},{6,4},{7,5},{8,10},{9,11},{10,... | collective-permute-start | bytes 196616 | tf_op jit(solution)/shard_map/ppermute | solution.py:395
  80.0 4.3 %collective-permute-start.23 = (bf16[128,256]{1,0:T(8,128)(2,1)S(1)}, bf16[128,256]{1,0:T(8,128)(2,1)S(1)}, u32[]{:S(2)}, u32[]{:S(2)}) collective-permute-start(bf16[128,256]{1,0:T(8,128)(2,1)S(1)} %get-tuple-element.88), channel_id=1, source_target_pairs={{0,1},{1,0},{2,3},{3,2},{4,5},{5,4},{6,7},{7,6},{8,9},{9,8},{10,11... | collective-permute-start | bytes 196616 | tf_op jit(solution)/shard_map/ppermute | solution.py:395
  84.3 5.9 %collective-permute-start.26 = (bf16[128,256]{1,0:T(8,128)(2,1)S(1)}, bf16[128,256]{1,0:T(8,128)(2,1)S(1)}, u32[]{:S(2)}, u32[]{:S(2)}) collective-permute-start(bf16[128,256]{1,0:T(8,128)(2,1)S(1)} %add_convert_fusion.1.refs_0_), channel_id=1, source_target_pairs={{0,4},{1,5},{2,6},{3,7},{4,0},{5,1},{6,2},{7,3},{8,12},{9,13},{10,... | collective-permute-start | bytes 196616 | tf_op jit(solution)/shard_map/ppermute | solution.py:395
  90.4 5.1 %collective-permute-start.29 = (f32[8,256]{1,0:T(8,128)S(1)}, f32[8,256]{1,0:T(8,128)S(1)}, u32[]{:S(2)}, u32[]{:S(2)}) collective-permute-start(f32[8,256]{1,0:T(8,128)S(1)} %get-tuple-element.91.refs_1_), channel_id=1, source_target_pairs={{0,24},{8,16},{16,8},{24,0},{1,25},{9,17},{17,9},{25,1},{2,26},{10... | collective-permute-start | bytes 24584 | tf_op jit(solution)/shard_map/ppermute | solution.py:400
  90.5 5.1 %collective-permute-start.28 = (f32[8,256]{1,0:T(8,128)S(1)}, f32[8,256]{1,0:T(8,128)S(1)}, u32[]{:S(2)}, u32[]{:S(2)}) collective-permute-start(f32[8,256]{1,0:T(8,128)S(1)} %get-tuple-element.91.refs_1_), channel_id=1, source_target_pairs={{0,16},{8,24},{16,0},{24,8},{1,17},{9,25},{17,1},{25,9},{2,18},{10... | collective-permute-start | bytes 24584 | tf_op jit(solution)/shard_map/ppermute | solution.py:400
  91.8 3.8 %collective-permute-start.27 = (f32[8,256]{1,0:T(8,128)S(1)}, f32[8,256]{1,0:T(8,128)S(1)}, u32[]{:S(2)}, u32[]{:S(2)}) collective-permute-start(f32[8,256]{1,0:T(8,128)S(1)} %get-tuple-element.91.refs_1_), channel_id=1, source_target_pairs={{0,8},{8,0},{16,24},{24,16},{1,9},{9,1},{17,25},{25,17},{2,10},{10... | collective-permute-start | bytes 24584 | tf_op jit(solution)/shard_map/ppermute | solution.py:400
  99.6 5.7 %collective-permute-start.32 = (bf16[128,256]{1,0:T(8,128)(2,1)S(1)}, bf16[128,256]{1,0:T(8,128)(2,1)S(1)}, u32[]{:S(2)}, u32[]{:S(2)}) collective-permute-start(bf16[128,256]{1,0:T(8,128)(2,1)S(1)} %get-tuple-element.98), channel_id=1, source_target_pairs={{0,3},{1,2},{2,1},{3,0},{4,7},{5,6},{6,5},{7,4},{8,11},{9,10},{10,... | collective-permute-start | bytes 196616 | tf_op jit(solution)/shard_map/ppermute | solution.py:395
  100.7 4.7 %collective-permute-start.31 = (bf16[128,256]{1,0:T(8,128)(2,1)S(1)}, bf16[128,256]{1,0:T(8,128)(2,1)S(1)}, u32[]{:S(2)}, u32[]{:S(2)}) collective-permute-start(bf16[128,256]{1,0:T(8,128)(2,1)S(1)} %get-tuple-element.98), channel_id=1, source_target_pairs={{0,2},{1,3},{2,0},{3,1},{4,6},{5,7},{6,4},{7,5},{8,10},{9,11},{10,... | collective-permute-start | bytes 196616 | tf_op jit(solution)/shard_map/ppermute | solution.py:395
  101.6 4.6 %collective-permute-start.30 = (bf16[128,256]{1,0:T(8,128)(2,1)S(1)}, bf16[128,256]{1,0:T(8,128)(2,1)S(1)}, u32[]{:S(2)}, u32[]{:S(2)}) collective-permute-start(bf16[128,256]{1,0:T(8,128)(2,1)S(1)} %get-tuple-element.98), channel_id=1, source_target_pairs={{0,1},{1,0},{2,3},{3,2},{4,5},{5,4},{6,7},{7,6},{8,9},{9,8},{10,11... | collective-permute-start | bytes 196616 | tf_op jit(solution)/shard_map/ppermute | solution.py:395
  106.2 6.0 %collective-permute-start.33 = (bf16[128,256]{1,0:T(8,128)(2,1)S(1)}, bf16[128,256]{1,0:T(8,128)(2,1)S(1)}, u32[]{:S(2)}, u32[]{:S(2)}) collective-permute-start(bf16[128,256]{1,0:T(8,128)(2,1)S(1)} %add_convert_fusion.refs_0_), channel_id=1, source_target_pairs={{0,4},{1,5},{2,6},{3,7},{4,0},{5,1},{6,2},{7,3},{8,12},{9,13},{10,... | collective-permute-start | bytes 196616 | tf_op jit(solution)/shard_map/ppermute | solution.py:395
  112.4 3.1 %collective-permute-start.36 = (f32[8,256]{1,0:T(8,128)S(1)}, f32[8,256]{1,0:T(8,128)S(1)}, u32[]{:S(2)}, u32[]{:S(2)}) collective-permute-start(f32[8,256]{1,0:T(8,128)S(1)} %get-tuple-element.101.refs_1_), channel_id=1, source_target_pairs={{0,24},{8,16},{16,8},{24,0},{1,25},{9,17},{17,9},{25,1},{2,26},{10... | collective-permute-start | bytes 24584 | tf_op jit(solution)/shard_map/ppermute | solution.py:400
  112.5 3.8 %collective-permute-start.35 = (f32[8,256]{1,0:T(8,128)S(1)}, f32[8,256]{1,0:T(8,128)S(1)}, u32[]{:S(2)}, u32[]{:S(2)}) collective-permute-start(f32[8,256]{1,0:T(8,128)S(1)} %get-tuple-element.101.refs_1_), channel_id=1, source_target_pairs={{0,16},{8,24},{16,0},{24,8},{1,17},{9,25},{17,1},{25,9},{2,18},{10... | collective-permute-start | bytes 24584 | tf_op jit(solution)/shard_map/ppermute | solution.py:400
  113.4 2.8 %collective-permute-start.34 = (f32[8,256]{1,0:T(8,128)S(1)}, f32[8,256]{1,0:T(8,128)S(1)}, u32[]{:S(2)}, u32[]{:S(2)}) collective-permute-start(f32[8,256]{1,0:T(8,128)S(1)} %get-tuple-element.101.refs_1_), channel_id=1, source_target_pairs={{0,8},{8,0},{16,24},{24,16},{1,9},{9,1},{17,25},{25,17},{2,10},{10... | collective-permute-start | bytes 24584 | tf_op jit(solution)/shard_map/ppermute | solution.py:400

commit v4 on v3

--- a/solution.py
+++ b/solution.py
@@ -33,15 +33,8 @@
     slot = 0
     for number, ref in enumerate(refs):
         blocks = ref.shape[0]
-        if blocks <= OCTET:
-            body(number, ref, 0, slot, blocks)
-        else:
-
-            @pl.loop(0, blocks // OCTET)
-            def _(i, number=number, ref=ref, slot=slot):
-                at = pl.multiple_of(i * OCTET, OCTET)
-                body(number, ref, at, pl.multiple_of(slot + at, OCTET), OCTET)
-
+        for at in range(0, blocks, OCTET):
+            body(number, ref, at, slot + at, min(OCTET, blocks - at))
         slot += -(-blocks // OCTET) * OCTET
 
 
@@ -153,12 +146,12 @@
 
 
 def setup_kernel(cjac_ref, ajac_ref, *refs):
-    far_refs, refs = refs[:8], refs[8:]
-    (out_cjac_ref, out_ajac_ref, coef_ref, put1_ref, put2_ref, pick1_ref, pick2_ref, t1_ref, t2_ref) = refs[:9]
-    live_ref, q1_ref, q2_ref, index_ref, sems = refs[9:14]
-    near_refs, near_sems = refs[14:22], refs[22]
+    far_refs, refs = refs[:9], refs[9:]
+    (out_cjac_ref, out_ajac_ref, coef_ref, put1_ref, put2_ref, pick1_ref, pick2_ref, t1_ref, t2_ref, damp_ref) = refs[:10]
+    live_ref, q1_ref, q2_ref, index_ref, sems = refs[10:15]
+    near_refs, near_sems = refs[15:24], refs[24]
     near = fetch(list(zip(far_refs, near_refs)), near_sems)
-    ce_ref, cres_ref, ae_ref, ares_ref, count_ref, own_ref, group_ref, other_ref = near_refs
+    ce_ref, cres_ref, ae_ref, ares_ref, count_ref, own_ref, group_ref, other_ref, scale_ref = near_refs
     copies = []
     for ref, out_ref in ((cjac_ref, out_cjac_ref), (ajac_ref, out_ajac_ref)):
         for at in range(0, ref.shape[0], OCTET):
@@ -171,6 +164,8 @@
         copy.wait()
     live_ref[0:links] = jnp.ones((links, live_ref.shape[1]), F32)
     live_rows(count_ref, live_ref.at[links:blocks])
+    for i in range(scenes):
+        damp_ref[i : i + 1, :] = jnp.full((1, damp_ref.shape[1]), scale_ref[0, i], F32)
     for rows, e_ref, res_ref in ((slice(0, links), ce_ref, cres_ref), (slice(links, blocks), ae_ref, ares_ref)):
         c = elimination(e_ref[:, 0, :], e_ref[:, 1, :], live_ref[rows])
         for i in range(3):
@@ -328,11 +323,7 @@
     r1, r2 = out_obs_ref[:, :ties], out_obs_ref[:, ties:]
     q1_ref[...], q2_ref[...] = settled(coef_ref[0], coef_ref[1], coef_ref[2], r1, r2)
     c_ref[...] = backward(q1_ref, q2_ref, put1_ref, put2_ref, cjac_ref, ajac_ref, ejac_ref, t1_ref, t2_ref)
-    inside = now_res_ref[own]
-    damped = jnp.zeros_like(inside)
-    for i in range(scenes):
-        damped = jnp.where(row_of(inside.shape) == i, damp_ref[0, i] * inside, damped)
-    c_ref[own] = c_ref[own] + damped
+    c_ref[own] = c_ref[own] + damp_ref[...] * now_res_ref[own]
     sent_ref[...] = c_ref[...].astype(BF16)
 
 
@@ -447,7 +438,7 @@
     part_tie = (blocks, ties)
     put = ((rows, slots), BF16)
     pick = ((slots, rows), BF16)
-    cjac, ajac, coef, put1, put2, pick1, pick2, t1, t2 = call(
+    cjac, ajac, coef, put1, put2, pick1, pick2, t1, t2, damp = call(
         setup_kernel,
         [
             (cjac.shape, BF16),
@@ -459,6 +450,7 @@
             pick,
             ((blocks, width), F32),
             ((blocks, width), F32),
+            (own, F32),
         ],
         [(part_tie, F32)] * 3
         + [((OCTET, lanes), jnp.int32), sems((blocks // OCTET,))]
@@ -466,12 +458,12 @@
         + [((scenes, 2, ties), F32)] * 2
         + [pltpu.SMEM((1, scenes), jnp.int32)]
         + [((1, links), jnp.int32)] * 3
-        + [sems((8,))],
+        + [pltpu.SMEM((1, scenes), F32), sems((9,))],
         "setup",
         (cjac, ajac, cross_e[0], cross_res[0], along_e[0], along_res[0], along_count)
-        + (cross_own, cross_group[:, :, 0], cross_other),
+        + (cross_own, cross_group[:, :, 0], cross_other, damping),
         work,
-        {i: pltpu.HBM for i in range(10)},
+        {i: pltpu.HBM for i in range(11)},
     )
     jacs = (cjac, ajac, ejac)
 
@@ -508,8 +500,7 @@
     sums = group_sum_but_last(sent, turn(0, half, (cjac,), sent), more)
     res, packets = finish(sums)
     part = project(res, (True, True, False, False), turned + [ajac, ejac])
-    fixed = (coef, put1, put2, damping) + jacs
-    damp_at = {8: pltpu.SMEM}
+    fixed = (coef, put1, put2, damp) + jacs
     scratch = [(pair, F32), (tie, F32), (tie, F32)] + term_space + [(full, F32)]
     sent, obs = call(
         functools.partial(step_kernel, 0, scenes),
@@ -518,7 +509,6 @@
         "step",
         (part, *packets) + fixed + (res,),
         work,
-        damp_at,
     )
     turned += turn(0, scenes, (ajac, ejac), sent)
     state = ()
@@ -533,7 +523,6 @@
             "step",
             (part, *packets) + fixed + (res, field, obs, x) + state,
             work,
-            damp_at,
         )
         state = (image, shadow, direction, scal)
     field, packets = finish(group_sum_but_last(sent), res)

time: 117 us -> 105 us (0.90)
  Pallas kernels: 45.5 us -> 34 us
    pallas_call x20, Pallas kernels: 45.5 us -> 34 us  [call(): pl.pallas_call(kernel, out_shape=[jax.ShapeDtypeStruct(*o) for o in outs]...]
  transfers between devices with their start and end apart: 37 -> 37, of which waited for: 20 -> 20; matrix products, arithmetic and copies ran while one was open for 0% -> 0% of each run, Pallas kernels for 24% -> 22%
where the time goes in v4:
time: 105 us
  starting transfers between devices  42.4 us (40%)
  Pallas kernels  34 us (32%)
  waiting for transfers between devices  27.7 us (26%)
    pallas_call x20, Pallas kernels, call(): pl.pallas_call(kernel, out_shape=[jax.ShapeDtypeStruct(*o) for o in outs]...  34 us
    ppermute x20, starting transfers between devices, swap(): lax.ppermute(block, axis, [(i, i ^ mask) for i in range(lax.axis_size(axi...  29.7 us
    ppermute x20, waiting for transfers between devices, swap(): lax.ppermute(block, axis, [(i, i ^ mask) for i in range(lax.axis_size(axi...  25.7 us
    ppermute x15, starting transfers between devices, orbit_packets(): lax.ppermute(packet, 'orbit', [(i, i ^ mask) for i in range(n)])  9.61 us
    ppermute x2, starting transfers between devices, pass_on(): return lax.ppermute(block, 'orbit', [(i, (i + 1) % n) for i in range(n)])  3.13 us
  transfers between devices with their start and end apart: 37, of which 20 were waited for; matrix products, arithmetic and copies ran while one was open for 0% of the time, Pallas kernels for 22%

profile of v4, /device:TPU:0, one launch (start us, length us, event | category | flops | bytes accessed | tf_op | source)
XLA Modules:
  0.0 105.1 jit_solution(316998373240795163)
XLA Ops:
  0.6 0.9 pack.1
  1.6 0.5 collective-permute-start.1
  2.1 2.6 %collective-permute-start = (f32[8,128]{1,0:T(8,128)S(1)}, f32[8,128]{1,0:T(8,128)S(1)}, u32[]{:S(2)}, u32[]{:S(2)}) collective-permute-start(f32[8,128]{1,0:T(8,128)S(1)} %get-tuple-element.59), channel_id=1, source_target_pairs={{0,8},{8,16},{16,24},{24,0},{1,9},{9,17},{17,25},{25,1},{2,10},{10... | collective-permute-start | bytes 12296 | tf_op jit(solution)/shard_map/ppermute | solution.py:417
  4.7 7.5 %setup.1 = (bf16[64,256,256]{2,1,0:T(8,128)(2,1)S(1)}, bf16[16,256,256]{2,1,0:T(8,128)(2,1)S(1)}, f32[3,80,128]{2,1,0:T(8,128)S(1)}, bf16[128,88]{1,0:T(8,128)(2...) custom-call(bf16[64,256,256]{2,1,0:T(8,128)(2,1)} %bitcast.9, ...), custom_call_target="tpu_custom_call" | custom-call | flops 339738624 | bytes 10650496 | tf_op jit(solution)/shard_map/setup/pallas_call | solution.py:347
  12.7 2.6 %collective-permute-start.4 = (bf16[128,256]{1,0:T(8,128)(2,1)S(1)}, bf16[128,256]{1,0:T(8,128)(2,1)S(1)}, u32[]{:S(2)}, u32[]{:S(2)}) collective-permute-start(bf16[128,256]{1,0:T(8,128)(2,1)S(1)} %get-tuple-element.63.after_ref), channel_id=1, source_target_pairs={{0,3},{1,2},{2,1},{3,0},{4,7},{5,6},{6,5},{7,4},{8,11},{9,10},{10,... | collective-permute-start | bytes 196616 | tf_op jit(solution)/shard_map/ppermute | solution.py:386
  15.3 0.4 collective-permute-start.3
  15.7 0.5 collective-permute-start.2
  16.2 2.8 %turn.3.refs_0_ = bf16[32,256,256]{2,1,0:T(8,128)(2,1)S(1)} custom-call(bf16[128,256]{1,0:T(8,128)(2,1)S(1)} %get-tuple-element.63.after_ref, bf16[64,256,256]{2,1,0:T(8,128)(2,1)S(1)} %get-tuple-element.64.refs_0_.refs_9_), custom_call_target="tpu_custom_call" | custom-call | flops 135895456 | bytes 8454144 | tf_op jit(solution)/shard_map/turn/pallas_call | solution.py:347
  19.0 0.5 collective-permute-done.3
  19.5 0.4 collective-permute-done.2
  20.0 2.7 %collective-permute-start.5 = (bf16[128,256]{1,0:T(8,128)(2,1)S(1)}, bf16[128,256]{1,0:T(8,128)(2,1)S(1)}, u32[]{:S(2)}, u32[]{:S(2)}) collective-permute-start(bf16[128,256]{1,0:T(8,128)(2,1)S(1)} %add_convert_fusion.4.refs_0_.after_ref), channel_id=1, source_target_pairs={{0,4},{1,5},{2,6},{3,7},{4,0},{5,1},{6,2},{7,3},{8,12},{9,13},{10,... | collective-permute-start | bytes 196616 | tf_op jit(solution)/shard_map/ppermute | solution.py:386
  22.7 2.8 %turn.4.refs_1_ = bf16[32,256,256]{2,1,0:T(8,128)(2,1)S(1)} custom-call(bf16[128,256]{1,0:T(8,128)(2,1)S(1)} %add_convert_fusion.4.refs_0_.after_ref, bf16[64,256,256]{2,1,0:T(8,128)(2,1)S(1)} %get-tuple-element.64.refs_0_.refs_9_), custom_call_target="tpu_custom_call" | custom-call | flops 135895456 | bytes 8454144 | tf_op jit(solution)/shard_map/turn/pallas_call | solution.py:347
  25.6 0.6 collective-permute-start.7
  26.2 1.2 %collective-permute-start.6 = (f32[8,256]{1,0:T(8,128)S(1)}, f32[8,256]{1,0:T(8,128)S(1)}, u32[]{:S(2)}, u32[]{:S(2)}) collective-permute-start(f32[8,256]{1,0:T(8,128)S(1)} %get-tuple-element.71.refs_1_), channel_id=1, source_target_pairs={{0,8},{8,0},{16,24},{24,16},{1,9},{9,1},{17,25},{25,17},{2,10},{10... | collective-permute-start | bytes 24584 | tf_op jit(solution)/shard_map/ppermute | solution.py:391
  27.5 2.3 %project.4.refs_0_ = f32[88,256]{1,0:T(8,128)S(1)} custom-call(f32[128,256]{1,0:T(8,128)S(1)} %get-tuple-element.66.field_ref.refs_12_.refs_2_, bf16[88,128]{1,0:T(8,128)(2,1)S(1)} %get-tuple-element.67.pick1_ref, bf16[88,128]{1,0:T(8,128)(2,1)S(1)} %get-tuple-element.68.pick2_ref, bf16[32,256,256]{2,1,0:T(8,128)(2,1)S(1)} %turn.3.refs_0_, ...), custom_call_target="tpu_custom_call" | custom-call | flops 339738624 | bytes 10792960 | tf_op jit(solution)/shard_map/project/pallas_call | solution.py:347
  29.8 1.9 %step.4 = (bf16[128,256]{1,0:T(8,128)(2,1)S(1)}, f32[88,256]{1,0:T(8,128)S(1)}) custom-call(f32[88,256]{1,0:T(8,128)S(1)} %project.4.refs_0_, f32[8,256]{1,0:T(8,128)S(1)} %get-tuple-element.71.refs_1_, f32[8,256]{1,0:T(8,128)S(1)} %collective-permute-done.6.refs_2_, f32[8,256]{1,0:T(8,128)S(1)} %collective-permute-done.7.refs_3_, ...), custom_call_target="tpu_custom_call" | custom-call | flops 339738624 | bytes 11067392 | tf_op jit(solution)/shard_map/step/pallas_call | solution.py:347
  31.7 1.7 %collective-permute-start.11 = (bf16[128,256]{1,0:T(8,128)(2,1)S(1)}, bf16[128,256]{1,0:T(8,128)(2,1)S(1)}, u32[]{:S(2)}, u32[]{:S(2)}) collective-permute-start(bf16[128,256]{1,0:T(8,128)(2,1)S(1)} %get-tuple-element.74.after_ref), channel_id=1, source_target_pairs={{0,3},{1,2},{2,1},{3,0},{4,7},{5,6},{6,5},{7,4},{8,11},{9,10},{10,... | collective-permute-start | bytes 196616 | tf_op jit(solution)/shard_map/ppermute | solution.py:386
  33.4 0.4 collective-permute-start.10
  33.9 1.4 %collective-permute-start.9 = (bf16[128,256]{1,0:T(8,128)(2,1)S(1)}, bf16[128,256]{1,0:T(8,128)(2,1)S(1)}, u32[]{:S(2)}, u32[]{:S(2)}) collective-permute-start(bf16[128,256]{1,0:T(8,128)(2,1)S(1)} %get-tuple-element.74.after_ref), channel_id=1, source_target_pairs={{0,1},{1,0},{2,3},{3,2},{4,5},{5,4},{6,7},{7,6},{8,9},{9,8},{10,11... | collective-permute-start | bytes 196616 | tf_op jit(solution)/shard_map/ppermute | solution.py:386
  35.3 2.0 %collective-permute-done.11 = bf16[128,256]{1,0:T(8,128)(2,1)S(1)} collective-permute-done((bf16[128,256]{1,0:T(8,128)(2,1)S(1)}, bf16[128,256]{1,0:T(8,128)(2,1)S(1)}, u32[]{:S(2)}, u32[]{:S(2)}) %collective-permute-start.11) | collective-permute-done | bytes 65568 | tf_op jit(solution)/shard_map/ppermute | solution.py:386
  37.3 0.4 collective-permute-done.10
  37.7 0.4 collective-permute-done.9
  38.2 2.7 %collective-permute-start.12 = (bf16[128,256]{1,0:T(8,128)(2,1)S(1)}, bf16[128,256]{1,0:T(8,128)(2,1)S(1)}, u32[]{:S(2)}, u32[]{:S(2)}) collective-permute-start(bf16[128,256]{1,0:T(8,128)(2,1)S(1)} %add_convert_fusion.3.refs_0_), channel_id=1, source_target_pairs={{0,4},{1,5},{2,6},{3,7},{4,0},{5,1},{6,2},{7,3},{8,12},{9,13},{10,... | collective-permute-start | bytes 196616 | tf_op jit(solution)/shard_map/ppermute | solution.py:386
  40.8 1.6 %turn.5 = (bf16[16,256,256]{2,1,0:T(8,128)(2,1)S(1)}, bf16[1,256,256]{2,1,0:T(8,128)(2,1)S(1)}) custom-call(bf16[128,256]{1,0:T(8,128)(2,1)S(1)} %get-tuple-element.74.after_ref, bf16[16,256,256]{2,1,0:T(8,128)(2,1)S(1)} %get-tuple-element.70.refs_2_.refs_10_.refs_0_, bf16[1,256,256]{2,1,0:T(8,128)(2,1)S(1)} %collective-permute-done.1.ejac_ref.refs_3_.refs_11_.refs_1_), custom_call_target="tpu_custom_call" | custom-call | flops 72194456 | bytes 2293760 | tf_op jit(solution)/shard_map/turn/pallas_call | solution.py:347
  42.5 1.0 collective-permute-done.12.refs_1_
  43.8 1.8 %collective-permute-start.14 = (f32[8,256]{1,0:T(8,128)S(1)}, f32[8,256]{1,0:T(8,128)S(1)}, u32[]{:S(2)}, u32[]{:S(2)}) collective-permute-start(f32[8,256]{1,0:T(8,128)S(1)} %get-tuple-element.78.refs_1_), channel_id=1, source_target_pairs={{0,16},{8,24},{16,0},{24,8},{1,17},{9,25},{17,1},{25,9},{2,18},{10... | collective-permute-start | bytes 24584 | tf_op jit(solution)/shard_map/ppermute | solution.py:391
  45.6 2.0 %project.5.refs_0_ = f32[88,256]{1,0:T(8,128)S(1)} custom-call(f32[128,256]{1,0:T(8,128)S(1)} %get-tuple-element.75.field_ref.refs_13_, bf16[88,128]{1,0:T(8,128)(2,1)S(1)} %get-tuple-element.67.pick1_ref, bf16[88,128]{1,0:T(8,128)(2,1)S(1)} %get-tuple-element.68.pick2_ref, bf16[32,256,256]{2,1,0:T(8,128)(2,1)S(1)} %turn.3.refs_0_, ...), custom_call_target="tpu_custom_call" | custom-call | flops 339738624 | bytes 10792960 | tf_op jit(solution)/shard_map/project/pallas_call | solution.py:347
  47.7 1.9 %step.5 = (bf16[128,256]{1,0:T(8,128)(2,1)S(1)}, f32[88,256]{1,0:T(8,128)S(1)}, f32[128,256]{1,0:T(8,128)S(1)}, f32[128,256]{1,0:T(8,128)S(1)}, f32[88,256]{1,0:...) custom-call(f32[88,256]{1,0:T(8,128)S(1)} %project.5.refs_0_, ...), custom_call_target="tpu_custom_call" | custom-call | flops 339738624 | bytes 11304960 | tf_op jit(solution)/shard_map/step/pallas_call | solution.py:347
  49.6 2.3 %collective-permute-start.18 = (bf16[128,256]{1,0:T(8,128)(2,1)S(1)}, bf16[128,256]{1,0:T(8,128)(2,1)S(1)}, u32[]{:S(2)}, u32[]{:S(2)}) collective-permute-start(bf16[128,256]{1,0:T(8,128)(2,1)S(1)} %get-tuple-element.80), channel_id=1, source_target_pairs={{0,3},{1,2},{2,1},{3,0},{4,7},{5,6},{6,5},{7,4},{8,11},{9,10},{10,... | collective-permute-start | bytes 196616 | tf_op jit(solution)/shard_map/ppermute | solution.py:386
  52.0 0.6 collective-permute-start.17
  52.5 0.7 collective-permute-start.16
  53.2 2.4 %collective-permute-done.18 = bf16[128,256]{1,0:T(8,128)(2,1)S(1)} collective-permute-done((bf16[128,256]{1,0:T(8,128)(2,1)S(1)}, bf16[128,256]{1,0:T(8,128)(2,1)S(1)}, u32[]{:S(2)}, u32[]{:S(2)}) %collective-permute-start.18) | collective-permute-done | bytes 65568 | tf_op jit(solution)/shard_map/ppermute | solution.py:386
  55.6 0.7 collective-permute-done.17
  56.2 0.6 collective-permute-done.16
  56.8 2.6 %collective-permute-start.19 = (bf16[128,256]{1,0:T(8,128)(2,1)S(1)}, bf16[128,256]{1,0:T(8,128)(2,1)S(1)}, u32[]{:S(2)}, u32[]{:S(2)}) collective-permute-start(bf16[128,256]{1,0:T(8,128)(2,1)S(1)} %add_convert_fusion.2.refs_0_), channel_id=1, source_target_pairs={{0,4},{1,5},{2,6},{3,7},{4,0},{5,1},{6,2},{7,3},{8,12},{9,13},{10,... | collective-permute-start | bytes 196616 | tf_op jit(solution)/shard_map/ppermute | solution.py:386
  59.4 2.9 %collective-permute-done.19.refs_1_ = bf16[128,256]{1,0:T(8,128)(2,1)S(1)} collective-permute-done((bf16[128,256]{1,0:T(8,128)(2,1)S(1)}, bf16[128,256]{1,0:T(8,128)(2,1)S(1)}, u32[]{:S(2)}, u32[]{:S(2)}) %collective-permute-start.19) | collective-permute-done | bytes 65568 | tf_op jit(solution)/shard_map/ppermute | solution.py:386
  62.5 0.8 collective-permute-start.21
  63.4 1.0 collective-permute-start.20
  64.4 2.0 %project.6.refs_0_ = f32[88,256]{1,0:T(8,128)S(1)} custom-call(f32[128,256]{1,0:T(8,128)S(1)} %get-tuple-element.82.field_ref.refs_13_, bf16[88,128]{1,0:T(8,128)(2,1)S(1)} %get-tuple-element.67.pick1_ref, bf16[88,128]{1,0:T(8,128)(2,1)S(1)} %get-tuple-element.68.pick2_ref, bf16[32,256,256]{2,1,0:T(8,128)(2,1)S(1)} %turn.3.refs_0_, ...), custom_call_target="tpu_custom_call" | custom-call | flops 339738624 | bytes 10792960 | tf_op jit(solution)/shard_map/project/pallas_call | solution.py:347
  66.4 1.9 %step.6 = (bf16[128,256]{1,0:T(8,128)(2,1)S(1)}, f32[88,256]{1,0:T(8,128)S(1)}, f32[128,256]{1,0:T(8,128)S(1)}, f32[128,256]{1,0:T(8,128)S(1)}, f32[88,256]{1,0:...) custom-call(f32[88,256]{1,0:T(8,128)S(1)} %project.6.refs_0_, ...), custom_call_target="tpu_custom_call" | custom-call | flops 339738624 | bytes 11546624 | tf_op jit(solution)/shard_map/step/pallas_call | solution.py:347
  68.4 1.7 %collective-permute-start.25 = (bf16[128,256]{1,0:T(8,128)(2,1)S(1)}, bf16[128,256]{1,0:T(8,128)(2,1)S(1)}, u32[]{:S(2)}, u32[]{:S(2)}) collective-permute-start(bf16[128,256]{1,0:T(8,128)(2,1)S(1)} %get-tuple-element.90), channel_id=1, source_target_pairs={{0,3},{1,2},{2,1},{3,0},{4,7},{5,6},{6,5},{7,4},{8,11},{9,10},{10,... | collective-permute-start | bytes 196616 | tf_op jit(solution)/shard_map/ppermute | solution.py:386
  70.0 1.0 collective-permute-start.24
  71.1 0.9 collective-permute-start.23
  71.9 2.2 %collective-permute-done.25 = bf16[128,256]{1,0:T(8,128)(2,1)S(1)} collective-permute-done((bf16[128,256]{1,0:T(8,128)(2,1)S(1)}, bf16[128,256]{1,0:T(8,128)(2,1)S(1)}, u32[]{:S(2)}, u32[]{:S(2)}) %collective-permute-start.25) | collective-permute-done | bytes 65568 | tf_op jit(solution)/shard_map/ppermute | solution.py:386
  74.1 0.8 collective-permute-done.24
  74.9 0.4 collective-permute-done.23
  75.4 2.1 %collective-permute-start.26 = (bf16[128,256]{1,0:T(8,128)(2,1)S(1)}, bf16[128,256]{1,0:T(8,128)(2,1)S(1)}, u32[]{:S(2)}, u32[]{:S(2)}) collective-permute-start(bf16[128,256]{1,0:T(8,128)(2,1)S(1)} %add_convert_fusion.1.refs_0_), channel_id=1, source_target_pairs={{0,4},{1,5},{2,6},{3,7},{4,0},{5,1},{6,2},{7,3},{8,12},{9,13},{10,... | collective-permute-start | bytes 196616 | tf_op jit(solution)/shard_map/ppermute | solution.py:386
  77.5 3.8 %collective-permute-done.26.refs_1_ = bf16[128,256]{1,0:T(8,128)(2,1)S(1)} collective-permute-done((bf16[128,256]{1,0:T(8,128)(2,1)S(1)}, bf16[128,256]{1,0:T(8,128)(2,1)S(1)}, u32[]{:S(2)}, u32[]{:S(2)}) %collective-permute-start.26) | collective-permute-done | bytes 65568 | tf_op jit(solution)/shard_map/ppermute | solution.py:386
  81.6 1.3 %collective-permute-start.28 = (f32[8,256]{1,0:T(8,128)S(1)}, f32[8,256]{1,0:T(8,128)S(1)}, u32[]{:S(2)}, u32[]{:S(2)}) collective-permute-start(f32[8,256]{1,0:T(8,128)S(1)} %get-tuple-element.93.refs_1_), channel_id=1, source_target_pairs={{0,16},{8,24},{16,0},{24,8},{1,17},{9,25},{17,1},{25,9},{2,18},{10... | collective-permute-start | bytes 24584 | tf_op jit(solution)/shard_map/ppermute | solution.py:391
  82.9 0.6 collective-permute-start.27
  83.4 2.0 %project.7.refs_0_ = f32[88,256]{1,0:T(8,128)S(1)} custom-call(f32[128,256]{1,0:T(8,128)S(1)} %get-tuple-element.92.field_ref.refs_13_, bf16[88,128]{1,0:T(8,128)(2,1)S(1)} %get-tuple-element.67.pick1_ref, bf16[88,128]{1,0:T(8,128)(2,1)S(1)} %get-tuple-element.68.pick2_ref, bf16[32,256,256]{2,1,0:T(8,128)(2,1)S(1)} %turn.3.refs_0_, ...), custom_call_target="tpu_custom_call" | custom-call | flops 339738624 | bytes 10792960 | tf_op jit(solution)/shard_map/project/pallas_call | solution.py:347
  85.5 2.4 %step.7 = (bf16[128,256]{1,0:T(8,128)(2,1)S(1)}, f32[88,256]{1,0:T(8,128)}, f32[128,256]{1,0:T(8,128)S(1)}, f32[128,256]{1,0:T(8,128)S(1)}, f32[88,256]{1,0:T(8,...) custom-call(f32[88,256]{1,0:T(8,128)S(1)} %project.7.refs_0_, ...), custom_call_target="tpu_custom_call" | custom-call | flops 339738624 | bytes 11546624 | tf_op jit(solution)/shard_map/step/pallas_call | solution.py:347
  87.8 1.2 %collective-permute-start.32 = (bf16[128,256]{1,0:T(8,128)(2,1)S(1)}, bf16[128,256]{1,0:T(8,128)(2,1)S(1)}, u32[]{:S(2)}, u32[]{:S(2)}) collective-permute-start(bf16[128,256]{1,0:T(8,128)(2,1)S(1)} %get-tuple-element.100), channel_id=1, source_target_pairs={{0,3},{1,2},{2,1},{3,0},{4,7},{5,6},{6,5},{7,4},{8,11},{9,10},{10,... | collective-permute-start | bytes 196616 | tf_op jit(solution)/shard_map/ppermute | solution.py:386
  89.0 0.9 collective-permute-start.31
  89.9 1.5 %collective-permute-start.30 = (bf16[128,256]{1,0:T(8,128)(2,1)S(1)}, bf16[128,256]{1,0:T(8,128)(2,1)S(1)}, u32[]{:S(2)}, u32[]{:S(2)}) collective-permute-start(bf16[128,256]{1,0:T(8,128)(2,1)S(1)} %get-tuple-element.100), channel_id=1, source_target_pairs={{0,1},{1,0},{2,3},{3,2},{4,5},{5,4},{6,7},{7,6},{8,9},{9,8},{10,11... | collective-permute-start | bytes 196616 | tf_op jit(solution)/shard_map/ppermute | solution.py:386
  91.3 2.2 %collective-permute-done.32 = bf16[128,256]{1,0:T(8,128)(2,1)S(1)} collective-permute-done((bf16[128,256]{1,0:T(8,128)(2,1)S(1)}, bf16[128,256]{1,0:T(8,128)(2,1)S(1)}, u32[]{:S(2)}, u32[]{:S(2)}) %collective-permute-start.32) | collective-permute-done | bytes 65568 | tf_op jit(solution)/shard_map/ppermute | solution.py:386
  93.7 0.7 collective-permute-done.30
  94.5 1.9 %collective-permute-start.33 = (bf16[128,256]{1,0:T(8,128)(2,1)S(1)}, bf16[128,256]{1,0:T(8,128)(2,1)S(1)}, u32[]{:S(2)}, u32[]{:S(2)}) collective-permute-start(bf16[128,256]{1,0:T(8,128)(2,1)S(1)} %add_convert_fusion.refs_0_), channel_id=1, source_target_pairs={{0,4},{1,5},{2,6},{3,7},{4,0},{5,1},{6,2},{7,3},{8,12},{9,13},{10,... | collective-permute-start | bytes 196616 | tf_op jit(solution)/shard_map/ppermute | solution.py:386
  96.4 4.0 %collective-permute-done.33.refs_1_ = bf16[128,256]{1,0:T(8,128)(2,1)S(1)} collective-permute-done((bf16[128,256]{1,0:T(8,128)(2,1)S(1)}, bf16[128,256]{1,0:T(8,128)(2,1)S(1)}, u32[]{:S(2)}, u32[]{:S(2)}) %collective-permute-start.33) | collective-permute-done | bytes 65568 | tf_op jit(solution)/shard_map/ppermute | solution.py:386
  100.7 1.0 collective-permute-start.35
  101.7 0.9 collective-permute-start.34
  102.6 1.2 %collective-permute-done.36.refs_4_ = f32[8,256]{1,0:T(8,128)S(1)} collective-permute-done((f32[8,256]{1,0:T(8,128)S(1)}, f32[8,256]{1,0:T(8,128)S(1)}, u32[]{:S(2)}, u32[]{:S(2)}) %collective-permute-start.36) | collective-permute-done | bytes 8224 | tf_op jit(solution)/shard_map/ppermute | solution.py:391
  103.8 0.7 collective-permute-done.35.refs_3_
  104.5 0.6 final.1
  (36 shorter events, 1.9 us)
Async XLA Ops:
  1.6 10.7 %collective-permute-start.1 = (bf16[1,256,256]{2,1,0:T(8,128)(2,1)S(1)}, bf16[1,256,256]{2,1,0:T(8,128)(2,1)S(1)}, u32[]{:S(2)}, u32[]{:S(2)}) collective-permute-start(bf16[1,256,256]{2,1,0:T(8,128)(2,1)S(1)} %get-tuple-element.60), channel_id=1, source_target_pairs={{0,8},{8,16},{16,24},{24,0},{1,9},{9,17},{17,25},{25,1},{2,10},{10... | collective-permute-start | bytes 393224 | tf_op jit(solution)/shard_map/ppermute | solution.py:417
  2.1 10.1 %collective-permute-start = (f32[8,128]{1,0:T(8,128)S(1)}, f32[8,128]{1,0:T(8,128)S(1)}, u32[]{:S(2)}, u32[]{:S(2)}) collective-permute-start(f32[8,128]{1,0:T(8,128)S(1)} %get-tuple-element.59), channel_id=1, source_target_pairs={{0,8},{8,16},{16,24},{24,0},{1,9},{9,17},{17,25},{25,1},{2,10},{10... | collective-permute-start | bytes 12296 | tf_op jit(solution)/shard_map/ppermute | solution.py:417
  12.7 6.4 %collective-permute-start.4 = (bf16[128,256]{1,0:T(8,128)(2,1)S(1)}, bf16[128,256]{1,0:T(8,128)(2,1)S(1)}, u32[]{:S(2)}, u32[]{:S(2)}) collective-permute-start(bf16[128,256]{1,0:T(8,128)(2,1)S(1)} %get-tuple-element.63.after_ref), channel_id=1, source_target_pairs={{0,3},{1,2},{2,1},{3,0},{4,7},{5,6},{6,5},{7,4},{8,11},{9,10},{10,... | collective-permute-start | bytes 196616 | tf_op jit(solution)/shard_map/ppermute | solution.py:386
  15.3 4.3 %collective-permute-start.3 = (bf16[128,256]{1,0:T(8,128)(2,1)S(1)}, bf16[128,256]{1,0:T(8,128)(2,1)S(1)}, u32[]{:S(2)}, u32[]{:S(2)}) collective-permute-start(bf16[128,256]{1,0:T(8,128)(2,1)S(1)} %get-tuple-element.63.after_ref), channel_id=1, source_target_pairs={{0,2},{1,3},{2,0},{3,1},{4,6},{5,7},{6,4},{7,5},{8,10},{9,11},{10,... | collective-permute-start | bytes 196616 | tf_op jit(solution)/shard_map/ppermute | solution.py:386
  15.7 4.3 %collective-permute-start.2 = (bf16[128,256]{1,0:T(8,128)(2,1)S(1)}, bf16[128,256]{1,0:T(8,128)(2,1)S(1)}, u32[]{:S(2)}, u32[]{:S(2)}) collective-permute-start(bf16[128,256]{1,0:T(8,128)(2,1)S(1)} %get-tuple-element.63.after_ref), channel_id=1, source_target_pairs={{0,1},{1,0},{2,3},{3,2},{4,5},{5,4},{6,7},{7,6},{8,9},{9,8},{10,11... | collective-permute-start | bytes 196616 | tf_op jit(solution)/shard_map/ppermute | solution.py:386
  20.0 5.5 %collective-permute-start.5 = (bf16[128,256]{1,0:T(8,128)(2,1)S(1)}, bf16[128,256]{1,0:T(8,128)(2,1)S(1)}, u32[]{:S(2)}, u32[]{:S(2)}) collective-permute-start(bf16[128,256]{1,0:T(8,128)(2,1)S(1)} %add_convert_fusion.4.refs_0_.after_ref), channel_id=1, source_target_pairs={{0,4},{1,5},{2,6},{3,7},{4,0},{5,1},{6,2},{7,3},{8,12},{9,13},{10,... | collective-permute-start | bytes 196616 | tf_op jit(solution)/shard_map/ppermute | solution.py:386
  25.5 4.2 %collective-permute-start.8 = (f32[8,256]{1,0:T(8,128)S(1)}, f32[8,256]{1,0:T(8,128)S(1)}, u32[]{:S(2)}, u32[]{:S(2)}) collective-permute-start(f32[8,256]{1,0:T(8,128)S(1)} %get-tuple-element.71.refs_1_), channel_id=1, source_target_pairs={{0,24},{8,16},{16,8},{24,0},{1,25},{9,17},{17,9},{25,1},{2,26},{10... | collective-permute-start | bytes 24584 | tf_op jit(solution)/shard_map/ppermute | solution.py:391
  25.6 4.2 %collective-permute-start.7 = (f32[8,256]{1,0:T(8,128)S(1)}, f32[8,256]{1,0:T(8,128)S(1)}, u32[]{:S(2)}, u32[]{:S(2)}) collective-permute-start(f32[8,256]{1,0:T(8,128)S(1)} %get-tuple-element.71.refs_1_), channel_id=1, source_target_pairs={{0,16},{8,24},{16,0},{24,8},{1,17},{9,25},{17,1},{25,9},{2,18},{10... | collective-permute-start | bytes 24584 | tf_op jit(solution)/shard_map/ppermute | solution.py:391
  26.2 3.6 %collective-permute-start.6 = (f32[8,256]{1,0:T(8,128)S(1)}, f32[8,256]{1,0:T(8,128)S(1)}, u32[]{:S(2)}, u32[]{:S(2)}) collective-permute-start(f32[8,256]{1,0:T(8,128)S(1)} %get-tuple-element.71.refs_1_), channel_id=1, source_target_pairs={{0,8},{8,0},{16,24},{24,16},{1,9},{9,1},{17,25},{25,17},{2,10},{10... | collective-permute-start | bytes 24584 | tf_op jit(solution)/shard_map/ppermute | solution.py:391
  31.7 5.6 %collective-permute-start.11 = (bf16[128,256]{1,0:T(8,128)(2,1)S(1)}, bf16[128,256]{1,0:T(8,128)(2,1)S(1)}, u32[]{:S(2)}, u32[]{:S(2)}) collective-permute-start(bf16[128,256]{1,0:T(8,128)(2,1)S(1)} %get-tuple-element.74.after_ref), channel_id=1, source_target_pairs={{0,3},{1,2},{2,1},{3,0},{4,7},{5,6},{6,5},{7,4},{8,11},{9,10},{10,... | collective-permute-start | bytes 196616 | tf_op jit(solution)/shard_map/ppermute | solution.py:386
  33.4 4.3 %collective-permute-start.10 = (bf16[128,256]{1,0:T(8,128)(2,1)S(1)}, bf16[128,256]{1,0:T(8,128)(2,1)S(1)}, u32[]{:S(2)}, u32[]{:S(2)}) collective-permute-start(bf16[128,256]{1,0:T(8,128)(2,1)S(1)} %get-tuple-element.74.after_ref), channel_id=1, source_target_pairs={{0,2},{1,3},{2,0},{3,1},{4,6},{5,7},{6,4},{7,5},{8,10},{9,11},{10,... | collective-permute-start | bytes 196616 | tf_op jit(solution)/shard_map/ppermute | solution.py:386
  33.9 4.3 %collective-permute-start.9 = (bf16[128,256]{1,0:T(8,128)(2,1)S(1)}, bf16[128,256]{1,0:T(8,128)(2,1)S(1)}, u32[]{:S(2)}, u32[]{:S(2)}) collective-permute-start(bf16[128,256]{1,0:T(8,128)(2,1)S(1)} %get-tuple-element.74.after_ref), channel_id=1, source_target_pairs={{0,1},{1,0},{2,3},{3,2},{4,5},{5,4},{6,7},{7,6},{8,9},{9,8},{10,11... | collective-permute-start | bytes 196616 | tf_op jit(solution)/shard_map/ppermute | solution.py:386
  38.2 5.3 %collective-permute-start.12 = (bf16[128,256]{1,0:T(8,128)(2,1)S(1)}, bf16[128,256]{1,0:T(8,128)(2,1)S(1)}, u32[]{:S(2)}, u32[]{:S(2)}) collective-permute-start(bf16[128,256]{1,0:T(8,128)(2,1)S(1)} %add_convert_fusion.3.refs_0_), channel_id=1, source_target_pairs={{0,4},{1,5},{2,6},{3,7},{4,0},{5,1},{6,2},{7,3},{8,12},{9,13},{10,... | collective-permute-start | bytes 196616 | tf_op jit(solution)/shard_map/ppermute | solution.py:386
  43.7 4.0 %collective-permute-start.15 = (f32[8,256]{1,0:T(8,128)S(1)}, f32[8,256]{1,0:T(8,128)S(1)}, u32[]{:S(2)}, u32[]{:S(2)}) collective-permute-start(f32[8,256]{1,0:T(8,128)S(1)} %get-tuple-element.78.refs_1_), channel_id=1, source_target_pairs={{0,24},{8,16},{16,8},{24,0},{1,25},{9,17},{17,9},{25,1},{2,26},{10... | collective-permute-start | bytes 24584 | tf_op jit(solution)/shard_map/ppermute | solution.py:391
  43.8 3.9 %collective-permute-start.14 = (f32[8,256]{1,0:T(8,128)S(1)}, f32[8,256]{1,0:T(8,128)S(1)}, u32[]{:S(2)}, u32[]{:S(2)}) collective-permute-start(f32[8,256]{1,0:T(8,128)S(1)} %get-tuple-element.78.refs_1_), channel_id=1, source_target_pairs={{0,16},{8,24},{16,0},{24,8},{1,17},{9,25},{17,1},{25,9},{2,18},{10... | collective-permute-start | bytes 24584 | tf_op jit(solution)/shard_map/ppermute | solution.py:391
  45.6 2.1 %collective-permute-start.13 = (f32[8,256]{1,0:T(8,128)S(1)}, f32[8,256]{1,0:T(8,128)S(1)}, u32[]{:S(2)}, u32[]{:S(2)}) collective-permute-start(f32[8,256]{1,0:T(8,128)S(1)} %get-tuple-element.78.refs_1_), channel_id=1, source_target_pairs={{0,8},{8,0},{16,24},{24,16},{1,9},{9,1},{17,25},{25,17},{2,10},{10... | collective-permute-start | bytes 24584 | tf_op jit(solution)/shard_map/ppermute | solution.py:391
  49.6 5.9 %collective-permute-start.18 = (bf16[128,256]{1,0:T(8,128)(2,1)S(1)}, bf16[128,256]{1,0:T(8,128)(2,1)S(1)}, u32[]{:S(2)}, u32[]{:S(2)}) collective-permute-start(bf16[128,256]{1,0:T(8,128)(2,1)S(1)} %get-tuple-element.80), channel_id=1, source_target_pairs={{0,3},{1,2},{2,1},{3,0},{4,7},{5,6},{6,5},{7,4},{8,11},{9,10},{10,... | collective-permute-start | bytes 196616 | tf_op jit(solution)/shard_map/ppermute | solution.py:386
  52.0 4.3 %collective-permute-start.17 = (bf16[128,256]{1,0:T(8,128)(2,1)S(1)}, bf16[128,256]{1,0:T(8,128)(2,1)S(1)}, u32[]{:S(2)}, u32[]{:S(2)}) collective-permute-start(bf16[128,256]{1,0:T(8,128)(2,1)S(1)} %get-tuple-element.80), channel_id=1, source_target_pairs={{0,2},{1,3},{2,0},{3,1},{4,6},{5,7},{6,4},{7,5},{8,10},{9,11},{10,... | collective-permute-start | bytes 196616 | tf_op jit(solution)/shard_map/ppermute | solution.py:386
  52.5 4.3 %collective-permute-start.16 = (bf16[128,256]{1,0:T(8,128)(2,1)S(1)}, bf16[128,256]{1,0:T(8,128)(2,1)S(1)}, u32[]{:S(2)}, u32[]{:S(2)}) collective-permute-start(bf16[128,256]{1,0:T(8,128)(2,1)S(1)} %get-tuple-element.80), channel_id=1, source_target_pairs={{0,1},{1,0},{2,3},{3,2},{4,5},{5,4},{6,7},{7,6},{8,9},{9,8},{10,11... | collective-permute-start | bytes 196616 | tf_op jit(solution)/shard_map/ppermute | solution.py:386
  56.8 5.4 %collective-permute-start.19 = (bf16[128,256]{1,0:T(8,128)(2,1)S(1)}, bf16[128,256]{1,0:T(8,128)(2,1)S(1)}, u32[]{:S(2)}, u32[]{:S(2)}) collective-permute-start(bf16[128,256]{1,0:T(8,128)(2,1)S(1)} %add_convert_fusion.2.refs_0_), channel_id=1, source_target_pairs={{0,4},{1,5},{2,6},{3,7},{4,0},{5,1},{6,2},{7,3},{8,12},{9,13},{10,... | collective-permute-start | bytes 196616 | tf_op jit(solution)/shard_map/ppermute | solution.py:386
  62.5 4.0 %collective-permute-start.22 = (f32[8,256]{1,0:T(8,128)S(1)}, f32[8,256]{1,0:T(8,128)S(1)}, u32[]{:S(2)}, u32[]{:S(2)}) collective-permute-start(f32[8,256]{1,0:T(8,128)S(1)} %get-tuple-element.83.refs_1_), channel_id=1, source_target_pairs={{0,24},{8,16},{16,8},{24,0},{1,25},{9,17},{17,9},{25,1},{2,26},{10... | collective-permute-start | bytes 24584 | tf_op jit(solution)/shard_map/ppermute | solution.py:391
  62.5 3.9 %collective-permute-start.21 = (f32[8,256]{1,0:T(8,128)S(1)}, f32[8,256]{1,0:T(8,128)S(1)}, u32[]{:S(2)}, u32[]{:S(2)}) collective-permute-start(f32[8,256]{1,0:T(8,128)S(1)} %get-tuple-element.83.refs_1_), channel_id=1, source_target_pairs={{0,16},{8,24},{16,0},{24,8},{1,17},{9,25},{17,1},{25,9},{2,18},{10... | collective-permute-start | bytes 24584 | tf_op jit(solution)/shard_map/ppermute | solution.py:391
  63.4 3.1 %collective-permute-start.20 = (f32[8,256]{1,0:T(8,128)S(1)}, f32[8,256]{1,0:T(8,128)S(1)}, u32[]{:S(2)}, u32[]{:S(2)}) collective-permute-start(f32[8,256]{1,0:T(8,128)S(1)} %get-tuple-element.83.refs_1_), channel_id=1, source_target_pairs={{0,8},{8,0},{16,24},{24,16},{1,9},{9,1},{17,25},{25,17},{2,10},{10... | collective-permute-start | bytes 24584 | tf_op jit(solution)/shard_map/ppermute | solution.py:391
  68.4 5.8 %collective-permute-start.25 = (bf16[128,256]{1,0:T(8,128)(2,1)S(1)}, bf16[128,256]{1,0:T(8,128)(2,1)S(1)}, u32[]{:S(2)}, u32[]{:S(2)}) collective-permute-start(bf16[128,256]{1,0:T(8,128)(2,1)S(1)} %get-tuple-element.90), channel_id=1, source_target_pairs={{0,3},{1,2},{2,1},{3,0},{4,7},{5,6},{6,5},{7,4},{8,11},{9,10},{10,... | collective-permute-start | bytes 196616 | tf_op jit(solution)/shard_map/ppermute | solution.py:386
  70.0 4.9 %collective-permute-start.24 = (bf16[128,256]{1,0:T(8,128)(2,1)S(1)}, bf16[128,256]{1,0:T(8,128)(2,1)S(1)}, u32[]{:S(2)}, u32[]{:S(2)}) collective-permute-start(bf16[128,256]{1,0:T(8,128)(2,1)S(1)} %get-tuple-element.90), channel_id=1, source_target_pairs={{0,2},{1,3},{2,0},{3,1},{4,6},{5,7},{6,4},{7,5},{8,10},{9,11},{10,... | collective-permute-start | bytes 196616 | tf_op jit(solution)/shard_map/ppermute | solution.py:386
  71.1 4.3 %collective-permute-start.23 = (bf16[128,256]{1,0:T(8,128)(2,1)S(1)}, bf16[128,256]{1,0:T(8,128)(2,1)S(1)}, u32[]{:S(2)}, u32[]{:S(2)}) collective-permute-start(bf16[128,256]{1,0:T(8,128)(2,1)S(1)} %get-tuple-element.90), channel_id=1, source_target_pairs={{0,1},{1,0},{2,3},{3,2},{4,5},{5,4},{6,7},{7,6},{8,9},{9,8},{10,11... | collective-permute-start | bytes 196616 | tf_op jit(solution)/shard_map/ppermute | solution.py:386
  75.4 5.9 %collective-permute-start.26 = (bf16[128,256]{1,0:T(8,128)(2,1)S(1)}, bf16[128,256]{1,0:T(8,128)(2,1)S(1)}, u32[]{:S(2)}, u32[]{:S(2)}) collective-permute-start(bf16[128,256]{1,0:T(8,128)(2,1)S(1)} %add_convert_fusion.1.refs_0_), channel_id=1, source_target_pairs={{0,4},{1,5},{2,6},{3,7},{4,0},{5,1},{6,2},{7,3},{8,12},{9,13},{10,... | collective-permute-start | bytes 196616 | tf_op jit(solution)/shard_map/ppermute | solution.py:386
  81.5 4.0 %collective-permute-start.29 = (f32[8,256]{1,0:T(8,128)S(1)}, f32[8,256]{1,0:T(8,128)S(1)}, u32[]{:S(2)}, u32[]{:S(2)}) collective-permute-start(f32[8,256]{1,0:T(8,128)S(1)} %get-tuple-element.93.refs_1_), channel_id=1, source_target_pairs={{0,24},{8,16},{16,8},{24,0},{1,25},{9,17},{17,9},{25,1},{2,26},{10... | collective-permute-start | bytes 24584 | tf_op jit(solution)/shard_map/ppermute | solution.py:391
  81.6 3.9 %collective-permute-start.28 = (f32[8,256]{1,0:T(8,128)S(1)}, f32[8,256]{1,0:T(8,128)S(1)}, u32[]{:S(2)}, u32[]{:S(2)}) collective-permute-start(f32[8,256]{1,0:T(8,128)S(1)} %get-tuple-element.93.refs_1_), channel_id=1, source_target_pairs={{0,16},{8,24},{16,0},{24,8},{1,17},{9,25},{17,1},{25,9},{2,18},{10... | collective-permute-start | bytes 24584 | tf_op jit(solution)/shard_map/ppermute | solution.py:391
  82.9 2.6 %collective-permute-start.27 = (f32[8,256]{1,0:T(8,128)S(1)}, f32[8,256]{1,0:T(8,128)S(1)}, u32[]{:S(2)}, u32[]{:S(2)}) collective-permute-start(f32[8,256]{1,0:T(8,128)S(1)} %get-tuple-element.93.refs_1_), channel_id=1, source_target_pairs={{0,8},{8,0},{16,24},{24,16},{1,9},{9,1},{17,25},{25,17},{2,10},{10... | collective-permute-start | bytes 24584 | tf_op jit(solution)/shard_map/ppermute | solution.py:391
  87.8 5.7 %collective-permute-start.32 = (bf16[128,256]{1,0:T(8,128)(2,1)S(1)}, bf16[128,256]{1,0:T(8,128)(2,1)S(1)}, u32[]{:S(2)}, u32[]{:S(2)}) collective-permute-start(bf16[128,256]{1,0:T(8,128)(2,1)S(1)} %get-tuple-element.100), channel_id=1, source_target_pairs={{0,3},{1,2},{2,1},{3,0},{4,7},{5,6},{6,5},{7,4},{8,11},{9,10},{10,... | collective-permute-start | bytes 196616 | tf_op jit(solution)/shard_map/ppermute | solution.py:386
  89.0 4.7 %collective-permute-start.31 = (bf16[128,256]{1,0:T(8,128)(2,1)S(1)}, bf16[128,256]{1,0:T(8,128)(2,1)S(1)}, u32[]{:S(2)}, u32[]{:S(2)}) collective-permute-start(bf16[128,256]{1,0:T(8,128)(2,1)S(1)} %get-tuple-element.100), channel_id=1, source_target_pairs={{0,2},{1,3},{2,0},{3,1},{4,6},{5,7},{6,4},{7,5},{8,10},{9,11},{10,... | collective-permute-start | bytes 196616 | tf_op jit(solution)/shard_map/ppermute | solution.py:386
  89.9 4.6 %collective-permute-start.30 = (bf16[128,256]{1,0:T(8,128)(2,1)S(1)}, bf16[128,256]{1,0:T(8,128)(2,1)S(1)}, u32[]{:S(2)}, u32[]{:S(2)}) collective-permute-start(bf16[128,256]{1,0:T(8,128)(2,1)S(1)} %get-tuple-element.100), channel_id=1, source_target_pairs={{0,1},{1,0},{2,3},{3,2},{4,5},{5,4},{6,7},{7,6},{8,9},{9,8},{10,11... | collective-permute-start | bytes 196616 | tf_op jit(solution)/shard_map/ppermute | solution.py:386
  94.5 6.0 %collective-permute-start.33 = (bf16[128,256]{1,0:T(8,128)(2,1)S(1)}, bf16[128,256]{1,0:T(8,128)(2,1)S(1)}, u32[]{:S(2)}, u32[]{:S(2)}) collective-permute-start(bf16[128,256]{1,0:T(8,128)(2,1)S(1)} %add_convert_fusion.refs_0_), channel_id=1, source_target_pairs={{0,4},{1,5},{2,6},{3,7},{4,0},{5,1},{6,2},{7,3},{8,12},{9,13},{10,... | collective-permute-start | bytes 196616 | tf_op jit(solution)/shard_map/ppermute | solution.py:386
  100.6 3.1 %collective-permute-start.36 = (f32[8,256]{1,0:T(8,128)S(1)}, f32[8,256]{1,0:T(8,128)S(1)}, u32[]{:S(2)}, u32[]{:S(2)}) collective-permute-start(f32[8,256]{1,0:T(8,128)S(1)} %get-tuple-element.103.refs_1_), channel_id=1, source_target_pairs={{0,24},{8,16},{16,8},{24,0},{1,25},{9,17},{17,9},{25,1},{2,26},{10... | collective-permute-start | bytes 24584 | tf_op jit(solution)/shard_map/ppermute | solution.py:391
  100.7 3.8 %collective-permute-start.35 = (f32[8,256]{1,0:T(8,128)S(1)}, f32[8,256]{1,0:T(8,128)S(1)}, u32[]{:S(2)}, u32[]{:S(2)}) collective-permute-start(f32[8,256]{1,0:T(8,128)S(1)} %get-tuple-element.103.refs_1_), channel_id=1, source_target_pairs={{0,16},{8,24},{16,0},{24,8},{1,17},{9,25},{17,1},{25,9},{2,18},{10... | collective-permute-start | bytes 24584 | tf_op jit(solution)/shard_map/ppermute | solution.py:391
  101.7 2.8 %collective-permute-start.34 = (f32[8,256]{1,0:T(8,128)S(1)}, f32[8,256]{1,0:T(8,128)S(1)}, u32[]{:S(2)}, u32[]{:S(2)}) collective-permute-start(f32[8,256]{1,0:T(8,128)S(1)} %get-tuple-element.103.refs_1_), channel_id=1, source_target_pairs={{0,8},{8,0},{16,24},{24,16},{1,9},{9,1},{17,25},{25,17},{2,10},{10... | collective-permute-start | bytes 24584 | tf_op jit(solution)/shard_map/ppermute | solution.py:391

commit v5 on v4

--- a/solution.py
+++ b/solution.py
@@ -123,12 +123,13 @@
     return copies
 
 
-def pack_kernel(jac_ref, e_ref, res_ref, count_ref, out_jac_ref, out_ref, pair_ref, tally_ref, sems):
+def pack_kernel(jac_ref, e_ref, res_ref, count_ref, out_ref, pair_ref, tally_ref, wide_ref, sems):
     last = jac_ref.shape[0] - 1
     block = pl.ds(last, 1)
+    height = jac_ref.shape[1]
     copies = fetch(
         [
-            (jac_ref.at[block], out_jac_ref),
+            (jac_ref.at[block], out_ref.at[:, :height]),
             (e_ref.at[block], pair_ref.at[0:1]),
             (res_ref.at[block], pair_ref.at[1:2]),
             (count_ref, tally_ref),
@@ -137,11 +138,17 @@
     )
     for copy in copies[1:]:
         copy.wait()
-    lane = lax.broadcasted_iota(jnp.int32, (1, out_ref.shape[1]), 1)
-    out_ref[...] = jnp.zeros_like(out_ref)
-    out_ref[0:2, :] = pair_ref[0]
-    out_ref[2:4, :] = pair_ref[1]
-    out_ref[4:5, :] = jnp.where(lane < tally_ref[0, last], 1.0, 0.0)
+    ties = pair_ref.shape[2]
+    lane = lax.broadcasted_iota(jnp.int32, (1, ties), 1)
+    wide_ref[...] = jnp.zeros_like(wide_ref)
+    for i in range(2):
+        rest = pair_ref[i]
+        for j in range(3):
+            part = rest.astype(BF16).astype(F32)
+            rest = rest - part
+            wide_ref[4 * j + 2 * i : 4 * j + 2 * i + 2, :ties] = part
+    wide_ref[12:13, :ties] = jnp.where(lane < tally_ref[0, last], 1.0, 0.0)
+    out_ref[0, height:] = wide_ref[...].astype(BF16)
     copies[0].wait()
 
 
@@ -157,11 +164,14 @@
         for at in range(0, ref.shape[0], OCTET):
             part = pl.ds(at, OCTET)
             copies.append(pltpu.make_async_copy(ref.at[part], out_ref.at[part], sems.at[len(copies)]))
-            copies[-1].start()
+    for copy in copies[:2]:
+        copy.start()
     links, scenes = cjac_ref.shape[0], ajac_ref.shape[0]
     blocks = links + scenes
     for copy in near:
         copy.wait()
+    for copy in copies[2:]:
+        copy.start()
     live_ref[0:links] = jnp.ones((links, live_ref.shape[1]), F32)
     live_rows(count_ref, live_ref.at[links:blocks])
     for i in range(scenes):
@@ -196,11 +206,14 @@
             octet += 1
 
 
-def rhs_kernel(coef_ref, t1_ref, t2_ref, small_ref, ejac_ref, put1_ref, put2_ref, out_ref, out_coef_ref, all1_ref, all2_ref):
-    blocks = t1_ref.shape[0]
+def rhs_kernel(coef_ref, t1_ref, t2_ref, edge_ref, put1_ref, put2_ref, out_ref, out_coef_ref, ejac_ref, all1_ref, all2_ref):
+    blocks, ties = t1_ref.shape[0], coef_ref.shape[2]
+    height = ejac_ref.shape[1]
     rows = pl.ds(blocks, OCTET)
-    e1, e2, r1, r2, live = (small_ref[i : i + 1, :] for i in range(5))
-    c = elimination(e1, e2, live)
+    ejac_ref[...] = edge_ref[:, :height]
+    parts = edge_ref[0, height:, :ties].astype(F32)
+    e1, e2, r1, r2 = (parts[i : i + 1] + parts[i + 4 : i + 5] + parts[i + 8 : i + 9] for i in range(4))
+    c = elimination(e1, e2, parts[12:13])
     fill = lambda x: jnp.where(row_of((OCTET, x.shape[1])) == 0, x, 0.0)
     for i in range(3):
         out_coef_ref[i, :blocks] = coef_ref[i]
@@ -425,15 +438,15 @@
     term_space = [((slots, width), F32)] * 2
     sems = pltpu.SemaphoreType.DMA
     pack_args = (ajac, along_e[0], along_res[0], along_count)
-    packed = call(
+    edge = call(
         pack_kernel,
-        [((1, 2 * ties, width), BF16), ((OCTET, ties), F32)],
-        [((2, 2, ties), F32), pltpu.SMEM((1, scenes), jnp.int32), sems((4,))],
+        [((1, 2 * ties + 2 * OCTET, width), BF16)],
+        [((2, 2, ties), F32), pltpu.SMEM((1, scenes), jnp.int32), ((2 * OCTET, width), F32), sems((4,))],
         "pack",
         pack_args,
         spaces={i: pltpu.HBM for i in range(4)},
     )
-    ejac, small = pass_on(packed[0]), pass_on(packed[1])
+    edge = pass_on(edge[0])
     blocks = links + scenes
     part_tie = (blocks, ties)
     put = ((rows, slots), BF16)
@@ -465,7 +478,6 @@
         work,
         {i: pltpu.HBM for i in range(11)},
     )
-    jacs = (cjac, ajac, ejac)
 
     def turn(start, count, refs, after):
         outs = [((min(count, j.shape[0]),) + j.shape[1:], BF16) for j in refs]
@@ -483,14 +495,15 @@
         field, packet = call(kernel, [(full, F32), ((OCTET, width), F32)], [], "finish", args)
         return field, orbit_packets(packet)
 
-    sent, coef = call(
+    sent, coef, ejac = call(
         rhs_kernel,
-        [(full, BF16), ((3,) + tie, F32)],
+        [(full, BF16), ((3,) + tie, F32), ((1, 2 * ties, width), BF16)],
         term_space,
         "rhs",
-        (coef, t1, t2, small, ejac, put1, put2),
+        (coef, t1, t2, edge, put1, put2),
         work // blocks,
     )
+    jacs = (cjac, ajac, ejac)
     half = links // 2
     turned = []
 

time: 105 us -> 103 us (0.981)
  starting transfers between devices: 42.4 us -> 36.5 us
  waiting for transfers between devices: 27.7 us -> 33.5 us
  Pallas kernels: 34 us -> 32 us
    ppermute x20, waiting for transfers between devices: 25.7 us -> 31.6 us  [swap(): lax.ppermute(block, axis, [(i, i ^ mask) for i in range(lax.axis_size(axi...]
    ppermute x20, starting transfers between devices: 29.7 us -> 26.4 us  [swap(): lax.ppermute(block, axis, [(i, i ^ mask) for i in range(lax.axis_size(axi...]
    ppermute x2 -> x1, starting transfers between devices: 3.13 us -> 0.54 us  [pass_on(): return lax.ppermute(block, 'orbit', [(i, (i + 1) % n) for i in range(n)])]
    pallas_call x20, Pallas kernels: 34 us -> 32 us  [call(): pl.pallas_call(kernel, out_shape=[jax.ShapeDtypeStruct(*o) for o in outs]...]
  transfers between devices with their start and end apart: 37 -> 36, of which waited for: 20 -> 19; matrix products, arithmetic and copies ran while one was open for 0% -> 0% of each run, Pallas kernels for 22% -> 21%
where the time goes in v5:
time: 103 us
  starting transfers between devices  36.5 us (35%)
  waiting for transfers between devices  33.5 us (33%)
  Pallas kernels  32 us (31%)
    pallas_call x20, Pallas kernels, call(): pl.pallas_call(kernel, out_shape=[jax.ShapeDtypeStruct(*o) for o in outs]...  32 us
    ppermute x20, waiting for transfers between devices, swap(): lax.ppermute(block, axis, [(i, i ^ mask) for i in range(lax.axis_size(axi...  31.6 us
    ppermute x20, starting transfers between devices, swap(): lax.ppermute(block, axis, [(i, i ^ mask) for i in range(lax.axis_size(axi...  26.4 us
    ppermute x15, starting transfers between devices, orbit_packets(): lax.ppermute(packet, 'orbit', [(i, i ^ mask) for i in range(n)])  9.59 us
  transfers between devices with their start and end apart: 36, of which 19 were waited for; matrix products, arithmetic and copies ran while one was open for 0% of the time, Pallas kernels for 21%

profile of v5, /device:TPU:0, one launch (start us, length us, event | category | flops | bytes accessed | tf_op | source)
XLA Modules:
  0.0 103.1 jit_solution(1528495616172042036)
XLA Ops:
  0.6 0.9 pack.1
  1.6 0.5 collective-permute-start
  2.1 5.5 %setup.1 = (bf16[64,256,256]{2,1,0:T(8,128)(2,1)S(1)}, bf16[16,256,256]{2,1,0:T(8,128)(2,1)S(1)}, f32[3,80,128]{2,1,0:T(8,128)S(1)}, bf16[128,88]{1,0:T(8,128)(2...) custom-call(bf16[64,256,256]{2,1,0:T(8,128)(2,1)} %bitcast.9, ...), custom_call_target="tpu_custom_call" | custom-call | flops 339738624 | bytes 10650496 | tf_op jit(solution)/shard_map/setup/pallas_call | solution.py:360
  7.7 0.4 rhs.1
  8.1 3.6 %collective-permute-start.3 = (bf16[128,256]{1,0:T(8,128)(2,1)S(1)}, bf16[128,256]{1,0:T(8,128)(2,1)S(1)}, u32[]{:S(2)}, u32[]{:S(2)}) collective-permute-start(bf16[128,256]{1,0:T(8,128)(2,1)S(1)} %get-tuple-element.60.after_ref), channel_id=1, source_target_pairs={{0,3},{1,2},{2,1},{3,0},{4,7},{5,6},{6,5},{7,4},{8,11},{9,10},{10,... | collective-permute-start | bytes 196616 | tf_op jit(solution)/shard_map/ppermute | solution.py:399
  11.7 0.5 collective-permute-start.2
  12.3 2.8 %turn.3.refs_0_ = bf16[32,256,256]{2,1,0:T(8,128)(2,1)S(1)} custom-call(bf16[128,256]{1,0:T(8,128)(2,1)S(1)} %get-tuple-element.60.after_ref, bf16[64,256,256]{2,1,0:T(8,128)(2,1)S(1)} %get-tuple-element.61.refs_0_.refs_9_), custom_call_target="tpu_custom_call" | custom-call | flops 135895456 | bytes 8454144 | tf_op jit(solution)/shard_map/turn/pallas_call | solution.py:360
  15.1 1.2 %collective-permute-done.2 = bf16[128,256]{1,0:T(8,128)(2,1)S(1)} collective-permute-done((bf16[128,256]{1,0:T(8,128)(2,1)S(1)}, bf16[128,256]{1,0:T(8,128)(2,1)S(1)}, u32[]{:S(2)}, u32[]{:S(2)}) %collective-permute-start.2) | collective-permute-done | bytes 65568 | tf_op jit(solution)/shard_map/ppermute | solution.py:399
  16.3 0.7 collective-permute-done.1
  17.1 2.7 %collective-permute-start.4 = (bf16[128,256]{1,0:T(8,128)(2,1)S(1)}, bf16[128,256]{1,0:T(8,128)(2,1)S(1)}, u32[]{:S(2)}, u32[]{:S(2)}) collective-permute-start(bf16[128,256]{1,0:T(8,128)(2,1)S(1)} %add_convert_fusion.4.refs_0_.after_ref), channel_id=1, source_target_pairs={{0,4},{1,5},{2,6},{3,7},{4,0},{5,1},{6,2},{7,3},{8,12},{9,13},{10,... | collective-permute-start | bytes 196616 | tf_op jit(solution)/shard_map/ppermute | solution.py:399
  19.7 2.8 %turn.4.refs_1_ = bf16[32,256,256]{2,1,0:T(8,128)(2,1)S(1)} custom-call(bf16[128,256]{1,0:T(8,128)(2,1)S(1)} %add_convert_fusion.4.refs_0_.after_ref, bf16[64,256,256]{2,1,0:T(8,128)(2,1)S(1)} %get-tuple-element.61.refs_0_.refs_9_), custom_call_target="tpu_custom_call" | custom-call | flops 135895456 | bytes 8454144 | tf_op jit(solution)/shard_map/turn/pallas_call | solution.py:360
  22.6 1.2 %collective-permute-done.4.refs_1_ = bf16[128,256]{1,0:T(8,128)(2,1)S(1)} collective-permute-done((bf16[128,256]{1,0:T(8,128)(2,1)S(1)}, bf16[128,256]{1,0:T(8,128)(2,1)S(1)}, u32[]{:S(2)}, u32[]{:S(2)}) %collective-permute-start.4) | collective-permute-done | bytes 65568 | tf_op jit(solution)/shard_map/ppermute | solution.py:399
  23.8 0.3 collective-permute-start.6
  24.1 1.5 %collective-permute-start.5 = (f32[8,256]{1,0:T(8,128)S(1)}, f32[8,256]{1,0:T(8,128)S(1)}, u32[]{:S(2)}, u32[]{:S(2)}) collective-permute-start(f32[8,256]{1,0:T(8,128)S(1)} %get-tuple-element.69.refs_1_), channel_id=1, source_target_pairs={{0,8},{8,0},{16,24},{24,16},{1,9},{9,1},{17,25},{25,17},{2,10},{10... | collective-permute-start | bytes 24584 | tf_op jit(solution)/shard_map/ppermute | solution.py:404
  25.7 2.3 %project.4.refs_0_ = f32[88,256]{1,0:T(8,128)S(1)} custom-call(f32[128,256]{1,0:T(8,128)S(1)} %get-tuple-element.63.field_ref.refs_12_.refs_2_, bf16[88,128]{1,0:T(8,128)(2,1)S(1)} %get-tuple-element.64.pick1_ref, bf16[88,128]{1,0:T(8,128)(2,1)S(1)} %get-tuple-element.65.pick2_ref, bf16[32,256,256]{2,1,0:T(8,128)(2,1)S(1)} %turn.3.refs_0_, ...), custom_call_target="tpu_custom_call" | custom-call | flops 339738624 | bytes 10792960 | tf_op jit(solution)/shard_map/project/pallas_call | solution.py:360
  28.0 1.9 %step.4 = (bf16[128,256]{1,0:T(8,128)(2,1)S(1)}, f32[88,256]{1,0:T(8,128)S(1)}) custom-call(f32[88,256]{1,0:T(8,128)S(1)} %project.4.refs_0_, f32[8,256]{1,0:T(8,128)S(1)} %get-tuple-element.69.refs_1_, f32[8,256]{1,0:T(8,128)S(1)} %collective-permute-done.5.refs_2_, f32[8,256]{1,0:T(8,128)S(1)} %collective-permute-done.6.refs_3_, ...), custom_call_target="tpu_custom_call" | custom-call | flops 339738624 | bytes 11067392 | tf_op jit(solution)/shard_map/step/pallas_call | solution.py:360
  29.9 0.9 collective-permute-start.10
  30.9 1.5 %collective-permute-start.9 = (bf16[128,256]{1,0:T(8,128)(2,1)S(1)}, bf16[128,256]{1,0:T(8,128)(2,1)S(1)}, u32[]{:S(2)}, u32[]{:S(2)}) collective-permute-start(bf16[128,256]{1,0:T(8,128)(2,1)S(1)} %get-tuple-element.72.after_ref), channel_id=1, source_target_pairs={{0,2},{1,3},{2,0},{3,1},{4,6},{5,7},{6,4},{7,5},{8,10},{9,11},{10,... | collective-permute-start | bytes 196616 | tf_op jit(solution)/shard_map/ppermute | solution.py:399
  32.3 1.2 %collective-permute-start.8 = (bf16[128,256]{1,0:T(8,128)(2,1)S(1)}, bf16[128,256]{1,0:T(8,128)(2,1)S(1)}, u32[]{:S(2)}, u32[]{:S(2)}) collective-permute-start(bf16[128,256]{1,0:T(8,128)(2,1)S(1)} %get-tuple-element.72.after_ref), channel_id=1, source_target_pairs={{0,1},{1,0},{2,3},{3,2},{4,5},{5,4},{6,7},{7,6},{8,9},{9,8},{10,11... | collective-permute-start | bytes 196616 | tf_op jit(solution)/shard_map/ppermute | solution.py:399
  33.5 2.2 %collective-permute-done.10 = bf16[128,256]{1,0:T(8,128)(2,1)S(1)} collective-permute-done((bf16[128,256]{1,0:T(8,128)(2,1)S(1)}, bf16[128,256]{1,0:T(8,128)(2,1)S(1)}, u32[]{:S(2)}, u32[]{:S(2)}) %collective-permute-start.10) | collective-permute-done | bytes 65568 | tf_op jit(solution)/shard_map/ppermute | solution.py:399
  35.7 0.9 collective-permute-done.8
  36.6 2.0 %collective-permute-start.11 = (bf16[128,256]{1,0:T(8,128)(2,1)S(1)}, bf16[128,256]{1,0:T(8,128)(2,1)S(1)}, u32[]{:S(2)}, u32[]{:S(2)}) collective-permute-start(bf16[128,256]{1,0:T(8,128)(2,1)S(1)} %add_convert_fusion.3.refs_0_), channel_id=1, source_target_pairs={{0,4},{1,5},{2,6},{3,7},{4,0},{5,1},{6,2},{7,3},{8,12},{9,13},{10,... | collective-permute-start | bytes 196616 | tf_op jit(solution)/shard_map/ppermute | solution.py:399
  38.6 1.6 %turn.5 = (bf16[16,256,256]{2,1,0:T(8,128)(2,1)S(1)}, bf16[1,256,256]{2,1,0:T(8,128)(2,1)S(1)}) custom-call(bf16[128,256]{1,0:T(8,128)(2,1)S(1)} %get-tuple-element.72.after_ref, bf16[16,256,256]{2,1,0:T(8,128)(2,1)S(1)} %get-tuple-element.67.refs_2_.refs_10_.refs_0_, bf16[1,256,256]{2,1,0:T(8,128)(2,1)S(1)} %get-tuple-element.68.refs_3_.refs_11_.refs_1_), custom_call_target="tpu_custom_call" | custom-call | flops 72194456 | bytes 2293760 | tf_op jit(solution)/shard_map/turn/pallas_call | solution.py:360
  40.2 2.3 %collective-permute-done.11.refs_1_ = bf16[128,256]{1,0:T(8,128)(2,1)S(1)} collective-permute-done((bf16[128,256]{1,0:T(8,128)(2,1)S(1)}, bf16[128,256]{1,0:T(8,128)(2,1)S(1)}, u32[]{:S(2)}, u32[]{:S(2)}) %collective-permute-start.11) | collective-permute-done | bytes 65568 | tf_op jit(solution)/shard_map/ppermute | solution.py:399
  42.8 1.2 %collective-permute-start.13 = (f32[8,256]{1,0:T(8,128)S(1)}, f32[8,256]{1,0:T(8,128)S(1)}, u32[]{:S(2)}, u32[]{:S(2)}) collective-permute-start(f32[8,256]{1,0:T(8,128)S(1)} %get-tuple-element.76.refs_1_), channel_id=1, source_target_pairs={{0,16},{8,24},{16,0},{24,8},{1,17},{9,25},{17,1},{25,9},{2,18},{10... | collective-permute-start | bytes 24584 | tf_op jit(solution)/shard_map/ppermute | solution.py:404
  44.0 0.6 collective-permute-start.12
  44.7 2.0 %project.5.refs_0_ = f32[88,256]{1,0:T(8,128)S(1)} custom-call(f32[128,256]{1,0:T(8,128)S(1)} %get-tuple-element.73.field_ref.refs_13_, bf16[88,128]{1,0:T(8,128)(2,1)S(1)} %get-tuple-element.64.pick1_ref, bf16[88,128]{1,0:T(8,128)(2,1)S(1)} %get-tuple-element.65.pick2_ref, bf16[32,256,256]{2,1,0:T(8,128)(2,1)S(1)} %turn.3.refs_0_, ...), custom_call_target="tpu_custom_call" | custom-call | flops 339738624 | bytes 10792960 | tf_op jit(solution)/shard_map/project/pallas_call | solution.py:360
  46.7 1.9 %step.5 = (bf16[128,256]{1,0:T(8,128)(2,1)S(1)}, f32[88,256]{1,0:T(8,128)S(1)}, f32[128,256]{1,0:T(8,128)S(1)}, f32[128,256]{1,0:T(8,128)S(1)}, f32[88,256]{1,0:...) custom-call(f32[88,256]{1,0:T(8,128)S(1)} %project.5.refs_0_, ...), custom_call_target="tpu_custom_call" | custom-call | flops 339738624 | bytes 11304960 | tf_op jit(solution)/shard_map/step/pallas_call | solution.py:360
  48.6 1.1 %collective-permute-start.17 = (bf16[128,256]{1,0:T(8,128)(2,1)S(1)}, bf16[128,256]{1,0:T(8,128)(2,1)S(1)}, u32[]{:S(2)}, u32[]{:S(2)}) collective-permute-start(bf16[128,256]{1,0:T(8,128)(2,1)S(1)} %get-tuple-element.78), channel_id=1, source_target_pairs={{0,3},{1,2},{2,1},{3,0},{4,7},{5,6},{6,5},{7,4},{8,11},{9,10},{10,... | collective-permute-start | bytes 196616 | tf_op jit(solution)/shard_map/ppermute | solution.py:399
  49.7 1.6 %collective-permute-start.16 = (bf16[128,256]{1,0:T(8,128)(2,1)S(1)}, bf16[128,256]{1,0:T(8,128)(2,1)S(1)}, u32[]{:S(2)}, u32[]{:S(2)}) collective-permute-start(bf16[128,256]{1,0:T(8,128)(2,1)S(1)} %get-tuple-element.78), channel_id=1, source_target_pairs={{0,2},{1,3},{2,0},{3,1},{4,6},{5,7},{6,4},{7,5},{8,10},{9,11},{10,... | collective-permute-start | bytes 196616 | tf_op jit(solution)/shard_map/ppermute | solution.py:399
  51.3 0.9 collective-permute-start.15
  52.2 2.2 %collective-permute-done.17 = bf16[128,256]{1,0:T(8,128)(2,1)S(1)} collective-permute-done((bf16[128,256]{1,0:T(8,128)(2,1)S(1)}, bf16[128,256]{1,0:T(8,128)(2,1)S(1)}, u32[]{:S(2)}, u32[]{:S(2)}) %collective-permute-start.17) | collective-permute-done | bytes 65568 | tf_op jit(solution)/shard_map/ppermute | solution.py:399
  54.4 0.3 collective-permute-done.16
  54.7 0.9 collective-permute-done.15
  55.6 1.4 %collective-permute-start.18 = (bf16[128,256]{1,0:T(8,128)(2,1)S(1)}, bf16[128,256]{1,0:T(8,128)(2,1)S(1)}, u32[]{:S(2)}, u32[]{:S(2)}) collective-permute-start(bf16[128,256]{1,0:T(8,128)(2,1)S(1)} %add_convert_fusion.2.refs_0_), channel_id=1, source_target_pairs={{0,4},{1,5},{2,6},{3,7},{4,0},{5,1},{6,2},{7,3},{8,12},{9,13},{10,... | collective-permute-start | bytes 196616 | tf_op jit(solution)/shard_map/ppermute | solution.py:399
  57.0 4.4 %collective-permute-done.18.refs_1_ = bf16[128,256]{1,0:T(8,128)(2,1)S(1)} collective-permute-done((bf16[128,256]{1,0:T(8,128)(2,1)S(1)}, bf16[128,256]{1,0:T(8,128)(2,1)S(1)}, u32[]{:S(2)}, u32[]{:S(2)}) %collective-permute-start.18) | collective-permute-done | bytes 65568 | tf_op jit(solution)/shard_map/ppermute | solution.py:399
  61.7 0.8 collective-permute-start.20
  62.5 1.0 collective-permute-start.19
  63.6 2.0 %project.6.refs_0_ = f32[88,256]{1,0:T(8,128)S(1)} custom-call(f32[128,256]{1,0:T(8,128)S(1)} %get-tuple-element.80.field_ref.refs_13_, bf16[88,128]{1,0:T(8,128)(2,1)S(1)} %get-tuple-element.64.pick1_ref, bf16[88,128]{1,0:T(8,128)(2,1)S(1)} %get-tuple-element.65.pick2_ref, bf16[32,256,256]{2,1,0:T(8,128)(2,1)S(1)} %turn.3.refs_0_, ...), custom_call_target="tpu_custom_call" | custom-call | flops 339738624 | bytes 10792960 | tf_op jit(solution)/shard_map/project/pallas_call | solution.py:360
  65.6 1.9 %step.6 = (bf16[128,256]{1,0:T(8,128)(2,1)S(1)}, f32[88,256]{1,0:T(8,128)S(1)}, f32[128,256]{1,0:T(8,128)S(1)}, f32[128,256]{1,0:T(8,128)S(1)}, f32[88,256]{1,0:...) custom-call(f32[88,256]{1,0:T(8,128)S(1)} %project.6.refs_0_, ...), custom_call_target="tpu_custom_call" | custom-call | flops 339738624 | bytes 11546624 | tf_op jit(solution)/shard_map/step/pallas_call | solution.py:360
  67.5 0.3 collective-permute-start.24
  67.9 2.1 %collective-permute-start.23 = (bf16[128,256]{1,0:T(8,128)(2,1)S(1)}, bf16[128,256]{1,0:T(8,128)(2,1)S(1)}, u32[]{:S(2)}, u32[]{:S(2)}) collective-permute-start(bf16[128,256]{1,0:T(8,128)(2,1)S(1)} %get-tuple-element.88), channel_id=1, source_target_pairs={{0,2},{1,3},{2,0},{3,1},{4,6},{5,7},{6,4},{7,5},{8,10},{9,11},{10,... | collective-permute-start | bytes 196616 | tf_op jit(solution)/shard_map/ppermute | solution.py:399
  70.0 1.1 %collective-permute-start.22 = (bf16[128,256]{1,0:T(8,128)(2,1)S(1)}, bf16[128,256]{1,0:T(8,128)(2,1)S(1)}, u32[]{:S(2)}, u32[]{:S(2)}) collective-permute-start(bf16[128,256]{1,0:T(8,128)(2,1)S(1)} %get-tuple-element.88), channel_id=1, source_target_pairs={{0,1},{1,0},{2,3},{3,2},{4,5},{5,4},{6,7},{7,6},{8,9},{9,8},{10,11... | collective-permute-start | bytes 196616 | tf_op jit(solution)/shard_map/ppermute | solution.py:399
  71.1 2.2 %collective-permute-done.24 = bf16[128,256]{1,0:T(8,128)(2,1)S(1)} collective-permute-done((bf16[128,256]{1,0:T(8,128)(2,1)S(1)}, bf16[128,256]{1,0:T(8,128)(2,1)S(1)}, u32[]{:S(2)}, u32[]{:S(2)}) %collective-permute-start.24) | collective-permute-done | bytes 65568 | tf_op jit(solution)/shard_map/ppermute | solution.py:399
  73.3 0.9 collective-permute-done.22
  74.3 1.0 collective-permute-start.25
  75.2 4.4 %collective-permute-done.25.refs_1_ = bf16[128,256]{1,0:T(8,128)(2,1)S(1)} collective-permute-done((bf16[128,256]{1,0:T(8,128)(2,1)S(1)}, bf16[128,256]{1,0:T(8,128)(2,1)S(1)}, u32[]{:S(2)}, u32[]{:S(2)}) %collective-permute-start.25) | collective-permute-done | bytes 65568 | tf_op jit(solution)/shard_map/ppermute | solution.py:399
  79.9 1.1 %collective-permute-start.27 = (f32[8,256]{1,0:T(8,128)S(1)}, f32[8,256]{1,0:T(8,128)S(1)}, u32[]{:S(2)}, u32[]{:S(2)}) collective-permute-start(f32[8,256]{1,0:T(8,128)S(1)} %get-tuple-element.91.refs_1_), channel_id=1, source_target_pairs={{0,16},{8,24},{16,0},{24,8},{1,17},{9,25},{17,1},{25,9},{2,18},{10... | collective-permute-start | bytes 24584 | tf_op jit(solution)/shard_map/ppermute | solution.py:404
  81.0 0.7 collective-permute-start.26
  81.7 2.0 %project.7.refs_0_ = f32[88,256]{1,0:T(8,128)S(1)} custom-call(f32[128,256]{1,0:T(8,128)S(1)} %get-tuple-element.90.field_ref.refs_13_, bf16[88,128]{1,0:T(8,128)(2,1)S(1)} %get-tuple-element.64.pick1_ref, bf16[88,128]{1,0:T(8,128)(2,1)S(1)} %get-tuple-element.65.pick2_ref, bf16[32,256,256]{2,1,0:T(8,128)(2,1)S(1)} %turn.3.refs_0_, ...), custom_call_target="tpu_custom_call" | custom-call | flops 339738624 | bytes 10792960 | tf_op jit(solution)/shard_map/project/pallas_call | solution.py:360
  83.8 2.4 %step.7 = (bf16[128,256]{1,0:T(8,128)(2,1)S(1)}, f32[88,256]{1,0:T(8,128)}, f32[128,256]{1,0:T(8,128)S(1)}, f32[128,256]{1,0:T(8,128)S(1)}, f32[88,256]{1,0:T(8,...) custom-call(f32[88,256]{1,0:T(8,128)S(1)} %project.7.refs_0_, ...), custom_call_target="tpu_custom_call" | custom-call | flops 339738624 | bytes 11546624 | tf_op jit(solution)/shard_map/step/pallas_call | solution.py:360
  86.2 0.4 collective-permute-start.31
  86.6 2.2 %collective-permute-start.30 = (bf16[128,256]{1,0:T(8,128)(2,1)S(1)}, bf16[128,256]{1,0:T(8,128)(2,1)S(1)}, u32[]{:S(2)}, u32[]{:S(2)}) collective-permute-start(bf16[128,256]{1,0:T(8,128)(2,1)S(1)} %get-tuple-element.98), channel_id=1, source_target_pairs={{0,2},{1,3},{2,0},{3,1},{4,6},{5,7},{6,4},{7,5},{8,10},{9,11},{10,... | collective-permute-start | bytes 196616 | tf_op jit(solution)/shard_map/ppermute | solution.py:399
  88.8 0.9 collective-permute-start.29
  89.7 2.2 %collective-permute-done.31 = bf16[128,256]{1,0:T(8,128)(2,1)S(1)} collective-permute-done((bf16[128,256]{1,0:T(8,128)(2,1)S(1)}, bf16[128,256]{1,0:T(8,128)(2,1)S(1)}, u32[]{:S(2)}, u32[]{:S(2)}) %collective-permute-start.31) | collective-permute-done | bytes 65568 | tf_op jit(solution)/shard_map/ppermute | solution.py:399
  91.9 0.3 collective-permute-done.30
  92.1 0.9 collective-permute-done.29
  93.1 1.0 collective-permute-start.32
  94.0 4.4 %collective-permute-done.32.refs_1_ = bf16[128,256]{1,0:T(8,128)(2,1)S(1)} collective-permute-done((bf16[128,256]{1,0:T(8,128)(2,1)S(1)}, bf16[128,256]{1,0:T(8,128)(2,1)S(1)}, u32[]{:S(2)}, u32[]{:S(2)}) %collective-permute-start.32) | collective-permute-done | bytes 65568 | tf_op jit(solution)/shard_map/ppermute | solution.py:399
  98.7 1.1 %collective-permute-start.34 = (f32[8,256]{1,0:T(8,128)S(1)}, f32[8,256]{1,0:T(8,128)S(1)}, u32[]{:S(2)}, u32[]{:S(2)}) collective-permute-start(f32[8,256]{1,0:T(8,128)S(1)} %get-tuple-element.101.refs_1_), channel_id=1, source_target_pairs={{0,16},{8,24},{16,0},{24,8},{1,17},{9,25},{17,1},{25,9},{2,18},{10... | collective-permute-start | bytes 24584 | tf_op jit(solution)/shard_map/ppermute | solution.py:404
  99.8 0.7 collective-permute-start.33
  100.6 1.2 %collective-permute-done.35.refs_4_ = f32[8,256]{1,0:T(8,128)S(1)} collective-permute-done((f32[8,256]{1,0:T(8,128)S(1)}, f32[8,256]{1,0:T(8,128)S(1)}, u32[]{:S(2)}, u32[]{:S(2)}) %collective-permute-start.35) | collective-permute-done | bytes 8224 | tf_op jit(solution)/shard_map/ppermute | solution.py:404
  101.8 0.7 collective-permute-done.34.refs_3_
  102.4 0.6 final.1
  (34 shorter events, 1.5 us)
Async XLA Ops:
  1.6 6.1 %collective-permute-start = (bf16[1,272,256]{2,1,0:T(8,128)(2,1)S(1)}, bf16[1,272,256]{2,1,0:T(8,128)(2,1)S(1)}, u32[]{:S(2)}, u32[]{:S(2)}) collective-permute-start(bf16[1,272,256]{2,1,0:T(8,128)(2,1)S(1)} %pack.1), channel_id=1, source_target_pairs={{0,8},{8,16},{16,24},{24,0},{1,9},{9,17},{17,25},{25,1},{2,10},{10... | collective-permute-start | bytes 417800 | tf_op jit(solution)/shard_map/ppermute | solution.py:430
  8.1 7.1 %collective-permute-start.3 = (bf16[128,256]{1,0:T(8,128)(2,1)S(1)}, bf16[128,256]{1,0:T(8,128)(2,1)S(1)}, u32[]{:S(2)}, u32[]{:S(2)}) collective-permute-start(bf16[128,256]{1,0:T(8,128)(2,1)S(1)} %get-tuple-element.60.after_ref), channel_id=1, source_target_pairs={{0,3},{1,2},{2,1},{3,0},{4,7},{5,6},{6,5},{7,4},{8,11},{9,10},{10,... | collective-permute-start | bytes 196616 | tf_op jit(solution)/shard_map/ppermute | solution.py:399
  11.7 4.6 %collective-permute-start.2 = (bf16[128,256]{1,0:T(8,128)(2,1)S(1)}, bf16[128,256]{1,0:T(8,128)(2,1)S(1)}, u32[]{:S(2)}, u32[]{:S(2)}) collective-permute-start(bf16[128,256]{1,0:T(8,128)(2,1)S(1)} %get-tuple-element.60.after_ref), channel_id=1, source_target_pairs={{0,2},{1,3},{2,0},{3,1},{4,6},{5,7},{6,4},{7,5},{8,10},{9,11},{10,... | collective-permute-start | bytes 196616 | tf_op jit(solution)/shard_map/ppermute | solution.py:399
  12.1 4.9 %collective-permute-start.1 = (bf16[128,256]{1,0:T(8,128)(2,1)S(1)}, bf16[128,256]{1,0:T(8,128)(2,1)S(1)}, u32[]{:S(2)}, u32[]{:S(2)}) collective-permute-start(bf16[128,256]{1,0:T(8,128)(2,1)S(1)} %get-tuple-element.60.after_ref), channel_id=1, source_target_pairs={{0,1},{1,0},{2,3},{3,2},{4,5},{5,4},{6,7},{7,6},{8,9},{9,8},{10,11... | collective-permute-start | bytes 196616 | tf_op jit(solution)/shard_map/ppermute | solution.py:399
  17.1 6.6 %collective-permute-start.4 = (bf16[128,256]{1,0:T(8,128)(2,1)S(1)}, bf16[128,256]{1,0:T(8,128)(2,1)S(1)}, u32[]{:S(2)}, u32[]{:S(2)}) collective-permute-start(bf16[128,256]{1,0:T(8,128)(2,1)S(1)} %add_convert_fusion.4.refs_0_.after_ref), channel_id=1, source_target_pairs={{0,4},{1,5},{2,6},{3,7},{4,0},{5,1},{6,2},{7,3},{8,12},{9,13},{10,... | collective-permute-start | bytes 196616 | tf_op jit(solution)/shard_map/ppermute | solution.py:399
  23.7 4.2 %collective-permute-start.7 = (f32[8,256]{1,0:T(8,128)S(1)}, f32[8,256]{1,0:T(8,128)S(1)}, u32[]{:S(2)}, u32[]{:S(2)}) collective-permute-start(f32[8,256]{1,0:T(8,128)S(1)} %get-tuple-element.69.refs_1_), channel_id=1, source_target_pairs={{0,24},{8,16},{16,8},{24,0},{1,25},{9,17},{17,9},{25,1},{2,26},{10... | collective-permute-start | bytes 24584 | tf_op jit(solution)/shard_map/ppermute | solution.py:404
  23.8 4.2 %collective-permute-start.6 = (f32[8,256]{1,0:T(8,128)S(1)}, f32[8,256]{1,0:T(8,128)S(1)}, u32[]{:S(2)}, u32[]{:S(2)}) collective-permute-start(f32[8,256]{1,0:T(8,128)S(1)} %get-tuple-element.69.refs_1_), channel_id=1, source_target_pairs={{0,16},{8,24},{16,0},{24,8},{1,17},{9,25},{17,1},{25,9},{2,18},{10... | collective-permute-start | bytes 24584 | tf_op jit(solution)/shard_map/ppermute | solution.py:404
  24.1 3.9 %collective-permute-start.5 = (f32[8,256]{1,0:T(8,128)S(1)}, f32[8,256]{1,0:T(8,128)S(1)}, u32[]{:S(2)}, u32[]{:S(2)}) collective-permute-start(f32[8,256]{1,0:T(8,128)S(1)} %get-tuple-element.69.refs_1_), channel_id=1, source_target_pairs={{0,8},{8,0},{16,24},{24,16},{1,9},{9,1},{17,25},{25,17},{2,10},{10... | collective-permute-start | bytes 24584 | tf_op jit(solution)/shard_map/ppermute | solution.py:404
  29.9 5.8 %collective-permute-start.10 = (bf16[128,256]{1,0:T(8,128)(2,1)S(1)}, bf16[128,256]{1,0:T(8,128)(2,1)S(1)}, u32[]{:S(2)}, u32[]{:S(2)}) collective-permute-start(bf16[128,256]{1,0:T(8,128)(2,1)S(1)} %get-tuple-element.72.after_ref), channel_id=1, source_target_pairs={{0,3},{1,2},{2,1},{3,0},{4,7},{5,6},{6,5},{7,4},{8,11},{9,10},{10,... | collective-permute-start | bytes 196616 | tf_op jit(solution)/shard_map/ppermute | solution.py:399
  30.9 4.8 %collective-permute-start.9 = (bf16[128,256]{1,0:T(8,128)(2,1)S(1)}, bf16[128,256]{1,0:T(8,128)(2,1)S(1)}, u32[]{:S(2)}, u32[]{:S(2)}) collective-permute-start(bf16[128,256]{1,0:T(8,128)(2,1)S(1)} %get-tuple-element.72.after_ref), channel_id=1, source_target_pairs={{0,2},{1,3},{2,0},{3,1},{4,6},{5,7},{6,4},{7,5},{8,10},{9,11},{10,... | collective-permute-start | bytes 196616 | tf_op jit(solution)/shard_map/ppermute | solution.py:399
  32.3 4.3 %collective-permute-start.8 = (bf16[128,256]{1,0:T(8,128)(2,1)S(1)}, bf16[128,256]{1,0:T(8,128)(2,1)S(1)}, u32[]{:S(2)}, u32[]{:S(2)}) collective-permute-start(bf16[128,256]{1,0:T(8,128)(2,1)S(1)} %get-tuple-element.72.after_ref), channel_id=1, source_target_pairs={{0,1},{1,0},{2,3},{3,2},{4,5},{5,4},{6,7},{7,6},{8,9},{9,8},{10,11... | collective-permute-start | bytes 196616 | tf_op jit(solution)/shard_map/ppermute | solution.py:399
  36.6 5.9 %collective-permute-start.11 = (bf16[128,256]{1,0:T(8,128)(2,1)S(1)}, bf16[128,256]{1,0:T(8,128)(2,1)S(1)}, u32[]{:S(2)}, u32[]{:S(2)}) collective-permute-start(bf16[128,256]{1,0:T(8,128)(2,1)S(1)} %add_convert_fusion.3.refs_0_), channel_id=1, source_target_pairs={{0,4},{1,5},{2,6},{3,7},{4,0},{5,1},{6,2},{7,3},{8,12},{9,13},{10,... | collective-permute-start | bytes 196616 | tf_op jit(solution)/shard_map/ppermute | solution.py:399
  42.7 4.0 %collective-permute-start.14 = (f32[8,256]{1,0:T(8,128)S(1)}, f32[8,256]{1,0:T(8,128)S(1)}, u32[]{:S(2)}, u32[]{:S(2)}) collective-permute-start(f32[8,256]{1,0:T(8,128)S(1)} %get-tuple-element.76.refs_1_), channel_id=1, source_target_pairs={{0,24},{8,16},{16,8},{24,0},{1,25},{9,17},{17,9},{25,1},{2,26},{10... | collective-permute-start | bytes 24584 | tf_op jit(solution)/shard_map/ppermute | solution.py:404
  42.8 3.9 %collective-permute-start.13 = (f32[8,256]{1,0:T(8,128)S(1)}, f32[8,256]{1,0:T(8,128)S(1)}, u32[]{:S(2)}, u32[]{:S(2)}) collective-permute-start(f32[8,256]{1,0:T(8,128)S(1)} %get-tuple-element.76.refs_1_), channel_id=1, source_target_pairs={{0,16},{8,24},{16,0},{24,8},{1,17},{9,25},{17,1},{25,9},{2,18},{10... | collective-permute-start | bytes 24584 | tf_op jit(solution)/shard_map/ppermute | solution.py:404
  44.0 2.7 %collective-permute-start.12 = (f32[8,256]{1,0:T(8,128)S(1)}, f32[8,256]{1,0:T(8,128)S(1)}, u32[]{:S(2)}, u32[]{:S(2)}) collective-permute-start(f32[8,256]{1,0:T(8,128)S(1)} %get-tuple-element.76.refs_1_), channel_id=1, source_target_pairs={{0,8},{8,0},{16,24},{24,16},{1,9},{9,1},{17,25},{25,17},{2,10},{10... | collective-permute-start | bytes 24584 | tf_op jit(solution)/shard_map/ppermute | solution.py:404
  48.6 5.8 %collective-permute-start.17 = (bf16[128,256]{1,0:T(8,128)(2,1)S(1)}, bf16[128,256]{1,0:T(8,128)(2,1)S(1)}, u32[]{:S(2)}, u32[]{:S(2)}) collective-permute-start(bf16[128,256]{1,0:T(8,128)(2,1)S(1)} %get-tuple-element.78), channel_id=1, source_target_pairs={{0,3},{1,2},{2,1},{3,0},{4,7},{5,6},{6,5},{7,4},{8,11},{9,10},{10,... | collective-permute-start | bytes 196616 | tf_op jit(solution)/shard_map/ppermute | solution.py:399
  49.7 5.0 %collective-permute-start.16 = (bf16[128,256]{1,0:T(8,128)(2,1)S(1)}, bf16[128,256]{1,0:T(8,128)(2,1)S(1)}, u32[]{:S(2)}, u32[]{:S(2)}) collective-permute-start(bf16[128,256]{1,0:T(8,128)(2,1)S(1)} %get-tuple-element.78), channel_id=1, source_target_pairs={{0,2},{1,3},{2,0},{3,1},{4,6},{5,7},{6,4},{7,5},{8,10},{9,11},{10,... | collective-permute-start | bytes 196616 | tf_op jit(solution)/shard_map/ppermute | solution.py:399
  51.3 4.3 %collective-permute-start.15 = (bf16[128,256]{1,0:T(8,128)(2,1)S(1)}, bf16[128,256]{1,0:T(8,128)(2,1)S(1)}, u32[]{:S(2)}, u32[]{:S(2)}) collective-permute-start(bf16[128,256]{1,0:T(8,128)(2,1)S(1)} %get-tuple-element.78), channel_id=1, source_target_pairs={{0,1},{1,0},{2,3},{3,2},{4,5},{5,4},{6,7},{7,6},{8,9},{9,8},{10,11... | collective-permute-start | bytes 196616 | tf_op jit(solution)/shard_map/ppermute | solution.py:399
  55.6 5.8 %collective-permute-start.18 = (bf16[128,256]{1,0:T(8,128)(2,1)S(1)}, bf16[128,256]{1,0:T(8,128)(2,1)S(1)}, u32[]{:S(2)}, u32[]{:S(2)}) collective-permute-start(bf16[128,256]{1,0:T(8,128)(2,1)S(1)} %add_convert_fusion.2.refs_0_), channel_id=1, source_target_pairs={{0,4},{1,5},{2,6},{3,7},{4,0},{5,1},{6,2},{7,3},{8,12},{9,13},{10,... | collective-permute-start | bytes 196616 | tf_op jit(solution)/shard_map/ppermute | solution.py:399
  61.6 4.0 %collective-permute-start.21 = (f32[8,256]{1,0:T(8,128)S(1)}, f32[8,256]{1,0:T(8,128)S(1)}, u32[]{:S(2)}, u32[]{:S(2)}) collective-permute-start(f32[8,256]{1,0:T(8,128)S(1)} %get-tuple-element.81.refs_1_), channel_id=1, source_target_pairs={{0,24},{8,16},{16,8},{24,0},{1,25},{9,17},{17,9},{25,1},{2,26},{10... | collective-permute-start | bytes 24584 | tf_op jit(solution)/shard_map/ppermute | solution.py:404
  61.7 3.9 %collective-permute-start.20 = (f32[8,256]{1,0:T(8,128)S(1)}, f32[8,256]{1,0:T(8,128)S(1)}, u32[]{:S(2)}, u32[]{:S(2)}) collective-permute-start(f32[8,256]{1,0:T(8,128)S(1)} %get-tuple-element.81.refs_1_), channel_id=1, source_target_pairs={{0,16},{8,24},{16,0},{24,8},{1,17},{9,25},{17,1},{25,9},{2,18},{10... | collective-permute-start | bytes 24584 | tf_op jit(solution)/shard_map/ppermute | solution.py:404
  62.5 3.1 %collective-permute-start.19 = (f32[8,256]{1,0:T(8,128)S(1)}, f32[8,256]{1,0:T(8,128)S(1)}, u32[]{:S(2)}, u32[]{:S(2)}) collective-permute-start(f32[8,256]{1,0:T(8,128)S(1)} %get-tuple-element.81.refs_1_), channel_id=1, source_target_pairs={{0,8},{8,0},{16,24},{24,16},{1,9},{9,1},{17,25},{25,17},{2,10},{10... | collective-permute-start | bytes 24584 | tf_op jit(solution)/shard_map/ppermute | solution.py:404
  67.5 5.8 %collective-permute-start.24 = (bf16[128,256]{1,0:T(8,128)(2,1)S(1)}, bf16[128,256]{1,0:T(8,128)(2,1)S(1)}, u32[]{:S(2)}, u32[]{:S(2)}) collective-permute-start(bf16[128,256]{1,0:T(8,128)(2,1)S(1)} %get-tuple-element.88), channel_id=1, source_target_pairs={{0,3},{1,2},{2,1},{3,0},{4,7},{5,6},{6,5},{7,4},{8,11},{9,10},{10,... | collective-permute-start | bytes 196616 | tf_op jit(solution)/shard_map/ppermute | solution.py:399
  67.9 5.5 %collective-permute-start.23 = (bf16[128,256]{1,0:T(8,128)(2,1)S(1)}, bf16[128,256]{1,0:T(8,128)(2,1)S(1)}, u32[]{:S(2)}, u32[]{:S(2)}) collective-permute-start(bf16[128,256]{1,0:T(8,128)(2,1)S(1)} %get-tuple-element.88), channel_id=1, source_target_pairs={{0,2},{1,3},{2,0},{3,1},{4,6},{5,7},{6,4},{7,5},{8,10},{9,11},{10,... | collective-permute-start | bytes 196616 | tf_op jit(solution)/shard_map/ppermute | solution.py:399
  70.0 4.3 %collective-permute-start.22 = (bf16[128,256]{1,0:T(8,128)(2,1)S(1)}, bf16[128,256]{1,0:T(8,128)(2,1)S(1)}, u32[]{:S(2)}, u32[]{:S(2)}) collective-permute-start(bf16[128,256]{1,0:T(8,128)(2,1)S(1)} %get-tuple-element.88), channel_id=1, source_target_pairs={{0,1},{1,0},{2,3},{3,2},{4,5},{5,4},{6,7},{7,6},{8,9},{9,8},{10,11... | collective-permute-start | bytes 196616 | tf_op jit(solution)/shard_map/ppermute | solution.py:399
  74.3 5.4 %collective-permute-start.25 = (bf16[128,256]{1,0:T(8,128)(2,1)S(1)}, bf16[128,256]{1,0:T(8,128)(2,1)S(1)}, u32[]{:S(2)}, u32[]{:S(2)}) collective-permute-start(bf16[128,256]{1,0:T(8,128)(2,1)S(1)} %add_convert_fusion.1.refs_0_), channel_id=1, source_target_pairs={{0,4},{1,5},{2,6},{3,7},{4,0},{5,1},{6,2},{7,3},{8,12},{9,13},{10,... | collective-permute-start | bytes 196616 | tf_op jit(solution)/shard_map/ppermute | solution.py:399
  79.8 4.0 %collective-permute-start.28 = (f32[8,256]{1,0:T(8,128)S(1)}, f32[8,256]{1,0:T(8,128)S(1)}, u32[]{:S(2)}, u32[]{:S(2)}) collective-permute-start(f32[8,256]{1,0:T(8,128)S(1)} %get-tuple-element.91.refs_1_), channel_id=1, source_target_pairs={{0,24},{8,16},{16,8},{24,0},{1,25},{9,17},{17,9},{25,1},{2,26},{10... | collective-permute-start | bytes 24584 | tf_op jit(solution)/shard_map/ppermute | solution.py:404
  79.9 3.9 %collective-permute-start.27 = (f32[8,256]{1,0:T(8,128)S(1)}, f32[8,256]{1,0:T(8,128)S(1)}, u32[]{:S(2)}, u32[]{:S(2)}) collective-permute-start(f32[8,256]{1,0:T(8,128)S(1)} %get-tuple-element.91.refs_1_), channel_id=1, source_target_pairs={{0,16},{8,24},{16,0},{24,8},{1,17},{9,25},{17,1},{25,9},{2,18},{10... | collective-permute-start | bytes 24584 | tf_op jit(solution)/shard_map/ppermute | solution.py:404
  81.0 2.8 %collective-permute-start.26 = (f32[8,256]{1,0:T(8,128)S(1)}, f32[8,256]{1,0:T(8,128)S(1)}, u32[]{:S(2)}, u32[]{:S(2)}) collective-permute-start(f32[8,256]{1,0:T(8,128)S(1)} %get-tuple-element.91.refs_1_), channel_id=1, source_target_pairs={{0,8},{8,0},{16,24},{24,16},{1,9},{9,1},{17,25},{25,17},{2,10},{10... | collective-permute-start | bytes 24584 | tf_op jit(solution)/shard_map/ppermute | solution.py:404
  86.2 5.7 %collective-permute-start.31 = (bf16[128,256]{1,0:T(8,128)(2,1)S(1)}, bf16[128,256]{1,0:T(8,128)(2,1)S(1)}, u32[]{:S(2)}, u32[]{:S(2)}) collective-permute-start(bf16[128,256]{1,0:T(8,128)(2,1)S(1)} %get-tuple-element.98), channel_id=1, source_target_pairs={{0,3},{1,2},{2,1},{3,0},{4,7},{5,6},{6,5},{7,4},{8,11},{9,10},{10,... | collective-permute-start | bytes 196616 | tf_op jit(solution)/shard_map/ppermute | solution.py:399
  86.6 5.5 %collective-permute-start.30 = (bf16[128,256]{1,0:T(8,128)(2,1)S(1)}, bf16[128,256]{1,0:T(8,128)(2,1)S(1)}, u32[]{:S(2)}, u32[]{:S(2)}) collective-permute-start(bf16[128,256]{1,0:T(8,128)(2,1)S(1)} %get-tuple-element.98), channel_id=1, source_target_pairs={{0,2},{1,3},{2,0},{3,1},{4,6},{5,7},{6,4},{7,5},{8,10},{9,11},{10,... | collective-permute-start | bytes 196616 | tf_op jit(solution)/shard_map/ppermute | solution.py:399
  88.8 4.3 %collective-permute-start.29 = (bf16[128,256]{1,0:T(8,128)(2,1)S(1)}, bf16[128,256]{1,0:T(8,128)(2,1)S(1)}, u32[]{:S(2)}, u32[]{:S(2)}) collective-permute-start(bf16[128,256]{1,0:T(8,128)(2,1)S(1)} %get-tuple-element.98), channel_id=1, source_target_pairs={{0,1},{1,0},{2,3},{3,2},{4,5},{5,4},{6,7},{7,6},{8,9},{9,8},{10,11... | collective-permute-start | bytes 196616 | tf_op jit(solution)/shard_map/ppermute | solution.py:399
  93.1 5.4 %collective-permute-start.32 = (bf16[128,256]{1,0:T(8,128)(2,1)S(1)}, bf16[128,256]{1,0:T(8,128)(2,1)S(1)}, u32[]{:S(2)}, u32[]{:S(2)}) collective-permute-start(bf16[128,256]{1,0:T(8,128)(2,1)S(1)} %add_convert_fusion.refs_0_), channel_id=1, source_target_pairs={{0,4},{1,5},{2,6},{3,7},{4,0},{5,1},{6,2},{7,3},{8,12},{9,13},{10,... | collective-permute-start | bytes 196616 | tf_op jit(solution)/shard_map/ppermute | solution.py:399
  98.6 3.1 %collective-permute-start.35 = (f32[8,256]{1,0:T(8,128)S(1)}, f32[8,256]{1,0:T(8,128)S(1)}, u32[]{:S(2)}, u32[]{:S(2)}) collective-permute-start(f32[8,256]{1,0:T(8,128)S(1)} %get-tuple-element.101.refs_1_), channel_id=1, source_target_pairs={{0,24},{8,16},{16,8},{24,0},{1,25},{9,17},{17,9},{25,1},{2,26},{10... | collective-permute-start | bytes 24584 | tf_op jit(solution)/shard_map/ppermute | solution.py:404
  98.7 3.7 %collective-permute-start.34 = (f32[8,256]{1,0:T(8,128)S(1)}, f32[8,256]{1,0:T(8,128)S(1)}, u32[]{:S(2)}, u32[]{:S(2)}) collective-permute-start(f32[8,256]{1,0:T(8,128)S(1)} %get-tuple-element.101.refs_1_), channel_id=1, source_target_pairs={{0,16},{8,24},{16,0},{24,8},{1,17},{9,25},{17,1},{25,9},{2,18},{10... | collective-permute-start | bytes 24584 | tf_op jit(solution)/shard_map/ppermute | solution.py:404
  99.8 2.6 %collective-permute-start.33 = (f32[8,256]{1,0:T(8,128)S(1)}, f32[8,256]{1,0:T(8,128)S(1)}, u32[]{:S(2)}, u32[]{:S(2)}) collective-permute-start(f32[8,256]{1,0:T(8,128)S(1)} %get-tuple-element.101.refs_1_), channel_id=1, source_target_pairs={{0,8},{8,0},{16,24},{24,16},{1,9},{9,1},{17,25},{25,17},{2,10},{10... | collective-permute-start | bytes 24584 | tf_op jit(solution)/shard_map/ppermute | solution.py:404

commit v6 on v5

--- a/solution.py
+++ b/solution.py
@@ -35,17 +35,26 @@
         blocks = ref.shape[0]
         for at in range(0, blocks, OCTET):
             body(number, ref, at, slot + at, min(OCTET, blocks - at))
-        slot += -(-blocks // OCTET) * OCTET
-
-
-def project_kernel(turned, field_ref, pick1_ref, pick2_ref, *refs):
+        slot += padded(blocks)
+
+
+def padded(blocks):
+    return -(-blocks // OCTET) * OCTET
+
+
+def project_kernel(turned, starts, field_ref, pick1_ref, pick2_ref, *refs):
     *jac_refs, out_ref, l1_ref, l2_ref = refs
     product = [dot if is_turned else dot_t for is_turned in turned]
     ties = out_ref.shape[1] // 2
     high, low = halves(field_ref[...])
-    for pick_ref, left_ref in ((pick1_ref, l1_ref), (pick2_ref, l2_ref)):
-        left_ref[0] = dot(pick_ref[...], high)
-        left_ref[1] = dot(pick_ref[...], low)
+    to = 0
+    for ref, start in zip(jac_refs, starts):
+        count = padded(ref.shape[0])
+        for pick_ref, left_ref in ((pick1_ref, l1_ref), (pick2_ref, l2_ref)):
+            pick = pick_ref[start : start + count]
+            left_ref[0, to : to + count] = dot(pick, high)
+            left_ref[1, to : to + count] = dot(pick, low)
+        to += count
 
     def body(number, ref, at, slot, count):
         rows = pl.ds(slot, OCTET)
@@ -289,10 +298,10 @@
     return jnp.concatenate([x, x], axis=1)
 
 
-def step_kernel(step, scenes, *refs):
+def step_kernel(step, scenes, places, *refs):
     refs = list(refs)
     take = lambda n: [refs.pop(0) for _ in range(n)]
-    (part_ref,) = take(1)
+    part_refs = take(2)
     packet_refs = take(4)
     coef_ref, put1_ref, put2_ref, damp_ref, cjac_ref, ajac_ref, ejac_ref = take(7)
     (res_ref,) = take(1)
@@ -308,7 +317,11 @@
     first = pl.multiple_of(lax.axis_index("group") * scenes, scenes)
     own = pl.ds(first, scenes)
 
-    part_scr[...] = part_ref[...]
+    for part_ref, pieces in zip(part_refs, places):
+        at = 0
+        for start, count in pieces:
+            part_scr[start : start + count] = part_ref[at : at + count]
+            at += count
     outside(packet_refs, ajac_ref, ejac_ref, part_scr, cjac_ref.shape[0])
     if step == 0:
         out_obs_ref[...] = part_scr[...]
@@ -399,9 +412,8 @@
     return lax.ppermute(block, axis, [(i, i ^ mask) for i in range(lax.axis_size(axis))])
 
 
-def orbit_packets(packet):
-    n = lax.axis_size("orbit")
-    return [packet] + [lax.ppermute(packet, "orbit", [(i, i ^ mask) for i in range(n)]) for mask in range(1, n)]
+def far_packets(packet):
+    return swap(packet, "orbit", 1), swap(packet, "orbit", 3)
 
 
 def on_device(
@@ -484,16 +496,36 @@
         share = work * sum(o[0][0] for o in outs) // blocks
         return call(functools.partial(turn_kernel, start), outs, [], "turn", (after,) + refs, share)
 
-    def project(field, turned, refs):
-        scratch = [((2, slots, width), F32)] * 2
-        kernel = functools.partial(project_kernel, turned)
-        return call(kernel, [(pair, F32)], scratch, "project", (field, pick1, pick2) + tuple(refs), work)[0]
+    half = links // 2
+    places = (((0, half), (links, scenes)), ((half, links - half), (blocks, OCTET)))
+
+    def project(field, pieces, turned, refs):
+        count = sum(n for _, n in pieces)
+        kernel = functools.partial(project_kernel, turned, [at for at, _ in pieces])
+        return call(
+            kernel,
+            [((count, 2 * ties), F32)],
+            [((2, count, width), F32)] * 2,
+            "project",
+            (field, pick1, pick2) + tuple(refs),
+            work * count // blocks,
+        )[0]
+
+    def meet(field, packet, turned, refs):
+        near, far = far_packets(packet)
+        parts = []
+        if refs is not None:
+            parts.append(project(field, places[0], turned[0::2], refs[0::2]))
+            far, parts[0] = lax.optimization_barrier((far, parts[0]))
+        opposite = swap(far, "orbit", 1)
+        if refs is not None:
+            parts.append(project(field, places[1], turned[1::2], refs[1::2]))
+        return parts, (packet, near, opposite, far)
 
     def finish(sums, res=None):
         args = sums if res is None else sums + [res]
         kernel = functools.partial(gather_kernel, scenes, res is None, len(sums))
-        field, packet = call(kernel, [(full, F32), ((OCTET, width), F32)], [], "finish", args)
-        return field, orbit_packets(packet)
+        return call(kernel, [(full, F32), ((OCTET, width), F32)], [], "finish", args)
 
     sent, coef, ejac = call(
         rhs_kernel,
@@ -504,41 +536,41 @@
         work // blocks,
     )
     jacs = (cjac, ajac, ejac)
-    half = links // 2
     turned = []
 
     def more(after, done):
         turned.extend([*done, *turn(half, links - half, (cjac,), after)])
 
     sums = group_sum_but_last(sent, turn(0, half, (cjac,), sent), more)
-    res, packets = finish(sums)
-    part = project(res, (True, True, False, False), turned + [ajac, ejac])
+    res, packet = finish(sums)
+    parts, packets = meet(res, packet, (True, True, False, False), turned + [ajac, ejac])
     fixed = (coef, put1, put2, damp) + jacs
     scratch = [(pair, F32), (tie, F32), (tie, F32)] + term_space + [(full, F32)]
     sent, obs = call(
-        functools.partial(step_kernel, 0, scenes),
+        functools.partial(step_kernel, 0, scenes, places),
         [(full, BF16), (pair, F32)],
         scratch,
         "step",
-        (part, *packets) + fixed + (res,),
+        (*parts, *packets) + fixed + (res,),
         work,
     )
     turned += turn(0, scenes, (ajac, ejac), sent)
     state = ()
     x = jnp.zeros(own, F32)
     for step in range(1, ITERS):
-        field, packets = finish(group_sum_but_last(sent), res)
-        part = project(field, (True,) * 4, turned)
+        field, packet = finish(group_sum_but_last(sent), res)
+        parts, packets = meet(field, packet, (True,) * 4, turned)
         sent, obs, res, image, shadow, direction, x, scal = call(
-            functools.partial(step_kernel, step, scenes),
+            functools.partial(step_kernel, step, scenes, places),
             [(full, BF16), (pair, F32), (full, F32), (full, F32), (pair, F32), (own, F32), (own, F32), ((OCTET, width // 2), F32)],
             scratch,
             "step",
-            (part, *packets) + fixed + (res, field, obs, x) + state,
+            (*parts, *packets) + fixed + (res, field, obs, x) + state,
             work,
         )
         state = (image, shadow, direction, scal)
-    field, packets = finish(group_sum_but_last(sent), res)
+    field, packet = finish(group_sum_but_last(sent), res)
+    _, packets = meet(field, packet, None, None)
     x, res = call(
         functools.partial(final_kernel, ITERS - 1, scenes),
         [(own, F32), (own, F32)],

time: 103 us -> 106 us (1.029)
  waiting for transfers between devices: 33.5 us -> 39.1 us
  starting transfers between devices: 36.5 us -> 32.9 us
    ppermute x15 -> x0, starting transfers between devices: 9.59 us -> none  [orbit_packets(): lax.ppermute(packet, 'orbit', [(i, i ^ mask) for i in range(n)])]
    ppermute x20 -> x35, waiting for transfers between devices: 31.6 us -> 39.1 us  [swap(): lax.ppermute(block, axis, [(i, i ^ mask) for i in range(lax.axis_size(axi...]
    ppermute x20 -> x35, starting transfers between devices: 26.4 us -> 32.4 us  [swap(): lax.ppermute(block, axis, [(i, i ^ mask) for i in range(lax.axis_size(axi...]
    ppermute x15 -> x0, waiting for transfers between devices: 1.92 us -> none  [orbit_packets(): lax.ppermute(packet, 'orbit', [(i, i ^ mask) for i in range(n)])]
    pallas_call x20 -> x24, Pallas kernels: 32 us -> 32.8 us  [call(): pl.pallas_call(kernel, out_shape=[jax.ShapeDtypeStruct(*o) for o in outs]...]
  transfers between devices with their start and end apart: 36 -> 36, of which waited for: 19 -> 23; matrix products, arithmetic and copies ran while one was open for 0% -> 0% of each run, Pallas kernels for 21% -> 21%
where the time goes in v6:
time: 106 us
  waiting for transfers between devices  39.1 us (37%)
  starting transfers between devices  32.9 us (31%)
  Pallas kernels  32.8 us (31%)
    ppermute x35, waiting for transfers between devices, swap(): lax.ppermute(block, axis, [(i, i ^ mask) for i in range(lax.axis_size(axi...  39.1 us
    pallas_call x24, Pallas kernels, call(): pl.pallas_call(kernel, out_shape=[jax.ShapeDtypeStruct(*o) for o in outs]...  32.8 us
    ppermute x35, starting transfers between devices, swap(): lax.ppermute(block, axis, [(i, i ^ mask) for i in range(lax.axis_size(axi...  32.4 us
  transfers between devices with their start and end apart: 36, of which 23 were waited for; matrix products, arithmetic and copies ran while one was open for 0% of the time, Pallas kernels for 21%

profile of v6, /device:TPU:0, one launch (start us, length us, event | category | flops | bytes accessed | tf_op | source)
XLA Modules:
  0.0 105.9 jit_solution(14153806379438524557)
XLA Ops:
  0.6 0.9 pack.1
  1.6 0.5 collective-permute-start
  2.1 5.5 %setup.1 = (bf16[64,256,256]{2,1,0:T(8,128)(2,1)S(1)}, bf16[16,256,256]{2,1,0:T(8,128)(2,1)S(1)}, f32[3,80,128]{2,1,0:T(8,128)S(1)}, bf16[128,88]{1,0:T(8,128)(2...) custom-call(bf16[64,256,256]{2,1,0:T(8,128)(2,1)} %bitcast.9, ...), custom_call_target="tpu_custom_call" | custom-call | flops 339738624 | bytes 10650496 | tf_op jit(solution)/shard_map/setup/pallas_call | solution.py:373
  8.1 3.6 %collective-permute-start.3 = (bf16[128,256]{1,0:T(8,128)(2,1)S(1)}, bf16[128,256]{1,0:T(8,128)(2,1)S(1)}, u32[]{:S(2)}, u32[]{:S(2)}) collective-permute-start(bf16[128,256]{1,0:T(8,128)(2,1)S(1)} %get-tuple-element.68.after_ref), channel_id=1, source_target_pairs={{0,3},{1,2},{2,1},{3,0},{4,7},{5,6},{6,5},{7,4},{8,11},{9,10},{10,... | collective-permute-start | bytes 196616 | tf_op jit(solution)/shard_map/ppermute | solution.py:412
  11.7 0.5 collective-permute-start.2
  12.3 2.8 %turn.3.refs_0_ = bf16[32,256,256]{2,1,0:T(8,128)(2,1)S(1)} custom-call(bf16[128,256]{1,0:T(8,128)(2,1)S(1)} %get-tuple-element.68.after_ref, bf16[64,256,256]{2,1,0:T(8,128)(2,1)S(1)} %get-tuple-element.69.refs_0_.refs_10_), custom_call_target="tpu_custom_call" | custom-call | flops 135895456 | bytes 8454144 | tf_op jit(solution)/shard_map/turn/pallas_call | solution.py:373
  15.1 1.2 %collective-permute-done.2 = bf16[128,256]{1,0:T(8,128)(2,1)S(1)} collective-permute-done((bf16[128,256]{1,0:T(8,128)(2,1)S(1)}, bf16[128,256]{1,0:T(8,128)(2,1)S(1)}, u32[]{:S(2)}, u32[]{:S(2)}) %collective-permute-start.2) | collective-permute-done | bytes 65568 | tf_op jit(solution)/shard_map/ppermute | solution.py:412
  16.3 0.7 collective-permute-done.1
  17.1 2.7 %collective-permute-start.4 = (bf16[128,256]{1,0:T(8,128)(2,1)S(1)}, bf16[128,256]{1,0:T(8,128)(2,1)S(1)}, u32[]{:S(2)}, u32[]{:S(2)}) collective-permute-start(bf16[128,256]{1,0:T(8,128)(2,1)S(1)} %add_convert_fusion.4.refs_0_.after_ref), channel_id=1, source_target_pairs={{0,4},{1,5},{2,6},{3,7},{4,0},{5,1},{6,2},{7,3},{8,12},{9,13},{10,... | collective-permute-start | bytes 196616 | tf_op jit(solution)/shard_map/ppermute | solution.py:412
  19.7 2.8 %turn.4.refs_0_ = bf16[32,256,256]{2,1,0:T(8,128)(2,1)S(1)} custom-call(bf16[128,256]{1,0:T(8,128)(2,1)S(1)} %add_convert_fusion.4.refs_0_.after_ref, bf16[64,256,256]{2,1,0:T(8,128)(2,1)S(1)} %get-tuple-element.69.refs_0_.refs_10_), custom_call_target="tpu_custom_call" | custom-call | flops 135895456 | bytes 8454144 | tf_op jit(solution)/shard_map/turn/pallas_call | solution.py:373
  22.6 1.2 %collective-permute-done.4.refs_1_ = bf16[128,256]{1,0:T(8,128)(2,1)S(1)} collective-permute-done((bf16[128,256]{1,0:T(8,128)(2,1)S(1)}, bf16[128,256]{1,0:T(8,128)(2,1)S(1)}, u32[]{:S(2)}, u32[]{:S(2)}) %collective-permute-start.4) | collective-permute-done | bytes 65568 | tf_op jit(solution)/shard_map/ppermute | solution.py:412
  23.9 1.5 %project.8.refs_0_ = f32[48,256]{1,0:T(8,128)S(1)} custom-call(f32[128,256]{1,0:T(8,128)S(1)} %get-tuple-element.72.field_ref.refs_13_.refs_2_, bf16[88,128]{1,0:T(8,128)(2,1)S(1)} %get-tuple-element.73.pick1_ref, bf16[88,128]{1,0:T(8,128)(2,1)S(1)} %get-tuple-element.74.pick2_ref, bf16[32,256,256]{2,1,0:T(8,128)(2,1)S(1)} %turn.3.refs_0_, ...), custom_call_target="tpu_custom_call" | custom-call | flops 203843168 | bytes 6467584 | tf_op jit(solution)/shard_map/project/pallas_call | solution.py:373
  25.4 1.5 %collective-permute-done.5.refs_5_ = f32[8,256]{1,0:T(8,128)S(1)} collective-permute-done((f32[8,256]{1,0:T(8,128)S(1)}, f32[8,256]{1,0:T(8,128)S(1)}, u32[]{:S(2)}, u32[]{:S(2)}) %collective-permute-start.5) | collective-permute-done | bytes 8224 | tf_op jit(solution)/shard_map/ppermute | solution.py:412
  27.0 0.4 collective-permute-start.7
  27.4 1.0 project.9.refs_1_
  28.4 1.9 %step.4 = (bf16[128,256]{1,0:T(8,128)(2,1)S(1)}, f32[88,256]{1,0:T(8,128)S(1)}) custom-call(f32[48,256]{1,0:T(8,128)S(1)} %project.8.refs_0_, f32[40,256]{1,0:T(8,128)S(1)} %project.9.refs_1_, f32[8,256]{1,0:T(8,128)S(1)} %get-tuple-element.71.refs_2_, f32[8,256]{1,0:T(8,128)S(1)} %collective-permute-done.6.refs_3_, ...), custom_call_target="tpu_custom_call" | custom-call | flops 339738624 | bytes 11067392 | tf_op jit(solution)/shard_map/step/pallas_call | solution.py:373
  30.3 0.9 collective-permute-start.10
  31.3 1.5 %collective-permute-start.9 = (bf16[128,256]{1,0:T(8,128)(2,1)S(1)}, bf16[128,256]{1,0:T(8,128)(2,1)S(1)}, u32[]{:S(2)}, u32[]{:S(2)}) collective-permute-start(bf16[128,256]{1,0:T(8,128)(2,1)S(1)} %get-tuple-element.82.after_ref), channel_id=1, source_target_pairs={{0,2},{1,3},{2,0},{3,1},{4,6},{5,7},{6,4},{7,5},{8,10},{9,11},{10,... | collective-permute-start | bytes 196616 | tf_op jit(solution)/shard_map/ppermute | solution.py:412
  32.7 1.2 %collective-permute-start.8 = (bf16[128,256]{1,0:T(8,128)(2,1)S(1)}, bf16[128,256]{1,0:T(8,128)(2,1)S(1)}, u32[]{:S(2)}, u32[]{:S(2)}) collective-permute-start(bf16[128,256]{1,0:T(8,128)(2,1)S(1)} %get-tuple-element.82.after_ref), channel_id=1, source_target_pairs={{0,1},{1,0},{2,3},{3,2},{4,5},{5,4},{6,7},{7,6},{8,9},{9,8},{10,11... | collective-permute-start | bytes 196616 | tf_op jit(solution)/shard_map/ppermute | solution.py:412
  33.9 2.4 %collective-permute-done.10 = bf16[128,256]{1,0:T(8,128)(2,1)S(1)} collective-permute-done((bf16[128,256]{1,0:T(8,128)(2,1)S(1)}, bf16[128,256]{1,0:T(8,128)(2,1)S(1)}, u32[]{:S(2)}, u32[]{:S(2)}) %collective-permute-start.10) | collective-permute-done | bytes 65568 | tf_op jit(solution)/shard_map/ppermute | solution.py:412
  36.3 0.7 collective-permute-done.8
  37.0 2.0 %collective-permute-start.11 = (bf16[128,256]{1,0:T(8,128)(2,1)S(1)}, bf16[128,256]{1,0:T(8,128)(2,1)S(1)}, u32[]{:S(2)}, u32[]{:S(2)}) collective-permute-start(bf16[128,256]{1,0:T(8,128)(2,1)S(1)} %add_convert_fusion.3.refs_0_), channel_id=1, source_target_pairs={{0,4},{1,5},{2,6},{3,7},{4,0},{5,1},{6,2},{7,3},{8,12},{9,13},{10,... | collective-permute-start | bytes 196616 | tf_op jit(solution)/shard_map/ppermute | solution.py:412
  39.0 1.6 %turn.5 = (bf16[16,256,256]{2,1,0:T(8,128)(2,1)S(1)}, bf16[1,256,256]{2,1,0:T(8,128)(2,1)S(1)}) custom-call(bf16[128,256]{1,0:T(8,128)(2,1)S(1)} %get-tuple-element.82.after_ref, bf16[16,256,256]{2,1,0:T(8,128)(2,1)S(1)} %get-tuple-element.76.refs_1_.refs_11_.refs_0_, bf16[1,256,256]{2,1,0:T(8,128)(2,1)S(1)} %get-tuple-element.78.refs_1_.refs_12_), custom_call_target="tpu_custom_call" | custom-call | flops 72194456 | bytes 2293760 | tf_op jit(solution)/shard_map/turn/pallas_call | solution.py:373
  40.6 2.3 %collective-permute-done.11.refs_1_ = bf16[128,256]{1,0:T(8,128)(2,1)S(1)} collective-permute-done((bf16[128,256]{1,0:T(8,128)(2,1)S(1)}, bf16[128,256]{1,0:T(8,128)(2,1)S(1)}, u32[]{:S(2)}, u32[]{:S(2)}) %collective-permute-start.11) | collective-permute-done | bytes 65568 | tf_op jit(solution)/shard_map/ppermute | solution.py:412
  43.2 1.2 %collective-permute-start.12 = (f32[8,256]{1,0:T(8,128)S(1)}, f32[8,256]{1,0:T(8,128)S(1)}, u32[]{:S(2)}, u32[]{:S(2)}) collective-permute-start(f32[8,256]{1,0:T(8,128)S(1)} %get-tuple-element.83.refs_2_), channel_id=1, source_target_pairs={{0,24},{8,16},{16,8},{24,0},{1,25},{9,17},{17,9},{25,1},{2,26},{10... | collective-permute-start | bytes 24584 | tf_op jit(solution)/shard_map/ppermute | solution.py:412
  44.5 1.3 %project.10.refs_0_ = f32[48,256]{1,0:T(8,128)S(1)} custom-call(f32[128,256]{1,0:T(8,128)S(1)} %get-tuple-element.84.field_ref.refs_14_, bf16[88,128]{1,0:T(8,128)(2,1)S(1)} %get-tuple-element.73.pick1_ref, bf16[88,128]{1,0:T(8,128)(2,1)S(1)} %get-tuple-element.74.pick2_ref, bf16[32,256,256]{2,1,0:T(8,128)(2,1)S(1)} %turn.3.refs_0_, ...), custom_call_target="tpu_custom_call" | custom-call | flops 203843168 | bytes 6467584 | tf_op jit(solution)/shard_map/project/pallas_call | solution.py:373
  45.7 0.6 collective-permute-done.12.refs_5_
  46.4 0.4 collective-permute-start.14
  46.8 0.9 project.11.refs_1_
  47.8 1.9 %step.5 = (bf16[128,256]{1,0:T(8,128)(2,1)S(1)}, f32[88,256]{1,0:T(8,128)S(1)}, f32[128,256]{1,0:T(8,128)S(1)}, f32[128,256]{1,0:T(8,128)S(1)}, f32[88,256]{1,0:...) custom-call(f32[48,256]{1,0:T(8,128)S(1)} %project.10.refs_0_, ...), custom_call_target="tpu_custom_call" | custom-call | flops 339738624 | bytes 11304960 | tf_op jit(solution)/shard_map/step/pallas_call | solution.py:373
  49.7 1.0 collective-permute-start.17
  50.7 1.6 %collective-permute-start.16 = (bf16[128,256]{1,0:T(8,128)(2,1)S(1)}, bf16[128,256]{1,0:T(8,128)(2,1)S(1)}, u32[]{:S(2)}, u32[]{:S(2)}) collective-permute-start(bf16[128,256]{1,0:T(8,128)(2,1)S(1)} %get-tuple-element.90), channel_id=1, source_target_pairs={{0,2},{1,3},{2,0},{3,1},{4,6},{5,7},{6,4},{7,5},{8,10},{9,11},{10,... | collective-permute-start | bytes 196616 | tf_op jit(solution)/shard_map/ppermute | solution.py:412
  52.4 0.9 collective-permute-start.15
  53.3 2.4 %collective-permute-done.17 = bf16[128,256]{1,0:T(8,128)(2,1)S(1)} collective-permute-done((bf16[128,256]{1,0:T(8,128)(2,1)S(1)}, bf16[128,256]{1,0:T(8,128)(2,1)S(1)}, u32[]{:S(2)}, u32[]{:S(2)}) %collective-permute-start.17) | collective-permute-done | bytes 65568 | tf_op jit(solution)/shard_map/ppermute | solution.py:412
  56.0 0.7 collective-permute-done.15
  56.7 1.4 %collective-permute-start.18 = (bf16[128,256]{1,0:T(8,128)(2,1)S(1)}, bf16[128,256]{1,0:T(8,128)(2,1)S(1)}, u32[]{:S(2)}, u32[]{:S(2)}) collective-permute-start(bf16[128,256]{1,0:T(8,128)(2,1)S(1)} %add_convert_fusion.2.refs_0_), channel_id=1, source_target_pairs={{0,4},{1,5},{2,6},{3,7},{4,0},{5,1},{6,2},{7,3},{8,12},{9,13},{10,... | collective-permute-start | bytes 196616 | tf_op jit(solution)/shard_map/ppermute | solution.py:412
  58.1 4.4 %collective-permute-done.18.refs_1_ = bf16[128,256]{1,0:T(8,128)(2,1)S(1)} collective-permute-done((bf16[128,256]{1,0:T(8,128)(2,1)S(1)}, bf16[128,256]{1,0:T(8,128)(2,1)S(1)}, u32[]{:S(2)}, u32[]{:S(2)}) %collective-permute-start.18) | collective-permute-done | bytes 65568 | tf_op jit(solution)/shard_map/ppermute | solution.py:412
  62.7 0.8 collective-permute-start.19
  63.6 1.3 %project.12.refs_0_ = f32[48,256]{1,0:T(8,128)S(1)} custom-call(f32[128,256]{1,0:T(8,128)S(1)} %get-tuple-element.93.field_ref.refs_14_, bf16[88,128]{1,0:T(8,128)(2,1)S(1)} %get-tuple-element.73.pick1_ref, bf16[88,128]{1,0:T(8,128)(2,1)S(1)} %get-tuple-element.74.pick2_ref, bf16[32,256,256]{2,1,0:T(8,128)(2,1)S(1)} %turn.3.refs_0_, ...), custom_call_target="tpu_custom_call" | custom-call | flops 203843168 | bytes 6467584 | tf_op jit(solution)/shard_map/project/pallas_call | solution.py:373
  64.8 1.0 collective-permute-done.19.refs_5_
  65.9 0.4 collective-permute-start.21
  66.3 0.9 project.13.refs_1_
  67.3 1.9 %step.6 = (bf16[128,256]{1,0:T(8,128)(2,1)S(1)}, f32[88,256]{1,0:T(8,128)S(1)}, f32[128,256]{1,0:T(8,128)S(1)}, f32[128,256]{1,0:T(8,128)S(1)}, f32[88,256]{1,0:...) custom-call(f32[48,256]{1,0:T(8,128)S(1)} %project.12.refs_0_, ...), custom_call_target="tpu_custom_call" | custom-call | flops 339738624 | bytes 11546624 | tf_op jit(solution)/shard_map/step/pallas_call | solution.py:373
  69.5 2.1 %collective-permute-start.23 = (bf16[128,256]{1,0:T(8,128)(2,1)S(1)}, bf16[128,256]{1,0:T(8,128)(2,1)S(1)}, u32[]{:S(2)}, u32[]{:S(2)}) collective-permute-start(bf16[128,256]{1,0:T(8,128)(2,1)S(1)} %get-tuple-element.102), channel_id=1, source_target_pairs={{0,2},{1,3},{2,0},{3,1},{4,6},{5,7},{6,4},{7,5},{8,10},{9,11},{10,... | collective-permute-start | bytes 196616 | tf_op jit(solution)/shard_map/ppermute | solution.py:412
  71.6 1.1 %collective-permute-start.22 = (bf16[128,256]{1,0:T(8,128)(2,1)S(1)}, bf16[128,256]{1,0:T(8,128)(2,1)S(1)}, u32[]{:S(2)}, u32[]{:S(2)}) collective-permute-start(bf16[128,256]{1,0:T(8,128)(2,1)S(1)} %get-tuple-element.102), channel_id=1, source_target_pairs={{0,1},{1,0},{2,3},{3,2},{4,5},{5,4},{6,7},{7,6},{8,9},{9,8},{10,11... | collective-permute-start | bytes 196616 | tf_op jit(solution)/shard_map/ppermute | solution.py:412
  72.8 2.4 %collective-permute-done.24 = bf16[128,256]{1,0:T(8,128)(2,1)S(1)} collective-permute-done((bf16[128,256]{1,0:T(8,128)(2,1)S(1)}, bf16[128,256]{1,0:T(8,128)(2,1)S(1)}, u32[]{:S(2)}, u32[]{:S(2)}) %collective-permute-start.24) | collective-permute-done | bytes 65568 | tf_op jit(solution)/shard_map/ppermute | solution.py:412
  75.2 0.7 collective-permute-done.22
  75.9 1.0 collective-permute-start.25
  76.9 4.5 %collective-permute-done.25.refs_1_ = bf16[128,256]{1,0:T(8,128)(2,1)S(1)} collective-permute-done((bf16[128,256]{1,0:T(8,128)(2,1)S(1)}, bf16[128,256]{1,0:T(8,128)(2,1)S(1)}, u32[]{:S(2)}, u32[]{:S(2)}) %collective-permute-start.25) | collective-permute-done | bytes 65568 | tf_op jit(solution)/shard_map/ppermute | solution.py:412
  81.7 1.0 collective-permute-start.26
  82.7 1.3 %project.14.refs_0_ = f32[48,256]{1,0:T(8,128)S(1)} custom-call(f32[128,256]{1,0:T(8,128)S(1)} %get-tuple-element.105.field_ref.refs_14_, bf16[88,128]{1,0:T(8,128)(2,1)S(1)} %get-tuple-element.73.pick1_ref, bf16[88,128]{1,0:T(8,128)(2,1)S(1)} %get-tuple-element.74.pick2_ref, bf16[32,256,256]{2,1,0:T(8,128)(2,1)S(1)} %turn.3.refs_0_, ...), custom_call_target="tpu_custom_call" | custom-call | flops 203843168 | bytes 6467584 | tf_op jit(solution)/shard_map/project/pallas_call | solution.py:373
  84.0 0.8 collective-permute-done.26.refs_5_
  85.3 0.9 project.15.refs_1_
  86.2 2.4 %step.7 = (bf16[128,256]{1,0:T(8,128)(2,1)S(1)}, f32[88,256]{1,0:T(8,128)}, f32[128,256]{1,0:T(8,128)S(1)}, f32[128,256]{1,0:T(8,128)S(1)}, f32[88,256]{1,0:T(8,...) custom-call(f32[48,256]{1,0:T(8,128)S(1)} %project.14.refs_0_, ...), custom_call_target="tpu_custom_call" | custom-call | flops 339738624 | bytes 11546624 | tf_op jit(solution)/shard_map/step/pallas_call | solution.py:373
  88.9 2.1 %collective-permute-start.30 = (bf16[128,256]{1,0:T(8,128)(2,1)S(1)}, bf16[128,256]{1,0:T(8,128)(2,1)S(1)}, u32[]{:S(2)}, u32[]{:S(2)}) collective-permute-start(bf16[128,256]{1,0:T(8,128)(2,1)S(1)} %get-tuple-element.114), channel_id=1, source_target_pairs={{0,2},{1,3},{2,0},{3,1},{4,6},{5,7},{6,4},{7,5},{8,10},{9,11},{10,... | collective-permute-start | bytes 196616 | tf_op jit(solution)/shard_map/ppermute | solution.py:412
  91.1 1.0 collective-permute-start.29
  92.1 2.4 %collective-permute-done.31 = bf16[128,256]{1,0:T(8,128)(2,1)S(1)} collective-permute-done((bf16[128,256]{1,0:T(8,128)(2,1)S(1)}, bf16[128,256]{1,0:T(8,128)(2,1)S(1)}, u32[]{:S(2)}, u32[]{:S(2)}) %collective-permute-start.31) | collective-permute-done | bytes 65568 | tf_op jit(solution)/shard_map/ppermute | solution.py:412
  94.7 0.7 collective-permute-done.29
  95.4 0.9 collective-permute-start.32
  96.3 4.4 %collective-permute-done.32.refs_1_ = bf16[128,256]{1,0:T(8,128)(2,1)S(1)} collective-permute-done((bf16[128,256]{1,0:T(8,128)(2,1)S(1)}, bf16[128,256]{1,0:T(8,128)(2,1)S(1)}, u32[]{:S(2)}, u32[]{:S(2)}) %collective-permute-start.32) | collective-permute-done | bytes 65568 | tf_op jit(solution)/shard_map/ppermute | solution.py:412
  101.0 0.8 collective-permute-start.33
  101.9 2.2 %collective-permute-done.34.refs_4_ = f32[8,256]{1,0:T(8,128)S(1)} collective-permute-done((f32[8,256]{1,0:T(8,128)S(1)}, f32[8,256]{1,0:T(8,128)S(1)}, u32[]{:S(2)}, u32[]{:S(2)}) %collective-permute-start.34) | collective-permute-done | bytes 8224 | tf_op jit(solution)/shard_map/ppermute | solution.py:412
  104.1 1.2 %collective-permute-done.35.refs_3_ = f32[8,256]{1,0:T(8,128)S(1)} collective-permute-done((f32[8,256]{1,0:T(8,128)S(1)}, f32[8,256]{1,0:T(8,128)S(1)}, u32[]{:S(2)}, u32[]{:S(2)}) %collective-permute-start.35) | collective-permute-done | bytes 8224 | tf_op jit(solution)/shard_map/ppermute | solution.py:412
  105.3 0.6 final.1
  (38 shorter events, 3.5 us)
Async XLA Ops:
  1.6 6.1 %collective-permute-start = (bf16[1,272,256]{2,1,0:T(8,128)(2,1)S(1)}, bf16[1,272,256]{2,1,0:T(8,128)(2,1)S(1)}, u32[]{:S(2)}, u32[]{:S(2)}) collective-permute-start(bf16[1,272,256]{2,1,0:T(8,128)(2,1)S(1)} %pack.1), channel_id=1, source_target_pairs={{0,8},{8,16},{16,24},{24,0},{1,9},{9,17},{17,25},{25,1},{2,10},{10... | collective-permute-start | bytes 417800 | tf_op jit(solution)/shard_map/ppermute | solution.py:442
  8.1 7.1 %collective-permute-start.3 = (bf16[128,256]{1,0:T(8,128)(2,1)S(1)}, bf16[128,256]{1,0:T(8,128)(2,1)S(1)}, u32[]{:S(2)}, u32[]{:S(2)}) collective-permute-start(bf16[128,256]{1,0:T(8,128)(2,1)S(1)} %get-tuple-element.68.after_ref), channel_id=1, source_target_pairs={{0,3},{1,2},{2,1},{3,0},{4,7},{5,6},{6,5},{7,4},{8,11},{9,10},{10,... | collective-permute-start | bytes 196616 | tf_op jit(solution)/shard_map/ppermute | solution.py:412
  11.7 4.6 %collective-permute-start.2 = (bf16[128,256]{1,0:T(8,128)(2,1)S(1)}, bf16[128,256]{1,0:T(8,128)(2,1)S(1)}, u32[]{:S(2)}, u32[]{:S(2)}) collective-permute-start(bf16[128,256]{1,0:T(8,128)(2,1)S(1)} %get-tuple-element.68.after_ref), channel_id=1, source_target_pairs={{0,2},{1,3},{2,0},{3,1},{4,6},{5,7},{6,4},{7,5},{8,10},{9,11},{10,... | collective-permute-start | bytes 196616 | tf_op jit(solution)/shard_map/ppermute | solution.py:412
  12.1 4.9 %collective-permute-start.1 = (bf16[128,256]{1,0:T(8,128)(2,1)S(1)}, bf16[128,256]{1,0:T(8,128)(2,1)S(1)}, u32[]{:S(2)}, u32[]{:S(2)}) collective-permute-start(bf16[128,256]{1,0:T(8,128)(2,1)S(1)} %get-tuple-element.68.after_ref), channel_id=1, source_target_pairs={{0,1},{1,0},{2,3},{3,2},{4,5},{5,4},{6,7},{7,6},{8,9},{9,8},{10,11... | collective-permute-start | bytes 196616 | tf_op jit(solution)/shard_map/ppermute | solution.py:412
  17.1 6.6 %collective-permute-start.4 = (bf16[128,256]{1,0:T(8,128)(2,1)S(1)}, bf16[128,256]{1,0:T(8,128)(2,1)S(1)}, u32[]{:S(2)}, u32[]{:S(2)}) collective-permute-start(bf16[128,256]{1,0:T(8,128)(2,1)S(1)} %add_convert_fusion.4.refs_0_.after_ref), channel_id=1, source_target_pairs={{0,4},{1,5},{2,6},{3,7},{4,0},{5,1},{6,2},{7,3},{8,12},{9,13},{10,... | collective-permute-start | bytes 196616 | tf_op jit(solution)/shard_map/ppermute | solution.py:412
  23.7 4.6 %collective-permute-start.6 = (f32[8,256]{1,0:T(8,128)S(1)}, f32[8,256]{1,0:T(8,128)S(1)}, u32[]{:S(2)}, u32[]{:S(2)}) collective-permute-start(f32[8,256]{1,0:T(8,128)S(1)} %get-tuple-element.71.refs_2_), channel_id=1, source_target_pairs={{0,8},{8,0},{16,24},{24,16},{1,9},{9,1},{17,25},{25,17},{2,10},{10... | collective-permute-start | bytes 24584 | tf_op jit(solution)/shard_map/ppermute | solution.py:412
  23.8 3.1 %collective-permute-start.5 = (f32[8,256]{1,0:T(8,128)S(1)}, f32[8,256]{1,0:T(8,128)S(1)}, u32[]{:S(2)}, u32[]{:S(2)}) collective-permute-start(f32[8,256]{1,0:T(8,128)S(1)} %get-tuple-element.71.refs_2_), channel_id=1, source_target_pairs={{0,24},{8,16},{16,8},{24,0},{1,25},{9,17},{17,9},{25,1},{2,26},{10... | collective-permute-start | bytes 24584 | tf_op jit(solution)/shard_map/ppermute | solution.py:412
  27.0 1.4 %collective-permute-start.7 = (f32[8,256]{1,0:T(8,128)S(1)}, f32[8,256]{1,0:T(8,128)S(1)}, u32[]{:S(2)}, u32[]{:S(2)}) collective-permute-start(f32[8,256]{1,0:T(8,128)S(1)} %collective-permute-done.5.refs_5_), channel_id=1, source_target_pairs={{0,8},{8,0},{16,24},{24,16},{1,9},{9,1},{17,25},{25,17},{2,10},{10... | collective-permute-start | bytes 24584 | tf_op jit(solution)/shard_map/ppermute | solution.py:412
  30.3 5.9 %collective-permute-start.10 = (bf16[128,256]{1,0:T(8,128)(2,1)S(1)}, bf16[128,256]{1,0:T(8,128)(2,1)S(1)}, u32[]{:S(2)}, u32[]{:S(2)}) collective-permute-start(bf16[128,256]{1,0:T(8,128)(2,1)S(1)} %get-tuple-element.82.after_ref), channel_id=1, source_target_pairs={{0,3},{1,2},{2,1},{3,0},{4,7},{5,6},{6,5},{7,4},{8,11},{9,10},{10,... | collective-permute-start | bytes 196616 | tf_op jit(solution)/shard_map/ppermute | solution.py:412
  31.3 5.0 %collective-permute-start.9 = (bf16[128,256]{1,0:T(8,128)(2,1)S(1)}, bf16[128,256]{1,0:T(8,128)(2,1)S(1)}, u32[]{:S(2)}, u32[]{:S(2)}) collective-permute-start(bf16[128,256]{1,0:T(8,128)(2,1)S(1)} %get-tuple-element.82.after_ref), channel_id=1, source_target_pairs={{0,2},{1,3},{2,0},{3,1},{4,6},{5,7},{6,4},{7,5},{8,10},{9,11},{10,... | collective-permute-start | bytes 196616 | tf_op jit(solution)/shard_map/ppermute | solution.py:412
  32.7 4.3 %collective-permute-start.8 = (bf16[128,256]{1,0:T(8,128)(2,1)S(1)}, bf16[128,256]{1,0:T(8,128)(2,1)S(1)}, u32[]{:S(2)}, u32[]{:S(2)}) collective-permute-start(bf16[128,256]{1,0:T(8,128)(2,1)S(1)} %get-tuple-element.82.after_ref), channel_id=1, source_target_pairs={{0,1},{1,0},{2,3},{3,2},{4,5},{5,4},{6,7},{7,6},{8,9},{9,8},{10,11... | collective-permute-start | bytes 196616 | tf_op jit(solution)/shard_map/ppermute | solution.py:412
  37.0 5.9 %collective-permute-start.11 = (bf16[128,256]{1,0:T(8,128)(2,1)S(1)}, bf16[128,256]{1,0:T(8,128)(2,1)S(1)}, u32[]{:S(2)}, u32[]{:S(2)}) collective-permute-start(bf16[128,256]{1,0:T(8,128)(2,1)S(1)} %add_convert_fusion.3.refs_0_), channel_id=1, source_target_pairs={{0,4},{1,5},{2,6},{3,7},{4,0},{5,1},{6,2},{7,3},{8,12},{9,13},{10,... | collective-permute-start | bytes 196616 | tf_op jit(solution)/shard_map/ppermute | solution.py:412
  43.1 4.6 %collective-permute-start.13 = (f32[8,256]{1,0:T(8,128)S(1)}, f32[8,256]{1,0:T(8,128)S(1)}, u32[]{:S(2)}, u32[]{:S(2)}) collective-permute-start(f32[8,256]{1,0:T(8,128)S(1)} %get-tuple-element.83.refs_2_), channel_id=1, source_target_pairs={{0,8},{8,0},{16,24},{24,16},{1,9},{9,1},{17,25},{25,17},{2,10},{10... | collective-permute-start | bytes 24584 | tf_op jit(solution)/shard_map/ppermute | solution.py:412
  43.2 3.1 %collective-permute-start.12 = (f32[8,256]{1,0:T(8,128)S(1)}, f32[8,256]{1,0:T(8,128)S(1)}, u32[]{:S(2)}, u32[]{:S(2)}) collective-permute-start(f32[8,256]{1,0:T(8,128)S(1)} %get-tuple-element.83.refs_2_), channel_id=1, source_target_pairs={{0,24},{8,16},{16,8},{24,0},{1,25},{9,17},{17,9},{25,1},{2,26},{10... | collective-permute-start | bytes 24584 | tf_op jit(solution)/shard_map/ppermute | solution.py:412
  46.4 1.4 %collective-permute-start.14 = (f32[8,256]{1,0:T(8,128)S(1)}, f32[8,256]{1,0:T(8,128)S(1)}, u32[]{:S(2)}, u32[]{:S(2)}) collective-permute-start(f32[8,256]{1,0:T(8,128)S(1)} %collective-permute-done.12.refs_5_), channel_id=1, source_target_pairs={{0,8},{8,0},{16,24},{24,16},{1,9},{9,1},{17,25},{25,17},{2,10},{10... | collective-permute-start | bytes 24584 | tf_op jit(solution)/shard_map/ppermute | solution.py:412
  49.7 6.0 %collective-permute-start.17 = (bf16[128,256]{1,0:T(8,128)(2,1)S(1)}, bf16[128,256]{1,0:T(8,128)(2,1)S(1)}, u32[]{:S(2)}, u32[]{:S(2)}) collective-permute-start(bf16[128,256]{1,0:T(8,128)(2,1)S(1)} %get-tuple-element.90), channel_id=1, source_target_pairs={{0,3},{1,2},{2,1},{3,0},{4,7},{5,6},{6,5},{7,4},{8,11},{9,10},{10,... | collective-permute-start | bytes 196616 | tf_op jit(solution)/shard_map/ppermute | solution.py:412
  50.7 5.2 %collective-permute-start.16 = (bf16[128,256]{1,0:T(8,128)(2,1)S(1)}, bf16[128,256]{1,0:T(8,128)(2,1)S(1)}, u32[]{:S(2)}, u32[]{:S(2)}) collective-permute-start(bf16[128,256]{1,0:T(8,128)(2,1)S(1)} %get-tuple-element.90), channel_id=1, source_target_pairs={{0,2},{1,3},{2,0},{3,1},{4,6},{5,7},{6,4},{7,5},{8,10},{9,11},{10,... | collective-permute-start | bytes 196616 | tf_op jit(solution)/shard_map/ppermute | solution.py:412
  52.4 4.3 %collective-permute-start.15 = (bf16[128,256]{1,0:T(8,128)(2,1)S(1)}, bf16[128,256]{1,0:T(8,128)(2,1)S(1)}, u32[]{:S(2)}, u32[]{:S(2)}) collective-permute-start(bf16[128,256]{1,0:T(8,128)(2,1)S(1)} %get-tuple-element.90), channel_id=1, source_target_pairs={{0,1},{1,0},{2,3},{3,2},{4,5},{5,4},{6,7},{7,6},{8,9},{9,8},{10,11... | collective-permute-start | bytes 196616 | tf_op jit(solution)/shard_map/ppermute | solution.py:412
  56.7 5.8 %collective-permute-start.18 = (bf16[128,256]{1,0:T(8,128)(2,1)S(1)}, bf16[128,256]{1,0:T(8,128)(2,1)S(1)}, u32[]{:S(2)}, u32[]{:S(2)}) collective-permute-start(bf16[128,256]{1,0:T(8,128)(2,1)S(1)} %add_convert_fusion.2.refs_0_), channel_id=1, source_target_pairs={{0,4},{1,5},{2,6},{3,7},{4,0},{5,1},{6,2},{7,3},{8,12},{9,13},{10,... | collective-permute-start | bytes 196616 | tf_op jit(solution)/shard_map/ppermute | solution.py:412
  62.7 4.6 %collective-permute-start.20 = (f32[8,256]{1,0:T(8,128)S(1)}, f32[8,256]{1,0:T(8,128)S(1)}, u32[]{:S(2)}, u32[]{:S(2)}) collective-permute-start(f32[8,256]{1,0:T(8,128)S(1)} %get-tuple-element.92.refs_2_), channel_id=1, source_target_pairs={{0,8},{8,0},{16,24},{24,16},{1,9},{9,1},{17,25},{25,17},{2,10},{10... | collective-permute-start | bytes 24584 | tf_op jit(solution)/shard_map/ppermute | solution.py:412
  62.7 3.1 %collective-permute-start.19 = (f32[8,256]{1,0:T(8,128)S(1)}, f32[8,256]{1,0:T(8,128)S(1)}, u32[]{:S(2)}, u32[]{:S(2)}) collective-permute-start(f32[8,256]{1,0:T(8,128)S(1)} %get-tuple-element.92.refs_2_), channel_id=1, source_target_pairs={{0,24},{8,16},{16,8},{24,0},{1,25},{9,17},{17,9},{25,1},{2,26},{10... | collective-permute-start | bytes 24584 | tf_op jit(solution)/shard_map/ppermute | solution.py:412
  65.9 1.4 %collective-permute-start.21 = (f32[8,256]{1,0:T(8,128)S(1)}, f32[8,256]{1,0:T(8,128)S(1)}, u32[]{:S(2)}, u32[]{:S(2)}) collective-permute-start(f32[8,256]{1,0:T(8,128)S(1)} %collective-permute-done.19.refs_5_), channel_id=1, source_target_pairs={{0,8},{8,0},{16,24},{24,16},{1,9},{9,1},{17,25},{25,17},{2,10},{10... | collective-permute-start | bytes 24584 | tf_op jit(solution)/shard_map/ppermute | solution.py:412
  69.2 6.0 %collective-permute-start.24 = (bf16[128,256]{1,0:T(8,128)(2,1)S(1)}, bf16[128,256]{1,0:T(8,128)(2,1)S(1)}, u32[]{:S(2)}, u32[]{:S(2)}) collective-permute-start(bf16[128,256]{1,0:T(8,128)(2,1)S(1)} %get-tuple-element.102), channel_id=1, source_target_pairs={{0,3},{1,2},{2,1},{3,0},{4,7},{5,6},{6,5},{7,4},{8,11},{9,10},{10,... | collective-permute-start | bytes 196616 | tf_op jit(solution)/shard_map/ppermute | solution.py:412
  69.5 5.7 %collective-permute-start.23 = (bf16[128,256]{1,0:T(8,128)(2,1)S(1)}, bf16[128,256]{1,0:T(8,128)(2,1)S(1)}, u32[]{:S(2)}, u32[]{:S(2)}) collective-permute-start(bf16[128,256]{1,0:T(8,128)(2,1)S(1)} %get-tuple-element.102), channel_id=1, source_target_pairs={{0,2},{1,3},{2,0},{3,1},{4,6},{5,7},{6,4},{7,5},{8,10},{9,11},{10,... | collective-permute-start | bytes 196616 | tf_op jit(solution)/shard_map/ppermute | solution.py:412
  71.6 4.3 %collective-permute-start.22 = (bf16[128,256]{1,0:T(8,128)(2,1)S(1)}, bf16[128,256]{1,0:T(8,128)(2,1)S(1)}, u32[]{:S(2)}, u32[]{:S(2)}) collective-permute-start(bf16[128,256]{1,0:T(8,128)(2,1)S(1)} %get-tuple-element.102), channel_id=1, source_target_pairs={{0,1},{1,0},{2,3},{3,2},{4,5},{5,4},{6,7},{7,6},{8,9},{9,8},{10,11... | collective-permute-start | bytes 196616 | tf_op jit(solution)/shard_map/ppermute | solution.py:412
  75.9 5.5 %collective-permute-start.25 = (bf16[128,256]{1,0:T(8,128)(2,1)S(1)}, bf16[128,256]{1,0:T(8,128)(2,1)S(1)}, u32[]{:S(2)}, u32[]{:S(2)}) collective-permute-start(bf16[128,256]{1,0:T(8,128)(2,1)S(1)} %add_convert_fusion.1.refs_0_), channel_id=1, source_target_pairs={{0,4},{1,5},{2,6},{3,7},{4,0},{5,1},{6,2},{7,3},{8,12},{9,13},{10,... | collective-permute-start | bytes 196616 | tf_op jit(solution)/shard_map/ppermute | solution.py:412
  81.6 4.6 %collective-permute-start.27 = (f32[8,256]{1,0:T(8,128)S(1)}, f32[8,256]{1,0:T(8,128)S(1)}, u32[]{:S(2)}, u32[]{:S(2)}) collective-permute-start(f32[8,256]{1,0:T(8,128)S(1)} %get-tuple-element.104.refs_2_), channel_id=1, source_target_pairs={{0,8},{8,0},{16,24},{24,16},{1,9},{9,1},{17,25},{25,17},{2,10},{10... | collective-permute-start | bytes 24584 | tf_op jit(solution)/shard_map/ppermute | solution.py:412
  81.7 3.1 %collective-permute-start.26 = (f32[8,256]{1,0:T(8,128)S(1)}, f32[8,256]{1,0:T(8,128)S(1)}, u32[]{:S(2)}, u32[]{:S(2)}) collective-permute-start(f32[8,256]{1,0:T(8,128)S(1)} %get-tuple-element.104.refs_2_), channel_id=1, source_target_pairs={{0,24},{8,16},{16,8},{24,0},{1,25},{9,17},{17,9},{25,1},{2,26},{10... | collective-permute-start | bytes 24584 | tf_op jit(solution)/shard_map/ppermute | solution.py:412
  84.9 1.4 %collective-permute-start.28 = (f32[8,256]{1,0:T(8,128)S(1)}, f32[8,256]{1,0:T(8,128)S(1)}, u32[]{:S(2)}, u32[]{:S(2)}) collective-permute-start(f32[8,256]{1,0:T(8,128)S(1)} %collective-permute-done.26.refs_5_), channel_id=1, source_target_pairs={{0,8},{8,0},{16,24},{24,16},{1,9},{9,1},{17,25},{25,17},{2,10},{10... | collective-permute-start | bytes 24584 | tf_op jit(solution)/shard_map/ppermute | solution.py:412
  88.6 5.9 %collective-permute-start.31 = (bf16[128,256]{1,0:T(8,128)(2,1)S(1)}, bf16[128,256]{1,0:T(8,128)(2,1)S(1)}, u32[]{:S(2)}, u32[]{:S(2)}) collective-permute-start(bf16[128,256]{1,0:T(8,128)(2,1)S(1)} %get-tuple-element.114), channel_id=1, source_target_pairs={{0,3},{1,2},{2,1},{3,0},{4,7},{5,6},{6,5},{7,4},{8,11},{9,10},{10,... | collective-permute-start | bytes 196616 | tf_op jit(solution)/shard_map/ppermute | solution.py:412
  88.9 5.7 %collective-permute-start.30 = (bf16[128,256]{1,0:T(8,128)(2,1)S(1)}, bf16[128,256]{1,0:T(8,128)(2,1)S(1)}, u32[]{:S(2)}, u32[]{:S(2)}) collective-permute-start(bf16[128,256]{1,0:T(8,128)(2,1)S(1)} %get-tuple-element.114), channel_id=1, source_target_pairs={{0,2},{1,3},{2,0},{3,1},{4,6},{5,7},{6,4},{7,5},{8,10},{9,11},{10,... | collective-permute-start | bytes 196616 | tf_op jit(solution)/shard_map/ppermute | solution.py:412
  91.1 4.3 %collective-permute-start.29 = (bf16[128,256]{1,0:T(8,128)(2,1)S(1)}, bf16[128,256]{1,0:T(8,128)(2,1)S(1)}, u32[]{:S(2)}, u32[]{:S(2)}) collective-permute-start(bf16[128,256]{1,0:T(8,128)(2,1)S(1)} %get-tuple-element.114), channel_id=1, source_target_pairs={{0,1},{1,0},{2,3},{3,2},{4,5},{5,4},{6,7},{7,6},{8,9},{9,8},{10,11... | collective-permute-start | bytes 196616 | tf_op jit(solution)/shard_map/ppermute | solution.py:412
  95.4 5.4 %collective-permute-start.32 = (bf16[128,256]{1,0:T(8,128)(2,1)S(1)}, bf16[128,256]{1,0:T(8,128)(2,1)S(1)}, u32[]{:S(2)}, u32[]{:S(2)}) collective-permute-start(bf16[128,256]{1,0:T(8,128)(2,1)S(1)} %add_convert_fusion.refs_0_), channel_id=1, source_target_pairs={{0,4},{1,5},{2,6},{3,7},{4,0},{5,1},{6,2},{7,3},{8,12},{9,13},{10,... | collective-permute-start | bytes 196616 | tf_op jit(solution)/shard_map/ppermute | solution.py:412
  100.9 3.1 %collective-permute-start.34 = (f32[8,256]{1,0:T(8,128)S(1)}, f32[8,256]{1,0:T(8,128)S(1)}, u32[]{:S(2)}, u32[]{:S(2)}) collective-permute-start(f32[8,256]{1,0:T(8,128)S(1)} %get-tuple-element.117.refs_1_), channel_id=1, source_target_pairs={{0,24},{8,16},{16,8},{24,0},{1,25},{9,17},{17,9},{25,1},{2,26},{10... | collective-permute-start | bytes 24584 | tf_op jit(solution)/shard_map/ppermute | solution.py:412
  101.0 3.1 %collective-permute-start.33 = (f32[8,256]{1,0:T(8,128)S(1)}, f32[8,256]{1,0:T(8,128)S(1)}, u32[]{:S(2)}, u32[]{:S(2)}) collective-permute-start(f32[8,256]{1,0:T(8,128)S(1)} %get-tuple-element.117.refs_1_), channel_id=1, source_target_pairs={{0,8},{8,0},{16,24},{24,16},{1,9},{9,1},{17,25},{25,17},{2,10},{10... | collective-permute-start | bytes 24584 | tf_op jit(solution)/shard_map/ppermute | solution.py:412
  104.1 1.2 %collective-permute-start.35 = (f32[8,256]{1,0:T(8,128)S(1)}, f32[8,256]{1,0:T(8,128)S(1)}, u32[]{:S(2)}, u32[]{:S(2)}) collective-permute-start(f32[8,256]{1,0:T(8,128)S(1)} %collective-permute-done.34.refs_4_), channel_id=1, source_target_pairs={{0,8},{8,0},{16,24},{24,16},{1,9},{9,1},{17,25},{25,17},{2,10},{10... | collective-permute-start | bytes 24584 | tf_op jit(solution)/shard_map/ppermute | solution.py:412

commit v7 on v5

--- a/solution.py
+++ b/solution.py
@@ -123,59 +123,42 @@
     return copies
 
 
-def pack_kernel(jac_ref, e_ref, res_ref, count_ref, out_ref, pair_ref, tally_ref, wide_ref, sems):
-    last = jac_ref.shape[0] - 1
-    block = pl.ds(last, 1)
-    height = jac_ref.shape[1]
-    copies = fetch(
-        [
-            (jac_ref.at[block], out_ref.at[:, :height]),
-            (e_ref.at[block], pair_ref.at[0:1]),
-            (res_ref.at[block], pair_ref.at[1:2]),
-            (count_ref, tally_ref),
-        ],
-        sems,
-    )
-    for copy in copies[1:]:
+def pack_kernel(*refs):
+    far_refs, count_ref, scale_ref, refs = refs[:8], refs[8], refs[9], refs[10:]
+    near_refs, out_ref, live_ref, damp_ref = refs[:8], refs[8], refs[9], refs[10]
+    tally_ref, factor_ref, wide_ref, sems = refs[11:]
+    jac_ref, near_jac_ref, e_ref, res_ref = far_refs[0], near_refs[0], near_refs[1], near_refs[2]
+    last, height, ties = jac_ref.shape[0] - 1, jac_ref.shape[1], e_ref.shape[2]
+    pairs = list(zip(far_refs[1:], near_refs[1:])) + [(count_ref, tally_ref), (scale_ref, factor_ref)]
+    copies = fetch(pairs + [(jac_ref.at[pl.ds(last, 1)], out_ref.at[:, :height]), (jac_ref, near_jac_ref)], sems)
+    for copy in copies[: len(pairs)]:
         copy.wait()
-    ties = pair_ref.shape[2]
-    lane = lax.broadcasted_iota(jnp.int32, (1, ties), 1)
     wide_ref[...] = jnp.zeros_like(wide_ref)
-    for i in range(2):
-        rest = pair_ref[i]
+    for i, ref in enumerate((e_ref, res_ref)):
+        rest = ref[last]
         for j in range(3):
             part = rest.astype(BF16).astype(F32)
             rest = rest - part
             wide_ref[4 * j + 2 * i : 4 * j + 2 * i + 2, :ties] = part
-    wide_ref[12:13, :ties] = jnp.where(lane < tally_ref[0, last], 1.0, 0.0)
+    live_rows(tally_ref, live_ref)
+    wide_ref[12:13, :ties] = live_ref[last : last + 1, :]
     out_ref[0, height:] = wide_ref[...].astype(BF16)
-    copies[0].wait()
+    for i in range(damp_ref.shape[0]):
+        damp_ref[i : i + 1, :] = jnp.full((1, damp_ref.shape[1]), factor_ref[0, i], F32)
+    for copy in copies[len(pairs) :]:
+        copy.wait()
 
 
 def setup_kernel(cjac_ref, ajac_ref, *refs):
-    far_refs, refs = refs[:9], refs[9:]
-    (out_cjac_ref, out_ajac_ref, coef_ref, put1_ref, put2_ref, pick1_ref, pick2_ref, t1_ref, t2_ref, damp_ref) = refs[:10]
-    live_ref, q1_ref, q2_ref, index_ref, sems = refs[10:15]
-    near_refs, near_sems = refs[15:24], refs[24]
-    near = fetch(list(zip(far_refs, near_refs)), near_sems)
-    ce_ref, cres_ref, ae_ref, ares_ref, count_ref, own_ref, group_ref, other_ref, scale_ref = near_refs
-    copies = []
-    for ref, out_ref in ((cjac_ref, out_cjac_ref), (ajac_ref, out_ajac_ref)):
-        for at in range(0, ref.shape[0], OCTET):
-            part = pl.ds(at, OCTET)
-            copies.append(pltpu.make_async_copy(ref.at[part], out_ref.at[part], sems.at[len(copies)]))
-    for copy in copies[:2]:
-        copy.start()
+    ae_ref, ares_ref, ce_ref, cres_ref, own_ref, group_ref, other_ref, lived_ref = refs[:8]
+    out_cjac_ref, coef_ref, put1_ref, put2_ref, pick1_ref, pick2_ref, t1_ref, t2_ref = refs[8:16]
+    live_ref, q1_ref, q2_ref, index_ref, sems = refs[16:]
+    parts = [pl.ds(at, OCTET) for at in range(0, cjac_ref.shape[0], OCTET)]
+    copies = fetch([(cjac_ref.at[part], out_cjac_ref.at[part]) for part in parts], sems)
     links, scenes = cjac_ref.shape[0], ajac_ref.shape[0]
     blocks = links + scenes
-    for copy in near:
-        copy.wait()
-    for copy in copies[2:]:
-        copy.start()
     live_ref[0:links] = jnp.ones((links, live_ref.shape[1]), F32)
-    live_rows(count_ref, live_ref.at[links:blocks])
-    for i in range(scenes):
-        damp_ref[i : i + 1, :] = jnp.full((1, damp_ref.shape[1]), scale_ref[0, i], F32)
+    live_ref[links:blocks] = lived_ref[...]
     for rows, e_ref, res_ref in ((slice(0, links), ce_ref, cres_ref), (slice(links, blocks), ae_ref, ares_ref)):
         c = elimination(e_ref[:, 0, :], e_ref[:, 1, :], live_ref[rows])
         for i in range(3):
@@ -197,13 +180,12 @@
         put_ref[...] = table[:, :slots].astype(BF16)
         pick_ref[...] = table.T[:slots].astype(BF16)
 
-    octet = 0
-    for ref in (out_cjac_ref, out_ajac_ref):
+    for ref, slot in ((ajac_ref, links), (out_cjac_ref, 0)):
         for at in range(0, ref.shape[0], OCTET):
-            copies[octet].wait()
-            rows = pl.ds(octet * OCTET, OCTET)
+            if ref is out_cjac_ref:
+                copies[at // OCTET].wait()
+            rows = pl.ds(slot + at, OCTET)
             t1_ref[rows], t2_ref[rows] = terms(q1_ref[rows], q2_ref[rows], ref, at, OCTET)
-            octet += 1
 
 
 def rhs_kernel(coef_ref, t1_ref, t2_ref, edge_ref, put1_ref, put2_ref, out_ref, out_coef_ref, ejac_ref, all1_ref, all2_ref):
@@ -437,46 +419,31 @@
     lanes = -(-slots // 128) * 128
     term_space = [((slots, width), F32)] * 2
     sems = pltpu.SemaphoreType.DMA
-    pack_args = (ajac, along_e[0], along_res[0], along_count)
-    edge = call(
+    blocks = links + scenes
+    small = [ajac, along_e[0], along_res[0], cross_e[0], cross_res[0], cross_own, cross_group[:, :, 0], cross_other]
+    near = call(
         pack_kernel,
-        [((1, 2 * ties + 2 * OCTET, width), BF16)],
-        [((2, 2, ties), F32), pltpu.SMEM((1, scenes), jnp.int32), ((2 * OCTET, width), F32), sems((4,))],
+        [(a.shape, a.dtype) for a in small]
+        + [((1, 2 * ties + 2 * OCTET, width), BF16), ((scenes, ties), F32), (own, F32)],
+        [pltpu.SMEM((1, scenes), jnp.int32), pltpu.SMEM((1, scenes), F32)]
+        + [((2 * OCTET, width), F32), sems((len(small) + 3,))],
         "pack",
-        pack_args,
-        spaces={i: pltpu.HBM for i in range(4)},
-    )
-    edge = pass_on(edge[0])
-    blocks = links + scenes
+        small + [along_count, damping],
+        spaces={i: pltpu.HBM for i in range(len(small) + 2)},
+    )
+    ajac, edge, live, damp = near[0], pass_on(near[8]), near[9], near[10]
     part_tie = (blocks, ties)
     put = ((rows, slots), BF16)
     pick = ((slots, rows), BF16)
-    cjac, ajac, coef, put1, put2, pick1, pick2, t1, t2, damp = call(
+    term = ((blocks, width), F32)
+    cjac, coef, put1, put2, pick1, pick2, t1, t2 = call(
         setup_kernel,
-        [
-            (cjac.shape, BF16),
-            (ajac.shape, BF16),
-            ((3,) + part_tie, F32),
-            put,
-            put,
-            pick,
-            pick,
-            ((blocks, width), F32),
-            ((blocks, width), F32),
-            (own, F32),
-        ],
-        [(part_tie, F32)] * 3
-        + [((OCTET, lanes), jnp.int32), sems((blocks // OCTET,))]
-        + [((links, 2, ties), F32)] * 2
-        + [((scenes, 2, ties), F32)] * 2
-        + [pltpu.SMEM((1, scenes), jnp.int32)]
-        + [((1, links), jnp.int32)] * 3
-        + [pltpu.SMEM((1, scenes), F32), sems((9,))],
+        [(cjac.shape, BF16), ((3,) + part_tie, F32), put, put, pick, pick, term, term],
+        [(part_tie, F32)] * 3 + [((OCTET, lanes), jnp.int32), sems((links // OCTET,))],
         "setup",
-        (cjac, ajac, cross_e[0], cross_res[0], along_e[0], along_res[0], along_count)
-        + (cross_own, cross_group[:, :, 0], cross_other, damping),
+        [cjac, *near[:8], live],
         work,
-        {i: pltpu.HBM for i in range(11)},
+        {0: pltpu.HBM},
     )
 
     def turn(start, count, refs, after):

time: 103 us -> 104 us (level)
  transfers between devices with their start and end apart: 36 -> 36, of which waited for: 19 -> 19; matrix products, arithmetic and copies ran while one was open for 0% -> 0% of each run, Pallas kernels for 21% -> 20%
where the time goes in v7:
time: 104 us; the launch traced here: 103 us
  starting transfers between devices  36.5 us (35%)
  waiting for transfers between devices  33.5 us (32%)
  Pallas kernels  32.2 us (31%)
    pallas_call x20, Pallas kernels, call(): pl.pallas_call(kernel, out_shape=[jax.ShapeDtypeStruct(*o) for o in outs]...  32.2 us
    ppermute x20, waiting for transfers between devices, swap(): lax.ppermute(block, axis, [(i, i ^ mask) for i in range(lax.axis_size(axi...  31.6 us
    ppermute x20, starting transfers between devices, swap(): lax.ppermute(block, axis, [(i, i ^ mask) for i in range(lax.axis_size(axi...  26.4 us
    ppermute x15, starting transfers between devices, orbit_packets(): lax.ppermute(packet, 'orbit', [(i, i ^ mask) for i in range(n)])  9.59 us
  transfers between devices with their start and end apart: 36, of which 19 were waited for; matrix products, arithmetic and copies ran while one was open for 0% of the time, Pallas kernels for 20%

profile of v7, /device:TPU:0, one launch (start us, length us, event | category | flops | bytes accessed | tf_op | source)
XLA Modules:
  0.0 103.3 jit_solution(16290524292519983439)
XLA Ops:
  0.6 1.9 %pack.1 = (bf16[16,256,256]{2,1,0:T(8,128)(2,1)S(1)}, f32[16,2,128]{2,1,0:T(2,128)S(1)}, f32[16,2,128]{2,1,0:T(2,128)S(1)}, f32[64,2,128]{2,1,0:T(2,128)S(1)}, f...) custom-call(bf16[16,256,256]{2,1,0:T(8,128)(2,1)} %bitcast.10, ...), custom_call_target="tpu_custom_call" | custom-call | bytes 2261888 | tf_op jit(solution)/shard_map/pack/pallas_call | solution.py:342
  2.6 0.5 collective-permute-start
  3.1 4.8 %setup.1 = (bf16[64,256,256]{2,1,0:T(8,128)(2,1)S(1)}, f32[3,80,128]{2,1,0:T(8,128)S(1)}, bf16[128,88]{1,0:T(8,128)(2,1)S(1)}, bf16[128,88]{1,0:T(8,128)(2,1)S(1...) custom-call(bf16[64,256,256]{2,1,0:T(8,128)(2,1)} %bitcast.9, ...), custom_call_target="tpu_custom_call" | custom-call | flops 339738624 | bytes 10658560 | tf_op jit(solution)/shard_map/setup/pallas_call | solution.py:342
  7.9 0.4 rhs.1
  8.3 3.6 %collective-permute-start.3 = (bf16[128,256]{1,0:T(8,128)(2,1)S(1)}, bf16[128,256]{1,0:T(8,128)(2,1)S(1)}, u32[]{:S(2)}, u32[]{:S(2)}) collective-permute-start(bf16[128,256]{1,0:T(8,128)(2,1)S(1)} %get-tuple-element.79.after_ref), channel_id=1, source_target_pairs={{0,3},{1,2},{2,1},{3,0},{4,7},{5,6},{6,5},{7,4},{8,11},{9,10},{10,... | collective-permute-start | bytes 196616 | tf_op jit(solution)/shard_map/ppermute | solution.py:381
  11.9 0.4 collective-permute-start.2
  12.5 2.8 %turn.3.refs_0_ = bf16[32,256,256]{2,1,0:T(8,128)(2,1)S(1)} custom-call(bf16[128,256]{1,0:T(8,128)(2,1)S(1)} %get-tuple-element.79.after_ref, bf16[64,256,256]{2,1,0:T(8,128)(2,1)S(1)} %get-tuple-element.80.refs_0_.refs_9_), custom_call_target="tpu_custom_call" | custom-call | flops 135895456 | bytes 8454144 | tf_op jit(solution)/shard_map/turn/pallas_call | solution.py:342
  15.4 1.2 %collective-permute-done.2 = bf16[128,256]{1,0:T(8,128)(2,1)S(1)} collective-permute-done((bf16[128,256]{1,0:T(8,128)(2,1)S(1)}, bf16[128,256]{1,0:T(8,128)(2,1)S(1)}, u32[]{:S(2)}, u32[]{:S(2)}) %collective-permute-start.2) | collective-permute-done | bytes 65568 | tf_op jit(solution)/shard_map/ppermute | solution.py:381
  16.5 0.7 collective-permute-done.1
  17.3 2.7 %collective-permute-start.4 = (bf16[128,256]{1,0:T(8,128)(2,1)S(1)}, bf16[128,256]{1,0:T(8,128)(2,1)S(1)}, u32[]{:S(2)}, u32[]{:S(2)}) collective-permute-start(bf16[128,256]{1,0:T(8,128)(2,1)S(1)} %add_convert_fusion.4.refs_0_.after_ref), channel_id=1, source_target_pairs={{0,4},{1,5},{2,6},{3,7},{4,0},{5,1},{6,2},{7,3},{8,12},{9,13},{10,... | collective-permute-start | bytes 196616 | tf_op jit(solution)/shard_map/ppermute | solution.py:381
  20.0 2.8 %turn.4.refs_1_ = bf16[32,256,256]{2,1,0:T(8,128)(2,1)S(1)} custom-call(bf16[128,256]{1,0:T(8,128)(2,1)S(1)} %add_convert_fusion.4.refs_0_.after_ref, bf16[64,256,256]{2,1,0:T(8,128)(2,1)S(1)} %get-tuple-element.80.refs_0_.refs_9_), custom_call_target="tpu_custom_call" | custom-call | flops 135895456 | bytes 8454144 | tf_op jit(solution)/shard_map/turn/pallas_call | solution.py:342
  22.8 1.2 %collective-permute-done.4.refs_1_ = bf16[128,256]{1,0:T(8,128)(2,1)S(1)} collective-permute-done((bf16[128,256]{1,0:T(8,128)(2,1)S(1)}, bf16[128,256]{1,0:T(8,128)(2,1)S(1)}, u32[]{:S(2)}, u32[]{:S(2)}) %collective-permute-start.4) | collective-permute-done | bytes 65568 | tf_op jit(solution)/shard_map/ppermute | solution.py:381
  24.0 0.3 collective-permute-start.6
  24.4 1.5 %collective-permute-start.5 = (f32[8,256]{1,0:T(8,128)S(1)}, f32[8,256]{1,0:T(8,128)S(1)}, u32[]{:S(2)}, u32[]{:S(2)}) collective-permute-start(f32[8,256]{1,0:T(8,128)S(1)} %get-tuple-element.87.refs_1_), channel_id=1, source_target_pairs={{0,8},{8,0},{16,24},{24,16},{1,9},{9,1},{17,25},{25,17},{2,10},{10... | collective-permute-start | bytes 24584 | tf_op jit(solution)/shard_map/ppermute | solution.py:386
  25.9 2.3 %project.4.refs_0_ = f32[88,256]{1,0:T(8,128)S(1)} custom-call(f32[128,256]{1,0:T(8,128)S(1)} %get-tuple-element.82.field_ref.refs_12_.refs_2_, bf16[88,128]{1,0:T(8,128)(2,1)S(1)} %get-tuple-element.83.pick1_ref, bf16[88,128]{1,0:T(8,128)(2,1)S(1)} %get-tuple-element.84.pick2_ref, bf16[32,256,256]{2,1,0:T(8,128)(2,1)S(1)} %turn.3.refs_0_, ...), custom_call_target="tpu_custom_call" | custom-call | flops 339738624 | bytes 10792960 | tf_op jit(solution)/shard_map/project/pallas_call | solution.py:342
  28.2 1.9 %step.4 = (bf16[128,256]{1,0:T(8,128)(2,1)S(1)}, f32[88,256]{1,0:T(8,128)S(1)}) custom-call(f32[88,256]{1,0:T(8,128)S(1)} %project.4.refs_0_, f32[8,256]{1,0:T(8,128)S(1)} %get-tuple-element.87.refs_1_, f32[8,256]{1,0:T(8,128)S(1)} %collective-permute-done.5.refs_2_, f32[8,256]{1,0:T(8,128)S(1)} %collective-permute-done.6.refs_3_, ...), custom_call_target="tpu_custom_call" | custom-call | flops 339738624 | bytes 11067392 | tf_op jit(solution)/shard_map/step/pallas_call | solution.py:342
  30.1 0.9 collective-permute-start.10
  31.1 1.5 %collective-permute-start.9 = (bf16[128,256]{1,0:T(8,128)(2,1)S(1)}, bf16[128,256]{1,0:T(8,128)(2,1)S(1)}, u32[]{:S(2)}, u32[]{:S(2)}) collective-permute-start(bf16[128,256]{1,0:T(8,128)(2,1)S(1)} %get-tuple-element.90.after_ref), channel_id=1, source_target_pairs={{0,2},{1,3},{2,0},{3,1},{4,6},{5,7},{6,4},{7,5},{8,10},{9,11},{10,... | collective-permute-start | bytes 196616 | tf_op jit(solution)/shard_map/ppermute | solution.py:381
  32.5 1.2 %collective-permute-start.8 = (bf16[128,256]{1,0:T(8,128)(2,1)S(1)}, bf16[128,256]{1,0:T(8,128)(2,1)S(1)}, u32[]{:S(2)}, u32[]{:S(2)}) collective-permute-start(bf16[128,256]{1,0:T(8,128)(2,1)S(1)} %get-tuple-element.90.after_ref), channel_id=1, source_target_pairs={{0,1},{1,0},{2,3},{3,2},{4,5},{5,4},{6,7},{7,6},{8,9},{9,8},{10,11... | collective-permute-start | bytes 196616 | tf_op jit(solution)/shard_map/ppermute | solution.py:381
  33.7 2.2 %collective-permute-done.10 = bf16[128,256]{1,0:T(8,128)(2,1)S(1)} collective-permute-done((bf16[128,256]{1,0:T(8,128)(2,1)S(1)}, bf16[128,256]{1,0:T(8,128)(2,1)S(1)}, u32[]{:S(2)}, u32[]{:S(2)}) %collective-permute-start.10) | collective-permute-done | bytes 65568 | tf_op jit(solution)/shard_map/ppermute | solution.py:381
  35.9 0.9 collective-permute-done.8
  36.8 2.0 %collective-permute-start.11 = (bf16[128,256]{1,0:T(8,128)(2,1)S(1)}, bf16[128,256]{1,0:T(8,128)(2,1)S(1)}, u32[]{:S(2)}, u32[]{:S(2)}) collective-permute-start(bf16[128,256]{1,0:T(8,128)(2,1)S(1)} %add_convert_fusion.3.refs_0_), channel_id=1, source_target_pairs={{0,4},{1,5},{2,6},{3,7},{4,0},{5,1},{6,2},{7,3},{8,12},{9,13},{10,... | collective-permute-start | bytes 196616 | tf_op jit(solution)/shard_map/ppermute | solution.py:381
  38.8 1.6 %turn.5 = (bf16[16,256,256]{2,1,0:T(8,128)(2,1)S(1)}, bf16[1,256,256]{2,1,0:T(8,128)(2,1)S(1)}) custom-call(bf16[128,256]{1,0:T(8,128)(2,1)S(1)} %get-tuple-element.90.after_ref, bf16[16,256,256]{2,1,0:T(8,128)(2,1)S(1)} %get-tuple-element.64.ajac_ref.refs_2_.refs_10_.refs_0_, bf16[1,256,256]{2,1,0:T(8,128)(2,1)S(1)} %get-tuple-element.86.refs_3_.refs_11_.refs_1_), custom_call_target="tpu_custom_call" | custom-call | flops 72194456 | bytes 2293760 | tf_op jit(solution)/shard_map/turn/pallas_call | solution.py:342
  40.5 2.3 %collective-permute-done.11.refs_1_ = bf16[128,256]{1,0:T(8,128)(2,1)S(1)} collective-permute-done((bf16[128,256]{1,0:T(8,128)(2,1)S(1)}, bf16[128,256]{1,0:T(8,128)(2,1)S(1)}, u32[]{:S(2)}, u32[]{:S(2)}) %collective-permute-start.11) | collective-permute-done | bytes 65568 | tf_op jit(solution)/shard_map/ppermute | solution.py:381
  43.0 1.2 %collective-permute-start.13 = (f32[8,256]{1,0:T(8,128)S(1)}, f32[8,256]{1,0:T(8,128)S(1)}, u32[]{:S(2)}, u32[]{:S(2)}) collective-permute-start(f32[8,256]{1,0:T(8,128)S(1)} %get-tuple-element.94.refs_1_), channel_id=1, source_target_pairs={{0,16},{8,24},{16,0},{24,8},{1,17},{9,25},{17,1},{25,9},{2,18},{10... | collective-permute-start | bytes 24584 | tf_op jit(solution)/shard_map/ppermute | solution.py:386
  44.3 0.6 collective-permute-start.12
  44.9 2.0 %project.5.refs_0_ = f32[88,256]{1,0:T(8,128)S(1)} custom-call(f32[128,256]{1,0:T(8,128)S(1)} %get-tuple-element.91.field_ref.refs_13_, bf16[88,128]{1,0:T(8,128)(2,1)S(1)} %get-tuple-element.83.pick1_ref, bf16[88,128]{1,0:T(8,128)(2,1)S(1)} %get-tuple-element.84.pick2_ref, bf16[32,256,256]{2,1,0:T(8,128)(2,1)S(1)} %turn.3.refs_0_, ...), custom_call_target="tpu_custom_call" | custom-call | flops 339738624 | bytes 10792960 | tf_op jit(solution)/shard_map/project/pallas_call | solution.py:342
  47.0 1.9 %step.5 = (bf16[128,256]{1,0:T(8,128)(2,1)S(1)}, f32[88,256]{1,0:T(8,128)S(1)}, f32[128,256]{1,0:T(8,128)S(1)}, f32[128,256]{1,0:T(8,128)S(1)}, f32[88,256]{1,0:...) custom-call(f32[88,256]{1,0:T(8,128)S(1)} %project.5.refs_0_, ...), custom_call_target="tpu_custom_call" | custom-call | flops 339738624 | bytes 11304960 | tf_op jit(solution)/shard_map/step/pallas_call | solution.py:342
  48.9 1.0 %collective-permute-start.17 = (bf16[128,256]{1,0:T(8,128)(2,1)S(1)}, bf16[128,256]{1,0:T(8,128)(2,1)S(1)}, u32[]{:S(2)}, u32[]{:S(2)}) collective-permute-start(bf16[128,256]{1,0:T(8,128)(2,1)S(1)} %get-tuple-element.96), channel_id=1, source_target_pairs={{0,3},{1,2},{2,1},{3,0},{4,7},{5,6},{6,5},{7,4},{8,11},{9,10},{10,... | collective-permute-start | bytes 196616 | tf_op jit(solution)/shard_map/ppermute | solution.py:381
  49.9 1.6 %collective-permute-start.16 = (bf16[128,256]{1,0:T(8,128)(2,1)S(1)}, bf16[128,256]{1,0:T(8,128)(2,1)S(1)}, u32[]{:S(2)}, u32[]{:S(2)}) collective-permute-start(bf16[128,256]{1,0:T(8,128)(2,1)S(1)} %get-tuple-element.96), channel_id=1, source_target_pairs={{0,2},{1,3},{2,0},{3,1},{4,6},{5,7},{6,4},{7,5},{8,10},{9,11},{10,... | collective-permute-start | bytes 196616 | tf_op jit(solution)/shard_map/ppermute | solution.py:381
  51.6 0.9 collective-permute-start.15
  52.4 2.2 %collective-permute-done.17 = bf16[128,256]{1,0:T(8,128)(2,1)S(1)} collective-permute-done((bf16[128,256]{1,0:T(8,128)(2,1)S(1)}, bf16[128,256]{1,0:T(8,128)(2,1)S(1)}, u32[]{:S(2)}, u32[]{:S(2)}) %collective-permute-start.17) | collective-permute-done | bytes 65568 | tf_op jit(solution)/shard_map/ppermute | solution.py:381
  54.6 0.3 collective-permute-done.16
  54.9 0.9 collective-permute-done.15
  55.9 1.4 %collective-permute-start.18 = (bf16[128,256]{1,0:T(8,128)(2,1)S(1)}, bf16[128,256]{1,0:T(8,128)(2,1)S(1)}, u32[]{:S(2)}, u32[]{:S(2)}) collective-permute-start(bf16[128,256]{1,0:T(8,128)(2,1)S(1)} %add_convert_fusion.2.refs_0_), channel_id=1, source_target_pairs={{0,4},{1,5},{2,6},{3,7},{4,0},{5,1},{6,2},{7,3},{8,12},{9,13},{10,... | collective-permute-start | bytes 196616 | tf_op jit(solution)/shard_map/ppermute | solution.py:381
  57.3 4.4 %collective-permute-done.18.refs_1_ = bf16[128,256]{1,0:T(8,128)(2,1)S(1)} collective-permute-done((bf16[128,256]{1,0:T(8,128)(2,1)S(1)}, bf16[128,256]{1,0:T(8,128)(2,1)S(1)}, u32[]{:S(2)}, u32[]{:S(2)}) %collective-permute-start.18) | collective-permute-done | bytes 65568 | tf_op jit(solution)/shard_map/ppermute | solution.py:381
  61.9 0.8 collective-permute-start.20
  62.8 1.0 collective-permute-start.19
  63.8 2.0 %project.6.refs_0_ = f32[88,256]{1,0:T(8,128)S(1)} custom-call(f32[128,256]{1,0:T(8,128)S(1)} %get-tuple-element.98.field_ref.refs_13_, bf16[88,128]{1,0:T(8,128)(2,1)S(1)} %get-tuple-element.83.pick1_ref, bf16[88,128]{1,0:T(8,128)(2,1)S(1)} %get-tuple-element.84.pick2_ref, bf16[32,256,256]{2,1,0:T(8,128)(2,1)S(1)} %turn.3.refs_0_, ...), custom_call_target="tpu_custom_call" | custom-call | flops 339738624 | bytes 10792960 | tf_op jit(solution)/shard_map/project/pallas_call | solution.py:342
  65.8 1.9 %step.6 = (bf16[128,256]{1,0:T(8,128)(2,1)S(1)}, f32[88,256]{1,0:T(8,128)S(1)}, f32[128,256]{1,0:T(8,128)S(1)}, f32[128,256]{1,0:T(8,128)S(1)}, f32[88,256]{1,0:...) custom-call(f32[88,256]{1,0:T(8,128)S(1)} %project.6.refs_0_, ...), custom_call_target="tpu_custom_call" | custom-call | flops 339738624 | bytes 11546624 | tf_op jit(solution)/shard_map/step/pallas_call | solution.py:342
  67.8 0.3 collective-permute-start.24
  68.1 2.1 %collective-permute-start.23 = (bf16[128,256]{1,0:T(8,128)(2,1)S(1)}, bf16[128,256]{1,0:T(8,128)(2,1)S(1)}, u32[]{:S(2)}, u32[]{:S(2)}) collective-permute-start(bf16[128,256]{1,0:T(8,128)(2,1)S(1)} %get-tuple-element.106), channel_id=1, source_target_pairs={{0,2},{1,3},{2,0},{3,1},{4,6},{5,7},{6,4},{7,5},{8,10},{9,11},{10,... | collective-permute-start | bytes 196616 | tf_op jit(solution)/shard_map/ppermute | solution.py:381
  70.2 1.1 %collective-permute-start.22 = (bf16[128,256]{1,0:T(8,128)(2,1)S(1)}, bf16[128,256]{1,0:T(8,128)(2,1)S(1)}, u32[]{:S(2)}, u32[]{:S(2)}) collective-permute-start(bf16[128,256]{1,0:T(8,128)(2,1)S(1)} %get-tuple-element.106), channel_id=1, source_target_pairs={{0,1},{1,0},{2,3},{3,2},{4,5},{5,4},{6,7},{7,6},{8,9},{9,8},{10,11... | collective-permute-start | bytes 196616 | tf_op jit(solution)/shard_map/ppermute | solution.py:381
  71.3 2.2 %collective-permute-done.24 = bf16[128,256]{1,0:T(8,128)(2,1)S(1)} collective-permute-done((bf16[128,256]{1,0:T(8,128)(2,1)S(1)}, bf16[128,256]{1,0:T(8,128)(2,1)S(1)}, u32[]{:S(2)}, u32[]{:S(2)}) %collective-permute-start.24) | collective-permute-done | bytes 65568 | tf_op jit(solution)/shard_map/ppermute | solution.py:381
  73.6 0.9 collective-permute-done.22
  74.5 1.0 collective-permute-start.25
  75.5 4.4 %collective-permute-done.25.refs_1_ = bf16[128,256]{1,0:T(8,128)(2,1)S(1)} collective-permute-done((bf16[128,256]{1,0:T(8,128)(2,1)S(1)}, bf16[128,256]{1,0:T(8,128)(2,1)S(1)}, u32[]{:S(2)}, u32[]{:S(2)}) %collective-permute-start.25) | collective-permute-done | bytes 65568 | tf_op jit(solution)/shard_map/ppermute | solution.py:381
  80.1 1.1 %collective-permute-start.27 = (f32[8,256]{1,0:T(8,128)S(1)}, f32[8,256]{1,0:T(8,128)S(1)}, u32[]{:S(2)}, u32[]{:S(2)}) collective-permute-start(f32[8,256]{1,0:T(8,128)S(1)} %get-tuple-element.109.refs_1_), channel_id=1, source_target_pairs={{0,16},{8,24},{16,0},{24,8},{1,17},{9,25},{17,1},{25,9},{2,18},{10... | collective-permute-start | bytes 24584 | tf_op jit(solution)/shard_map/ppermute | solution.py:386
  81.3 0.7 collective-permute-start.26
  82.0 2.0 %project.7.refs_0_ = f32[88,256]{1,0:T(8,128)S(1)} custom-call(f32[128,256]{1,0:T(8,128)S(1)} %get-tuple-element.108.field_ref.refs_13_, bf16[88,128]{1,0:T(8,128)(2,1)S(1)} %get-tuple-element.83.pick1_ref, bf16[88,128]{1,0:T(8,128)(2,1)S(1)} %get-tuple-element.84.pick2_ref, bf16[32,256,256]{2,1,0:T(8,128)(2,1)S(1)} %turn.3.refs_0_, ...), custom_call_target="tpu_custom_call" | custom-call | flops 339738624 | bytes 10792960 | tf_op jit(solution)/shard_map/project/pallas_call | solution.py:342
  84.0 2.4 %step.7 = (bf16[128,256]{1,0:T(8,128)(2,1)S(1)}, f32[88,256]{1,0:T(8,128)}, f32[128,256]{1,0:T(8,128)S(1)}, f32[128,256]{1,0:T(8,128)S(1)}, f32[88,256]{1,0:T(8,...) custom-call(f32[88,256]{1,0:T(8,128)S(1)} %project.7.refs_0_, ...), custom_call_target="tpu_custom_call" | custom-call | flops 339738624 | bytes 11546624 | tf_op jit(solution)/shard_map/step/pallas_call | solution.py:342
  86.4 0.4 collective-permute-start.31
  86.8 2.1 %collective-permute-start.30 = (bf16[128,256]{1,0:T(8,128)(2,1)S(1)}, bf16[128,256]{1,0:T(8,128)(2,1)S(1)}, u32[]{:S(2)}, u32[]{:S(2)}) collective-permute-start(bf16[128,256]{1,0:T(8,128)(2,1)S(1)} %get-tuple-element.116), channel_id=1, source_target_pairs={{0,2},{1,3},{2,0},{3,1},{4,6},{5,7},{6,4},{7,5},{8,10},{9,11},{10,... | collective-permute-start | bytes 196616 | tf_op jit(solution)/shard_map/ppermute | solution.py:381
  89.0 0.9 collective-permute-start.29
  89.9 2.2 %collective-permute-done.31 = bf16[128,256]{1,0:T(8,128)(2,1)S(1)} collective-permute-done((bf16[128,256]{1,0:T(8,128)(2,1)S(1)}, bf16[128,256]{1,0:T(8,128)(2,1)S(1)}, u32[]{:S(2)}, u32[]{:S(2)}) %collective-permute-start.31) | collective-permute-done | bytes 65568 | tf_op jit(solution)/shard_map/ppermute | solution.py:381
  92.1 0.3 collective-permute-done.30
  92.4 0.9 collective-permute-done.29
  93.3 1.0 collective-permute-start.32
  94.3 4.4 %collective-permute-done.32.refs_1_ = bf16[128,256]{1,0:T(8,128)(2,1)S(1)} collective-permute-done((bf16[128,256]{1,0:T(8,128)(2,1)S(1)}, bf16[128,256]{1,0:T(8,128)(2,1)S(1)}, u32[]{:S(2)}, u32[]{:S(2)}) %collective-permute-start.32) | collective-permute-done | bytes 65568 | tf_op jit(solution)/shard_map/ppermute | solution.py:381
  98.9 1.1 %collective-permute-start.34 = (f32[8,256]{1,0:T(8,128)S(1)}, f32[8,256]{1,0:T(8,128)S(1)}, u32[]{:S(2)}, u32[]{:S(2)}) collective-permute-start(f32[8,256]{1,0:T(8,128)S(1)} %get-tuple-element.119.refs_1_), channel_id=1, source_target_pairs={{0,16},{8,24},{16,0},{24,8},{1,17},{9,25},{17,1},{25,9},{2,18},{10... | collective-permute-start | bytes 24584 | tf_op jit(solution)/shard_map/ppermute | solution.py:386
  100.0 0.7 collective-permute-start.33
  100.8 1.2 %collective-permute-done.35.refs_4_ = f32[8,256]{1,0:T(8,128)S(1)} collective-permute-done((f32[8,256]{1,0:T(8,128)S(1)}, f32[8,256]{1,0:T(8,128)S(1)}, u32[]{:S(2)}, u32[]{:S(2)}) %collective-permute-start.35) | collective-permute-done | bytes 8224 | tf_op jit(solution)/shard_map/ppermute | solution.py:386
  102.0 0.7 collective-permute-done.34.refs_3_
  102.6 0.6 final.1
  (34 shorter events, 1.6 us)
Async XLA Ops:
  2.6 5.4 %collective-permute-start = (bf16[1,272,256]{2,1,0:T(8,128)(2,1)S(1)}, bf16[1,272,256]{2,1,0:T(8,128)(2,1)S(1)}, u32[]{:S(2)}, u32[]{:S(2)}) collective-permute-start(bf16[1,272,256]{2,1,0:T(8,128)(2,1)S(1)} %get-tuple-element.76), channel_id=1, source_target_pairs={{0,8},{8,16},{16,24},{24,0},{1,9},{9,17},{17,25},{25,1},{2,10},{10... | collective-permute-start | bytes 417800 | tf_op jit(solution)/shard_map/ppermute | solution.py:412
  8.3 7.1 %collective-permute-start.3 = (bf16[128,256]{1,0:T(8,128)(2,1)S(1)}, bf16[128,256]{1,0:T(8,128)(2,1)S(1)}, u32[]{:S(2)}, u32[]{:S(2)}) collective-permute-start(bf16[128,256]{1,0:T(8,128)(2,1)S(1)} %get-tuple-element.79.after_ref), channel_id=1, source_target_pairs={{0,3},{1,2},{2,1},{3,0},{4,7},{5,6},{6,5},{7,4},{8,11},{9,10},{10,... | collective-permute-start | bytes 196616 | tf_op jit(solution)/shard_map/ppermute | solution.py:381
  11.9 4.6 %collective-permute-start.2 = (bf16[128,256]{1,0:T(8,128)(2,1)S(1)}, bf16[128,256]{1,0:T(8,128)(2,1)S(1)}, u32[]{:S(2)}, u32[]{:S(2)}) collective-permute-start(bf16[128,256]{1,0:T(8,128)(2,1)S(1)} %get-tuple-element.79.after_ref), channel_id=1, source_target_pairs={{0,2},{1,3},{2,0},{3,1},{4,6},{5,7},{6,4},{7,5},{8,10},{9,11},{10,... | collective-permute-start | bytes 196616 | tf_op jit(solution)/shard_map/ppermute | solution.py:381
  12.4 4.9 %collective-permute-start.1 = (bf16[128,256]{1,0:T(8,128)(2,1)S(1)}, bf16[128,256]{1,0:T(8,128)(2,1)S(1)}, u32[]{:S(2)}, u32[]{:S(2)}) collective-permute-start(bf16[128,256]{1,0:T(8,128)(2,1)S(1)} %get-tuple-element.79.after_ref), channel_id=1, source_target_pairs={{0,1},{1,0},{2,3},{3,2},{4,5},{5,4},{6,7},{7,6},{8,9},{9,8},{10,11... | collective-permute-start | bytes 196616 | tf_op jit(solution)/shard_map/ppermute | solution.py:381
  17.3 6.6 %collective-permute-start.4 = (bf16[128,256]{1,0:T(8,128)(2,1)S(1)}, bf16[128,256]{1,0:T(8,128)(2,1)S(1)}, u32[]{:S(2)}, u32[]{:S(2)}) collective-permute-start(bf16[128,256]{1,0:T(8,128)(2,1)S(1)} %add_convert_fusion.4.refs_0_.after_ref), channel_id=1, source_target_pairs={{0,4},{1,5},{2,6},{3,7},{4,0},{5,1},{6,2},{7,3},{8,12},{9,13},{10,... | collective-permute-start | bytes 196616 | tf_op jit(solution)/shard_map/ppermute | solution.py:381
  24.0 4.2 %collective-permute-start.7 = (f32[8,256]{1,0:T(8,128)S(1)}, f32[8,256]{1,0:T(8,128)S(1)}, u32[]{:S(2)}, u32[]{:S(2)}) collective-permute-start(f32[8,256]{1,0:T(8,128)S(1)} %get-tuple-element.87.refs_1_), channel_id=1, source_target_pairs={{0,24},{8,16},{16,8},{24,0},{1,25},{9,17},{17,9},{25,1},{2,26},{10... | collective-permute-start | bytes 24584 | tf_op jit(solution)/shard_map/ppermute | solution.py:386
  24.0 4.2 %collective-permute-start.6 = (f32[8,256]{1,0:T(8,128)S(1)}, f32[8,256]{1,0:T(8,128)S(1)}, u32[]{:S(2)}, u32[]{:S(2)}) collective-permute-start(f32[8,256]{1,0:T(8,128)S(1)} %get-tuple-element.87.refs_1_), channel_id=1, source_target_pairs={{0,16},{8,24},{16,0},{24,8},{1,17},{9,25},{17,1},{25,9},{2,18},{10... | collective-permute-start | bytes 24584 | tf_op jit(solution)/shard_map/ppermute | solution.py:386
  24.4 3.9 %collective-permute-start.5 = (f32[8,256]{1,0:T(8,128)S(1)}, f32[8,256]{1,0:T(8,128)S(1)}, u32[]{:S(2)}, u32[]{:S(2)}) collective-permute-start(f32[8,256]{1,0:T(8,128)S(1)} %get-tuple-element.87.refs_1_), channel_id=1, source_target_pairs={{0,8},{8,0},{16,24},{24,16},{1,9},{9,1},{17,25},{25,17},{2,10},{10... | collective-permute-start | bytes 24584 | tf_op jit(solution)/shard_map/ppermute | solution.py:386
  30.1 5.8 %collective-permute-start.10 = (bf16[128,256]{1,0:T(8,128)(2,1)S(1)}, bf16[128,256]{1,0:T(8,128)(2,1)S(1)}, u32[]{:S(2)}, u32[]{:S(2)}) collective-permute-start(bf16[128,256]{1,0:T(8,128)(2,1)S(1)} %get-tuple-element.90.after_ref), channel_id=1, source_target_pairs={{0,3},{1,2},{2,1},{3,0},{4,7},{5,6},{6,5},{7,4},{8,11},{9,10},{10,... | collective-permute-start | bytes 196616 | tf_op jit(solution)/shard_map/ppermute | solution.py:381
  31.1 4.8 %collective-permute-start.9 = (bf16[128,256]{1,0:T(8,128)(2,1)S(1)}, bf16[128,256]{1,0:T(8,128)(2,1)S(1)}, u32[]{:S(2)}, u32[]{:S(2)}) collective-permute-start(bf16[128,256]{1,0:T(8,128)(2,1)S(1)} %get-tuple-element.90.after_ref), channel_id=1, source_target_pairs={{0,2},{1,3},{2,0},{3,1},{4,6},{5,7},{6,4},{7,5},{8,10},{9,11},{10,... | collective-permute-start | bytes 196616 | tf_op jit(solution)/shard_map/ppermute | solution.py:381
  32.5 4.3 %collective-permute-start.8 = (bf16[128,256]{1,0:T(8,128)(2,1)S(1)}, bf16[128,256]{1,0:T(8,128)(2,1)S(1)}, u32[]{:S(2)}, u32[]{:S(2)}) collective-permute-start(bf16[128,256]{1,0:T(8,128)(2,1)S(1)} %get-tuple-element.90.after_ref), channel_id=1, source_target_pairs={{0,1},{1,0},{2,3},{3,2},{4,5},{5,4},{6,7},{7,6},{8,9},{9,8},{10,11... | collective-permute-start | bytes 196616 | tf_op jit(solution)/shard_map/ppermute | solution.py:381
  36.8 5.9 %collective-permute-start.11 = (bf16[128,256]{1,0:T(8,128)(2,1)S(1)}, bf16[128,256]{1,0:T(8,128)(2,1)S(1)}, u32[]{:S(2)}, u32[]{:S(2)}) collective-permute-start(bf16[128,256]{1,0:T(8,128)(2,1)S(1)} %add_convert_fusion.3.refs_0_), channel_id=1, source_target_pairs={{0,4},{1,5},{2,6},{3,7},{4,0},{5,1},{6,2},{7,3},{8,12},{9,13},{10,... | collective-permute-start | bytes 196616 | tf_op jit(solution)/shard_map/ppermute | solution.py:381
  43.0 4.0 %collective-permute-start.14 = (f32[8,256]{1,0:T(8,128)S(1)}, f32[8,256]{1,0:T(8,128)S(1)}, u32[]{:S(2)}, u32[]{:S(2)}) collective-permute-start(f32[8,256]{1,0:T(8,128)S(1)} %get-tuple-element.94.refs_1_), channel_id=1, source_target_pairs={{0,24},{8,16},{16,8},{24,0},{1,25},{9,17},{17,9},{25,1},{2,26},{10... | collective-permute-start | bytes 24584 | tf_op jit(solution)/shard_map/ppermute | solution.py:386
  43.0 3.9 %collective-permute-start.13 = (f32[8,256]{1,0:T(8,128)S(1)}, f32[8,256]{1,0:T(8,128)S(1)}, u32[]{:S(2)}, u32[]{:S(2)}) collective-permute-start(f32[8,256]{1,0:T(8,128)S(1)} %get-tuple-element.94.refs_1_), channel_id=1, source_target_pairs={{0,16},{8,24},{16,0},{24,8},{1,17},{9,25},{17,1},{25,9},{2,18},{10... | collective-permute-start | bytes 24584 | tf_op jit(solution)/shard_map/ppermute | solution.py:386
  44.3 2.7 %collective-permute-start.12 = (f32[8,256]{1,0:T(8,128)S(1)}, f32[8,256]{1,0:T(8,128)S(1)}, u32[]{:S(2)}, u32[]{:S(2)}) collective-permute-start(f32[8,256]{1,0:T(8,128)S(1)} %get-tuple-element.94.refs_1_), channel_id=1, source_target_pairs={{0,8},{8,0},{16,24},{24,16},{1,9},{9,1},{17,25},{25,17},{2,10},{10... | collective-permute-start | bytes 24584 | tf_op jit(solution)/shard_map/ppermute | solution.py:386
  48.9 5.8 %collective-permute-start.17 = (bf16[128,256]{1,0:T(8,128)(2,1)S(1)}, bf16[128,256]{1,0:T(8,128)(2,1)S(1)}, u32[]{:S(2)}, u32[]{:S(2)}) collective-permute-start(bf16[128,256]{1,0:T(8,128)(2,1)S(1)} %get-tuple-element.96), channel_id=1, source_target_pairs={{0,3},{1,2},{2,1},{3,0},{4,7},{5,6},{6,5},{7,4},{8,11},{9,10},{10,... | collective-permute-start | bytes 196616 | tf_op jit(solution)/shard_map/ppermute | solution.py:381
  49.9 5.0 %collective-permute-start.16 = (bf16[128,256]{1,0:T(8,128)(2,1)S(1)}, bf16[128,256]{1,0:T(8,128)(2,1)S(1)}, u32[]{:S(2)}, u32[]{:S(2)}) collective-permute-start(bf16[128,256]{1,0:T(8,128)(2,1)S(1)} %get-tuple-element.96), channel_id=1, source_target_pairs={{0,2},{1,3},{2,0},{3,1},{4,6},{5,7},{6,4},{7,5},{8,10},{9,11},{10,... | collective-permute-start | bytes 196616 | tf_op jit(solution)/shard_map/ppermute | solution.py:381
  51.6 4.3 %collective-permute-start.15 = (bf16[128,256]{1,0:T(8,128)(2,1)S(1)}, bf16[128,256]{1,0:T(8,128)(2,1)S(1)}, u32[]{:S(2)}, u32[]{:S(2)}) collective-permute-start(bf16[128,256]{1,0:T(8,128)(2,1)S(1)} %get-tuple-element.96), channel_id=1, source_target_pairs={{0,1},{1,0},{2,3},{3,2},{4,5},{5,4},{6,7},{7,6},{8,9},{9,8},{10,11... | collective-permute-start | bytes 196616 | tf_op jit(solution)/shard_map/ppermute | solution.py:381
  55.9 5.8 %collective-permute-start.18 = (bf16[128,256]{1,0:T(8,128)(2,1)S(1)}, bf16[128,256]{1,0:T(8,128)(2,1)S(1)}, u32[]{:S(2)}, u32[]{:S(2)}) collective-permute-start(bf16[128,256]{1,0:T(8,128)(2,1)S(1)} %add_convert_fusion.2.refs_0_), channel_id=1, source_target_pairs={{0,4},{1,5},{2,6},{3,7},{4,0},{5,1},{6,2},{7,3},{8,12},{9,13},{10,... | collective-permute-start | bytes 196616 | tf_op jit(solution)/shard_map/ppermute | solution.py:381
  61.9 4.0 %collective-permute-start.21 = (f32[8,256]{1,0:T(8,128)S(1)}, f32[8,256]{1,0:T(8,128)S(1)}, u32[]{:S(2)}, u32[]{:S(2)}) collective-permute-start(f32[8,256]{1,0:T(8,128)S(1)} %get-tuple-element.99.refs_1_), channel_id=1, source_target_pairs={{0,24},{8,16},{16,8},{24,0},{1,25},{9,17},{17,9},{25,1},{2,26},{10... | collective-permute-start | bytes 24584 | tf_op jit(solution)/shard_map/ppermute | solution.py:386
  61.9 3.9 %collective-permute-start.20 = (f32[8,256]{1,0:T(8,128)S(1)}, f32[8,256]{1,0:T(8,128)S(1)}, u32[]{:S(2)}, u32[]{:S(2)}) collective-permute-start(f32[8,256]{1,0:T(8,128)S(1)} %get-tuple-element.99.refs_1_), channel_id=1, source_target_pairs={{0,16},{8,24},{16,0},{24,8},{1,17},{9,25},{17,1},{25,9},{2,18},{10... | collective-permute-start | bytes 24584 | tf_op jit(solution)/shard_map/ppermute | solution.py:386
  62.8 3.1 %collective-permute-start.19 = (f32[8,256]{1,0:T(8,128)S(1)}, f32[8,256]{1,0:T(8,128)S(1)}, u32[]{:S(2)}, u32[]{:S(2)}) collective-permute-start(f32[8,256]{1,0:T(8,128)S(1)} %get-tuple-element.99.refs_1_), channel_id=1, source_target_pairs={{0,8},{8,0},{16,24},{24,16},{1,9},{9,1},{17,25},{25,17},{2,10},{10... | collective-permute-start | bytes 24584 | tf_op jit(solution)/shard_map/ppermute | solution.py:386
  67.8 5.8 %collective-permute-start.24 = (bf16[128,256]{1,0:T(8,128)(2,1)S(1)}, bf16[128,256]{1,0:T(8,128)(2,1)S(1)}, u32[]{:S(2)}, u32[]{:S(2)}) collective-permute-start(bf16[128,256]{1,0:T(8,128)(2,1)S(1)} %get-tuple-element.106), channel_id=1, source_target_pairs={{0,3},{1,2},{2,1},{3,0},{4,7},{5,6},{6,5},{7,4},{8,11},{9,10},{10,... | collective-permute-start | bytes 196616 | tf_op jit(solution)/shard_map/ppermute | solution.py:381
  68.1 5.5 %collective-permute-start.23 = (bf16[128,256]{1,0:T(8,128)(2,1)S(1)}, bf16[128,256]{1,0:T(8,128)(2,1)S(1)}, u32[]{:S(2)}, u32[]{:S(2)}) collective-permute-start(bf16[128,256]{1,0:T(8,128)(2,1)S(1)} %get-tuple-element.106), channel_id=1, source_target_pairs={{0,2},{1,3},{2,0},{3,1},{4,6},{5,7},{6,4},{7,5},{8,10},{9,11},{10,... | collective-permute-start | bytes 196616 | tf_op jit(solution)/shard_map/ppermute | solution.py:381
  70.2 4.3 %collective-permute-start.22 = (bf16[128,256]{1,0:T(8,128)(2,1)S(1)}, bf16[128,256]{1,0:T(8,128)(2,1)S(1)}, u32[]{:S(2)}, u32[]{:S(2)}) collective-permute-start(bf16[128,256]{1,0:T(8,128)(2,1)S(1)} %get-tuple-element.106), channel_id=1, source_target_pairs={{0,1},{1,0},{2,3},{3,2},{4,5},{5,4},{6,7},{7,6},{8,9},{9,8},{10,11... | collective-permute-start | bytes 196616 | tf_op jit(solution)/shard_map/ppermute | solution.py:381
  74.5 5.4 %collective-permute-start.25 = (bf16[128,256]{1,0:T(8,128)(2,1)S(1)}, bf16[128,256]{1,0:T(8,128)(2,1)S(1)}, u32[]{:S(2)}, u32[]{:S(2)}) collective-permute-start(bf16[128,256]{1,0:T(8,128)(2,1)S(1)} %add_convert_fusion.1.refs_0_), channel_id=1, source_target_pairs={{0,4},{1,5},{2,6},{3,7},{4,0},{5,1},{6,2},{7,3},{8,12},{9,13},{10,... | collective-permute-start | bytes 196616 | tf_op jit(solution)/shard_map/ppermute | solution.py:381
  80.1 4.0 %collective-permute-start.28 = (f32[8,256]{1,0:T(8,128)S(1)}, f32[8,256]{1,0:T(8,128)S(1)}, u32[]{:S(2)}, u32[]{:S(2)}) collective-permute-start(f32[8,256]{1,0:T(8,128)S(1)} %get-tuple-element.109.refs_1_), channel_id=1, source_target_pairs={{0,24},{8,16},{16,8},{24,0},{1,25},{9,17},{17,9},{25,1},{2,26},{10... | collective-permute-start | bytes 24584 | tf_op jit(solution)/shard_map/ppermute | solution.py:386
  80.1 3.9 %collective-permute-start.27 = (f32[8,256]{1,0:T(8,128)S(1)}, f32[8,256]{1,0:T(8,128)S(1)}, u32[]{:S(2)}, u32[]{:S(2)}) collective-permute-start(f32[8,256]{1,0:T(8,128)S(1)} %get-tuple-element.109.refs_1_), channel_id=1, source_target_pairs={{0,16},{8,24},{16,0},{24,8},{1,17},{9,25},{17,1},{25,9},{2,18},{10... | collective-permute-start | bytes 24584 | tf_op jit(solution)/shard_map/ppermute | solution.py:386
  81.3 2.8 %collective-permute-start.26 = (f32[8,256]{1,0:T(8,128)S(1)}, f32[8,256]{1,0:T(8,128)S(1)}, u32[]{:S(2)}, u32[]{:S(2)}) collective-permute-start(f32[8,256]{1,0:T(8,128)S(1)} %get-tuple-element.109.refs_1_), channel_id=1, source_target_pairs={{0,8},{8,0},{16,24},{24,16},{1,9},{9,1},{17,25},{25,17},{2,10},{10... | collective-permute-start | bytes 24584 | tf_op jit(solution)/shard_map/ppermute | solution.py:386
  86.4 5.7 %collective-permute-start.31 = (bf16[128,256]{1,0:T(8,128)(2,1)S(1)}, bf16[128,256]{1,0:T(8,128)(2,1)S(1)}, u32[]{:S(2)}, u32[]{:S(2)}) collective-permute-start(bf16[128,256]{1,0:T(8,128)(2,1)S(1)} %get-tuple-element.116), channel_id=1, source_target_pairs={{0,3},{1,2},{2,1},{3,0},{4,7},{5,6},{6,5},{7,4},{8,11},{9,10},{10,... | collective-permute-start | bytes 196616 | tf_op jit(solution)/shard_map/ppermute | solution.py:381
  86.8 5.5 %collective-permute-start.30 = (bf16[128,256]{1,0:T(8,128)(2,1)S(1)}, bf16[128,256]{1,0:T(8,128)(2,1)S(1)}, u32[]{:S(2)}, u32[]{:S(2)}) collective-permute-start(bf16[128,256]{1,0:T(8,128)(2,1)S(1)} %get-tuple-element.116), channel_id=1, source_target_pairs={{0,2},{1,3},{2,0},{3,1},{4,6},{5,7},{6,4},{7,5},{8,10},{9,11},{10,... | collective-permute-start | bytes 196616 | tf_op jit(solution)/shard_map/ppermute | solution.py:381
  89.0 4.3 %collective-permute-start.29 = (bf16[128,256]{1,0:T(8,128)(2,1)S(1)}, bf16[128,256]{1,0:T(8,128)(2,1)S(1)}, u32[]{:S(2)}, u32[]{:S(2)}) collective-permute-start(bf16[128,256]{1,0:T(8,128)(2,1)S(1)} %get-tuple-element.116), channel_id=1, source_target_pairs={{0,1},{1,0},{2,3},{3,2},{4,5},{5,4},{6,7},{7,6},{8,9},{9,8},{10,11... | collective-permute-start | bytes 196616 | tf_op jit(solution)/shard_map/ppermute | solution.py:381
  93.3 5.4 %collective-permute-start.32 = (bf16[128,256]{1,0:T(8,128)(2,1)S(1)}, bf16[128,256]{1,0:T(8,128)(2,1)S(1)}, u32[]{:S(2)}, u32[]{:S(2)}) collective-permute-start(bf16[128,256]{1,0:T(8,128)(2,1)S(1)} %add_convert_fusion.refs_0_), channel_id=1, source_target_pairs={{0,4},{1,5},{2,6},{3,7},{4,0},{5,1},{6,2},{7,3},{8,12},{9,13},{10,... | collective-permute-start | bytes 196616 | tf_op jit(solution)/shard_map/ppermute | solution.py:381
  98.8 3.1 %collective-permute-start.35 = (f32[8,256]{1,0:T(8,128)S(1)}, f32[8,256]{1,0:T(8,128)S(1)}, u32[]{:S(2)}, u32[]{:S(2)}) collective-permute-start(f32[8,256]{1,0:T(8,128)S(1)} %get-tuple-element.119.refs_1_), channel_id=1, source_target_pairs={{0,24},{8,16},{16,8},{24,0},{1,25},{9,17},{17,9},{25,1},{2,26},{10... | collective-permute-start | bytes 24584 | tf_op jit(solution)/shard_map/ppermute | solution.py:386
  98.9 3.7 %collective-permute-start.34 = (f32[8,256]{1,0:T(8,128)S(1)}, f32[8,256]{1,0:T(8,128)S(1)}, u32[]{:S(2)}, u32[]{:S(2)}) collective-permute-start(f32[8,256]{1,0:T(8,128)S(1)} %get-tuple-element.119.refs_1_), channel_id=1, source_target_pairs={{0,16},{8,24},{16,0},{24,8},{1,17},{9,25},{17,1},{25,9},{2,18},{10... | collective-permute-start | bytes 24584 | tf_op jit(solution)/shard_map/ppermute | solution.py:386
  100.0 2.6 %collective-permute-start.33 = (f32[8,256]{1,0:T(8,128)S(1)}, f32[8,256]{1,0:T(8,128)S(1)}, u32[]{:S(2)}, u32[]{:S(2)}) collective-permute-start(f32[8,256]{1,0:T(8,128)S(1)} %get-tuple-element.119.refs_1_), channel_id=1, source_target_pairs={{0,8},{8,0},{16,24},{24,16},{1,9},{9,1},{17,25},{25,17},{2,10},{10... | collective-permute-start | bytes 24584 | tf_op jit(solution)/shard_map/ppermute | solution.py:386

commit v8 on v7

--- a/solution.py
+++ b/solution.py
@@ -124,13 +124,13 @@
 
 
 def pack_kernel(*refs):
-    far_refs, count_ref, scale_ref, refs = refs[:8], refs[8], refs[9], refs[10:]
-    near_refs, out_ref, live_ref, damp_ref = refs[:8], refs[8], refs[9], refs[10]
-    tally_ref, factor_ref, wide_ref, sems = refs[11:]
-    jac_ref, near_jac_ref, e_ref, res_ref = far_refs[0], near_refs[0], near_refs[1], near_refs[2]
+    jac_ref, far_refs, count_ref, scale_ref, refs = refs[0], refs[1:8], refs[8], refs[9], refs[10:]
+    near_refs, out_ref, live_ref, damp_ref = refs[:7], refs[7], refs[8], refs[9]
+    tally_ref, factor_ref, wide_ref, sems = refs[10:]
+    e_ref, res_ref = near_refs[:2]
     last, height, ties = jac_ref.shape[0] - 1, jac_ref.shape[1], e_ref.shape[2]
-    pairs = list(zip(far_refs[1:], near_refs[1:])) + [(count_ref, tally_ref), (scale_ref, factor_ref)]
-    copies = fetch(pairs + [(jac_ref.at[pl.ds(last, 1)], out_ref.at[:, :height]), (jac_ref, near_jac_ref)], sems)
+    pairs = list(zip(far_refs, near_refs)) + [(count_ref, tally_ref), (scale_ref, factor_ref)]
+    copies = fetch(pairs + [(jac_ref.at[pl.ds(last, 1)], out_ref.at[:, :height])], sems)
     for copy in copies[: len(pairs)]:
         copy.wait()
     wide_ref[...] = jnp.zeros_like(wide_ref)
@@ -151,10 +151,15 @@
 
 def setup_kernel(cjac_ref, ajac_ref, *refs):
     ae_ref, ares_ref, ce_ref, cres_ref, own_ref, group_ref, other_ref, lived_ref = refs[:8]
-    out_cjac_ref, coef_ref, put1_ref, put2_ref, pick1_ref, pick2_ref, t1_ref, t2_ref = refs[8:16]
-    live_ref, q1_ref, q2_ref, index_ref, sems = refs[16:]
-    parts = [pl.ds(at, OCTET) for at in range(0, cjac_ref.shape[0], OCTET)]
-    copies = fetch([(cjac_ref.at[part], out_cjac_ref.at[part]) for part in parts], sems)
+    out_cjac_ref, out_ajac_ref, coef_ref, put1_ref, put2_ref, pick1_ref, pick2_ref, t1_ref, t2_ref = refs[8:17]
+    live_ref, q1_ref, q2_ref, index_ref, sems = refs[17:]
+    copies = []
+    for ref, out_ref in ((cjac_ref, out_cjac_ref), (ajac_ref, out_ajac_ref)):
+        for at in range(0, ref.shape[0], OCTET):
+            part = pl.ds(at, OCTET)
+            copies.append(pltpu.make_async_copy(ref.at[part], out_ref.at[part], sems.at[len(copies)]))
+    for copy in copies:
+        copy.start()
     links, scenes = cjac_ref.shape[0], ajac_ref.shape[0]
     blocks = links + scenes
     live_ref[0:links] = jnp.ones((links, live_ref.shape[1]), F32)
@@ -180,12 +185,16 @@
         put_ref[...] = table[:, :slots].astype(BF16)
         pick_ref[...] = table.T[:slots].astype(BF16)
 
-    for ref, slot in ((ajac_ref, links), (out_cjac_ref, 0)):
-        for at in range(0, ref.shape[0], OCTET):
-            if ref is out_cjac_ref:
-                copies[at // OCTET].wait()
-            rows = pl.ds(slot + at, OCTET)
-            t1_ref[rows], t2_ref[rows] = terms(q1_ref[rows], q2_ref[rows], ref, at, OCTET)
+    count = len(copies)
+    cuts = [0, 2 * count // 5, 4 * count // 5, count]
+    for number in range(count):
+        if number in cuts:
+            for copy in copies[number : cuts[cuts.index(number) + 1]]:
+                copy.wait()
+        at = number * OCTET
+        ref, at = (out_cjac_ref, at) if at < links else (out_ajac_ref, at - links)
+        rows = pl.ds(number * OCTET, OCTET)
+        t1_ref[rows], t2_ref[rows] = terms(q1_ref[rows], q2_ref[rows], ref, at, OCTET)
 
 
 def rhs_kernel(coef_ref, t1_ref, t2_ref, edge_ref, put1_ref, put2_ref, out_ref, out_coef_ref, ejac_ref, all1_ref, all2_ref):
@@ -423,27 +432,27 @@
     small = [ajac, along_e[0], along_res[0], cross_e[0], cross_res[0], cross_own, cross_group[:, :, 0], cross_other]
     near = call(
         pack_kernel,
-        [(a.shape, a.dtype) for a in small]
+        [(a.shape, a.dtype) for a in small[1:]]
         + [((1, 2 * ties + 2 * OCTET, width), BF16), ((scenes, ties), F32), (own, F32)],
         [pltpu.SMEM((1, scenes), jnp.int32), pltpu.SMEM((1, scenes), F32)]
-        + [((2 * OCTET, width), F32), sems((len(small) + 3,))],
+        + [((2 * OCTET, width), F32), sems((len(small) + 2,))],
         "pack",
         small + [along_count, damping],
         spaces={i: pltpu.HBM for i in range(len(small) + 2)},
     )
-    ajac, edge, live, damp = near[0], pass_on(near[8]), near[9], near[10]
+    edge, live, damp = pass_on(near[7]), near[8], near[9]
     part_tie = (blocks, ties)
     put = ((rows, slots), BF16)
     pick = ((slots, rows), BF16)
     term = ((blocks, width), F32)
-    cjac, coef, put1, put2, pick1, pick2, t1, t2 = call(
+    cjac, ajac, coef, put1, put2, pick1, pick2, t1, t2 = call(
         setup_kernel,
-        [(cjac.shape, BF16), ((3,) + part_tie, F32), put, put, pick, pick, term, term],
-        [(part_tie, F32)] * 3 + [((OCTET, lanes), jnp.int32), sems((links // OCTET,))],
+        [(cjac.shape, BF16), (ajac.shape, BF16), ((3,) + part_tie, F32), put, put, pick, pick, term, term],
+        [(part_tie, F32)] * 3 + [((OCTET, lanes), jnp.int32), sems((blocks // OCTET,))],
         "setup",
-        [cjac, *near[:8], live],
+        [cjac, ajac, *near[:7], live],
         work,
-        {0: pltpu.HBM},
+        {0: pltpu.HBM, 1: pltpu.HBM},
     )
 
     def turn(start, count, refs, after):

time: 104 us -> 103 us (level)
  transfers between devices with their start and end apart: 36 -> 36, of which waited for: 19 -> 20; matrix products, arithmetic and copies ran while one was open for 0% -> 0% of each run, Pallas kernels for 20% -> 20%
where the time goes in v8:
time: 103 us; the launch traced here: 102 us
  starting transfers between devices  36.4 us (35%)
  waiting for transfers between devices  33.6 us (33%)
  Pallas kernels  31.2 us (30%)
    ppermute x20, waiting for transfers between devices, swap(): lax.ppermute(block, axis, [(i, i ^ mask) for i in range(lax.axis_size(axi...  31.6 us
    pallas_call x20, Pallas kernels, call(): pl.pallas_call(kernel, out_shape=[jax.ShapeDtypeStruct(*o) for o in outs]...  31.2 us
    ppermute x20, starting transfers between devices, swap(): lax.ppermute(block, axis, [(i, i ^ mask) for i in range(lax.axis_size(axi...  26.3 us
    ppermute x15, starting transfers between devices, orbit_packets(): lax.ppermute(packet, 'orbit', [(i, i ^ mask) for i in range(n)])  9.59 us
  transfers between devices with their start and end apart: 36, of which 20 were waited for; matrix products, arithmetic and copies ran while one was open for 0% of the time, Pallas kernels for 20%

profile of v8, /device:TPU:0, one launch (start us, length us, event | category | flops | bytes accessed | tf_op | source)
XLA Modules:
  0.0 102.2 jit_solution(13339666700695565698)
XLA Ops:
  0.6 1.1 %pack.1 = (f32[16,2,128]{2,1,0:T(2,128)S(1)}, f32[16,2,128]{2,1,0:T(2,128)S(1)}, f32[64,2,128]{2,1,0:T(2,128)S(1)}, f32[64,2,128]{2,1,0:T(2,128)S(1)}, s32[1,64]...) custom-call(bf16[16,256,256]{2,1,0:T(8,128)(2,1)} %bitcast.9, ...), custom_call_target="tpu_custom_call" | custom-call | bytes 2261888 | tf_op jit(solution)/shard_map/pack/pallas_call | solution.py:351
  1.8 0.5 collective-permute-start
  2.3 4.5 %setup.1 = (bf16[64,256,256]{2,1,0:T(8,128)(2,1)S(1)}, bf16[16,256,256]{2,1,0:T(8,128)(2,1)S(1)}, f32[3,80,128]{2,1,0:T(8,128)S(1)}, bf16[128,88]{1,0:T(8,128)(2...) custom-call(bf16[64,256,256]{2,1,0:T(8,128)(2,1)} %bitcast.11, ...), custom_call_target="tpu_custom_call" | custom-call | flops 339738624 | bytes 10658560 | tf_op jit(solution)/shard_map/setup/pallas_call | solution.py:351
  7.0 0.4 rhs.1
  7.4 3.5 %collective-permute-start.3 = (bf16[128,256]{1,0:T(8,128)(2,1)S(1)}, bf16[128,256]{1,0:T(8,128)(2,1)S(1)}, u32[]{:S(2)}, u32[]{:S(2)}) collective-permute-start(bf16[128,256]{1,0:T(8,128)(2,1)S(1)} %get-tuple-element.78.after_ref), channel_id=1, source_target_pairs={{0,3},{1,2},{2,1},{3,0},{4,7},{5,6},{6,5},{7,4},{8,11},{9,10},{10,... | collective-permute-start | bytes 196616 | tf_op jit(solution)/shard_map/ppermute | solution.py:390
  10.9 0.5 collective-permute-start.2
  11.5 2.8 %turn.3.refs_0_ = bf16[32,256,256]{2,1,0:T(8,128)(2,1)S(1)} custom-call(bf16[128,256]{1,0:T(8,128)(2,1)S(1)} %get-tuple-element.78.after_ref, bf16[64,256,256]{2,1,0:T(8,128)(2,1)S(1)} %get-tuple-element.79.refs_0_.refs_9_), custom_call_target="tpu_custom_call" | custom-call | flops 135895456 | bytes 8454144 | tf_op jit(solution)/shard_map/turn/pallas_call | solution.py:351
  14.3 1.2 %collective-permute-done.2 = bf16[128,256]{1,0:T(8,128)(2,1)S(1)} collective-permute-done((bf16[128,256]{1,0:T(8,128)(2,1)S(1)}, bf16[128,256]{1,0:T(8,128)(2,1)S(1)}, u32[]{:S(2)}, u32[]{:S(2)}) %collective-permute-start.2) | collective-permute-done | bytes 65568 | tf_op jit(solution)/shard_map/ppermute | solution.py:390
  15.5 0.7 collective-permute-done.1
  16.3 2.7 %collective-permute-start.4 = (bf16[128,256]{1,0:T(8,128)(2,1)S(1)}, bf16[128,256]{1,0:T(8,128)(2,1)S(1)}, u32[]{:S(2)}, u32[]{:S(2)}) collective-permute-start(bf16[128,256]{1,0:T(8,128)(2,1)S(1)} %add_convert_fusion.4.refs_0_.after_ref), channel_id=1, source_target_pairs={{0,4},{1,5},{2,6},{3,7},{4,0},{5,1},{6,2},{7,3},{8,12},{9,13},{10,... | collective-permute-start | bytes 196616 | tf_op jit(solution)/shard_map/ppermute | solution.py:390
  18.9 2.8 %turn.4.refs_1_ = bf16[32,256,256]{2,1,0:T(8,128)(2,1)S(1)} custom-call(bf16[128,256]{1,0:T(8,128)(2,1)S(1)} %add_convert_fusion.4.refs_0_.after_ref, bf16[64,256,256]{2,1,0:T(8,128)(2,1)S(1)} %get-tuple-element.79.refs_0_.refs_9_), custom_call_target="tpu_custom_call" | custom-call | flops 135895456 | bytes 8454144 | tf_op jit(solution)/shard_map/turn/pallas_call | solution.py:351
  21.7 1.2 %collective-permute-done.4.refs_1_ = bf16[128,256]{1,0:T(8,128)(2,1)S(1)} collective-permute-done((bf16[128,256]{1,0:T(8,128)(2,1)S(1)}, bf16[128,256]{1,0:T(8,128)(2,1)S(1)}, u32[]{:S(2)}, u32[]{:S(2)}) %collective-permute-start.4) | collective-permute-done | bytes 65568 | tf_op jit(solution)/shard_map/ppermute | solution.py:390
  23.0 0.3 collective-permute-start.6
  23.3 1.5 %collective-permute-start.5 = (f32[8,256]{1,0:T(8,128)S(1)}, f32[8,256]{1,0:T(8,128)S(1)}, u32[]{:S(2)}, u32[]{:S(2)}) collective-permute-start(f32[8,256]{1,0:T(8,128)S(1)} %get-tuple-element.87.refs_1_), channel_id=1, source_target_pairs={{0,8},{8,0},{16,24},{24,16},{1,9},{9,1},{17,25},{25,17},{2,10},{10... | collective-permute-start | bytes 24584 | tf_op jit(solution)/shard_map/ppermute | solution.py:395
  24.9 2.3 %project.4.refs_0_ = f32[88,256]{1,0:T(8,128)S(1)} custom-call(f32[128,256]{1,0:T(8,128)S(1)} %get-tuple-element.81.field_ref.refs_12_.refs_2_, bf16[88,128]{1,0:T(8,128)(2,1)S(1)} %get-tuple-element.82.pick1_ref, bf16[88,128]{1,0:T(8,128)(2,1)S(1)} %get-tuple-element.83.pick2_ref, bf16[32,256,256]{2,1,0:T(8,128)(2,1)S(1)} %turn.3.refs_0_, ...), custom_call_target="tpu_custom_call" | custom-call | flops 339738624 | bytes 10792960 | tf_op jit(solution)/shard_map/project/pallas_call | solution.py:351
  27.2 1.9 %step.4 = (bf16[128,256]{1,0:T(8,128)(2,1)S(1)}, f32[88,256]{1,0:T(8,128)S(1)}) custom-call(f32[88,256]{1,0:T(8,128)S(1)} %project.4.refs_0_, f32[8,256]{1,0:T(8,128)S(1)} %get-tuple-element.87.refs_1_, f32[8,256]{1,0:T(8,128)S(1)} %collective-permute-done.5.refs_2_, f32[8,256]{1,0:T(8,128)S(1)} %collective-permute-done.6.refs_3_, ...), custom_call_target="tpu_custom_call" | custom-call | flops 339738624 | bytes 11067392 | tf_op jit(solution)/shard_map/step/pallas_call | solution.py:351
  29.1 0.9 collective-permute-start.10
  30.1 1.5 %collective-permute-start.9 = (bf16[128,256]{1,0:T(8,128)(2,1)S(1)}, bf16[128,256]{1,0:T(8,128)(2,1)S(1)}, u32[]{:S(2)}, u32[]{:S(2)}) collective-permute-start(bf16[128,256]{1,0:T(8,128)(2,1)S(1)} %get-tuple-element.90.after_ref), channel_id=1, source_target_pairs={{0,2},{1,3},{2,0},{3,1},{4,6},{5,7},{6,4},{7,5},{8,10},{9,11},{10,... | collective-permute-start | bytes 196616 | tf_op jit(solution)/shard_map/ppermute | solution.py:390
  31.5 1.2 %collective-permute-start.8 = (bf16[128,256]{1,0:T(8,128)(2,1)S(1)}, bf16[128,256]{1,0:T(8,128)(2,1)S(1)}, u32[]{:S(2)}, u32[]{:S(2)}) collective-permute-start(bf16[128,256]{1,0:T(8,128)(2,1)S(1)} %get-tuple-element.90.after_ref), channel_id=1, source_target_pairs={{0,1},{1,0},{2,3},{3,2},{4,5},{5,4},{6,7},{7,6},{8,9},{9,8},{10,11... | collective-permute-start | bytes 196616 | tf_op jit(solution)/shard_map/ppermute | solution.py:390
  32.7 2.2 %collective-permute-done.10 = bf16[128,256]{1,0:T(8,128)(2,1)S(1)} collective-permute-done((bf16[128,256]{1,0:T(8,128)(2,1)S(1)}, bf16[128,256]{1,0:T(8,128)(2,1)S(1)}, u32[]{:S(2)}, u32[]{:S(2)}) %collective-permute-start.10) | collective-permute-done | bytes 65568 | tf_op jit(solution)/shard_map/ppermute | solution.py:390
  34.9 0.9 collective-permute-done.8
  35.8 2.0 %collective-permute-start.11 = (bf16[128,256]{1,0:T(8,128)(2,1)S(1)}, bf16[128,256]{1,0:T(8,128)(2,1)S(1)}, u32[]{:S(2)}, u32[]{:S(2)}) collective-permute-start(bf16[128,256]{1,0:T(8,128)(2,1)S(1)} %add_convert_fusion.3.refs_0_), channel_id=1, source_target_pairs={{0,4},{1,5},{2,6},{3,7},{4,0},{5,1},{6,2},{7,3},{8,12},{9,13},{10,... | collective-permute-start | bytes 196616 | tf_op jit(solution)/shard_map/ppermute | solution.py:390
  37.8 1.6 %turn.5 = (bf16[16,256,256]{2,1,0:T(8,128)(2,1)S(1)}, bf16[1,256,256]{2,1,0:T(8,128)(2,1)S(1)}) custom-call(bf16[128,256]{1,0:T(8,128)(2,1)S(1)} %get-tuple-element.90.after_ref, bf16[16,256,256]{2,1,0:T(8,128)(2,1)S(1)} %get-tuple-element.85.refs_2_.refs_10_.refs_0_, bf16[1,256,256]{2,1,0:T(8,128)(2,1)S(1)} %get-tuple-element.86.refs_3_.refs_11_.refs_1_), custom_call_target="tpu_custom_call" | custom-call | flops 72194456 | bytes 2293760 | tf_op jit(solution)/shard_map/turn/pallas_call | solution.py:351
  39.5 2.3 %collective-permute-done.11.refs_1_ = bf16[128,256]{1,0:T(8,128)(2,1)S(1)} collective-permute-done((bf16[128,256]{1,0:T(8,128)(2,1)S(1)}, bf16[128,256]{1,0:T(8,128)(2,1)S(1)}, u32[]{:S(2)}, u32[]{:S(2)}) %collective-permute-start.11) | collective-permute-done | bytes 65568 | tf_op jit(solution)/shard_map/ppermute | solution.py:390
  42.0 1.2 %collective-permute-start.13 = (f32[8,256]{1,0:T(8,128)S(1)}, f32[8,256]{1,0:T(8,128)S(1)}, u32[]{:S(2)}, u32[]{:S(2)}) collective-permute-start(f32[8,256]{1,0:T(8,128)S(1)} %get-tuple-element.94.refs_1_), channel_id=1, source_target_pairs={{0,16},{8,24},{16,0},{24,8},{1,17},{9,25},{17,1},{25,9},{2,18},{10... | collective-permute-start | bytes 24584 | tf_op jit(solution)/shard_map/ppermute | solution.py:395
  43.2 0.6 collective-permute-start.12
  43.9 2.0 %project.5.refs_0_ = f32[88,256]{1,0:T(8,128)S(1)} custom-call(f32[128,256]{1,0:T(8,128)S(1)} %get-tuple-element.91.field_ref.refs_13_, bf16[88,128]{1,0:T(8,128)(2,1)S(1)} %get-tuple-element.82.pick1_ref, bf16[88,128]{1,0:T(8,128)(2,1)S(1)} %get-tuple-element.83.pick2_ref, bf16[32,256,256]{2,1,0:T(8,128)(2,1)S(1)} %turn.3.refs_0_, ...), custom_call_target="tpu_custom_call" | custom-call | flops 339738624 | bytes 10792960 | tf_op jit(solution)/shard_map/project/pallas_call | solution.py:351
  45.9 1.9 %step.5 = (bf16[128,256]{1,0:T(8,128)(2,1)S(1)}, f32[88,256]{1,0:T(8,128)S(1)}, f32[128,256]{1,0:T(8,128)S(1)}, f32[128,256]{1,0:T(8,128)S(1)}, f32[88,256]{1,0:...) custom-call(f32[88,256]{1,0:T(8,128)S(1)} %project.5.refs_0_, ...), custom_call_target="tpu_custom_call" | custom-call | flops 339738624 | bytes 11304960 | tf_op jit(solution)/shard_map/step/pallas_call | solution.py:351
  47.8 1.0 %collective-permute-start.17 = (bf16[128,256]{1,0:T(8,128)(2,1)S(1)}, bf16[128,256]{1,0:T(8,128)(2,1)S(1)}, u32[]{:S(2)}, u32[]{:S(2)}) collective-permute-start(bf16[128,256]{1,0:T(8,128)(2,1)S(1)} %get-tuple-element.96), channel_id=1, source_target_pairs={{0,3},{1,2},{2,1},{3,0},{4,7},{5,6},{6,5},{7,4},{8,11},{9,10},{10,... | collective-permute-start | bytes 196616 | tf_op jit(solution)/shard_map/ppermute | solution.py:390
  48.9 1.6 %collective-permute-start.16 = (bf16[128,256]{1,0:T(8,128)(2,1)S(1)}, bf16[128,256]{1,0:T(8,128)(2,1)S(1)}, u32[]{:S(2)}, u32[]{:S(2)}) collective-permute-start(bf16[128,256]{1,0:T(8,128)(2,1)S(1)} %get-tuple-element.96), channel_id=1, source_target_pairs={{0,2},{1,3},{2,0},{3,1},{4,6},{5,7},{6,4},{7,5},{8,10},{9,11},{10,... | collective-permute-start | bytes 196616 | tf_op jit(solution)/shard_map/ppermute | solution.py:390
  50.5 0.9 collective-permute-start.15
  51.4 2.2 %collective-permute-done.17 = bf16[128,256]{1,0:T(8,128)(2,1)S(1)} collective-permute-done((bf16[128,256]{1,0:T(8,128)(2,1)S(1)}, bf16[128,256]{1,0:T(8,128)(2,1)S(1)}, u32[]{:S(2)}, u32[]{:S(2)}) %collective-permute-start.17) | collective-permute-done | bytes 65568 | tf_op jit(solution)/shard_map/ppermute | solution.py:390
  53.6 0.3 collective-permute-done.16
  53.9 0.9 collective-permute-done.15
  54.8 1.4 %collective-permute-start.18 = (bf16[128,256]{1,0:T(8,128)(2,1)S(1)}, bf16[128,256]{1,0:T(8,128)(2,1)S(1)}, u32[]{:S(2)}, u32[]{:S(2)}) collective-permute-start(bf16[128,256]{1,0:T(8,128)(2,1)S(1)} %add_convert_fusion.2.refs_0_), channel_id=1, source_target_pairs={{0,4},{1,5},{2,6},{3,7},{4,0},{5,1},{6,2},{7,3},{8,12},{9,13},{10,... | collective-permute-start | bytes 196616 | tf_op jit(solution)/shard_map/ppermute | solution.py:390
  56.2 4.4 %collective-permute-done.18.refs_1_ = bf16[128,256]{1,0:T(8,128)(2,1)S(1)} collective-permute-done((bf16[128,256]{1,0:T(8,128)(2,1)S(1)}, bf16[128,256]{1,0:T(8,128)(2,1)S(1)}, u32[]{:S(2)}, u32[]{:S(2)}) %collective-permute-start.18) | collective-permute-done | bytes 65568 | tf_op jit(solution)/shard_map/ppermute | solution.py:390
  60.9 0.8 collective-permute-start.20
  61.7 1.0 collective-permute-start.19
  62.7 2.0 %project.6.refs_0_ = f32[88,256]{1,0:T(8,128)S(1)} custom-call(f32[128,256]{1,0:T(8,128)S(1)} %get-tuple-element.98.field_ref.refs_13_, bf16[88,128]{1,0:T(8,128)(2,1)S(1)} %get-tuple-element.82.pick1_ref, bf16[88,128]{1,0:T(8,128)(2,1)S(1)} %get-tuple-element.83.pick2_ref, bf16[32,256,256]{2,1,0:T(8,128)(2,1)S(1)} %turn.3.refs_0_, ...), custom_call_target="tpu_custom_call" | custom-call | flops 339738624 | bytes 10792960 | tf_op jit(solution)/shard_map/project/pallas_call | solution.py:351
  64.8 1.9 %step.6 = (bf16[128,256]{1,0:T(8,128)(2,1)S(1)}, f32[88,256]{1,0:T(8,128)S(1)}, f32[128,256]{1,0:T(8,128)S(1)}, f32[128,256]{1,0:T(8,128)S(1)}, f32[88,256]{1,0:...) custom-call(f32[88,256]{1,0:T(8,128)S(1)} %project.6.refs_0_, ...), custom_call_target="tpu_custom_call" | custom-call | flops 339738624 | bytes 11546624 | tf_op jit(solution)/shard_map/step/pallas_call | solution.py:351
  66.7 0.3 collective-permute-start.24
  67.1 2.1 %collective-permute-start.23 = (bf16[128,256]{1,0:T(8,128)(2,1)S(1)}, bf16[128,256]{1,0:T(8,128)(2,1)S(1)}, u32[]{:S(2)}, u32[]{:S(2)}) collective-permute-start(bf16[128,256]{1,0:T(8,128)(2,1)S(1)} %get-tuple-element.106), channel_id=1, source_target_pairs={{0,2},{1,3},{2,0},{3,1},{4,6},{5,7},{6,4},{7,5},{8,10},{9,11},{10,... | collective-permute-start | bytes 196616 | tf_op jit(solution)/shard_map/ppermute | solution.py:390
  69.2 1.1 %collective-permute-start.22 = (bf16[128,256]{1,0:T(8,128)(2,1)S(1)}, bf16[128,256]{1,0:T(8,128)(2,1)S(1)}, u32[]{:S(2)}, u32[]{:S(2)}) collective-permute-start(bf16[128,256]{1,0:T(8,128)(2,1)S(1)} %get-tuple-element.106), channel_id=1, source_target_pairs={{0,1},{1,0},{2,3},{3,2},{4,5},{5,4},{6,7},{7,6},{8,9},{9,8},{10,11... | collective-permute-start | bytes 196616 | tf_op jit(solution)/shard_map/ppermute | solution.py:390
  70.3 2.2 %collective-permute-done.24 = bf16[128,256]{1,0:T(8,128)(2,1)S(1)} collective-permute-done((bf16[128,256]{1,0:T(8,128)(2,1)S(1)}, bf16[128,256]{1,0:T(8,128)(2,1)S(1)}, u32[]{:S(2)}, u32[]{:S(2)}) %collective-permute-start.24) | collective-permute-done | bytes 65568 | tf_op jit(solution)/shard_map/ppermute | solution.py:390
  72.5 0.9 collective-permute-done.22
  73.5 1.0 collective-permute-start.25
  74.4 4.4 %collective-permute-done.25.refs_1_ = bf16[128,256]{1,0:T(8,128)(2,1)S(1)} collective-permute-done((bf16[128,256]{1,0:T(8,128)(2,1)S(1)}, bf16[128,256]{1,0:T(8,128)(2,1)S(1)}, u32[]{:S(2)}, u32[]{:S(2)}) %collective-permute-start.25) | collective-permute-done | bytes 65568 | tf_op jit(solution)/shard_map/ppermute | solution.py:390
  79.1 1.1 %collective-permute-start.27 = (f32[8,256]{1,0:T(8,128)S(1)}, f32[8,256]{1,0:T(8,128)S(1)}, u32[]{:S(2)}, u32[]{:S(2)}) collective-permute-start(f32[8,256]{1,0:T(8,128)S(1)} %get-tuple-element.109.refs_1_), channel_id=1, source_target_pairs={{0,16},{8,24},{16,0},{24,8},{1,17},{9,25},{17,1},{25,9},{2,18},{10... | collective-permute-start | bytes 24584 | tf_op jit(solution)/shard_map/ppermute | solution.py:395
  80.2 0.7 collective-permute-start.26
  81.0 2.0 %project.7.refs_0_ = f32[88,256]{1,0:T(8,128)S(1)} custom-call(f32[128,256]{1,0:T(8,128)S(1)} %get-tuple-element.108.field_ref.refs_13_, bf16[88,128]{1,0:T(8,128)(2,1)S(1)} %get-tuple-element.82.pick1_ref, bf16[88,128]{1,0:T(8,128)(2,1)S(1)} %get-tuple-element.83.pick2_ref, bf16[32,256,256]{2,1,0:T(8,128)(2,1)S(1)} %turn.3.refs_0_, ...), custom_call_target="tpu_custom_call" | custom-call | flops 339738624 | bytes 10792960 | tf_op jit(solution)/shard_map/project/pallas_call | solution.py:351
  83.0 2.4 %step.7 = (bf16[128,256]{1,0:T(8,128)(2,1)S(1)}, f32[88,256]{1,0:T(8,128)}, f32[128,256]{1,0:T(8,128)S(1)}, f32[128,256]{1,0:T(8,128)S(1)}, f32[88,256]{1,0:T(8,...) custom-call(f32[88,256]{1,0:T(8,128)S(1)} %project.7.refs_0_, ...), custom_call_target="tpu_custom_call" | custom-call | flops 339738624 | bytes 11546624 | tf_op jit(solution)/shard_map/step/pallas_call | solution.py:351
  85.4 0.4 collective-permute-start.31
  85.8 2.2 %collective-permute-start.30 = (bf16[128,256]{1,0:T(8,128)(2,1)S(1)}, bf16[128,256]{1,0:T(8,128)(2,1)S(1)}, u32[]{:S(2)}, u32[]{:S(2)}) collective-permute-start(bf16[128,256]{1,0:T(8,128)(2,1)S(1)} %get-tuple-element.116), channel_id=1, source_target_pairs={{0,2},{1,3},{2,0},{3,1},{4,6},{5,7},{6,4},{7,5},{8,10},{9,11},{10,... | collective-permute-start | bytes 196616 | tf_op jit(solution)/shard_map/ppermute | solution.py:390
  88.0 0.9 collective-permute-start.29
  88.9 2.2 %collective-permute-done.31 = bf16[128,256]{1,0:T(8,128)(2,1)S(1)} collective-permute-done((bf16[128,256]{1,0:T(8,128)(2,1)S(1)}, bf16[128,256]{1,0:T(8,128)(2,1)S(1)}, u32[]{:S(2)}, u32[]{:S(2)}) %collective-permute-start.31) | collective-permute-done | bytes 65568 | tf_op jit(solution)/shard_map/ppermute | solution.py:390
  91.1 0.2 collective-permute-done.30
  91.3 0.9 collective-permute-done.29
  92.3 1.0 collective-permute-start.32
  93.2 4.4 %collective-permute-done.32.refs_1_ = bf16[128,256]{1,0:T(8,128)(2,1)S(1)} collective-permute-done((bf16[128,256]{1,0:T(8,128)(2,1)S(1)}, bf16[128,256]{1,0:T(8,128)(2,1)S(1)}, u32[]{:S(2)}, u32[]{:S(2)}) %collective-permute-start.32) | collective-permute-done | bytes 65568 | tf_op jit(solution)/shard_map/ppermute | solution.py:390
  97.9 1.1 %collective-permute-start.34 = (f32[8,256]{1,0:T(8,128)S(1)}, f32[8,256]{1,0:T(8,128)S(1)}, u32[]{:S(2)}, u32[]{:S(2)}) collective-permute-start(f32[8,256]{1,0:T(8,128)S(1)} %get-tuple-element.119.refs_1_), channel_id=1, source_target_pairs={{0,16},{8,24},{16,0},{24,8},{1,17},{9,25},{17,1},{25,9},{2,18},{10... | collective-permute-start | bytes 24584 | tf_op jit(solution)/shard_map/ppermute | solution.py:395
  99.0 0.7 collective-permute-start.33
  99.7 1.2 %collective-permute-done.35.refs_4_ = f32[8,256]{1,0:T(8,128)S(1)} collective-permute-done((f32[8,256]{1,0:T(8,128)S(1)}, f32[8,256]{1,0:T(8,128)S(1)}, u32[]{:S(2)}, u32[]{:S(2)}) %collective-permute-start.35) | collective-permute-done | bytes 8224 | tf_op jit(solution)/shard_map/ppermute | solution.py:395
  101.0 0.7 collective-permute-done.34.refs_3_
  101.6 0.6 final.1
  (34 shorter events, 1.7 us)
Async XLA Ops:
  1.8 5.2 %collective-permute-start = (bf16[1,272,256]{2,1,0:T(8,128)(2,1)S(1)}, bf16[1,272,256]{2,1,0:T(8,128)(2,1)S(1)}, u32[]{:S(2)}, u32[]{:S(2)}) collective-permute-start(bf16[1,272,256]{2,1,0:T(8,128)(2,1)S(1)} %get-tuple-element.75), channel_id=1, source_target_pairs={{0,8},{8,16},{16,24},{24,0},{1,9},{9,17},{17,25},{25,1},{2,10},{10... | collective-permute-start | bytes 417800 | tf_op jit(solution)/shard_map/ppermute | solution.py:421
  7.4 7.0 %collective-permute-start.3 = (bf16[128,256]{1,0:T(8,128)(2,1)S(1)}, bf16[128,256]{1,0:T(8,128)(2,1)S(1)}, u32[]{:S(2)}, u32[]{:S(2)}) collective-permute-start(bf16[128,256]{1,0:T(8,128)(2,1)S(1)} %get-tuple-element.78.after_ref), channel_id=1, source_target_pairs={{0,3},{1,2},{2,1},{3,0},{4,7},{5,6},{6,5},{7,4},{8,11},{9,10},{10,... | collective-permute-start | bytes 196616 | tf_op jit(solution)/shard_map/ppermute | solution.py:390
  10.9 4.6 %collective-permute-start.2 = (bf16[128,256]{1,0:T(8,128)(2,1)S(1)}, bf16[128,256]{1,0:T(8,128)(2,1)S(1)}, u32[]{:S(2)}, u32[]{:S(2)}) collective-permute-start(bf16[128,256]{1,0:T(8,128)(2,1)S(1)} %get-tuple-element.78.after_ref), channel_id=1, source_target_pairs={{0,2},{1,3},{2,0},{3,1},{4,6},{5,7},{6,4},{7,5},{8,10},{9,11},{10,... | collective-permute-start | bytes 196616 | tf_op jit(solution)/shard_map/ppermute | solution.py:390
  11.3 4.9 %collective-permute-start.1 = (bf16[128,256]{1,0:T(8,128)(2,1)S(1)}, bf16[128,256]{1,0:T(8,128)(2,1)S(1)}, u32[]{:S(2)}, u32[]{:S(2)}) collective-permute-start(bf16[128,256]{1,0:T(8,128)(2,1)S(1)} %get-tuple-element.78.after_ref), channel_id=1, source_target_pairs={{0,1},{1,0},{2,3},{3,2},{4,5},{5,4},{6,7},{7,6},{8,9},{9,8},{10,11... | collective-permute-start | bytes 196616 | tf_op jit(solution)/shard_map/ppermute | solution.py:390
  16.3 6.6 %collective-permute-start.4 = (bf16[128,256]{1,0:T(8,128)(2,1)S(1)}, bf16[128,256]{1,0:T(8,128)(2,1)S(1)}, u32[]{:S(2)}, u32[]{:S(2)}) collective-permute-start(bf16[128,256]{1,0:T(8,128)(2,1)S(1)} %add_convert_fusion.4.refs_0_.after_ref), channel_id=1, source_target_pairs={{0,4},{1,5},{2,6},{3,7},{4,0},{5,1},{6,2},{7,3},{8,12},{9,13},{10,... | collective-permute-start | bytes 196616 | tf_op jit(solution)/shard_map/ppermute | solution.py:390
  22.9 4.2 %collective-permute-start.7 = (f32[8,256]{1,0:T(8,128)S(1)}, f32[8,256]{1,0:T(8,128)S(1)}, u32[]{:S(2)}, u32[]{:S(2)}) collective-permute-start(f32[8,256]{1,0:T(8,128)S(1)} %get-tuple-element.87.refs_1_), channel_id=1, source_target_pairs={{0,24},{8,16},{16,8},{24,0},{1,25},{9,17},{17,9},{25,1},{2,26},{10... | collective-permute-start | bytes 24584 | tf_op jit(solution)/shard_map/ppermute | solution.py:395
  23.0 4.2 %collective-permute-start.6 = (f32[8,256]{1,0:T(8,128)S(1)}, f32[8,256]{1,0:T(8,128)S(1)}, u32[]{:S(2)}, u32[]{:S(2)}) collective-permute-start(f32[8,256]{1,0:T(8,128)S(1)} %get-tuple-element.87.refs_1_), channel_id=1, source_target_pairs={{0,16},{8,24},{16,0},{24,8},{1,17},{9,25},{17,1},{25,9},{2,18},{10... | collective-permute-start | bytes 24584 | tf_op jit(solution)/shard_map/ppermute | solution.py:395
  23.3 3.9 %collective-permute-start.5 = (f32[8,256]{1,0:T(8,128)S(1)}, f32[8,256]{1,0:T(8,128)S(1)}, u32[]{:S(2)}, u32[]{:S(2)}) collective-permute-start(f32[8,256]{1,0:T(8,128)S(1)} %get-tuple-element.87.refs_1_), channel_id=1, source_target_pairs={{0,8},{8,0},{16,24},{24,16},{1,9},{9,1},{17,25},{25,17},{2,10},{10... | collective-permute-start | bytes 24584 | tf_op jit(solution)/shard_map/ppermute | solution.py:395
  29.1 5.8 %collective-permute-start.10 = (bf16[128,256]{1,0:T(8,128)(2,1)S(1)}, bf16[128,256]{1,0:T(8,128)(2,1)S(1)}, u32[]{:S(2)}, u32[]{:S(2)}) collective-permute-start(bf16[128,256]{1,0:T(8,128)(2,1)S(1)} %get-tuple-element.90.after_ref), channel_id=1, source_target_pairs={{0,3},{1,2},{2,1},{3,0},{4,7},{5,6},{6,5},{7,4},{8,11},{9,10},{10,... | collective-permute-start | bytes 196616 | tf_op jit(solution)/shard_map/ppermute | solution.py:390
  30.1 4.8 %collective-permute-start.9 = (bf16[128,256]{1,0:T(8,128)(2,1)S(1)}, bf16[128,256]{1,0:T(8,128)(2,1)S(1)}, u32[]{:S(2)}, u32[]{:S(2)}) collective-permute-start(bf16[128,256]{1,0:T(8,128)(2,1)S(1)} %get-tuple-element.90.after_ref), channel_id=1, source_target_pairs={{0,2},{1,3},{2,0},{3,1},{4,6},{5,7},{6,4},{7,5},{8,10},{9,11},{10,... | collective-permute-start | bytes 196616 | tf_op jit(solution)/shard_map/ppermute | solution.py:390
  31.5 4.3 %collective-permute-start.8 = (bf16[128,256]{1,0:T(8,128)(2,1)S(1)}, bf16[128,256]{1,0:T(8,128)(2,1)S(1)}, u32[]{:S(2)}, u32[]{:S(2)}) collective-permute-start(bf16[128,256]{1,0:T(8,128)(2,1)S(1)} %get-tuple-element.90.after_ref), channel_id=1, source_target_pairs={{0,1},{1,0},{2,3},{3,2},{4,5},{5,4},{6,7},{7,6},{8,9},{9,8},{10,11... | collective-permute-start | bytes 196616 | tf_op jit(solution)/shard_map/ppermute | solution.py:390
  35.8 5.9 %collective-permute-start.11 = (bf16[128,256]{1,0:T(8,128)(2,1)S(1)}, bf16[128,256]{1,0:T(8,128)(2,1)S(1)}, u32[]{:S(2)}, u32[]{:S(2)}) collective-permute-start(bf16[128,256]{1,0:T(8,128)(2,1)S(1)} %add_convert_fusion.3.refs_0_), channel_id=1, source_target_pairs={{0,4},{1,5},{2,6},{3,7},{4,0},{5,1},{6,2},{7,3},{8,12},{9,13},{10,... | collective-permute-start | bytes 196616 | tf_op jit(solution)/shard_map/ppermute | solution.py:390
  41.9 4.0 %collective-permute-start.14 = (f32[8,256]{1,0:T(8,128)S(1)}, f32[8,256]{1,0:T(8,128)S(1)}, u32[]{:S(2)}, u32[]{:S(2)}) collective-permute-start(f32[8,256]{1,0:T(8,128)S(1)} %get-tuple-element.94.refs_1_), channel_id=1, source_target_pairs={{0,24},{8,16},{16,8},{24,0},{1,25},{9,17},{17,9},{25,1},{2,26},{10... | collective-permute-start | bytes 24584 | tf_op jit(solution)/shard_map/ppermute | solution.py:395
  42.0 3.9 %collective-permute-start.13 = (f32[8,256]{1,0:T(8,128)S(1)}, f32[8,256]{1,0:T(8,128)S(1)}, u32[]{:S(2)}, u32[]{:S(2)}) collective-permute-start(f32[8,256]{1,0:T(8,128)S(1)} %get-tuple-element.94.refs_1_), channel_id=1, source_target_pairs={{0,16},{8,24},{16,0},{24,8},{1,17},{9,25},{17,1},{25,9},{2,18},{10... | collective-permute-start | bytes 24584 | tf_op jit(solution)/shard_map/ppermute | solution.py:395
  43.2 2.7 %collective-permute-start.12 = (f32[8,256]{1,0:T(8,128)S(1)}, f32[8,256]{1,0:T(8,128)S(1)}, u32[]{:S(2)}, u32[]{:S(2)}) collective-permute-start(f32[8,256]{1,0:T(8,128)S(1)} %get-tuple-element.94.refs_1_), channel_id=1, source_target_pairs={{0,8},{8,0},{16,24},{24,16},{1,9},{9,1},{17,25},{25,17},{2,10},{10... | collective-permute-start | bytes 24584 | tf_op jit(solution)/shard_map/ppermute | solution.py:395
  47.8 5.8 %collective-permute-start.17 = (bf16[128,256]{1,0:T(8,128)(2,1)S(1)}, bf16[128,256]{1,0:T(8,128)(2,1)S(1)}, u32[]{:S(2)}, u32[]{:S(2)}) collective-permute-start(bf16[128,256]{1,0:T(8,128)(2,1)S(1)} %get-tuple-element.96), channel_id=1, source_target_pairs={{0,3},{1,2},{2,1},{3,0},{4,7},{5,6},{6,5},{7,4},{8,11},{9,10},{10,... | collective-permute-start | bytes 196616 | tf_op jit(solution)/shard_map/ppermute | solution.py:390
  48.9 5.0 %collective-permute-start.16 = (bf16[128,256]{1,0:T(8,128)(2,1)S(1)}, bf16[128,256]{1,0:T(8,128)(2,1)S(1)}, u32[]{:S(2)}, u32[]{:S(2)}) collective-permute-start(bf16[128,256]{1,0:T(8,128)(2,1)S(1)} %get-tuple-element.96), channel_id=1, source_target_pairs={{0,2},{1,3},{2,0},{3,1},{4,6},{5,7},{6,4},{7,5},{8,10},{9,11},{10,... | collective-permute-start | bytes 196616 | tf_op jit(solution)/shard_map/ppermute | solution.py:390
  50.5 4.3 %collective-permute-start.15 = (bf16[128,256]{1,0:T(8,128)(2,1)S(1)}, bf16[128,256]{1,0:T(8,128)(2,1)S(1)}, u32[]{:S(2)}, u32[]{:S(2)}) collective-permute-start(bf16[128,256]{1,0:T(8,128)(2,1)S(1)} %get-tuple-element.96), channel_id=1, source_target_pairs={{0,1},{1,0},{2,3},{3,2},{4,5},{5,4},{6,7},{7,6},{8,9},{9,8},{10,11... | collective-permute-start | bytes 196616 | tf_op jit(solution)/shard_map/ppermute | solution.py:390
  54.8 5.8 %collective-permute-start.18 = (bf16[128,256]{1,0:T(8,128)(2,1)S(1)}, bf16[128,256]{1,0:T(8,128)(2,1)S(1)}, u32[]{:S(2)}, u32[]{:S(2)}) collective-permute-start(bf16[128,256]{1,0:T(8,128)(2,1)S(1)} %add_convert_fusion.2.refs_0_), channel_id=1, source_target_pairs={{0,4},{1,5},{2,6},{3,7},{4,0},{5,1},{6,2},{7,3},{8,12},{9,13},{10,... | collective-permute-start | bytes 196616 | tf_op jit(solution)/shard_map/ppermute | solution.py:390
  60.8 4.0 %collective-permute-start.21 = (f32[8,256]{1,0:T(8,128)S(1)}, f32[8,256]{1,0:T(8,128)S(1)}, u32[]{:S(2)}, u32[]{:S(2)}) collective-permute-start(f32[8,256]{1,0:T(8,128)S(1)} %get-tuple-element.99.refs_1_), channel_id=1, source_target_pairs={{0,24},{8,16},{16,8},{24,0},{1,25},{9,17},{17,9},{25,1},{2,26},{10... | collective-permute-start | bytes 24584 | tf_op jit(solution)/shard_map/ppermute | solution.py:395
  60.9 3.9 %collective-permute-start.20 = (f32[8,256]{1,0:T(8,128)S(1)}, f32[8,256]{1,0:T(8,128)S(1)}, u32[]{:S(2)}, u32[]{:S(2)}) collective-permute-start(f32[8,256]{1,0:T(8,128)S(1)} %get-tuple-element.99.refs_1_), channel_id=1, source_target_pairs={{0,16},{8,24},{16,0},{24,8},{1,17},{9,25},{17,1},{25,9},{2,18},{10... | collective-permute-start | bytes 24584 | tf_op jit(solution)/shard_map/ppermute | solution.py:395
  61.7 3.1 %collective-permute-start.19 = (f32[8,256]{1,0:T(8,128)S(1)}, f32[8,256]{1,0:T(8,128)S(1)}, u32[]{:S(2)}, u32[]{:S(2)}) collective-permute-start(f32[8,256]{1,0:T(8,128)S(1)} %get-tuple-element.99.refs_1_), channel_id=1, source_target_pairs={{0,8},{8,0},{16,24},{24,16},{1,9},{9,1},{17,25},{25,17},{2,10},{10... | collective-permute-start | bytes 24584 | tf_op jit(solution)/shard_map/ppermute | solution.py:395
  66.7 5.8 %collective-permute-start.24 = (bf16[128,256]{1,0:T(8,128)(2,1)S(1)}, bf16[128,256]{1,0:T(8,128)(2,1)S(1)}, u32[]{:S(2)}, u32[]{:S(2)}) collective-permute-start(bf16[128,256]{1,0:T(8,128)(2,1)S(1)} %get-tuple-element.106), channel_id=1, source_target_pairs={{0,3},{1,2},{2,1},{3,0},{4,7},{5,6},{6,5},{7,4},{8,11},{9,10},{10,... | collective-permute-start | bytes 196616 | tf_op jit(solution)/shard_map/ppermute | solution.py:390
  67.1 5.5 %collective-permute-start.23 = (bf16[128,256]{1,0:T(8,128)(2,1)S(1)}, bf16[128,256]{1,0:T(8,128)(2,1)S(1)}, u32[]{:S(2)}, u32[]{:S(2)}) collective-permute-start(bf16[128,256]{1,0:T(8,128)(2,1)S(1)} %get-tuple-element.106), channel_id=1, source_target_pairs={{0,2},{1,3},{2,0},{3,1},{4,6},{5,7},{6,4},{7,5},{8,10},{9,11},{10,... | collective-permute-start | bytes 196616 | tf_op jit(solution)/shard_map/ppermute | solution.py:390
  69.2 4.3 %collective-permute-start.22 = (bf16[128,256]{1,0:T(8,128)(2,1)S(1)}, bf16[128,256]{1,0:T(8,128)(2,1)S(1)}, u32[]{:S(2)}, u32[]{:S(2)}) collective-permute-start(bf16[128,256]{1,0:T(8,128)(2,1)S(1)} %get-tuple-element.106), channel_id=1, source_target_pairs={{0,1},{1,0},{2,3},{3,2},{4,5},{5,4},{6,7},{7,6},{8,9},{9,8},{10,11... | collective-permute-start | bytes 196616 | tf_op jit(solution)/shard_map/ppermute | solution.py:390
  73.5 5.4 %collective-permute-start.25 = (bf16[128,256]{1,0:T(8,128)(2,1)S(1)}, bf16[128,256]{1,0:T(8,128)(2,1)S(1)}, u32[]{:S(2)}, u32[]{:S(2)}) collective-permute-start(bf16[128,256]{1,0:T(8,128)(2,1)S(1)} %add_convert_fusion.1.refs_0_), channel_id=1, source_target_pairs={{0,4},{1,5},{2,6},{3,7},{4,0},{5,1},{6,2},{7,3},{8,12},{9,13},{10,... | collective-permute-start | bytes 196616 | tf_op jit(solution)/shard_map/ppermute | solution.py:390
  79.0 4.0 %collective-permute-start.28 = (f32[8,256]{1,0:T(8,128)S(1)}, f32[8,256]{1,0:T(8,128)S(1)}, u32[]{:S(2)}, u32[]{:S(2)}) collective-permute-start(f32[8,256]{1,0:T(8,128)S(1)} %get-tuple-element.109.refs_1_), channel_id=1, source_target_pairs={{0,24},{8,16},{16,8},{24,0},{1,25},{9,17},{17,9},{25,1},{2,26},{10... | collective-permute-start | bytes 24584 | tf_op jit(solution)/shard_map/ppermute | solution.py:395
  79.1 3.9 %collective-permute-start.27 = (f32[8,256]{1,0:T(8,128)S(1)}, f32[8,256]{1,0:T(8,128)S(1)}, u32[]{:S(2)}, u32[]{:S(2)}) collective-permute-start(f32[8,256]{1,0:T(8,128)S(1)} %get-tuple-element.109.refs_1_), channel_id=1, source_target_pairs={{0,16},{8,24},{16,0},{24,8},{1,17},{9,25},{17,1},{25,9},{2,18},{10... | collective-permute-start | bytes 24584 | tf_op jit(solution)/shard_map/ppermute | solution.py:395
  80.2 2.8 %collective-permute-start.26 = (f32[8,256]{1,0:T(8,128)S(1)}, f32[8,256]{1,0:T(8,128)S(1)}, u32[]{:S(2)}, u32[]{:S(2)}) collective-permute-start(f32[8,256]{1,0:T(8,128)S(1)} %get-tuple-element.109.refs_1_), channel_id=1, source_target_pairs={{0,8},{8,0},{16,24},{24,16},{1,9},{9,1},{17,25},{25,17},{2,10},{10... | collective-permute-start | bytes 24584 | tf_op jit(solution)/shard_map/ppermute | solution.py:395
  85.4 5.7 %collective-permute-start.31 = (bf16[128,256]{1,0:T(8,128)(2,1)S(1)}, bf16[128,256]{1,0:T(8,128)(2,1)S(1)}, u32[]{:S(2)}, u32[]{:S(2)}) collective-permute-start(bf16[128,256]{1,0:T(8,128)(2,1)S(1)} %get-tuple-element.116), channel_id=1, source_target_pairs={{0,3},{1,2},{2,1},{3,0},{4,7},{5,6},{6,5},{7,4},{8,11},{9,10},{10,... | collective-permute-start | bytes 196616 | tf_op jit(solution)/shard_map/ppermute | solution.py:390
  85.8 5.5 %collective-permute-start.30 = (bf16[128,256]{1,0:T(8,128)(2,1)S(1)}, bf16[128,256]{1,0:T(8,128)(2,1)S(1)}, u32[]{:S(2)}, u32[]{:S(2)}) collective-permute-start(bf16[128,256]{1,0:T(8,128)(2,1)S(1)} %get-tuple-element.116), channel_id=1, source_target_pairs={{0,2},{1,3},{2,0},{3,1},{4,6},{5,7},{6,4},{7,5},{8,10},{9,11},{10,... | collective-permute-start | bytes 196616 | tf_op jit(solution)/shard_map/ppermute | solution.py:390
  88.0 4.3 %collective-permute-start.29 = (bf16[128,256]{1,0:T(8,128)(2,1)S(1)}, bf16[128,256]{1,0:T(8,128)(2,1)S(1)}, u32[]{:S(2)}, u32[]{:S(2)}) collective-permute-start(bf16[128,256]{1,0:T(8,128)(2,1)S(1)} %get-tuple-element.116), channel_id=1, source_target_pairs={{0,1},{1,0},{2,3},{3,2},{4,5},{5,4},{6,7},{7,6},{8,9},{9,8},{10,11... | collective-permute-start | bytes 196616 | tf_op jit(solution)/shard_map/ppermute | solution.py:390
  92.3 5.4 %collective-permute-start.32 = (bf16[128,256]{1,0:T(8,128)(2,1)S(1)}, bf16[128,256]{1,0:T(8,128)(2,1)S(1)}, u32[]{:S(2)}, u32[]{:S(2)}) collective-permute-start(bf16[128,256]{1,0:T(8,128)(2,1)S(1)} %add_convert_fusion.refs_0_), channel_id=1, source_target_pairs={{0,4},{1,5},{2,6},{3,7},{4,0},{5,1},{6,2},{7,3},{8,12},{9,13},{10,... | collective-permute-start | bytes 196616 | tf_op jit(solution)/shard_map/ppermute | solution.py:390
  97.8 3.1 %collective-permute-start.35 = (f32[8,256]{1,0:T(8,128)S(1)}, f32[8,256]{1,0:T(8,128)S(1)}, u32[]{:S(2)}, u32[]{:S(2)}) collective-permute-start(f32[8,256]{1,0:T(8,128)S(1)} %get-tuple-element.119.refs_1_), channel_id=1, source_target_pairs={{0,24},{8,16},{16,8},{24,0},{1,25},{9,17},{17,9},{25,1},{2,26},{10... | collective-permute-start | bytes 24584 | tf_op jit(solution)/shard_map/ppermute | solution.py:395
  97.9 3.7 %collective-permute-start.34 = (f32[8,256]{1,0:T(8,128)S(1)}, f32[8,256]{1,0:T(8,128)S(1)}, u32[]{:S(2)}, u32[]{:S(2)}) collective-permute-start(f32[8,256]{1,0:T(8,128)S(1)} %get-tuple-element.119.refs_1_), channel_id=1, source_target_pairs={{0,16},{8,24},{16,0},{24,8},{1,17},{9,25},{17,1},{25,9},{2,18},{10... | collective-permute-start | bytes 24584 | tf_op jit(solution)/shard_map/ppermute | solution.py:395
  99.0 2.6 %collective-permute-start.33 = (f32[8,256]{1,0:T(8,128)S(1)}, f32[8,256]{1,0:T(8,128)S(1)}, u32[]{:S(2)}, u32[]{:S(2)}) collective-permute-start(f32[8,256]{1,0:T(8,128)S(1)} %get-tuple-element.119.refs_1_), channel_id=1, source_target_pairs={{0,8},{8,0},{16,24},{24,16},{1,9},{9,1},{17,25},{25,17},{2,10},{10... | collective-permute-start | bytes 24584 | tf_op jit(solution)/shard_map/ppermute | solution.py:395

commit v9 on v8

--- a/solution.py
+++ b/solution.py
@@ -390,9 +390,10 @@
     return lax.ppermute(block, axis, [(i, i ^ mask) for i in range(lax.axis_size(axis))])
 
 
-def orbit_packets(packet):
-    n = lax.axis_size("orbit")
-    return [packet] + [lax.ppermute(packet, "orbit", [(i, i ^ mask) for i in range(n)]) for mask in range(1, n)]
+def orbit_packets(packet, scenes_only):
+    near, far = swap(packet, "orbit", 1), swap(packet, "orbit", 3)
+    opposite = packet if scenes_only else swap(packet, "orbit", 2)
+    return [packet, near, opposite, far]
 
 
 def on_device(
@@ -469,7 +470,7 @@
         args = sums if res is None else sums + [res]
         kernel = functools.partial(gather_kernel, scenes, res is None, len(sums))
         field, packet = call(kernel, [(full, F32), ((OCTET, width), F32)], [], "finish", args)
-        return field, orbit_packets(packet)
+        return field, orbit_packets(packet, res is None)
 
     sent, coef, ejac = call(
         rhs_kernel,

time: 103 us -> 101 us (0.981)
  starting transfers between devices: 36.4 us -> 34.5 us
    ppermute x15 -> x0, starting transfers between devices: 9.59 us -> none  [orbit_packets(): lax.ppermute(packet, 'orbit', [(i, i ^ mask) for i in range(n)])]
    ppermute x20 -> x34, starting transfers between devices: 26.3 us -> 33.9 us  [swap(): lax.ppermute(block, axis, [(i, i ^ mask) for i in range(lax.axis_size(axi...]
    ppermute x20 -> x34, waiting for transfers between devices: 31.6 us -> 34.4 us  [swap(): lax.ppermute(block, axis, [(i, i ^ mask) for i in range(lax.axis_size(axi...]
    ppermute x15 -> x0, waiting for transfers between devices: 1.92 us -> none  [orbit_packets(): lax.ppermute(packet, 'orbit', [(i, i ^ mask) for i in range(n)])]
  transfers between devices with their start and end apart: 36 -> 35, of which waited for: 20 -> 21; matrix products, arithmetic and copies ran while one was open for 0% -> 0% of each run, Pallas kernels for 20% -> 20%
where the time goes in v9:
time: 101 us
  starting transfers between devices  34.5 us (34%)
  waiting for transfers between devices  34.4 us (34%)
  Pallas kernels  31.2 us (31%)
    ppermute x34, waiting for transfers between devices, swap(): lax.ppermute(block, axis, [(i, i ^ mask) for i in range(lax.axis_size(axi...  34.4 us
    ppermute x34, starting transfers between devices, swap(): lax.ppermute(block, axis, [(i, i ^ mask) for i in range(lax.axis_size(axi...  33.9 us
    pallas_call x20, Pallas kernels, call(): pl.pallas_call(kernel, out_shape=[jax.ShapeDtypeStruct(*o) for o in outs]...  31.2 us
  transfers between devices with their start and end apart: 35, of which 21 were waited for; matrix products, arithmetic and copies ran while one was open for 0% of the time, Pallas kernels for 20%

profile of v9, /device:TPU:0, one launch (start us, length us, event | category | flops | bytes accessed | tf_op | source)
XLA Modules:
  0.0 101.2 jit_solution(14885319160123190969)
XLA Ops:
  0.6 1.1 %pack.1 = (f32[16,2,128]{2,1,0:T(2,128)S(1)}, f32[16,2,128]{2,1,0:T(2,128)S(1)}, f32[64,2,128]{2,1,0:T(2,128)S(1)}, f32[64,2,128]{2,1,0:T(2,128)S(1)}, s32[1,64]...) custom-call(bf16[16,256,256]{2,1,0:T(8,128)(2,1)} %bitcast.9, ...), custom_call_target="tpu_custom_call" | custom-call | bytes 2261888 | tf_op jit(solution)/shard_map/pack/pallas_call | solution.py:351
  1.8 0.5 collective-permute-start
  2.3 4.5 %setup.1 = (bf16[64,256,256]{2,1,0:T(8,128)(2,1)S(1)}, bf16[16,256,256]{2,1,0:T(8,128)(2,1)S(1)}, f32[3,80,128]{2,1,0:T(8,128)S(1)}, bf16[128,88]{1,0:T(8,128)(2...) custom-call(bf16[64,256,256]{2,1,0:T(8,128)(2,1)} %bitcast.11, ...), custom_call_target="tpu_custom_call" | custom-call | flops 339738624 | bytes 10658560 | tf_op jit(solution)/shard_map/setup/pallas_call | solution.py:351
  7.0 0.4 rhs.1
  7.4 3.5 %collective-permute-start.3 = (bf16[128,256]{1,0:T(8,128)(2,1)S(1)}, bf16[128,256]{1,0:T(8,128)(2,1)S(1)}, u32[]{:S(2)}, u32[]{:S(2)}) collective-permute-start(bf16[128,256]{1,0:T(8,128)(2,1)S(1)} %get-tuple-element.78.after_ref), channel_id=1, source_target_pairs={{0,3},{1,2},{2,1},{3,0},{4,7},{5,6},{6,5},{7,4},{8,11},{9,10},{10,... | collective-permute-start | bytes 196616 | tf_op jit(solution)/shard_map/ppermute | solution.py:390
  10.9 0.5 collective-permute-start.2
  11.3 0.2 collective-permute-start.1
  11.5 2.8 %turn.3.refs_0_ = bf16[32,256,256]{2,1,0:T(8,128)(2,1)S(1)} custom-call(bf16[128,256]{1,0:T(8,128)(2,1)S(1)} %get-tuple-element.78.after_ref, bf16[64,256,256]{2,1,0:T(8,128)(2,1)S(1)} %get-tuple-element.79.refs_0_.refs_9_), custom_call_target="tpu_custom_call" | custom-call | flops 135895456 | bytes 8454144 | tf_op jit(solution)/shard_map/turn/pallas_call | solution.py:351
  14.3 1.2 %collective-permute-done.2 = bf16[128,256]{1,0:T(8,128)(2,1)S(1)} collective-permute-done((bf16[128,256]{1,0:T(8,128)(2,1)S(1)}, bf16[128,256]{1,0:T(8,128)(2,1)S(1)}, u32[]{:S(2)}, u32[]{:S(2)}) %collective-permute-start.2) | collective-permute-done | bytes 65568 | tf_op jit(solution)/shard_map/ppermute | solution.py:390
  15.5 0.7 collective-permute-done.1
  16.3 2.7 %collective-permute-start.4 = (bf16[128,256]{1,0:T(8,128)(2,1)S(1)}, bf16[128,256]{1,0:T(8,128)(2,1)S(1)}, u32[]{:S(2)}, u32[]{:S(2)}) collective-permute-start(bf16[128,256]{1,0:T(8,128)(2,1)S(1)} %add_convert_fusion.4.refs_0_.after_ref), channel_id=1, source_target_pairs={{0,4},{1,5},{2,6},{3,7},{4,0},{5,1},{6,2},{7,3},{8,12},{9,13},{10,... | collective-permute-start | bytes 196616 | tf_op jit(solution)/shard_map/ppermute | solution.py:390
  18.9 2.8 %turn.4.refs_1_ = bf16[32,256,256]{2,1,0:T(8,128)(2,1)S(1)} custom-call(bf16[128,256]{1,0:T(8,128)(2,1)S(1)} %add_convert_fusion.4.refs_0_.after_ref, bf16[64,256,256]{2,1,0:T(8,128)(2,1)S(1)} %get-tuple-element.79.refs_0_.refs_9_), custom_call_target="tpu_custom_call" | custom-call | flops 135895456 | bytes 8454144 | tf_op jit(solution)/shard_map/turn/pallas_call | solution.py:351
  21.7 1.2 %collective-permute-done.4.refs_1_ = bf16[128,256]{1,0:T(8,128)(2,1)S(1)} collective-permute-done((bf16[128,256]{1,0:T(8,128)(2,1)S(1)}, bf16[128,256]{1,0:T(8,128)(2,1)S(1)}, u32[]{:S(2)}, u32[]{:S(2)}) %collective-permute-start.4) | collective-permute-done | bytes 65568 | tf_op jit(solution)/shard_map/ppermute | solution.py:390
  23.1 2.3 %project.4.refs_0_ = f32[88,256]{1,0:T(8,128)S(1)} custom-call(f32[128,256]{1,0:T(8,128)S(1)} %get-tuple-element.81.field_ref.refs_12_.refs_2_, bf16[88,128]{1,0:T(8,128)(2,1)S(1)} %get-tuple-element.82.pick1_ref, bf16[88,128]{1,0:T(8,128)(2,1)S(1)} %get-tuple-element.83.pick2_ref, bf16[32,256,256]{2,1,0:T(8,128)(2,1)S(1)} %turn.3.refs_0_, ...), custom_call_target="tpu_custom_call" | custom-call | flops 339738624 | bytes 10792960 | tf_op jit(solution)/shard_map/project/pallas_call | solution.py:351
  25.4 0.7 collective-permute-done.6.refs_4_
  26.1 1.9 %step.4 = (bf16[128,256]{1,0:T(8,128)(2,1)S(1)}, f32[88,256]{1,0:T(8,128)S(1)}) custom-call(f32[88,256]{1,0:T(8,128)S(1)} %project.4.refs_0_, f32[8,256]{1,0:T(8,128)S(1)} %get-tuple-element.87.refs_1_.refs_3_, f32[8,256]{1,0:T(8,128)S(1)} %collective-permute-done.5.refs_2_, f32[8,256]{1,0:T(8,128)S(1)} %get-tuple-element.87.refs_1_.refs_3_, ...), custom_call_target="tpu_custom_call" | custom-call | flops 339738624 | bytes 11067392 | tf_op jit(solution)/shard_map/step/pallas_call | solution.py:351
  28.0 1.3 %collective-permute-start.9 = (bf16[128,256]{1,0:T(8,128)(2,1)S(1)}, bf16[128,256]{1,0:T(8,128)(2,1)S(1)}, u32[]{:S(2)}, u32[]{:S(2)}) collective-permute-start(bf16[128,256]{1,0:T(8,128)(2,1)S(1)} %get-tuple-element.90.after_ref), channel_id=1, source_target_pairs={{0,3},{1,2},{2,1},{3,0},{4,7},{5,6},{6,5},{7,4},{8,11},{9,10},{10,... | collective-permute-start | bytes 196616 | tf_op jit(solution)/shard_map/ppermute | solution.py:390
  29.3 1.6 %collective-permute-start.8 = (bf16[128,256]{1,0:T(8,128)(2,1)S(1)}, bf16[128,256]{1,0:T(8,128)(2,1)S(1)}, u32[]{:S(2)}, u32[]{:S(2)}) collective-permute-start(bf16[128,256]{1,0:T(8,128)(2,1)S(1)} %get-tuple-element.90.after_ref), channel_id=1, source_target_pairs={{0,2},{1,3},{2,0},{3,1},{4,6},{5,7},{6,4},{7,5},{8,10},{9,11},{10,... | collective-permute-start | bytes 196616 | tf_op jit(solution)/shard_map/ppermute | solution.py:390
  30.9 0.6 collective-permute-start.7
  31.6 2.0 %collective-permute-done.9 = bf16[128,256]{1,0:T(8,128)(2,1)S(1)} collective-permute-done((bf16[128,256]{1,0:T(8,128)(2,1)S(1)}, bf16[128,256]{1,0:T(8,128)(2,1)S(1)}, u32[]{:S(2)}, u32[]{:S(2)}) %collective-permute-start.9) | collective-permute-done | bytes 65568 | tf_op jit(solution)/shard_map/ppermute | solution.py:390
  33.6 0.7 collective-permute-done.8
  34.3 0.9 collective-permute-done.7
  35.2 1.9 %collective-permute-start.10 = (bf16[128,256]{1,0:T(8,128)(2,1)S(1)}, bf16[128,256]{1,0:T(8,128)(2,1)S(1)}, u32[]{:S(2)}, u32[]{:S(2)}) collective-permute-start(bf16[128,256]{1,0:T(8,128)(2,1)S(1)} %add_convert_fusion.3.refs_0_), channel_id=1, source_target_pairs={{0,4},{1,5},{2,6},{3,7},{4,0},{5,1},{6,2},{7,3},{8,12},{9,13},{10,... | collective-permute-start | bytes 196616 | tf_op jit(solution)/shard_map/ppermute | solution.py:390
  37.1 1.6 %turn.5 = (bf16[16,256,256]{2,1,0:T(8,128)(2,1)S(1)}, bf16[1,256,256]{2,1,0:T(8,128)(2,1)S(1)}) custom-call(bf16[128,256]{1,0:T(8,128)(2,1)S(1)} %get-tuple-element.90.after_ref, bf16[16,256,256]{2,1,0:T(8,128)(2,1)S(1)} %get-tuple-element.85.refs_2_.refs_10_.refs_0_, bf16[1,256,256]{2,1,0:T(8,128)(2,1)S(1)} %get-tuple-element.86.refs_3_.refs_11_.refs_1_), custom_call_target="tpu_custom_call" | custom-call | flops 72194456 | bytes 2293760 | tf_op jit(solution)/shard_map/turn/pallas_call | solution.py:351
  38.8 2.4 %collective-permute-done.10.refs_1_ = bf16[128,256]{1,0:T(8,128)(2,1)S(1)} collective-permute-done((bf16[128,256]{1,0:T(8,128)(2,1)S(1)}, bf16[128,256]{1,0:T(8,128)(2,1)S(1)}, u32[]{:S(2)}, u32[]{:S(2)}) %collective-permute-start.10) | collective-permute-done | bytes 65568 | tf_op jit(solution)/shard_map/ppermute | solution.py:390
  41.4 0.9 collective-permute-start.12
  42.3 0.9 collective-permute-start.11
  43.3 2.0 %project.5.refs_0_ = f32[88,256]{1,0:T(8,128)S(1)} custom-call(f32[128,256]{1,0:T(8,128)S(1)} %get-tuple-element.91.field_ref.refs_13_, bf16[88,128]{1,0:T(8,128)(2,1)S(1)} %get-tuple-element.82.pick1_ref, bf16[88,128]{1,0:T(8,128)(2,1)S(1)} %get-tuple-element.83.pick2_ref, bf16[32,256,256]{2,1,0:T(8,128)(2,1)S(1)} %turn.3.refs_0_, ...), custom_call_target="tpu_custom_call" | custom-call | flops 339738624 | bytes 10792960 | tf_op jit(solution)/shard_map/project/pallas_call | solution.py:351
  45.3 1.9 %step.5 = (bf16[128,256]{1,0:T(8,128)(2,1)S(1)}, f32[88,256]{1,0:T(8,128)S(1)}, f32[128,256]{1,0:T(8,128)S(1)}, f32[128,256]{1,0:T(8,128)S(1)}, f32[88,256]{1,0:...) custom-call(f32[88,256]{1,0:T(8,128)S(1)} %project.5.refs_0_, ...), custom_call_target="tpu_custom_call" | custom-call | flops 339738624 | bytes 11304960 | tf_op jit(solution)/shard_map/step/pallas_call | solution.py:351
  47.3 0.5 collective-permute-start.16
  47.8 1.6 %collective-permute-start.15 = (bf16[128,256]{1,0:T(8,128)(2,1)S(1)}, bf16[128,256]{1,0:T(8,128)(2,1)S(1)}, u32[]{:S(2)}, u32[]{:S(2)}) collective-permute-start(bf16[128,256]{1,0:T(8,128)(2,1)S(1)} %get-tuple-element.96), channel_id=1, source_target_pairs={{0,2},{1,3},{2,0},{3,1},{4,6},{5,7},{6,4},{7,5},{8,10},{9,11},{10,... | collective-permute-start | bytes 196616 | tf_op jit(solution)/shard_map/ppermute | solution.py:390
  49.4 1.4 %collective-permute-start.14 = (bf16[128,256]{1,0:T(8,128)(2,1)S(1)}, bf16[128,256]{1,0:T(8,128)(2,1)S(1)}, u32[]{:S(2)}, u32[]{:S(2)}) collective-permute-start(bf16[128,256]{1,0:T(8,128)(2,1)S(1)} %get-tuple-element.96), channel_id=1, source_target_pairs={{0,1},{1,0},{2,3},{3,2},{4,5},{5,4},{6,7},{7,6},{8,9},{9,8},{10,11... | collective-permute-start | bytes 196616 | tf_op jit(solution)/shard_map/ppermute | solution.py:390
  50.8 2.2 %collective-permute-done.16 = bf16[128,256]{1,0:T(8,128)(2,1)S(1)} collective-permute-done((bf16[128,256]{1,0:T(8,128)(2,1)S(1)}, bf16[128,256]{1,0:T(8,128)(2,1)S(1)}, u32[]{:S(2)}, u32[]{:S(2)}) %collective-permute-start.16) | collective-permute-done | bytes 65568 | tf_op jit(solution)/shard_map/ppermute | solution.py:390
  53.0 0.7 collective-permute-done.14
  53.7 1.4 %collective-permute-start.17 = (bf16[128,256]{1,0:T(8,128)(2,1)S(1)}, bf16[128,256]{1,0:T(8,128)(2,1)S(1)}, u32[]{:S(2)}, u32[]{:S(2)}) collective-permute-start(bf16[128,256]{1,0:T(8,128)(2,1)S(1)} %add_convert_fusion.2.refs_0_), channel_id=1, source_target_pairs={{0,4},{1,5},{2,6},{3,7},{4,0},{5,1},{6,2},{7,3},{8,12},{9,13},{10,... | collective-permute-start | bytes 196616 | tf_op jit(solution)/shard_map/ppermute | solution.py:390
  55.1 4.4 %collective-permute-done.17.refs_1_ = bf16[128,256]{1,0:T(8,128)(2,1)S(1)} collective-permute-done((bf16[128,256]{1,0:T(8,128)(2,1)S(1)}, bf16[128,256]{1,0:T(8,128)(2,1)S(1)}, u32[]{:S(2)}, u32[]{:S(2)}) %collective-permute-start.17) | collective-permute-done | bytes 65568 | tf_op jit(solution)/shard_map/ppermute | solution.py:390
  59.5 0.2 finish.7
  59.8 1.4 %collective-permute-start.19 = (f32[8,256]{1,0:T(8,128)S(1)}, f32[8,256]{1,0:T(8,128)S(1)}, u32[]{:S(2)}, u32[]{:S(2)}) collective-permute-start(f32[8,256]{1,0:T(8,128)S(1)} %get-tuple-element.99.refs_1_), channel_id=1, source_target_pairs={{0,16},{8,24},{16,0},{24,8},{1,17},{9,25},{17,1},{25,9},{2,18},{10... | collective-permute-start | bytes 24584 | tf_op jit(solution)/shard_map/ppermute | solution.py:390
  61.2 0.4 collective-permute-start.18
  61.6 2.0 %project.6.refs_0_ = f32[88,256]{1,0:T(8,128)S(1)} custom-call(f32[128,256]{1,0:T(8,128)S(1)} %get-tuple-element.98.field_ref.refs_13_, bf16[88,128]{1,0:T(8,128)(2,1)S(1)} %get-tuple-element.82.pick1_ref, bf16[88,128]{1,0:T(8,128)(2,1)S(1)} %get-tuple-element.83.pick2_ref, bf16[32,256,256]{2,1,0:T(8,128)(2,1)S(1)} %turn.3.refs_0_, ...), custom_call_target="tpu_custom_call" | custom-call | flops 339738624 | bytes 10792960 | tf_op jit(solution)/shard_map/project/pallas_call | solution.py:351
  63.7 1.9 %step.6 = (bf16[128,256]{1,0:T(8,128)(2,1)S(1)}, f32[88,256]{1,0:T(8,128)S(1)}, f32[128,256]{1,0:T(8,128)S(1)}, f32[128,256]{1,0:T(8,128)S(1)}, f32[88,256]{1,0:...) custom-call(f32[88,256]{1,0:T(8,128)S(1)} %project.6.refs_0_, ...), custom_call_target="tpu_custom_call" | custom-call | flops 339738624 | bytes 11546624 | tf_op jit(solution)/shard_map/step/pallas_call | solution.py:351
  65.6 0.7 collective-permute-start.23
  66.4 2.1 %collective-permute-start.22 = (bf16[128,256]{1,0:T(8,128)(2,1)S(1)}, bf16[128,256]{1,0:T(8,128)(2,1)S(1)}, u32[]{:S(2)}, u32[]{:S(2)}) collective-permute-start(bf16[128,256]{1,0:T(8,128)(2,1)S(1)} %get-tuple-element.106), channel_id=1, source_target_pairs={{0,2},{1,3},{2,0},{3,1},{4,6},{5,7},{6,4},{7,5},{8,10},{9,11},{10,... | collective-permute-start | bytes 196616 | tf_op jit(solution)/shard_map/ppermute | solution.py:390
  68.5 0.7 collective-permute-start.21
  69.2 2.3 %collective-permute-done.23 = bf16[128,256]{1,0:T(8,128)(2,1)S(1)} collective-permute-done((bf16[128,256]{1,0:T(8,128)(2,1)S(1)}, bf16[128,256]{1,0:T(8,128)(2,1)S(1)}, u32[]{:S(2)}, u32[]{:S(2)}) %collective-permute-start.23) | collective-permute-done | bytes 65568 | tf_op jit(solution)/shard_map/ppermute | solution.py:390
  71.5 0.4 collective-permute-done.22
  71.8 0.9 collective-permute-done.21
  72.8 1.0 collective-permute-start.24
  73.8 4.4 %collective-permute-done.24.refs_1_ = bf16[128,256]{1,0:T(8,128)(2,1)S(1)} collective-permute-done((bf16[128,256]{1,0:T(8,128)(2,1)S(1)}, bf16[128,256]{1,0:T(8,128)(2,1)S(1)}, u32[]{:S(2)}, u32[]{:S(2)}) %collective-permute-start.24) | collective-permute-done | bytes 65568 | tf_op jit(solution)/shard_map/ppermute | solution.py:390
  78.4 1.0 %collective-permute-start.26 = (f32[8,256]{1,0:T(8,128)S(1)}, f32[8,256]{1,0:T(8,128)S(1)}, u32[]{:S(2)}, u32[]{:S(2)}) collective-permute-start(f32[8,256]{1,0:T(8,128)S(1)} %get-tuple-element.109.refs_1_), channel_id=1, source_target_pairs={{0,16},{8,24},{16,0},{24,8},{1,17},{9,25},{17,1},{25,9},{2,18},{10... | collective-permute-start | bytes 24584 | tf_op jit(solution)/shard_map/ppermute | solution.py:390
  79.4 0.8 collective-permute-start.25
  80.3 2.0 %project.7.refs_0_ = f32[88,256]{1,0:T(8,128)S(1)} custom-call(f32[128,256]{1,0:T(8,128)S(1)} %get-tuple-element.108.field_ref.refs_13_, bf16[88,128]{1,0:T(8,128)(2,1)S(1)} %get-tuple-element.82.pick1_ref, bf16[88,128]{1,0:T(8,128)(2,1)S(1)} %get-tuple-element.83.pick2_ref, bf16[32,256,256]{2,1,0:T(8,128)(2,1)S(1)} %turn.3.refs_0_, ...), custom_call_target="tpu_custom_call" | custom-call | flops 339738624 | bytes 10792960 | tf_op jit(solution)/shard_map/project/pallas_call | solution.py:351
  82.3 2.4 %step.7 = (bf16[128,256]{1,0:T(8,128)(2,1)S(1)}, f32[88,256]{1,0:T(8,128)}, f32[128,256]{1,0:T(8,128)S(1)}, f32[128,256]{1,0:T(8,128)S(1)}, f32[88,256]{1,0:T(8,...) custom-call(f32[88,256]{1,0:T(8,128)S(1)} %project.7.refs_0_, ...), custom_call_target="tpu_custom_call" | custom-call | flops 339738624 | bytes 11546624 | tf_op jit(solution)/shard_map/step/pallas_call | solution.py:351
  84.7 2.1 %collective-permute-start.29 = (bf16[128,256]{1,0:T(8,128)(2,1)S(1)}, bf16[128,256]{1,0:T(8,128)(2,1)S(1)}, u32[]{:S(2)}, u32[]{:S(2)}) collective-permute-start(bf16[128,256]{1,0:T(8,128)(2,1)S(1)} %get-tuple-element.116), channel_id=1, source_target_pairs={{0,2},{1,3},{2,0},{3,1},{4,6},{5,7},{6,4},{7,5},{8,10},{9,11},{10,... | collective-permute-start | bytes 196616 | tf_op jit(solution)/shard_map/ppermute | solution.py:390
  86.9 1.3 %collective-permute-start.28 = (bf16[128,256]{1,0:T(8,128)(2,1)S(1)}, bf16[128,256]{1,0:T(8,128)(2,1)S(1)}, u32[]{:S(2)}, u32[]{:S(2)}) collective-permute-start(bf16[128,256]{1,0:T(8,128)(2,1)S(1)} %get-tuple-element.116), channel_id=1, source_target_pairs={{0,1},{1,0},{2,3},{3,2},{4,5},{5,4},{6,7},{7,6},{8,9},{9,8},{10,11... | collective-permute-start | bytes 196616 | tf_op jit(solution)/shard_map/ppermute | solution.py:390
  88.2 2.2 %collective-permute-done.30 = bf16[128,256]{1,0:T(8,128)(2,1)S(1)} collective-permute-done((bf16[128,256]{1,0:T(8,128)(2,1)S(1)}, bf16[128,256]{1,0:T(8,128)(2,1)S(1)}, u32[]{:S(2)}, u32[]{:S(2)}) %collective-permute-start.30) | collective-permute-done | bytes 65568 | tf_op jit(solution)/shard_map/ppermute | solution.py:390
  90.4 0.8 collective-permute-done.28
  91.2 0.9 collective-permute-start.31
  92.1 4.4 %collective-permute-done.31.refs_1_ = bf16[128,256]{1,0:T(8,128)(2,1)S(1)} collective-permute-done((bf16[128,256]{1,0:T(8,128)(2,1)S(1)}, bf16[128,256]{1,0:T(8,128)(2,1)S(1)}, u32[]{:S(2)}, u32[]{:S(2)}) %collective-permute-start.31) | collective-permute-done | bytes 65568 | tf_op jit(solution)/shard_map/ppermute | solution.py:390
  96.8 1.4 %collective-permute-start.33 = (f32[8,256]{1,0:T(8,128)S(1)}, f32[8,256]{1,0:T(8,128)S(1)}, u32[]{:S(2)}, u32[]{:S(2)}) collective-permute-start(f32[8,256]{1,0:T(8,128)S(1)} %get-tuple-element.119.refs_1_), channel_id=1, source_target_pairs={{0,16},{8,24},{16,0},{24,8},{1,17},{9,25},{17,1},{25,9},{2,18},{10... | collective-permute-start | bytes 24584 | tf_op jit(solution)/shard_map/ppermute | solution.py:390
  98.2 0.4 collective-permute-start.32
  98.7 1.2 %collective-permute-done.34.refs_4_ = f32[8,256]{1,0:T(8,128)S(1)} collective-permute-done((f32[8,256]{1,0:T(8,128)S(1)}, f32[8,256]{1,0:T(8,128)S(1)}, u32[]{:S(2)}, u32[]{:S(2)}) %collective-permute-start.34) | collective-permute-done | bytes 8224 | tf_op jit(solution)/shard_map/ppermute | solution.py:390
  99.9 0.7 collective-permute-done.33.refs_3_
  100.5 0.6 final.1
  (32 shorter events, 1.4 us)
Async XLA Ops:
  1.8 5.2 %collective-permute-start = (bf16[1,272,256]{2,1,0:T(8,128)(2,1)S(1)}, bf16[1,272,256]{2,1,0:T(8,128)(2,1)S(1)}, u32[]{:S(2)}, u32[]{:S(2)}) collective-permute-start(bf16[1,272,256]{2,1,0:T(8,128)(2,1)S(1)} %get-tuple-element.75), channel_id=1, source_target_pairs={{0,8},{8,16},{16,24},{24,0},{1,9},{9,17},{17,25},{25,1},{2,10},{10... | collective-permute-start | bytes 417800 | tf_op jit(solution)/shard_map/ppermute | solution.py:422
  7.4 7.0 %collective-permute-start.3 = (bf16[128,256]{1,0:T(8,128)(2,1)S(1)}, bf16[128,256]{1,0:T(8,128)(2,1)S(1)}, u32[]{:S(2)}, u32[]{:S(2)}) collective-permute-start(bf16[128,256]{1,0:T(8,128)(2,1)S(1)} %get-tuple-element.78.after_ref), channel_id=1, source_target_pairs={{0,3},{1,2},{2,1},{3,0},{4,7},{5,6},{6,5},{7,4},{8,11},{9,10},{10,... | collective-permute-start | bytes 196616 | tf_op jit(solution)/shard_map/ppermute | solution.py:390
  10.9 4.6 %collective-permute-start.2 = (bf16[128,256]{1,0:T(8,128)(2,1)S(1)}, bf16[128,256]{1,0:T(8,128)(2,1)S(1)}, u32[]{:S(2)}, u32[]{:S(2)}) collective-permute-start(bf16[128,256]{1,0:T(8,128)(2,1)S(1)} %get-tuple-element.78.after_ref), channel_id=1, source_target_pairs={{0,2},{1,3},{2,0},{3,1},{4,6},{5,7},{6,4},{7,5},{8,10},{9,11},{10,... | collective-permute-start | bytes 196616 | tf_op jit(solution)/shard_map/ppermute | solution.py:390
  11.3 4.9 %collective-permute-start.1 = (bf16[128,256]{1,0:T(8,128)(2,1)S(1)}, bf16[128,256]{1,0:T(8,128)(2,1)S(1)}, u32[]{:S(2)}, u32[]{:S(2)}) collective-permute-start(bf16[128,256]{1,0:T(8,128)(2,1)S(1)} %get-tuple-element.78.after_ref), channel_id=1, source_target_pairs={{0,1},{1,0},{2,3},{3,2},{4,5},{5,4},{6,7},{7,6},{8,9},{9,8},{10,11... | collective-permute-start | bytes 196616 | tf_op jit(solution)/shard_map/ppermute | solution.py:390
  16.3 6.6 %collective-permute-start.4 = (bf16[128,256]{1,0:T(8,128)(2,1)S(1)}, bf16[128,256]{1,0:T(8,128)(2,1)S(1)}, u32[]{:S(2)}, u32[]{:S(2)}) collective-permute-start(bf16[128,256]{1,0:T(8,128)(2,1)S(1)} %add_convert_fusion.4.refs_0_.after_ref), channel_id=1, source_target_pairs={{0,4},{1,5},{2,6},{3,7},{4,0},{5,1},{6,2},{7,3},{8,12},{9,13},{10,... | collective-permute-start | bytes 196616 | tf_op jit(solution)/shard_map/ppermute | solution.py:390
  22.9 3.1 %collective-permute-start.6 = (f32[8,256]{1,0:T(8,128)S(1)}, f32[8,256]{1,0:T(8,128)S(1)}, u32[]{:S(2)}, u32[]{:S(2)}) collective-permute-start(f32[8,256]{1,0:T(8,128)S(1)} %get-tuple-element.87.refs_1_.refs_3_), channel_id=1, source_target_pairs={{0,24},{8,16},{16,8},{24,0},{1,25},{9,17},{17,9},{25,1},{2,26},{10... | collective-permute-start | bytes 24584 | tf_op jit(solution)/shard_map/ppermute | solution.py:390
  23.0 3.1 %collective-permute-start.5 = (f32[8,256]{1,0:T(8,128)S(1)}, f32[8,256]{1,0:T(8,128)S(1)}, u32[]{:S(2)}, u32[]{:S(2)}) collective-permute-start(f32[8,256]{1,0:T(8,128)S(1)} %get-tuple-element.87.refs_1_.refs_3_), channel_id=1, source_target_pairs={{0,8},{8,0},{16,24},{24,16},{1,9},{9,1},{17,25},{25,17},{2,10},{10... | collective-permute-start | bytes 24584 | tf_op jit(solution)/shard_map/ppermute | solution.py:390
  28.0 5.6 %collective-permute-start.9 = (bf16[128,256]{1,0:T(8,128)(2,1)S(1)}, bf16[128,256]{1,0:T(8,128)(2,1)S(1)}, u32[]{:S(2)}, u32[]{:S(2)}) collective-permute-start(bf16[128,256]{1,0:T(8,128)(2,1)S(1)} %get-tuple-element.90.after_ref), channel_id=1, source_target_pairs={{0,3},{1,2},{2,1},{3,0},{4,7},{5,6},{6,5},{7,4},{8,11},{9,10},{10,... | collective-permute-start | bytes 196616 | tf_op jit(solution)/shard_map/ppermute | solution.py:390
  29.3 5.0 %collective-permute-start.8 = (bf16[128,256]{1,0:T(8,128)(2,1)S(1)}, bf16[128,256]{1,0:T(8,128)(2,1)S(1)}, u32[]{:S(2)}, u32[]{:S(2)}) collective-permute-start(bf16[128,256]{1,0:T(8,128)(2,1)S(1)} %get-tuple-element.90.after_ref), channel_id=1, source_target_pairs={{0,2},{1,3},{2,0},{3,1},{4,6},{5,7},{6,4},{7,5},{8,10},{9,11},{10,... | collective-permute-start | bytes 196616 | tf_op jit(solution)/shard_map/ppermute | solution.py:390
  30.9 4.3 %collective-permute-start.7 = (bf16[128,256]{1,0:T(8,128)(2,1)S(1)}, bf16[128,256]{1,0:T(8,128)(2,1)S(1)}, u32[]{:S(2)}, u32[]{:S(2)}) collective-permute-start(bf16[128,256]{1,0:T(8,128)(2,1)S(1)} %get-tuple-element.90.after_ref), channel_id=1, source_target_pairs={{0,1},{1,0},{2,3},{3,2},{4,5},{5,4},{6,7},{7,6},{8,9},{9,8},{10,11... | collective-permute-start | bytes 196616 | tf_op jit(solution)/shard_map/ppermute | solution.py:390
  35.2 5.9 %collective-permute-start.10 = (bf16[128,256]{1,0:T(8,128)(2,1)S(1)}, bf16[128,256]{1,0:T(8,128)(2,1)S(1)}, u32[]{:S(2)}, u32[]{:S(2)}) collective-permute-start(bf16[128,256]{1,0:T(8,128)(2,1)S(1)} %add_convert_fusion.3.refs_0_), channel_id=1, source_target_pairs={{0,4},{1,5},{2,6},{3,7},{4,0},{5,1},{6,2},{7,3},{8,12},{9,13},{10,... | collective-permute-start | bytes 196616 | tf_op jit(solution)/shard_map/ppermute | solution.py:390
  41.3 4.0 %collective-permute-start.13 = (f32[8,256]{1,0:T(8,128)S(1)}, f32[8,256]{1,0:T(8,128)S(1)}, u32[]{:S(2)}, u32[]{:S(2)}) collective-permute-start(f32[8,256]{1,0:T(8,128)S(1)} %get-tuple-element.94.refs_1_), channel_id=1, source_target_pairs={{0,24},{8,16},{16,8},{24,0},{1,25},{9,17},{17,9},{25,1},{2,26},{10... | collective-permute-start | bytes 24584 | tf_op jit(solution)/shard_map/ppermute | solution.py:390
  41.4 3.9 %collective-permute-start.12 = (f32[8,256]{1,0:T(8,128)S(1)}, f32[8,256]{1,0:T(8,128)S(1)}, u32[]{:S(2)}, u32[]{:S(2)}) collective-permute-start(f32[8,256]{1,0:T(8,128)S(1)} %get-tuple-element.94.refs_1_), channel_id=1, source_target_pairs={{0,16},{8,24},{16,0},{24,8},{1,17},{9,25},{17,1},{25,9},{2,18},{10... | collective-permute-start | bytes 24584 | tf_op jit(solution)/shard_map/ppermute | solution.py:390
  42.3 3.0 %collective-permute-start.11 = (f32[8,256]{1,0:T(8,128)S(1)}, f32[8,256]{1,0:T(8,128)S(1)}, u32[]{:S(2)}, u32[]{:S(2)}) collective-permute-start(f32[8,256]{1,0:T(8,128)S(1)} %get-tuple-element.94.refs_1_), channel_id=1, source_target_pairs={{0,8},{8,0},{16,24},{24,16},{1,9},{9,1},{17,25},{25,17},{2,10},{10... | collective-permute-start | bytes 24584 | tf_op jit(solution)/shard_map/ppermute | solution.py:390
  47.3 5.7 %collective-permute-start.16 = (bf16[128,256]{1,0:T(8,128)(2,1)S(1)}, bf16[128,256]{1,0:T(8,128)(2,1)S(1)}, u32[]{:S(2)}, u32[]{:S(2)}) collective-permute-start(bf16[128,256]{1,0:T(8,128)(2,1)S(1)} %get-tuple-element.96), channel_id=1, source_target_pairs={{0,3},{1,2},{2,1},{3,0},{4,7},{5,6},{6,5},{7,4},{8,11},{9,10},{10,... | collective-permute-start | bytes 196616 | tf_op jit(solution)/shard_map/ppermute | solution.py:390
  47.8 5.2 %collective-permute-start.15 = (bf16[128,256]{1,0:T(8,128)(2,1)S(1)}, bf16[128,256]{1,0:T(8,128)(2,1)S(1)}, u32[]{:S(2)}, u32[]{:S(2)}) collective-permute-start(bf16[128,256]{1,0:T(8,128)(2,1)S(1)} %get-tuple-element.96), channel_id=1, source_target_pairs={{0,2},{1,3},{2,0},{3,1},{4,6},{5,7},{6,4},{7,5},{8,10},{9,11},{10,... | collective-permute-start | bytes 196616 | tf_op jit(solution)/shard_map/ppermute | solution.py:390
  49.4 4.3 %collective-permute-start.14 = (bf16[128,256]{1,0:T(8,128)(2,1)S(1)}, bf16[128,256]{1,0:T(8,128)(2,1)S(1)}, u32[]{:S(2)}, u32[]{:S(2)}) collective-permute-start(bf16[128,256]{1,0:T(8,128)(2,1)S(1)} %get-tuple-element.96), channel_id=1, source_target_pairs={{0,1},{1,0},{2,3},{3,2},{4,5},{5,4},{6,7},{7,6},{8,9},{9,8},{10,11... | collective-permute-start | bytes 196616 | tf_op jit(solution)/shard_map/ppermute | solution.py:390
  53.7 5.8 %collective-permute-start.17 = (bf16[128,256]{1,0:T(8,128)(2,1)S(1)}, bf16[128,256]{1,0:T(8,128)(2,1)S(1)}, u32[]{:S(2)}, u32[]{:S(2)}) collective-permute-start(bf16[128,256]{1,0:T(8,128)(2,1)S(1)} %add_convert_fusion.2.refs_0_), channel_id=1, source_target_pairs={{0,4},{1,5},{2,6},{3,7},{4,0},{5,1},{6,2},{7,3},{8,12},{9,13},{10,... | collective-permute-start | bytes 196616 | tf_op jit(solution)/shard_map/ppermute | solution.py:390
  59.7 4.0 %collective-permute-start.20 = (f32[8,256]{1,0:T(8,128)S(1)}, f32[8,256]{1,0:T(8,128)S(1)}, u32[]{:S(2)}, u32[]{:S(2)}) collective-permute-start(f32[8,256]{1,0:T(8,128)S(1)} %get-tuple-element.99.refs_1_), channel_id=1, source_target_pairs={{0,24},{8,16},{16,8},{24,0},{1,25},{9,17},{17,9},{25,1},{2,26},{10... | collective-permute-start | bytes 24584 | tf_op jit(solution)/shard_map/ppermute | solution.py:390
  59.8 3.9 %collective-permute-start.19 = (f32[8,256]{1,0:T(8,128)S(1)}, f32[8,256]{1,0:T(8,128)S(1)}, u32[]{:S(2)}, u32[]{:S(2)}) collective-permute-start(f32[8,256]{1,0:T(8,128)S(1)} %get-tuple-element.99.refs_1_), channel_id=1, source_target_pairs={{0,16},{8,24},{16,0},{24,8},{1,17},{9,25},{17,1},{25,9},{2,18},{10... | collective-permute-start | bytes 24584 | tf_op jit(solution)/shard_map/ppermute | solution.py:390
  61.2 2.5 %collective-permute-start.18 = (f32[8,256]{1,0:T(8,128)S(1)}, f32[8,256]{1,0:T(8,128)S(1)}, u32[]{:S(2)}, u32[]{:S(2)}) collective-permute-start(f32[8,256]{1,0:T(8,128)S(1)} %get-tuple-element.99.refs_1_), channel_id=1, source_target_pairs={{0,8},{8,0},{16,24},{24,16},{1,9},{9,1},{17,25},{25,17},{2,10},{10... | collective-permute-start | bytes 24584 | tf_op jit(solution)/shard_map/ppermute | solution.py:390
  65.6 5.9 %collective-permute-start.23 = (bf16[128,256]{1,0:T(8,128)(2,1)S(1)}, bf16[128,256]{1,0:T(8,128)(2,1)S(1)}, u32[]{:S(2)}, u32[]{:S(2)}) collective-permute-start(bf16[128,256]{1,0:T(8,128)(2,1)S(1)} %get-tuple-element.106), channel_id=1, source_target_pairs={{0,3},{1,2},{2,1},{3,0},{4,7},{5,6},{6,5},{7,4},{8,11},{9,10},{10,... | collective-permute-start | bytes 196616 | tf_op jit(solution)/shard_map/ppermute | solution.py:390
  66.4 5.5 %collective-permute-start.22 = (bf16[128,256]{1,0:T(8,128)(2,1)S(1)}, bf16[128,256]{1,0:T(8,128)(2,1)S(1)}, u32[]{:S(2)}, u32[]{:S(2)}) collective-permute-start(bf16[128,256]{1,0:T(8,128)(2,1)S(1)} %get-tuple-element.106), channel_id=1, source_target_pairs={{0,2},{1,3},{2,0},{3,1},{4,6},{5,7},{6,4},{7,5},{8,10},{9,11},{10,... | collective-permute-start | bytes 196616 | tf_op jit(solution)/shard_map/ppermute | solution.py:390
  68.5 4.3 %collective-permute-start.21 = (bf16[128,256]{1,0:T(8,128)(2,1)S(1)}, bf16[128,256]{1,0:T(8,128)(2,1)S(1)}, u32[]{:S(2)}, u32[]{:S(2)}) collective-permute-start(bf16[128,256]{1,0:T(8,128)(2,1)S(1)} %get-tuple-element.106), channel_id=1, source_target_pairs={{0,1},{1,0},{2,3},{3,2},{4,5},{5,4},{6,7},{7,6},{8,9},{9,8},{10,11... | collective-permute-start | bytes 196616 | tf_op jit(solution)/shard_map/ppermute | solution.py:390
  72.8 5.4 %collective-permute-start.24 = (bf16[128,256]{1,0:T(8,128)(2,1)S(1)}, bf16[128,256]{1,0:T(8,128)(2,1)S(1)}, u32[]{:S(2)}, u32[]{:S(2)}) collective-permute-start(bf16[128,256]{1,0:T(8,128)(2,1)S(1)} %add_convert_fusion.1.refs_0_), channel_id=1, source_target_pairs={{0,4},{1,5},{2,6},{3,7},{4,0},{5,1},{6,2},{7,3},{8,12},{9,13},{10,... | collective-permute-start | bytes 196616 | tf_op jit(solution)/shard_map/ppermute | solution.py:390
  78.3 4.0 %collective-permute-start.27 = (f32[8,256]{1,0:T(8,128)S(1)}, f32[8,256]{1,0:T(8,128)S(1)}, u32[]{:S(2)}, u32[]{:S(2)}) collective-permute-start(f32[8,256]{1,0:T(8,128)S(1)} %get-tuple-element.109.refs_1_), channel_id=1, source_target_pairs={{0,24},{8,16},{16,8},{24,0},{1,25},{9,17},{17,9},{25,1},{2,26},{10... | collective-permute-start | bytes 24584 | tf_op jit(solution)/shard_map/ppermute | solution.py:390
  78.4 3.9 %collective-permute-start.26 = (f32[8,256]{1,0:T(8,128)S(1)}, f32[8,256]{1,0:T(8,128)S(1)}, u32[]{:S(2)}, u32[]{:S(2)}) collective-permute-start(f32[8,256]{1,0:T(8,128)S(1)} %get-tuple-element.109.refs_1_), channel_id=1, source_target_pairs={{0,16},{8,24},{16,0},{24,8},{1,17},{9,25},{17,1},{25,9},{2,18},{10... | collective-permute-start | bytes 24584 | tf_op jit(solution)/shard_map/ppermute | solution.py:390
  79.4 2.9 %collective-permute-start.25 = (f32[8,256]{1,0:T(8,128)S(1)}, f32[8,256]{1,0:T(8,128)S(1)}, u32[]{:S(2)}, u32[]{:S(2)}) collective-permute-start(f32[8,256]{1,0:T(8,128)S(1)} %get-tuple-element.109.refs_1_), channel_id=1, source_target_pairs={{0,8},{8,0},{16,24},{24,16},{1,9},{9,1},{17,25},{25,17},{2,10},{10... | collective-permute-start | bytes 24584 | tf_op jit(solution)/shard_map/ppermute | solution.py:390
  84.7 5.7 %collective-permute-start.30 = (bf16[128,256]{1,0:T(8,128)(2,1)S(1)}, bf16[128,256]{1,0:T(8,128)(2,1)S(1)}, u32[]{:S(2)}, u32[]{:S(2)}) collective-permute-start(bf16[128,256]{1,0:T(8,128)(2,1)S(1)} %get-tuple-element.116), channel_id=1, source_target_pairs={{0,3},{1,2},{2,1},{3,0},{4,7},{5,6},{6,5},{7,4},{8,11},{9,10},{10,... | collective-permute-start | bytes 196616 | tf_op jit(solution)/shard_map/ppermute | solution.py:390
  84.7 5.7 %collective-permute-start.29 = (bf16[128,256]{1,0:T(8,128)(2,1)S(1)}, bf16[128,256]{1,0:T(8,128)(2,1)S(1)}, u32[]{:S(2)}, u32[]{:S(2)}) collective-permute-start(bf16[128,256]{1,0:T(8,128)(2,1)S(1)} %get-tuple-element.116), channel_id=1, source_target_pairs={{0,2},{1,3},{2,0},{3,1},{4,6},{5,7},{6,4},{7,5},{8,10},{9,11},{10,... | collective-permute-start | bytes 196616 | tf_op jit(solution)/shard_map/ppermute | solution.py:390
  86.9 4.3 %collective-permute-start.28 = (bf16[128,256]{1,0:T(8,128)(2,1)S(1)}, bf16[128,256]{1,0:T(8,128)(2,1)S(1)}, u32[]{:S(2)}, u32[]{:S(2)}) collective-permute-start(bf16[128,256]{1,0:T(8,128)(2,1)S(1)} %get-tuple-element.116), channel_id=1, source_target_pairs={{0,1},{1,0},{2,3},{3,2},{4,5},{5,4},{6,7},{7,6},{8,9},{9,8},{10,11... | collective-permute-start | bytes 196616 | tf_op jit(solution)/shard_map/ppermute | solution.py:390
  91.2 5.4 %collective-permute-start.31 = (bf16[128,256]{1,0:T(8,128)(2,1)S(1)}, bf16[128,256]{1,0:T(8,128)(2,1)S(1)}, u32[]{:S(2)}, u32[]{:S(2)}) collective-permute-start(bf16[128,256]{1,0:T(8,128)(2,1)S(1)} %add_convert_fusion.refs_0_), channel_id=1, source_target_pairs={{0,4},{1,5},{2,6},{3,7},{4,0},{5,1},{6,2},{7,3},{8,12},{9,13},{10,... | collective-permute-start | bytes 196616 | tf_op jit(solution)/shard_map/ppermute | solution.py:390
  96.7 3.1 %collective-permute-start.34 = (f32[8,256]{1,0:T(8,128)S(1)}, f32[8,256]{1,0:T(8,128)S(1)}, u32[]{:S(2)}, u32[]{:S(2)}) collective-permute-start(f32[8,256]{1,0:T(8,128)S(1)} %get-tuple-element.119.refs_1_), channel_id=1, source_target_pairs={{0,24},{8,16},{16,8},{24,0},{1,25},{9,17},{17,9},{25,1},{2,26},{10... | collective-permute-start | bytes 24584 | tf_op jit(solution)/shard_map/ppermute | solution.py:390
  96.8 3.7 %collective-permute-start.33 = (f32[8,256]{1,0:T(8,128)S(1)}, f32[8,256]{1,0:T(8,128)S(1)}, u32[]{:S(2)}, u32[]{:S(2)}) collective-permute-start(f32[8,256]{1,0:T(8,128)S(1)} %get-tuple-element.119.refs_1_), channel_id=1, source_target_pairs={{0,16},{8,24},{16,0},{24,8},{1,17},{9,25},{17,1},{25,9},{2,18},{10... | collective-permute-start | bytes 24584 | tf_op jit(solution)/shard_map/ppermute | solution.py:390
  98.2 2.3 %collective-permute-start.32 = (f32[8,256]{1,0:T(8,128)S(1)}, f32[8,256]{1,0:T(8,128)S(1)}, u32[]{:S(2)}, u32[]{:S(2)}) collective-permute-start(f32[8,256]{1,0:T(8,128)S(1)} %get-tuple-element.119.refs_1_), channel_id=1, source_target_pairs={{0,8},{8,0},{16,24},{24,16},{1,9},{9,1},{17,25},{25,17},{2,10},{10... | collective-permute-start | bytes 24584 | tf_op jit(solution)/shard_map/ppermute | solution.py:390
